TPU v7x, 32 devices: a whole 2x2x4 slice. The times are simulated.
32 devices in a mesh: groups: 2 (over x), tm: 8 (over z, y), mp: 2 (over core).
Axes of the slice: x: 2, y: 2, z: 4, core: 2. Of those that a mesh axis runs over, the one named last changes fastest.
Arguments:
- frames: bfloat16 [8192, 1024], P(('groups', 'tm')), parts along dimension 0, may hold values from -6 to 6
- weight_qkv: bfloat16 [1024, 3, 1024], P(None, None, 'mp'), as said below
- weight_out: bfloat16 [1024, 1024], P('mp'), may hold values from -0.1875 to 0.1875
- proj_in: bfloat16 [1024, 8192], P('tm', 'mp'), may hold values from -0.1875 to 0.1875
- norm_gain: float32 [8192], P('mp'), may hold values from 0.28 to 2.8, as said below
- proj_kv: bfloat16 [8192, 2048], P(('mp', 'tm')), may hold values from -0.0625 to 0.0625
- shifts: int32 [256], replicated, may hold values from 0 to 255, each once
- route: int32 [8, 8], replicated, may hold values from 0 to 7, each once within a row
- d_kv: bfloat16 [2048, 2048], P(('groups', 'tm'), 'mp'), parts along dimension 0, may hold values from -3 to 3
Outputs:
- kv: bfloat16 [2048, 2048], P(('groups', 'tm'), 'mp'), parts along dimension 0
- grad_qkv: float32 [2048, 3, 1024], P(('groups', 'tm'), None, 'mp'), parts along dimension 0
- grad_out: float32 [2048, 1024], P(('groups', 'mp', 'tm')), parts along dimension 0
There are 2 independent parts, one for each index of `groups`. A program takes and returns all parts, laid end to end along the dimension named above; an argument that names none is the same for every part. Nothing has to cross between parts.
Inputs may be any that keep to these rules, and one draw needn't show every extreme that they name: Row d of route is a permutation: it names each owner for exactly one piece of source d. shifts is a permutation of the whole numbers 0 to 255. `weight_qkv`: entries of order 1024**-0.5 times a few. `norm_gain`: positive gains.
All inputs are finite; a program needn't handle non-finite values.
Results may differ from a plain program's by a relative error of at most 0.02.
Values may be sent and summed in bfloat16 or wider, within the bound.
No kernel may reach another device: no remote copies, remote signals or barrier semaphores. Data moves between devices by JAX's collectives and lax.ppermute only.
A program may use at most 128 MiB of HBM per device.

v0:
```python
import functools

import jax
import jax.numpy as jnp
from jax import lax
from jax.experimental import pallas as pl
from jax.experimental.pallas import tpu as pltpu
from jax.sharding import PartitionSpec as P

HEAD = 64
WINDOW = 256
POOL = 4
LLM_D = 8192
BF = jnp.bfloat16
F32 = jnp.float32
VMEM_LIMIT = 48 << 20


def dot(a, b):
    return jnp.dot(a, b, preferred_element_type=F32)


def dot_nt(a, b):
    return lax.dot_general(a, b, (((1,), (1,)), ((), ())), preferred_element_type=F32)


def dot_tn(a, b):
    return lax.dot_general(a, b, (((0,), (0,)), ((), ())), preferred_element_type=F32)


def swap_tm(block, mask):
    n = lax.axis_size("tm")
    return lax.ppermute(block, "tm", [(i, i ^ mask) for i in range(n)])


def swap_mp(block):
    n = lax.axis_size("mp")
    return lax.ppermute(block, "mp", [(i, n - 1 - i) for i in range(n)])


def to_tm(block, step, cross):
    n, m = lax.axis_size("tm"), lax.axis_size("mp")
    pairs = []
    for i in range(n):
        for c in range(m):
            pairs.append((i * m + c, (i + step) % n * m + (m - 1 - c if cross else c)))
    return lax.ppermute(block, ("tm", "mp"), pairs)


def gather_xor(block):
    n = lax.axis_size("tm")
    parts = [None] * n
    parts[0] = block
    for k in range(2, n, 2):
        parts[k] = swap_tm(block, k)
    parts[1] = swap_tm(block, 1)
    for k in range(2, n, 2):
        parts[k + 1] = swap_tm(parts[k], 1)
    return parts


def scatter_xor(even, odd):
    got = swap_tm(odd, 1)
    half = even.astype(F32) + got.astype(F32)
    low = half.astype(BF)
    total = half[0]
    for j in range(1, even.shape[0]):
        total = total + swap_tm(low[j], 2 * j).astype(F32)
    return total


def halving_order(n):
    order, bit = [0], n // 2
    while bit > 1:
        order = order + [k | bit for k in order]
        bit //= 2
    return order


def scatter_halving(even, odd):
    n = lax.axis_size("tm")
    total = even.astype(F32) + swap_tm(odd, 1).astype(F32)
    mask = 2
    while mask < n:
        low = total.astype(BF)
        half = low.shape[0] // 2
        total = low[:half].astype(F32) + swap_tm(low[half:], mask).astype(F32)
        mask *= 2
    return total[0]


def small_scatter(rows):
    total = rows + swap_mp(rows)
    n = rows.shape[0]
    while n > 1:
        n //= 2
        total = total[:n] + swap_tm(total[n:], n)
    return total


def small_gather(row):
    n = 1
    while n < lax.axis_size("tm"):
        row = jnp.concatenate([row, swap_tm(row, n)], axis=0)
        n *= 2
    return row


def head_mask(shape, head):
    return lax.broadcasted_iota(jnp.int32, shape, 1) // HEAD == head


def forward_kernel(at, x_ref, wq_ref, wk_ref, wv_ref, wo_ref, normed, qkv, probs, pooled, out, attn):
    shift, border = at[0], at[1]
    rows = x_ref.shape[0]
    cols = wq_ref.shape[0]

    @pl.when(pl.program_id(0) == 0)
    def _():
        x = x_ref[...].astype(F32)
        scale = lax.rsqrt(jnp.mean(x * x, axis=-1, keepdims=True) + 1e-05)
        normed[...] = (x * scale).astype(BF)
        out[...] = jnp.zeros_like(out)

    base = normed[...]
    for i, w_ref in enumerate((wq_ref, wk_ref, wv_ref)):
        qkv[i] = dot_nt(base, w_ref[...]).astype(BF)
    for w in range(rows // WINDOW):
        span = pl.ds(w * WINDOW, WINDOW)
        q, k, v = qkv[0, span, :], qkv[1, span, :], qkv[2, span, :]
        square = (WINDOW, WINDOW)
        key_at = lax.broadcasted_iota(jnp.int32, square, 0) + w * WINDOW
        query_at = lax.broadcasted_iota(jnp.int32, square, 1) + w * WINDOW
        allowed = (key_at >= border) == (query_at >= border)
        attended = None
        for h in range(cols // HEAD):
            own = head_mask(k.shape, h)
            scores = dot_nt(jnp.where(own, k, jnp.zeros_like(k)), q) * HEAD ** (-0.5)
            scores = jnp.where(allowed, scores, -1e30)
            terms = jnp.exp(scores - jnp.max(scores, axis=0, keepdims=True))
            low = (terms * (1.0 / jnp.sum(terms, axis=0, keepdims=True))).astype(BF)
            probs[0, w, h] = low
            part = dot_tn(low, v)
            attended = part if attended is None else jnp.where(own, part, attended)
        attn[span, :] = attended.astype(BF)
    tok_shape = (pooled.shape[0], rows)
    tok_of = (lax.broadcasted_iota(jnp.int32, tok_shape, 1) + shift) // POOL
    member = tok_of == lax.broadcasted_iota(jnp.int32, tok_shape, 0)
    pool = jnp.where(member, 1.0 / POOL, 0.0).astype(BF)
    low = dot(pool, attn[...]).astype(BF)
    pooled[...] = low
    out[...] += dot(low, wo_ref[...])


def encoder_forward(x_roll, w_t, weight_out, at, ext_tok):
    rows, width = x_roll.shape
    heads_w = weight_out.shape[0]
    cols = 2 * HEAD
    pairs = heads_w // cols
    windows = rows // WINDOW
    weight = lambda i: pl.BlockSpec((cols, width), lambda p, at: (i * pairs + p, 0))
    return pl.pallas_call(
        forward_kernel,
        grid_spec=pltpu.PrefetchScalarGridSpec(
            num_scalar_prefetch=1,
            grid=(pairs,),
            in_specs=[
                pl.BlockSpec((rows, width), lambda p, at: (0, 0)),
                weight(0),
                weight(1),
                weight(2),
                weight(0),
            ],
            out_specs=[
                pl.BlockSpec((rows, width), lambda p, at: (0, 0)),
                pl.BlockSpec((3, rows, cols), lambda p, at: (0, 0, p)),
                pl.BlockSpec((1, windows, 2, WINDOW, WINDOW), lambda p, at: (p, 0, 0, 0, 0)),
                pl.BlockSpec((ext_tok, cols), lambda p, at: (0, p)),
                pl.BlockSpec((ext_tok, width), lambda p, at: (0, 0)),
            ],
            scratch_shapes=[pltpu.VMEM((rows, cols), BF)],
        ),
        out_shape=[
            jax.ShapeDtypeStruct((rows, width), BF),
            jax.ShapeDtypeStruct((3, rows, heads_w), BF),
            jax.ShapeDtypeStruct((pairs, windows, 2, WINDOW, WINDOW), BF),
            jax.ShapeDtypeStruct((ext_tok, heads_w), BF),
            jax.ShapeDtypeStruct((ext_tok, width), F32),
        ],
        compiler_params=pltpu.CompilerParams(vmem_limit_bytes=VMEM_LIMIT),
        name="encoder_forward",
    )(at, x_roll, w_t, w_t, w_t, weight_out)


def out_grad_kernel(n, at, d_ref, wo_ref, pa_ref, d_attn, even, odd, turned):
    me = at[2]
    block = even.shape[1]
    d_ext = d_ref[...]
    d_attn[...] = (dot_nt(d_ext, wo_ref[...]) * (1.0 / POOL)).astype(BF)
    turned[...] = pa_ref[...].T
    for bit, ref in enumerate((even, odd)):
        for j, k in enumerate(halving_order(n)):
            start = pl.multiple_of((me ^ (k | bit)) * block, block)
            ref[j] = dot(turned[pl.ds(start, block), :], d_ext).astype(BF)


def out_grad(d_ext, weight_out, pooled_attn, at, n):
    heads_w, width = weight_out.shape
    blocks = jax.ShapeDtypeStruct((n // 2, heads_w // n, width), BF)
    whole = pl.BlockSpec(memory_space=pltpu.VMEM)
    return pl.pallas_call(
        functools.partial(out_grad_kernel, n),
        in_specs=[pl.BlockSpec(memory_space=pltpu.SMEM), whole, whole, whole],
        out_specs=[whole] * 3,
        out_shape=[jax.ShapeDtypeStruct(pooled_attn.shape, BF), blocks, blocks],
        scratch_shapes=[pltpu.VMEM((heads_w, pooled_attn.shape[0]), BF)],
        compiler_params=pltpu.CompilerParams(vmem_limit_bytes=VMEM_LIMIT),
        name="out_grad",
    )(at, d_ext, weight_out, pooled_attn)


def backward_kernel(n, at, n_ref, qkv, probs, d_ref, even, odd, turned, grads):
    shift, me = at[0], at[2]
    rows = n_ref.shape[0]
    cols = d_ref.shape[1]
    block = even.shape[2]

    @pl.when(pl.program_id(0) == 0)
    def _():
        turned[...] = n_ref[...].T

    tok_shape = (rows, d_ref.shape[0])
    tok_of = (lax.broadcasted_iota(jnp.int32, tok_shape, 0) + shift) // POOL
    member = tok_of == lax.broadcasted_iota(jnp.int32, tok_shape, 1)
    d_rows = dot(jnp.where(member, 1.0, 0.0).astype(BF), d_ref[...]).astype(BF)
    for w in range(rows // WINDOW):
        span = pl.ds(w * WINDOW, WINDOW)
        q, k, v = qkv[0, span, :], qkv[1, span, :], qkv[2, span, :]
        d_out = d_rows[w * WINDOW : (w + 1) * WINDOW]
        none = jnp.zeros_like(q)
        sums = [0.0, 0.0, 0.0]
        for h in range(cols // HEAD):
            own = head_mask(q.shape, h)
            low = probs[0, w, h]
            weight = low.astype(F32)
            d_weight = dot_nt(jnp.where(own, v, none), d_out)
            centre = jnp.sum(weight * d_weight, axis=0, keepdims=True)
            d_score = (weight * (d_weight - centre) * HEAD ** (-0.5)).astype(BF)
            sums[0] += dot_tn(d_score, jnp.where(own, k, none))
            sums[1] += dot(d_score, jnp.where(own, q, none))
            sums[2] += dot(low, jnp.where(own, d_out, none))
        for i in range(3):
            grads[span, i * cols : (i + 1) * cols] = sums[i].astype(BF)
    d_all = grads[...]
    for bit, ref in enumerate((even, odd)):
        for j, k in enumerate(halving_order(n)):
            start = pl.multiple_of((me ^ (k | bit)) * block, block)
            term = dot(turned[pl.ds(start, block), :], d_all).astype(BF)
            for i in range(3):
                ref[j, i] = term[:, i * cols : (i + 1) * cols]


def encoder_backward(normed, qkv, probs, d_attn, at, n, first, count):
    rows, width = normed.shape
    cols = 2 * HEAD
    windows = rows // WINDOW
    block = width // n
    out = pl.BlockSpec((n // 2, 3, block, cols), lambda p, at: (0, 0, 0, p))
    shape = jax.ShapeDtypeStruct((n // 2, 3, block, cols * count), BF)
    return pl.pallas_call(
        functools.partial(backward_kernel, n),
        grid_spec=pltpu.PrefetchScalarGridSpec(
            num_scalar_prefetch=1,
            grid=(count,),
            in_specs=[
                pl.BlockSpec((rows, width), lambda p, at: (0, 0)),
                pl.BlockSpec((3, rows, cols), lambda p, at: (0, 0, p + first)),
                pl.BlockSpec(
                    (1, windows, 2, WINDOW, WINDOW), lambda p, at: (p + first, 0, 0, 0, 0)
                ),
                pl.BlockSpec((d_attn.shape[0], cols), lambda p, at: (0, p + first)),
            ],
            out_specs=[out, out],
            scratch_shapes=[pltpu.VMEM((width, rows), BF), pltpu.VMEM((rows, 3 * cols), BF)],
        ),
        out_shape=[shape, shape],
        compiler_params=pltpu.CompilerParams(vmem_limit_bytes=VMEM_LIMIT),
        name="encoder_backward",
    )(at, normed, qkv, probs, d_attn)


def on_device(frames, weight_qkv, weight_out, proj_in, norm_gain, proj_kv, shifts, route, d_kv):
    n = lax.axis_size("tm")
    me = lax.axis_index("tm")
    core = lax.axis_index("mp")
    rows, width = frames.shape
    half_w = width // 2
    shift = shifts[0]
    own_tok = rows // POOL
    tail_tok = WINDOW // POOL
    ext_tok = own_tok + tail_tok
    feats = proj_kv.shape[0]
    kv_half = proj_kv.shape[1] // 2
    piece = own_tok // n

    part = lax.dynamic_slice_in_dim(frames, core * (WINDOW // 2), WINDOW // 2, 0)
    mine = to_tm(part, -1, False)
    other = swap_mp(mine)
    halo = jnp.where(
        core == 0, jnp.concatenate([mine, other], 0), jnp.concatenate([other, mine], 0)
    )
    x_roll = lax.dynamic_slice_in_dim(jnp.concatenate([frames, halo], 0), shift, rows, 0)

    proj_in, x_roll = lax.optimization_barrier((proj_in, x_roll))
    blocks = [lax.dynamic_slice_in_dim(proj_in, me * feats, feats, 1)]
    for k in range(1, n):
        blocks.append(swap_tm(lax.dynamic_slice_in_dim(proj_in, (me ^ k) * feats, feats, 1), k))
    lift_w = jnp.take(jnp.stack(blocks), me ^ jnp.arange(n, dtype=jnp.int32), axis=0)
    lift_w = lift_w.reshape(width, feats)
    gain = lax.dynamic_slice_in_dim(norm_gain, me * feats, feats, 0)

    w_t = jnp.transpose(weight_qkv, (1, 2, 0)).reshape(-1, width)
    at = jnp.stack([shift, rows * n - shift - me * rows, me]).astype(jnp.int32)
    normed, qkv, probs, pooled_attn, out_part = encoder_forward(
        x_roll, w_t, weight_out, at, ext_tok
    )
    out_low = out_part.astype(BF)
    low_own = lax.dynamic_slice_in_dim(out_low, core * half_w, half_w, 1)
    low_other = lax.dynamic_slice_in_dim(out_low, (1 - core) * half_w, half_w, 1)
    from_core = swap_mp(low_other[:own_tok])
    tail_a = to_tm(low_own[own_tok:], 1, False)
    tail_b = to_tm(low_other[own_tok:], 1, True)
    own_pool = (
        jnp.arange(rows, dtype=jnp.int32)[None, :] // POOL
        == jnp.arange(own_tok, dtype=jnp.int32)[:, None]
    ).astype(BF) * (1.0 / POOL)
    x_mean = dot(own_pool, lax.dynamic_slice_in_dim(frames, core * half_w, half_w, 1))
    pooled = (
        x_mean
        + lax.dynamic_slice_in_dim(out_part, core * half_w, half_w, 1)[:own_tok]
        + from_core.astype(F32)
    )
    tail = tail_a.astype(F32) + tail_b.astype(F32)
    pooled = jnp.concatenate([pooled[:tail_tok] + tail, pooled[tail_tok:]], 0).astype(BF)

    tok_half = jnp.concatenate(gather_xor(pooled), 0)
    tok_other = swap_mp(tok_half)
    inverse = jnp.argsort(route, axis=1).astype(jnp.int32)
    owners = me ^ jnp.arange(n, dtype=jnp.int32)
    sources = jnp.arange(n, dtype=jnp.int32)
    piece_at = (sources[None, :] ^ me) * n + inverse.T[owners]
    row_at = (piece_at[:, :, None] * piece + jnp.arange(piece, dtype=jnp.int32)).reshape(-1)
    tok = jnp.concatenate([tok_half, tok_other], 1)
    tok = jnp.take(tok, row_at, axis=0)
    lift_own = jnp.concatenate(
        [
            lax.dynamic_slice_in_dim(lift_w, core * half_w, half_w, 0),
            lax.dynamic_slice_in_dim(lift_w, (1 - core) * half_w, half_w, 0),
        ],
        0,
    )
    lifted = dot(tok, lift_own)
    squares = jnp.sum(lifted * lifted, axis=-1).reshape(n, own_tok)
    square_sum = small_scatter(squares)
    inv_rms = lax.rsqrt(square_sum / LLM_D + 1e-05)
    scaled = (lifted * gain).astype(BF)
    kv_w_own = lax.dynamic_slice_in_dim(proj_kv, core * kv_half, kv_half, 1)
    kv_w_other = lax.dynamic_slice_in_dim(proj_kv, (1 - core) * kv_half, kv_half, 1)
    from_core = swap_mp(dot(scaled, kv_w_other).astype(BF))
    kv_part = (dot(scaled, kv_w_own) + from_core.astype(F32)).astype(BF)
    kv_part = kv_part.reshape(n // 2, 2, own_tok, kv_half)
    kv_sum = scatter_xor(kv_part[:, 0], kv_part[:, 1])
    kv = (kv_sum * inv_rms.reshape(own_tok, 1)).astype(BF)
    total_cot = (kv.astype(F32) + d_kv.astype(F32)).astype(BF)
    inner = jnp.sum(total_cot.astype(F32) * kv_sum, axis=-1).reshape(1, own_tok)
    inner = inner + swap_mp(inner)
    stats = small_gather(jnp.stack([inv_rms, inner], axis=1))
    inv_all = stats[:, 0].reshape(-1, 1)
    inner_all = stats[:, 1].reshape(-1, 1)
    cot_half = jnp.concatenate(gather_xor(total_cot), 0)
    cot_other = swap_mp(cot_half)
    d_normed = dot_nt(cot_half, kv_w_own) + dot_nt(cot_other, kv_w_other)
    d_lifted = (inv_all * gain * d_normed - lifted * (inv_all**3 * inner_all / LLM_D)).astype(BF)
    d_tok = dot_nt(d_lifted, lift_own).astype(BF)
    slot_of = (
        jnp.arange(n, dtype=jnp.int32)[None, :] * 0
        + (route[sources ^ me] ^ me) * n
        + (sources ^ me)[:, None]
    )
    back_at = (slot_of[:, :, None] * piece + jnp.arange(piece, dtype=jnp.int32)).reshape(-1)
    d_tok = jnp.take(d_tok, back_at, axis=0)
    from_core = swap_mp(d_tok[:, half_w:])
    d_part = (d_tok[:, :half_w].astype(F32) + from_core.astype(F32)).astype(BF)
    d_part = d_part.reshape(n // 2, 2, own_tok, half_w)
    d_half = scatter_xor(d_part[:, 0], d_part[:, 1]).astype(BF)

    d_other = swap_mp(d_half)
    next_a = to_tm(d_half[:tail_tok], -1, False)
    next_b = to_tm(d_half[:tail_tok], -1, True)
    left = jnp.concatenate([d_half, next_a], 0)
    right = jnp.concatenate([d_other, next_b], 0)
    d_ext = jnp.where(
        core == 0, jnp.concatenate([left, right], 1), jnp.concatenate([right, left], 1)
    )
    d_attn, out_even, out_odd = out_grad(d_ext, weight_out, pooled_attn, at, n)
    grad_out = scatter_halving(out_even, out_odd)
    chunks, count = [], weight_out.shape[0] // (4 * HEAD)
    for first in range(0, 2 * count, count):
        even, odd = encoder_backward(normed, qkv, probs, d_attn, at, n, first, count)
        chunks.append(scatter_halving(even, odd))
    grad_qkv = jnp.transpose(jnp.concatenate(chunks, axis=-1), (1, 0, 2))
    return kv, grad_qkv, grad_out


def solution(mesh):
    in_specs = (
        P(("groups", "tm"), None),
        P(None, None, "mp"),
        P("mp", None),
        P("tm", "mp"),
        P("mp"),
        P(("mp", "tm"), None),
        P(),
        P(),
        P(("groups", "tm"), "mp"),
    )
    out_specs = (
        P(("groups", "tm"), "mp"),
        P(("groups", "tm"), None, "mp"),
        P(("groups", "mp", "tm"), None),
    )
    return jax.shard_map(
        on_device, mesh=mesh, in_specs=in_specs, out_specs=out_specs, check_vma=False
    )
```

profile of v0, /device:TPU:0, one launch (start us, length us, event | category | flops | bytes accessed | tf_op | source)
XLA Modules:
  0.0 358.1 jit_solution(12097001402461676589)
XLA Ops:
  1.8 6.1 %collective-permute-start = (bf16[128,1024]{1,0:T(8,128)(2,1)S(1)}, bf16[128,1024]{1,0:T(8,128)(2,1)}, u32[]{:S(2)}, u32[]{:S(2)}) collective-permute-start(bf16[128,1024]{1,0:T(8,128)(2,1)S(1)} %constant_dynamic-slice_fusion.10), channel_id=1, source_target_pairs={{0,14},{1,15},{2,0},{3,1},{4,2},{5,3},{6,4},{7,5},{8,6},{9,7},{10,... | collective-permute-start | bytes 786440 | tf_op jit(solution)/shard_map/ppermute | solution.py:47
  15.5 4.8 %copy.16 = bf16[3,512,1024]{2,1,0:T(8,128)(2,1)} copy(bf16[3,512,1024]{1,2,0:T(8,128)(2,1)} %bitcast.118) | data formatting | bytes 6291456 | tf_op jit(solution)/shard_map/transpose | solution.py:322
  28.1 15.1 %encoder_forward.1 = (bf16[512,1024]{1,0:T(8,128)(2,1)S(1)}, bf16[3,512,512]{2,1,0:T(8,128)(2,1)S(1)}, bf16[4,2,2,256,256]{4,3,2,1,0:T(8,128)(2,1)}, bf16[192,512]{1,0:T(8,128)(2,1)S(1)}, f32[192,1024]{1,0:T(8,128)S(1)}) custom-call(s32[3]{0:T(128)S(1)} %pad_add_fusion.at, bf16[512,1024]{1,0:T(8,128)(2,1)S(1)} %fusion.3.x_ref, bf16[1536,1024]{1,0:T(8,128)(2,1)} %bitcast.113, ...), custom_call_target="tpu_custom_call" | custom-call | tf_op jit(solution)/shard_map/encoder_forward/pallas_call | solution.py:162
  46.0 5.3 %collective-permute-done.4 = bf16[64,512]{1,0:T(8,128)(2,1)S(1)} collective-permute-done((bf16[64,512]{1,0:T(8,128)(2,1)S(1)}, bf16[64,512]{1,0:T(8,128)(2,1)S(1)}, u32[]{:S(2)}, u32[]{:S(2)}) %collective-permute-start.4) | collective-permute-done | bytes 65568 | tf_op jit(solution)/shard_map/ppermute | solution.py:47
  61.2 3.5 collective-permute-done.16
  72.0 6.7 %collective-permute-done.8 = bf16[128,512]{1,0:T(8,128)(2,1)S(1)} collective-permute-done((bf16[128,512]{1,0:T(8,128)(2,1)S(1)}, bf16[128,512]{1,0:T(8,128)(2,1)S(1)}, u32[]{:S(2)}, u32[]{:S(2)}) %collective-permute-start.8) | collective-permute-done | bytes 131104 | tf_op jit(solution)/shard_map/ppermute | solution.py:33
  84.6 5.1 %collective-permute-done.9 = bf16[128,512]{1,0:T(8,128)(2,1)S(1)} collective-permute-done((bf16[128,512]{1,0:T(8,128)(2,1)S(1)}, bf16[128,512]{1,0:T(8,128)(2,1)S(1)}, u32[]{:S(2)}, u32[]{:S(2)}) %collective-permute-start.9) | collective-permute-done | bytes 131104 | tf_op jit(solution)/shard_map/ppermute | solution.py:33
  103.3 8.1 %gather_fusion.3 = bf16[1024,1024]{1,0:T(8,128)(2,1)} fusion(bf16[1024,1024]{1,0:T(8,128)(2,1)} %pad_maximum_fusion, s32[1024]{0:T(1024)S(1)} %fusion.41), kind=kCustom, calls=%fused_computation.clone | custom fusion | bytes 4198400 | tf_op jit(solution)/shard_map/jit(_take)/gather | solution.py:354
  118.0 4.1 %collective-permute-done.20 = bf16[1024,1024]{1,0:T(8,128)(2,1)} collective-permute-done((bf16[1024,1024]{1,0:T(8,128)(2,1)}, bf16[1024,1024]{1,0:T(8,128)(2,1)}, u32[]{:S(2)}, u32[]{:S(2)}) %collective-permute-start.20) | collective-permute-done | bytes 2097184 | tf_op jit(solution)/shard_map/ppermute | solution.py:38
  122.1 3.6 %add_convert_fusion = bf16[1024,1024]{1,0:T(8,128)(2,1)S(1)} fusion(bf16[1024,1024]{1,0:T(8,128)(2,1)} %collective-permute-done.20, bf16[512,2048]{1,0:T(8,128)(2,1)S(1)} %copy-done, s32[]{:T(128)S(6)} %select_n.121, f32[1024,512]{0,1:T(8,128)} %copy-done.10, f32[512]{0:T(512)S(1)} %dynamic_slice.73), kind=kOutput, calls=%fused_computation.5 | convolution fusion | flops 1077936128 | bytes 7342084 | tf_op jit(solution)/shard_map/dot_general | solution.py:20
  128.0 3.6 %collective-permute-done.26 = f32[4,128]{1,0:T(4,128)S(1)} collective-permute-done((f32[4,128]{1,0:T(4,128)S(1)}, f32[4,128]{1,0:T(4,128)S(1)}, u32[]{:S(2)}, u32[]{:S(2)}) %collective-permute-start.26) | collective-permute-done | bytes 2080 | tf_op jit(solution)/shard_map/ppermute | solution.py:33
  132.0 19.4 %collective-permute-done.21 = bf16[4,128,1024]{2,1,0:T(8,128)(2,1)S(1)} collective-permute-done((bf16[4,128,1024]{2,1,0:T(8,128)(2,1)S(1)}, bf16[4,128,1024]{2,1,0:T(8,128)(2,1)S(1)}, u32[]{:S(2)}, u32[]{:S(2)}) %collective-permute-start.21) | collective-permute-done | bytes 1048608 | tf_op jit(solution)/shard_map/ppermute | solution.py:33
  152.8 3.5 collective-permute-start.22
  156.7 3.3 collective-permute-done.28
  163.1 11.7 %collective-permute-done.23 = bf16[128,1024]{1,0:T(8,128)(2,1)S(1)} collective-permute-done((bf16[128,1024]{1,0:T(8,128)(2,1)S(1)}, bf16[128,1024]{1,0:T(8,128)(2,1)S(1)}, u32[]{:S(2)}, u32[]{:S(2)}) %collective-permute-start.23) | collective-permute-done | bytes 262176 | tf_op jit(solution)/shard_map/ppermute | solution.py:33
  182.4 5.6 %collective-permute-done.34 = bf16[128,1024]{1,0:T(8,128)(2,1)} collective-permute-done((bf16[128,1024]{1,0:T(8,128)(2,1)}, bf16[128,1024]{1,0:T(8,128)(2,1)}, u32[]{:S(2)}, u32[]{:S(2)}) %collective-permute-start.34) | collective-permute-done | bytes 262176 | tf_op jit(solution)/shard_map/ppermute | solution.py:33
  190.6 6.9 %collective-permute-done.36 = bf16[128,1024]{1,0:T(8,128)(2,1)} collective-permute-done((bf16[128,1024]{1,0:T(8,128)(2,1)}, bf16[128,1024]{1,0:T(8,128)(2,1)}, u32[]{:S(2)}, u32[]{:S(2)}) %collective-permute-start.36) | collective-permute-done | bytes 262176 | tf_op jit(solution)/shard_map/ppermute | solution.py:33
  217.3 3.3 collective-permute-done.31
  221.3 3.9 %collective-permute-done.32 = f32[4,2,128]{2,1,0:T(2,128)S(1)} collective-permute-done((f32[4,2,128]{2,1,0:T(2,128)S(1)}, f32[4,2,128]{2,1,0:T(2,128)S(1)}, u32[]{:S(2)}, u32[]{:S(2)}) %collective-permute-start.32) | collective-permute-done | bytes 4128 | tf_op jit(solution)/shard_map/ppermute | solution.py:33
  225.2 4.2 %fusion.5 = f32[1024,512]{0,1:T(8,128)} fusion(bf16[1024,1024]{1,0:T(8,128)(2,1)} %collective-permute-done.40, bf16[512,2048]{1,0:T(8,128)(2,1)S(1)} %copy-done, s32[]{:T(128)S(6)} %select_n.122), kind=kOutput, calls=%fused_computation.31 | convolution fusion | flops 1073741824 | bytes 5242884 | tf_op jit(solution)/shard_map/dot_general | solution.py:24
  229.4 7.0 %convolution_convert_fusion = bf16[1024,1024]{1,0:T(8,128)(2,1)} fusion(f32[1024,512]{0,1:T(8,128)} %copy-done.10, f32[1024,512]{0,1:T(8,128)} %fusion.5, bf16[1024,1024]{1,0:T(8,128)(2,1)} %constant_dynamic-update-slice_fusion.9, f32[1024]{0:T(1024)S(1)} %fusion.40, f32[1024]{0:T(1024)S(1)} %bitcast.123, f32[512]{0:T(512)S(1)} %dynamic_slice.73, ...), kind=kOutput, calls=%fused_computation.16 | convolution fusion | flops 2153775104 | bytes 10496004 | tf_op jit(solution)/shard_map/dot_general | solution.py:24
  236.4 7.9 %gather_fusion.4 = bf16[1024,1024]{1,0:T(8,128)(2,1)} fusion(bf16[1024,1024]{1,0:T(8,128)(2,1)} %convolution_convert_fusion, s32[1024]{0:T(1024)S(1)} %fusion.42), kind=kCustom, calls=%fused_computation.1.clone | custom fusion | bytes 4198400 | tf_op jit(solution)/shard_map/jit(_take)/gather | solution.py:391
  250.1 13.4 %collective-permute-done.42 = bf16[4,128,512]{2,1,0:T(8,128)(2,1)S(1)} collective-permute-done((bf16[4,128,512]{2,1,0:T(8,128)(2,1)S(1)}, bf16[4,128,512]{2,1,0:T(8,128)(2,1)S(1)}, u32[]{:S(2)}, u32[]{:S(2)}) %collective-permute-start.42) | collective-permute-done | bytes 524320 | tf_op jit(solution)/shard_map/ppermute | solution.py:33
  268.2 3.8 %collective-permute-done.45 = bf16[128,512]{1,0:T(8,128)(2,1)S(1)} collective-permute-done((bf16[128,512]{1,0:T(8,128)(2,1)S(1)}, bf16[128,512]{1,0:T(8,128)(2,1)S(1)}, u32[]{:S(2)}, u32[]{:S(2)}) %collective-permute-start.45) | collective-permute-done | bytes 131104 | tf_op jit(solution)/shard_map/ppermute | solution.py:33
  272.1 4.9 %collective-permute-done.44 = bf16[128,512]{1,0:T(8,128)(2,1)S(1)} collective-permute-done((bf16[128,512]{1,0:T(8,128)(2,1)S(1)}, bf16[128,512]{1,0:T(8,128)(2,1)S(1)}, u32[]{:S(2)}, u32[]{:S(2)}) %collective-permute-start.44) | collective-permute-done | bytes 131104 | tf_op jit(solution)/shard_map/ppermute | solution.py:33
  286.9 6.6 %encoder_backward.3 = (bf16[4,3,128,256]{3,2,1,0:T(8,128)(2,1)S(1)}, bf16[4,3,128,256]{3,2,1,0:T(8,128)(2,1)S(1)}) custom-call(s32[3]{0:T(128)S(1)} %pad_add_fusion.at, bf16[512,1024]{1,0:T(8,128)(2,1)S(1)} %get-tuple-element.23.n_ref, bf16[3,512,512]{2,1,0:T(8,128)(2,1)S(1)} %copy-done.2, bf16[4,2,2,256,256]{4,3,2,1,0:T(8,128)(2,1)} %get-tuple-element.25.probs, ...), custom_call_target="tpu_custom_call" | custom-call | tf_op jit(solution)/shard_map/encoder_backward/pallas_call | solution.py:270
  294.5 6.6 %encoder_backward.2 = (bf16[4,3,128,256]{3,2,1,0:T(8,128)(2,1)S(1)}, bf16[4,3,128,256]{3,2,1,0:T(8,128)(2,1)S(1)}) custom-call(s32[3]{0:T(128)S(1)} %pad_add_fusion.at, bf16[512,1024]{1,0:T(8,128)(2,1)S(1)} %get-tuple-element.23.n_ref, bf16[3,512,512]{2,1,0:T(8,128)(2,1)S(1)} %copy-done.2, bf16[4,2,2,256,256]{4,3,2,1,0:T(8,128)(2,1)} %get-tuple-element.25.probs, ...), custom_call_target="tpu_custom_call" | custom-call | tf_op jit(solution)/shard_map/encoder_backward/pallas_call | solution.py:270
  302.6 14.9 %collective-permute-done.52 = bf16[4,3,128,256]{3,2,1,0:T(8,128)(2,1)S(1)} collective-permute-done((bf16[4,3,128,256]{3,2,1,0:T(8,128)(2,1)S(1)}, bf16[4,3,128,256]{3,2,1,0:T(8,128)(2,1)S(1)}, u32[]{:S(2)}, u32[]{:S(2)}) %collective-permute-start.52) | collective-permute-done | bytes 786464 | tf_op jit(solution)/shard_map/ppermute | solution.py:33
  321.2 11.0 %collective-permute-done.49 = bf16[4,3,128,256]{3,2,1,0:T(8,128)(2,1)S(1)} collective-permute-done((bf16[4,3,128,256]{3,2,1,0:T(8,128)(2,1)S(1)}, bf16[4,3,128,256]{3,2,1,0:T(8,128)(2,1)S(1)}, u32[]{:S(2)}, u32[]{:S(2)}) %collective-permute-start.49) | collective-permute-done | bytes 786464 | tf_op jit(solution)/shard_map/ppermute | solution.py:33
  333.6 4.1 %collective-permute-start.54 = (bf16[1,3,128,256]{3,2,1,0:T(8,128)(2,1)S(1)}, bf16[1,3,128,256]{3,2,1,0:T(8,128)(2,1)S(1)}, u32[]{:S(2)}, u32[]{:S(2)}) collective-permute-start(bf16[1,3,128,256]{3,2,1,0:T(8,128)(2,1)S(1)} %slice.206), channel_id=1, source_target_pairs={{0,8},{2,10},{4,12},{6,14},{8,0},{10,2},{12,4},{14,6},{1,9},{3,11}... | collective-permute-start | bytes 589832 | tf_op jit(solution)/shard_map/ppermute | solution.py:33
  337.7 8.1 %collective-permute-done.50 = bf16[2,3,128,256]{3,2,1,0:T(8,128)(2,1)S(1)} collective-permute-done((bf16[2,3,128,256]{3,2,1,0:T(8,128)(2,1)S(1)}, bf16[2,3,128,256]{3,2,1,0:T(8,128)(2,1)S(1)}, u32[]{:S(2)}, u32[]{:S(2)}) %collective-permute-start.50) | collective-permute-done | bytes 393248 | tf_op jit(solution)/shard_map/ppermute | solution.py:33
  348.7 8.3 %collective-permute-done.51 = bf16[1,3,128,256]{3,2,1,0:T(8,128)(2,1)S(1)} collective-permute-done((bf16[1,3,128,256]{3,2,1,0:T(8,128)(2,1)S(1)}, bf16[1,3,128,256]{3,2,1,0:T(8,128)(2,1)S(1)}, u32[]{:S(2)}, u32[]{:S(2)}) %collective-permute-start.51) | collective-permute-done | bytes 196640 | tf_op jit(solution)/shard_map/ppermute | solution.py:33
  (226 shorter events, 129.7 us)
Async XLA Ops:
  1.8 11.6 %collective-permute-start = (bf16[128,1024]{1,0:T(8,128)(2,1)S(1)}, bf16[128,1024]{1,0:T(8,128)(2,1)}, u32[]{:S(2)}, u32[]{:S(2)}) collective-permute-start(bf16[128,1024]{1,0:T(8,128)(2,1)S(1)} %constant_dynamic-slice_fusion.10), channel_id=1, source_target_pairs={{0,14},{1,15},{2,0},{3,1},{4,2},{5,3},{6,4},{7,5},{8,6},{9,7},{10,... | collective-permute-start | bytes 786440 | tf_op jit(solution)/shard_map/ppermute | solution.py:47
  24.6 30.5 %collective-permute-start.13 = (bf16[128,512]{1,0:T(8,128)(2,1)S(1)}, bf16[128,512]{1,0:T(8,128)(2,1)S(1)}, u32[]{:S(2)}, u32[]{:S(2)}) collective-permute-start(bf16[128,512]{1,0:T(8,128)(2,1)S(1)} %get-tuple-element.56), channel_id=1, source_target_pairs={{0,2},{2,0},{4,6},{6,4},{8,10},{10,8},{12,14},{14,12},{1,3},{3,1},... | collective-permute-start | bytes 393224 | tf_op jit(solution)/shard_map/ppermute | solution.py:33
  25.1 32.3 %collective-permute-start.14 = (bf16[128,512]{1,0:T(8,128)(2,1)S(1)}, bf16[128,512]{1,0:T(8,128)(2,1)S(1)}, u32[]{:S(2)}, u32[]{:S(2)}) collective-permute-start(bf16[128,512]{1,0:T(8,128)(2,1)S(1)} %get-tuple-element.55), channel_id=1, source_target_pairs={{0,4},{2,6},{4,0},{6,2},{8,12},{10,14},{12,8},{14,10},{1,5},{3,7},... | collective-permute-start | bytes 393224 | tf_op jit(solution)/shard_map/ppermute | solution.py:33
  26.7 32.4 %collective-permute-start.15 = (bf16[128,512]{1,0:T(8,128)(2,1)S(1)}, bf16[128,512]{1,0:T(8,128)(2,1)S(1)}, u32[]{:S(2)}, u32[]{:S(2)}) collective-permute-start(bf16[128,512]{1,0:T(8,128)(2,1)S(1)} %get-tuple-element.54), channel_id=1, source_target_pairs={{0,6},{2,4},{4,2},{6,0},{8,14},{10,12},{12,10},{14,8},{1,7},{3,5},... | collective-permute-start | bytes 393224 | tf_op jit(solution)/shard_map/ppermute | solution.py:33
  51.2 13.4 %collective-permute-start.16 = (bf16[128,512]{1,0:T(8,128)(2,1)S(1)}, bf16[128,512]{1,0:T(8,128)(2,1)S(1)}, u32[]{:S(2)}, u32[]{:S(2)}) collective-permute-start(bf16[128,512]{1,0:T(8,128)(2,1)S(1)} %get-tuple-element.53), channel_id=1, source_target_pairs={{0,8},{2,10},{4,12},{6,14},{8,0},{10,2},{12,4},{14,6},{1,9},{3,11}... | collective-permute-start | bytes 393224 | tf_op jit(solution)/shard_map/ppermute | solution.py:33
  52.9 39.9 %collective-permute-start.17 = (bf16[128,512]{1,0:T(8,128)(2,1)S(1)}, bf16[128,512]{1,0:T(8,128)(2,1)S(1)}, u32[]{:S(2)}, u32[]{:S(2)}) collective-permute-start(bf16[128,512]{1,0:T(8,128)(2,1)S(1)} %get-tuple-element.52), channel_id=1, source_target_pairs={{0,10},{2,8},{4,14},{6,12},{8,2},{10,0},{12,6},{14,4},{1,11},{3,9}... | collective-permute-start | bytes 393224 | tf_op jit(solution)/shard_map/ppermute | solution.py:33
  55.1 38.4 %collective-permute-start.18 = (bf16[128,512]{1,0:T(8,128)(2,1)S(1)}, bf16[128,512]{1,0:T(8,128)(2,1)S(1)}, u32[]{:S(2)}, u32[]{:S(2)}) collective-permute-start(bf16[128,512]{1,0:T(8,128)(2,1)S(1)} %get-tuple-element.51), channel_id=1, source_target_pairs={{0,12},{2,14},{4,8},{6,10},{8,4},{10,6},{12,0},{14,2},{1,13},{3,15... | collective-permute-start | bytes 393224 | tf_op jit(solution)/shard_map/ppermute | solution.py:33
  59.1 11.5 %collective-permute-start.6 = (bf16[128,512]{1,0:T(8,128)(2,1)S(1)}, bf16[128,512]{1,0:T(8,128)(2,1)S(1)}, u32[]{:S(2)}, u32[]{:S(2)}) collective-permute-start(bf16[128,512]{1,0:T(8,128)(2,1)S(1)} %pad_maximum_fusion.4), channel_id=1, source_target_pairs={{0,4},{2,6},{4,0},{6,2},{8,12},{10,14},{12,8},{14,10},{1,5},{3,7},... | collective-permute-start | bytes 393224 | tf_op jit(solution)/shard_map/ppermute | solution.py:33
  64.7 14.0 %collective-permute-start.8 = (bf16[128,512]{1,0:T(8,128)(2,1)S(1)}, bf16[128,512]{1,0:T(8,128)(2,1)S(1)}, u32[]{:S(2)}, u32[]{:S(2)}) collective-permute-start(bf16[128,512]{1,0:T(8,128)(2,1)S(1)} %pad_maximum_fusion.4), channel_id=1, source_target_pairs={{0,8},{2,10},{4,12},{6,14},{8,0},{10,2},{12,4},{14,6},{1,9},{3,11}... | collective-permute-start | bytes 393224 | tf_op jit(solution)/shard_map/ppermute | solution.py:33
  65.4 15.9 %collective-permute-start.10 = (bf16[128,512]{1,0:T(8,128)(2,1)S(1)}, bf16[128,512]{1,0:T(8,128)(2,1)S(1)}, u32[]{:S(2)}, u32[]{:S(2)}) collective-permute-start(bf16[128,512]{1,0:T(8,128)(2,1)S(1)} %pad_maximum_fusion.4), channel_id=1, source_target_pairs={{0,12},{2,14},{4,8},{6,10},{8,4},{10,6},{12,0},{14,2},{1,13},{3,15... | collective-permute-start | bytes 393224 | tf_op jit(solution)/shard_map/ppermute | solution.py:33
  70.6 12.4 %collective-permute-start.7 = (bf16[128,512]{1,0:T(8,128)(2,1)S(1)}, bf16[128,512]{1,0:T(8,128)(2,1)S(1)}, u32[]{:S(2)}, u32[]{:S(2)}) collective-permute-start(bf16[128,512]{1,0:T(8,128)(2,1)S(1)} %collective-permute-done.6), channel_id=1, source_target_pairs={{0,2},{2,0},{4,6},{6,4},{8,10},{10,8},{12,14},{14,12},{1,3},{3,1},... | collective-permute-start | bytes 393224 | tf_op jit(solution)/shard_map/ppermute | solution.py:33
  78.7 15.4 %collective-permute-start.19 = (bf16[128,512]{1,0:T(8,128)(2,1)S(1)}, bf16[128,512]{1,0:T(8,128)(2,1)S(1)}, u32[]{:S(2)}, u32[]{:S(2)}) collective-permute-start(bf16[128,512]{1,0:T(8,128)(2,1)S(1)} %get-tuple-element.50), channel_id=1, source_target_pairs={{0,14},{2,12},{4,10},{6,8},{8,6},{10,4},{12,2},{14,0},{1,15},{3,13... | collective-permute-start | bytes 393224 | tf_op jit(solution)/shard_map/ppermute | solution.py:33
  125.8 25.5 %collective-permute-start.21 = (bf16[4,128,1024]{2,1,0:T(8,128)(2,1)S(1)}, bf16[4,128,1024]{2,1,0:T(8,128)(2,1)S(1)}, u32[]{:S(2)}, u32[]{:S(2)}) collective-permute-start(bf16[4,128,1024]{2,1,0:T(8,128)(2,1)S(1)} %slice_bitcast_fusion), channel_id=1, source_target_pairs={{0,2},{2,0},{4,6},{6,4},{8,10},{10,8},{12,14},{14,12},{1,3},{3,1},... | collective-permute-start | bytes 3145736 | tf_op jit(solution)/shard_map/ppermute | solution.py:33
  131.7 24.7 %collective-permute-start.27 = (f32[2,128]{1,0:T(2,128)S(1)}, f32[2,128]{1,0:T(2,128)S(1)}, u32[]{:S(2)}, u32[]{:S(2)}) collective-permute-start(f32[2,128]{1,0:T(2,128)S(1)} %slice.144), channel_id=1, source_target_pairs={{0,4},{2,6},{4,0},{6,2},{8,12},{10,14},{12,8},{14,10},{1,5},{3,7},... | collective-permute-start | bytes 3080 | tf_op jit(solution)/shard_map/ppermute | solution.py:33
  151.9 11.2 %collective-permute-start.24 = (bf16[128,1024]{1,0:T(8,128)(2,1)S(1)}, bf16[128,1024]{1,0:T(8,128)(2,1)S(1)}, u32[]{:S(2)}, u32[]{:S(2)}) collective-permute-start(bf16[128,1024]{1,0:T(8,128)(2,1)S(1)} %get-tuple-element.46), channel_id=1, source_target_pairs={{0,12},{2,14},{4,8},{6,10},{8,4},{10,6},{12,0},{14,2},{1,13},{3,15... | collective-permute-start | bytes 786440 | tf_op jit(solution)/shard_map/ppermute | solution.py:33
  152.8 22.0 %collective-permute-start.23 = (bf16[128,1024]{1,0:T(8,128)(2,1)S(1)}, bf16[128,1024]{1,0:T(8,128)(2,1)S(1)}, u32[]{:S(2)}, u32[]{:S(2)}) collective-permute-start(bf16[128,1024]{1,0:T(8,128)(2,1)S(1)} %get-tuple-element.47), channel_id=1, source_target_pairs={{0,8},{2,10},{4,12},{6,14},{8,0},{10,2},{12,4},{14,6},{1,9},{3,11}... | collective-permute-start | bytes 786440 | tf_op jit(solution)/shard_map/ppermute | solution.py:33
  152.8 22.0 %collective-permute-start.22 = (bf16[128,1024]{1,0:T(8,128)(2,1)S(1)}, bf16[128,1024]{1,0:T(8,128)(2,1)S(1)}, u32[]{:S(2)}, u32[]{:S(2)}) collective-permute-start(bf16[128,1024]{1,0:T(8,128)(2,1)S(1)} %get-tuple-element.45), channel_id=1, source_target_pairs={{0,4},{2,6},{4,0},{6,2},{8,12},{10,14},{12,8},{14,10},{1,5},{3,7},... | collective-permute-start | bytes 786440 | tf_op jit(solution)/shard_map/ppermute | solution.py:33
  175.9 12.1 %collective-permute-start.34 = (bf16[128,1024]{1,0:T(8,128)(2,1)}, bf16[128,1024]{1,0:T(8,128)(2,1)}, u32[]{:S(2)}, u32[]{:S(2)}) collective-permute-start(bf16[128,1024]{1,0:T(8,128)(2,1)} %get-tuple-element.35), channel_id=1, source_target_pairs={{0,4},{2,6},{4,0},{6,2},{8,12},{10,14},{12,8},{14,10},{1,5},{3,7},... | collective-permute-start | bytes 786440 | tf_op jit(solution)/shard_map/ppermute | solution.py:33
  175.9 21.7 %collective-permute-start.36 = (bf16[128,1024]{1,0:T(8,128)(2,1)}, bf16[128,1024]{1,0:T(8,128)(2,1)}, u32[]{:S(2)}, u32[]{:S(2)}) collective-permute-start(bf16[128,1024]{1,0:T(8,128)(2,1)} %get-tuple-element.35), channel_id=1, source_target_pairs={{0,8},{2,10},{4,12},{6,14},{8,0},{10,2},{12,4},{14,6},{1,9},{3,11}... | collective-permute-start | bytes 786440 | tf_op jit(solution)/shard_map/ppermute | solution.py:33
  178.6 20.5 %collective-permute-start.33 = (bf16[128,1024]{1,0:T(8,128)(2,1)}, bf16[128,1024]{1,0:T(8,128)(2,1)}, u32[]{:S(2)}, u32[]{:S(2)}) collective-permute-start(bf16[128,1024]{1,0:T(8,128)(2,1)} %get-tuple-element.35), channel_id=1, source_target_pairs={{0,2},{2,0},{4,6},{6,4},{8,10},{10,8},{12,14},{14,12},{1,3},{3,1},... | collective-permute-start | bytes 786440 | tf_op jit(solution)/shard_map/ppermute | solution.py:33
  180.6 21.8 %collective-permute-start.38 = (bf16[128,1024]{1,0:T(8,128)(2,1)}, bf16[128,1024]{1,0:T(8,128)(2,1)S(1)}, u32[]{:S(2)}, u32[]{:S(2)}) collective-permute-start(bf16[128,1024]{1,0:T(8,128)(2,1)} %get-tuple-element.35), channel_id=1, source_target_pairs={{0,12},{2,14},{4,8},{6,10},{8,4},{10,6},{12,0},{14,2},{1,13},{3,15... | collective-permute-start | bytes 786440 | tf_op jit(solution)/shard_map/ppermute | solution.py:33
  188.0 14.9 %collective-permute-start.35 = (bf16[128,1024]{1,0:T(8,128)(2,1)}, bf16[128,1024]{1,0:T(8,128)(2,1)S(1)}, u32[]{:S(2)}, u32[]{:S(2)}) collective-permute-start(bf16[128,1024]{1,0:T(8,128)(2,1)} %collective-permute-done.34), channel_id=1, source_target_pairs={{0,2},{2,0},{4,6},{6,4},{8,10},{10,8},{12,14},{14,12},{1,3},{3,1},... | collective-permute-start | bytes 786440 | tf_op jit(solution)/shard_map/ppermute | solution.py:33
  209.5 15.7 %collective-permute-start.40 = (bf16[1024,1024]{1,0:T(8,128)(2,1)}, bf16[1024,1024]{1,0:T(8,128)(2,1)}, u32[]{:S(2)}, u32[]{:S(2)}) collective-permute-start(bf16[1024,1024]{1,0:T(8,128)(2,1)} %constant_dynamic-update-slice_fusion.9), channel_id=1, source_target_pairs={{0,1},{1,0},{2,3},{3,2},{4,5},{5,4},{6,7},{7,6},{8,9},{9,8},{10,11... | collective-permute-start | bytes 6291464 | tf_op jit(solution)/shard_map/ppermute | solution.py:38
  249.5 14.0 %collective-permute-start.42 = (bf16[4,128,512]{2,1,0:T(8,128)(2,1)S(1)}, bf16[4,128,512]{2,1,0:T(8,128)(2,1)S(1)}, u32[]{:S(2)}, u32[]{:S(2)}) collective-permute-start(bf16[4,128,512]{2,1,0:T(8,128)(2,1)S(1)} %slice_bitcast_fusion.2), channel_id=1, source_target_pairs={{0,2},{2,0},{4,6},{6,4},{8,10},{10,8},{12,14},{14,12},{1,3},{3,1},... | collective-permute-start | bytes 1572872 | tf_op jit(solution)/shard_map/ppermute | solution.py:33
  285.7 16.6 %collective-permute-start.55 = (bf16[4,64,1024]{2,1,0:T(8,128)(2,1)S(1)}, bf16[4,64,1024]{2,1,0:T(8,128)(2,1)S(1)}, u32[]{:S(2)}, u32[]{:S(2)}) collective-permute-start(bf16[4,64,1024]{2,1,0:T(8,128)(2,1)S(1)} %get-tuple-element.33), channel_id=1, source_target_pairs={{0,2},{2,0},{4,6},{6,4},{8,10},{10,8},{12,14},{14,12},{1,3},{3,1},... | collective-permute-start | bytes 1572872 | tf_op jit(solution)/shard_map/ppermute | solution.py:33
  293.5 24.0 %collective-permute-start.52 = (bf16[4,3,128,256]{3,2,1,0:T(8,128)(2,1)S(1)}, bf16[4,3,128,256]{3,2,1,0:T(8,128)(2,1)S(1)}, u32[]{:S(2)}, u32[]{:S(2)}) collective-permute-start(bf16[4,3,128,256]{3,2,1,0:T(8,128)(2,1)S(1)} %get-tuple-element.31), channel_id=1, source_target_pairs={{0,2},{2,0},{4,6},{6,4},{8,10},{10,8},{12,14},{14,12},{1,3},{3,1},... | collective-permute-start | bytes 2359304 | tf_op jit(solution)/shard_map/ppermute | solution.py:33
  301.1 31.1 %collective-permute-start.49 = (bf16[4,3,128,256]{3,2,1,0:T(8,128)(2,1)S(1)}, bf16[4,3,128,256]{3,2,1,0:T(8,128)(2,1)S(1)}, u32[]{:S(2)}, u32[]{:S(2)}) collective-permute-start(bf16[4,3,128,256]{3,2,1,0:T(8,128)(2,1)S(1)} %get-tuple-element.29), channel_id=1, source_target_pairs={{0,2},{2,0},{4,6},{6,4},{8,10},{10,8},{12,14},{14,12},{1,3},{3,1},... | collective-permute-start | bytes 2359304 | tf_op jit(solution)/shard_map/ppermute | solution.py:33
  302.5 15.5 %collective-permute-start.56 = (bf16[2,64,1024]{2,1,0:T(8,128)(2,1)S(1)}, bf16[2,64,1024]{2,1,0:T(8,128)(2,1)S(1)}, u32[]{:S(2)}, u32[]{:S(2)}) collective-permute-start(bf16[2,64,1024]{2,1,0:T(8,128)(2,1)S(1)} %slice.208), channel_id=1, source_target_pairs={{0,4},{2,6},{4,0},{6,2},{8,12},{10,14},{12,8},{14,10},{1,5},{3,7},... | collective-permute-start | bytes 786440 | tf_op jit(solution)/shard_map/ppermute | solution.py:33
  317.8 15.7 %collective-permute-start.53 = (bf16[2,3,128,256]{3,2,1,0:T(8,128)(2,1)S(1)}, bf16[2,3,128,256]{3,2,1,0:T(8,128)(2,1)S(1)}, u32[]{:S(2)}, u32[]{:S(2)}) collective-permute-start(bf16[2,3,128,256]{3,2,1,0:T(8,128)(2,1)S(1)} %slice.204), channel_id=1, source_target_pairs={{0,4},{2,6},{4,0},{6,2},{8,12},{10,14},{12,8},{14,10},{1,5},{3,7},... | collective-permute-start | bytes 1179656 | tf_op jit(solution)/shard_map/ppermute | solution.py:33
  318.1 14.7 %collective-permute-start.57 = (bf16[1,64,1024]{2,1,0:T(8,128)(2,1)S(1)}, bf16[1,64,1024]{2,1,0:T(8,128)(2,1)S(1)}, u32[]{:S(2)}, u32[]{:S(2)}) collective-permute-start(bf16[1,64,1024]{2,1,0:T(8,128)(2,1)S(1)} %slice.210), channel_id=1, source_target_pairs={{0,8},{2,10},{4,12},{6,14},{8,0},{10,2},{12,4},{14,6},{1,9},{3,11}... | collective-permute-start | bytes 393224 | tf_op jit(solution)/shard_map/ppermute | solution.py:33
  332.5 13.3 %collective-permute-start.50 = (bf16[2,3,128,256]{3,2,1,0:T(8,128)(2,1)S(1)}, bf16[2,3,128,256]{3,2,1,0:T(8,128)(2,1)S(1)}, u32[]{:S(2)}, u32[]{:S(2)}) collective-permute-start(bf16[2,3,128,256]{3,2,1,0:T(8,128)(2,1)S(1)} %slice.200), channel_id=1, source_target_pairs={{0,4},{2,6},{4,0},{6,2},{8,12},{10,14},{12,8},{14,10},{1,5},{3,7},... | collective-permute-start | bytes 1179656 | tf_op jit(solution)/shard_map/ppermute | solution.py:33
  333.6 15.1 %collective-permute-start.54 = (bf16[1,3,128,256]{3,2,1,0:T(8,128)(2,1)S(1)}, bf16[1,3,128,256]{3,2,1,0:T(8,128)(2,1)S(1)}, u32[]{:S(2)}, u32[]{:S(2)}) collective-permute-start(bf16[1,3,128,256]{3,2,1,0:T(8,128)(2,1)S(1)} %slice.206), channel_id=1, source_target_pairs={{0,8},{2,10},{4,12},{6,14},{8,0},{10,2},{12,4},{14,6},{1,9},{3,11}... | collective-permute-start | bytes 589832 | tf_op jit(solution)/shard_map/ppermute | solution.py:33
  (37 other events, 424.2 us)
where the time goes:
time: 359 us; the launch traced here: 358 us
  waiting for transfers between devices  172 us (48%)
  starting transfers between devices  64.2 us (18%)
  local copies, waits for them, and re-layouts  50.8 us (14%)
  Pallas kernels  29.9 us (8%)
  matrix products  21.1 us (6%)
  other arithmetic  16.4 us (5%)
  between operations  3.92 us (1%)
    ppermute x44, waiting for transfers between devices, swap_tm(): return lax.ppermute(block, 'tm', [(i, i ^ mask) for i in range(n)])  149 us
    ppermute x44, starting transfers between devices, swap_tm(): return lax.ppermute(block, 'tm', [(i, i ^ mask) for i in range(n)])  51.6 us
    unnamed x45, local copies, waits for them, and re-layouts  19 us
    pallas_call x1, Pallas kernels, encoder_forward(): pl.pallas_call(forward_kernel, grid_spec=pltpu.PrefetchScalarGridSpec(num...  15.1 us
    pallas_call x2, Pallas kernels, encoder_backward(): pl.pallas_call(functools.partial(backward_kernel, n), grid_spec=pltpu.Pre...  13.3 us
    ppermute x5, waiting for transfers between devices, to_tm(): return lax.ppermute(block, ('tm', 'mp'), pairs)  11.9 us
    dot_general x2, matrix products, dot_nt(): lax.dot_general(a, b, (((1,), (1,)), ((), ())), preferred_element_type=F32)  11.2 us
    ppermute x5, starting transfers between devices, to_tm(): return lax.ppermute(block, ('tm', 'mp'), pairs)  11 us
  transfers between devices with their start and end apart: 58, of which 33 were waited for; matrix products, arithmetic and copies ran while one was open for 11% of the time, Pallas kernels for 8%

commit v1 on v0

--- a/solution.py
+++ b/solution.py
@@ -2,6 +2,7 @@
 
 import jax
 import jax.numpy as jnp
+import numpy as np
 from jax import lax
 from jax.experimental import pallas as pl
 from jax.experimental.pallas import tpu as pltpu
@@ -14,6 +15,8 @@
 BF = jnp.bfloat16
 F32 = jnp.float32
 VMEM_LIMIT = 48 << 20
+SPLIT = 1
+CHUNK = 512
 
 
 def dot(a, b):
@@ -47,63 +50,45 @@
     return lax.ppermute(block, ("tm", "mp"), pairs)
 
 
-def gather_xor(block):
+def offsets(masks):
+    order = [0]
+    for mask in reversed(masks):
+        order = order + [k | mask for k in order]
+    return order
+
+
+def tm_bits():
     n = lax.axis_size("tm")
-    parts = [None] * n
-    parts[0] = block
-    for k in range(2, n, 2):
-        parts[k] = swap_tm(block, k)
-    parts[1] = swap_tm(block, 1)
-    for k in range(2, n, 2):
-        parts[k + 1] = swap_tm(parts[k], 1)
-    return parts
-
-
-def scatter_xor(even, odd):
-    got = swap_tm(odd, 1)
-    half = even.astype(F32) + got.astype(F32)
-    low = half.astype(BF)
-    total = half[0]
-    for j in range(1, even.shape[0]):
-        total = total + swap_tm(low[j], 2 * j).astype(F32)
-    return total
-
-
-def halving_order(n):
-    order, bit = [0], n // 2
-    while bit > 1:
-        order = order + [k | bit for k in order]
-        bit //= 2
-    return order
-
-
-def scatter_halving(even, odd):
-    n = lax.axis_size("tm")
-    total = even.astype(F32) + swap_tm(odd, 1).astype(F32)
-    mask = 2
-    while mask < n:
-        low = total.astype(BF)
+    return [1 << i for i in range(n.bit_length() - 1)]
+
+
+def group_bits():
+    return [bit for bit in tm_bits() if bit != SPLIT]
+
+
+def gather_doubling(block, masks):
+    block = block[None]
+    for mask in reversed(masks):
+        block = jnp.concatenate([block, swap_tm(block, mask)], axis=0)
+    return block
+
+
+def scatter_halving(blocks, masks, kind):
+    total = blocks
+    for mask in masks:
+        low = total.astype(kind)
         half = low.shape[0] // 2
         total = low[:half].astype(F32) + swap_tm(low[half:], mask).astype(F32)
-        mask *= 2
     return total[0]
 
 
-def small_scatter(rows):
-    total = rows + swap_mp(rows)
-    n = rows.shape[0]
-    while n > 1:
-        n //= 2
-        total = total[:n] + swap_tm(total[n:], n)
-    return total
-
-
-def small_gather(row):
-    n = 1
-    while n < lax.axis_size("tm"):
-        row = jnp.concatenate([row, swap_tm(row, n)], axis=0)
-        n *= 2
-    return row
+def scatter_pair(even, odd):
+    total = even.astype(F32) + swap_tm(odd, 1).astype(F32)
+    return scatter_halving(total, tm_bits()[1:], BF)
+
+
+def halving_order(n):
+    return offsets([1 << i for i in range(1, n.bit_length() - 1)])
 
 
 def head_mask(shape, head):
@@ -289,6 +274,99 @@
     )(at, normed, qkv, probs, d_attn)
 
 
+def moves(order, piece):
+    count = len(order)
+    for e, offset in enumerate(order):
+        for b in range(2):
+            for i, step in enumerate(order):
+                owner = order.index(offset ^ step)
+                source_row = ((e * 2 + b) * count + i) * piece
+                owner_row = ((owner * count + i) * 2 + b) * piece
+                yield source_row, owner_row
+
+
+def chunks_of(rows):
+    return [slice(r, min(r + CHUNK, rows)) for r in range(0, rows, CHUNK)]
+
+
+def lift_kernel(table, at, ta, tb, w_ref, gain, kva, kvb, lifted, send, keep, tok):
+    half = ta.shape[1]
+    feats = kva.shape[0]
+    cols = send.shape[1]
+    piece = ta.shape[0] // len(table) if table else 0
+    for source_row, owner_row in table:
+        tok[owner_row : owner_row + piece, :half] = ta[source_row : source_row + piece]
+        tok[owner_row : owner_row + piece, half:] = tb[source_row : source_row + piece]
+    if not table:
+        tok[:, :half] = ta[...]
+        tok[:, half:] = tb[...]
+    core = at[3]
+    for rows in chunks_of(tok.shape[0]):
+        product = dot(tok[rows], w_ref[...])
+        lifted[rows] = product
+        low = (product * gain[...]).astype(BF)
+        for ref, side in ((send, 1 - core), (keep, core)):
+            span = pl.ds(pl.multiple_of(side * cols, cols), cols)
+            part = dot(low[:, :feats], kva[:, span]) + dot(low[:, feats:], kvb[:, span])
+            ref[rows] = part.astype(BF)
+
+
+def lift(table, at, ta, tb, weight, gain, kva, kvb):
+    rows, half = ta.shape
+    cols = kva.shape[1] // 2
+    whole = pl.BlockSpec(memory_space=pltpu.VMEM)
+    return pl.pallas_call(
+        functools.partial(lift_kernel, table),
+        in_specs=[pl.BlockSpec(memory_space=pltpu.SMEM)] + [whole] * 6,
+        out_specs=[whole] * 3,
+        out_shape=[
+            jax.ShapeDtypeStruct((rows, weight.shape[1]), F32),
+            jax.ShapeDtypeStruct((rows, cols), BF),
+            jax.ShapeDtypeStruct((rows, cols), BF),
+        ],
+        scratch_shapes=[pltpu.VMEM((rows, 2 * half), BF)],
+        compiler_params=pltpu.CompilerParams(vmem_limit_bytes=VMEM_LIMIT),
+        name="lift",
+    )(at, ta, tb, weight, gain, kva, kvb)
+
+
+def lower_kernel(table, at, ca, cb, kva, kvb, lifted, gain, inv, pull, w_ref, send, keep):
+    half = send.shape[1]
+    cols = ca.shape[1]
+    core = at[3]
+    own = pl.ds(pl.multiple_of(core * cols, cols), cols)
+    other = pl.ds(pl.multiple_of((1 - core) * cols, cols), cols)
+    piece = ca.shape[0] // len(table) if table else 0
+    for rows in chunks_of(ca.shape[0]):
+        parts = [
+            dot_nt(ca[rows], w[:, own]) + dot_nt(cb[rows], w[:, other]) for w in (kva, kvb)
+        ]
+        d_normed = jnp.concatenate(parts, axis=1)
+        d_lifted = inv[rows] * gain[...] * d_normed - lifted[rows] * pull[rows]
+        low = d_lifted.astype(BF)
+        for ref, w in ((send, w_ref[half:]), (keep, w_ref[:half])):
+            part = dot_nt(low, w).astype(BF)
+            if not table:
+                ref[rows] = part
+            for source_row, owner_row in table:
+                if rows.start <= owner_row < rows.stop:
+                    at_row = owner_row - rows.start
+                    ref[source_row : source_row + piece] = part[at_row : at_row + piece]
+
+
+def lower(table, at, ca, cb, kva, kvb, lifted, gain, inv, pull, weight):
+    whole = pl.BlockSpec(memory_space=pltpu.VMEM)
+    out = jax.ShapeDtypeStruct((ca.shape[0], weight.shape[0] // 2), BF)
+    return pl.pallas_call(
+        functools.partial(lower_kernel, table),
+        in_specs=[pl.BlockSpec(memory_space=pltpu.SMEM)] + [whole] * 9,
+        out_specs=[whole] * 2,
+        out_shape=[out] * 2,
+        compiler_params=pltpu.CompilerParams(vmem_limit_bytes=VMEM_LIMIT),
+        name="lower",
+    )(at, ca, cb, kva, kvb, lifted, gain, inv, pull, weight)
+
+
 def on_device(frames, weight_qkv, weight_out, proj_in, norm_gain, proj_kv, shifts, route, d_kv):
     n = lax.axis_size("tm")
     me = lax.axis_index("tm")
@@ -311,16 +389,45 @@
     )
     x_roll = lax.dynamic_slice_in_dim(jnp.concatenate([frames, halo], 0), shift, rows, 0)
 
-    proj_in, x_roll = lax.optimization_barrier((proj_in, x_roll))
-    blocks = [lax.dynamic_slice_in_dim(proj_in, me * feats, feats, 1)]
-    for k in range(1, n):
-        blocks.append(swap_tm(lax.dynamic_slice_in_dim(proj_in, (me ^ k) * feats, feats, 1), k))
-    lift_w = jnp.take(jnp.stack(blocks), me ^ jnp.arange(n, dtype=jnp.int32), axis=0)
-    lift_w = lift_w.reshape(width, feats)
-    gain = lax.dynamic_slice_in_dim(norm_gain, me * feats, feats, 0)
+    proj_in, proj_kv, x_roll = lax.optimization_barrier((proj_in, proj_kv, x_roll))
+    kva, kvb = proj_kv, swap_tm(proj_kv, SPLIT)
+    masks = group_bits()
+    order = offsets(masks)
+    members = order + [k | SPLIT for k in order]
+    blocks = []
+    for k in order:
+        pair = [
+            lax.dynamic_slice_in_dim(proj_in, (me ^ k ^ bit) * feats, feats, 1)
+            for bit in (0, SPLIT)
+        ]
+        pair = jnp.stack(pair)
+        blocks.append(swap_tm(pair, k) if k else pair)
+    here = jnp.stack(blocks, axis=1)
+    there = swap_tm(here[::-1], SPLIT)
+    lift_w = jnp.concatenate([here, there], axis=1)
+    natural = (jnp.arange(n, dtype=jnp.int32) + core * (n // 2)) % n
+    found = (natural ^ me)[:, None] == jnp.array(members, jnp.int32)[None, :]
+    place = jnp.sum(found * jnp.arange(n, dtype=jnp.int32)[None, :], axis=1)
+    lift_w = jnp.take(lift_w, place, axis=1).reshape(2, width, feats)
+    lift_w = jnp.concatenate([lift_w[0], lift_w[1]], axis=1)
+    gain = jnp.concatenate(
+        [
+            lax.dynamic_slice_in_dim(norm_gain, (me ^ bit) * feats, feats, 0)
+            for bit in (0, SPLIT)
+        ]
+    ).reshape(1, -1)
+    owner_at = (lax.dynamic_index_in_dim(route, me, 0, keepdims=False) ^ me)[None, :]
+    sort = owner_at == jnp.array(members, jnp.int32)[:, None]
+    sort = jnp.kron(sort.astype(BF), jnp.eye(piece, dtype=BF))
+    source_at = jnp.arange(n, dtype=jnp.int32) ^ me
+    spread = source_at[:, None] == jnp.array(
+        [k | bit for k in order for bit in (0, SPLIT)], jnp.int32
+    )
+    spread = jnp.kron(spread.astype(BF), jnp.eye(piece, dtype=BF))
+    d_kv = dot_tn(spread, d_kv)
 
     w_t = jnp.transpose(weight_qkv, (1, 2, 0)).reshape(-1, width)
-    at = jnp.stack([shift, rows * n - shift - me * rows, me]).astype(jnp.int32)
+    at = jnp.stack([shift, rows * n - shift - me * rows, me, core]).astype(jnp.int32)
     normed, qkv, probs, pooled_attn, out_part = encoder_forward(
         x_roll, w_t, weight_out, at, ext_tok
     )
@@ -343,56 +450,45 @@
     tail = tail_a.astype(F32) + tail_b.astype(F32)
     pooled = jnp.concatenate([pooled[:tail_tok] + tail, pooled[tail_tok:]], 0).astype(BF)
 
-    tok_half = jnp.concatenate(gather_xor(pooled), 0)
+    count = n // 2
+    sorted_tok = dot(sort, pooled).astype(BF).reshape(2, count * piece, half_w)
+    pair_tok = jnp.stack([sorted_tok[0], swap_tm(sorted_tok[1], SPLIT)])
+    tok_half = gather_doubling(pair_tok, masks).reshape(-1, half_w)
     tok_other = swap_mp(tok_half)
-    inverse = jnp.argsort(route, axis=1).astype(jnp.int32)
-    owners = me ^ jnp.arange(n, dtype=jnp.int32)
-    sources = jnp.arange(n, dtype=jnp.int32)
-    piece_at = (sources[None, :] ^ me) * n + inverse.T[owners]
-    row_at = (piece_at[:, :, None] * piece + jnp.arange(piece, dtype=jnp.int32)).reshape(-1)
-    tok = jnp.concatenate([tok_half, tok_other], 1)
-    tok = jnp.take(tok, row_at, axis=0)
-    lift_own = jnp.concatenate(
-        [
-            lax.dynamic_slice_in_dim(lift_w, core * half_w, half_w, 0),
-            lax.dynamic_slice_in_dim(lift_w, (1 - core) * half_w, half_w, 0),
-        ],
-        0,
-    )
-    lifted = dot(tok, lift_own)
-    squares = jnp.sum(lifted * lifted, axis=-1).reshape(n, own_tok)
-    square_sum = small_scatter(squares)
+    table = list(moves(order, piece))
+    source_rows = np.concatenate([np.arange(r, r + piece) for r, _ in table])
+    owner_rows = np.concatenate([np.arange(r, r + piece) for _, r in table])
+    by_xla = piece % 16 != 0
+    if by_xla:
+        at_owner = source_rows[np.argsort(owner_rows)]
+        tok_half, tok_other = tok_half[at_owner], tok_other[at_owner]
+        table = []
+    lifted, kv_send, kv_keep = lift(table, at, tok_half, tok_other, lift_w, gain, kva, kvb)
+    squares = jnp.sum(lifted * lifted, axis=-1).reshape(count, own_tok)
+    square_sum = scatter_halving(squares + swap_mp(squares), masks, F32)
     inv_rms = lax.rsqrt(square_sum / LLM_D + 1e-05)
-    scaled = (lifted * gain).astype(BF)
-    kv_w_own = lax.dynamic_slice_in_dim(proj_kv, core * kv_half, kv_half, 1)
-    kv_w_other = lax.dynamic_slice_in_dim(proj_kv, (1 - core) * kv_half, kv_half, 1)
-    from_core = swap_mp(dot(scaled, kv_w_other).astype(BF))
-    kv_part = (dot(scaled, kv_w_own) + from_core.astype(F32)).astype(BF)
-    kv_part = kv_part.reshape(n // 2, 2, own_tok, kv_half)
-    kv_sum = scatter_xor(kv_part[:, 0], kv_part[:, 1])
-    kv = (kv_sum * inv_rms.reshape(own_tok, 1)).astype(BF)
-    total_cot = (kv.astype(F32) + d_kv.astype(F32)).astype(BF)
-    inner = jnp.sum(total_cot.astype(F32) * kv_sum, axis=-1).reshape(1, own_tok)
+    kv_part = kv_keep.astype(F32) + swap_mp(kv_send).astype(F32)
+    kv_sum = scatter_halving(kv_part.reshape(count, own_tok, kv_half), masks, BF)
+    kv_low = (kv_sum * inv_rms[:, None]).astype(BF)
+    total_cot = (kv_low.astype(F32) + d_kv).astype(BF)
+    kv = dot(spread, kv_low).astype(BF)
+    inner = jnp.sum(total_cot.astype(F32) * kv_sum, axis=-1)
     inner = inner + swap_mp(inner)
-    stats = small_gather(jnp.stack([inv_rms, inner], axis=1))
+    stats = gather_doubling(jnp.stack([inv_rms, inner]), masks)
     inv_all = stats[:, 0].reshape(-1, 1)
-    inner_all = stats[:, 1].reshape(-1, 1)
-    cot_half = jnp.concatenate(gather_xor(total_cot), 0)
+    pull = inv_all**3 * stats[:, 1].reshape(-1, 1) / LLM_D
+    cot_half = gather_doubling(total_cot, masks).reshape(-1, kv_half)
     cot_other = swap_mp(cot_half)
-    d_normed = dot_nt(cot_half, kv_w_own) + dot_nt(cot_other, kv_w_other)
-    d_lifted = (inv_all * gain * d_normed - lifted * (inv_all**3 * inner_all / LLM_D)).astype(BF)
-    d_tok = dot_nt(d_lifted, lift_own).astype(BF)
-    slot_of = (
-        jnp.arange(n, dtype=jnp.int32)[None, :] * 0
-        + (route[sources ^ me] ^ me) * n
-        + (sources ^ me)[:, None]
-    )
-    back_at = (slot_of[:, :, None] * piece + jnp.arange(piece, dtype=jnp.int32)).reshape(-1)
-    d_tok = jnp.take(d_tok, back_at, axis=0)
-    from_core = swap_mp(d_tok[:, half_w:])
-    d_part = (d_tok[:, :half_w].astype(F32) + from_core.astype(F32)).astype(BF)
-    d_part = d_part.reshape(n // 2, 2, own_tok, half_w)
-    d_half = scatter_xor(d_part[:, 0], d_part[:, 1]).astype(BF)
+    d_send, d_keep = lower(
+        table, at, cot_half, cot_other, kva, kvb, lifted, gain, inv_all, pull, lift_w
+    )
+    if by_xla:
+        at_source = owner_rows[np.argsort(source_rows)]
+        d_send, d_keep = d_send[at_source], d_keep[at_source]
+    d_part = d_keep.astype(F32) + swap_mp(d_send).astype(F32)
+    d_pair = scatter_halving(d_part.reshape(count, 2, count * piece, half_w), masks, BF)
+    d_sorted = jnp.concatenate([d_pair[0].astype(BF), swap_tm(d_pair[1].astype(BF), SPLIT)], 0)
+    d_half = dot_tn(sort, d_sorted).astype(BF)
 
     d_other = swap_mp(d_half)
     next_a = to_tm(d_half[:tail_tok], -1, False)
@@ -403,11 +499,11 @@
         core == 0, jnp.concatenate([left, right], 1), jnp.concatenate([right, left], 1)
     )
     d_attn, out_even, out_odd = out_grad(d_ext, weight_out, pooled_attn, at, n)
-    grad_out = scatter_halving(out_even, out_odd)
+    grad_out = scatter_pair(out_even, out_odd)
     chunks, count = [], weight_out.shape[0] // (4 * HEAD)
     for first in range(0, 2 * count, count):
         even, odd = encoder_backward(normed, qkv, probs, d_attn, at, n, first, count)
-        chunks.append(scatter_halving(even, odd))
+        chunks.append(scatter_pair(even, odd))
     grad_qkv = jnp.transpose(jnp.concatenate(chunks, axis=-1), (1, 0, 2))
     return kv, grad_qkv, grad_out
 

time: 359 us -> 322 us (0.90)
  local copies, waits for them, and re-layouts: 50.8 us -> 25.9 us
  starting transfers between devices: 64.2 us -> 42.9 us
  matrix products: 21.1 us -> 1.95 us
  Pallas kernels: 29.9 us -> 43.5 us
  waiting for transfers between devices: 172 us -> 184 us
    ppermute x44 -> x28, starting transfers between devices: 51.6 us -> 30.9 us  [swap_tm(): return lax.ppermute(block, 'tm', [(i, i ^ mask) for i in range(n)])]
    ppermute x44 -> x28, waiting for transfers between devices: 149 us -> 169 us  [swap_tm(): return lax.ppermute(block, 'tm', [(i, i ^ mask) for i in range(n)])]
    gather x5 -> x1, local copies, waits for them, and re-layouts: 20 us -> 3.63 us  [on_device(): lift_w = jnp.take(lift_w, place, axis=1).reshape(2, width, feats)]
    pallas_call x0 -> x2, Pallas kernels: none -> 13.7 us  [the longest x1 7.09 us: lower(): pl.pallas_call(functools.partial(lower_kernel, table), in_specs=[pl.Block...]
    unnamed x45 -> x48, local copies, waits for them, and re-layouts: 19 us -> 6.89 us
    dot_general x2, matrix products: 11.2 us -> 0.54 us  [dot_tn(): lax.dot_general(a, b, (((0,), (0,)), ((), ())), preferred_element_type=F32)]
    dot_general x4 -> x3, matrix products: 9.88 us -> 1.41 us  [dot(): return jnp.dot(a, b, preferred_element_type=F32)]
    ppermute x9, waiting for transfers between devices: 10.9 us -> 6.16 us  [swap_mp(): return lax.ppermute(block, 'mp', [(i, n - 1 - i) for i in range(n)])]
  transfers between devices with their start and end apart: 58 -> 42, of which waited for: 33 -> 26; matrix products, arithmetic and copies ran while one was open for 11% -> 12% of each run, Pallas kernels for 8% -> 9%
where the time goes in v1:
time: 322 us; the launch traced here: 321 us
  waiting for transfers between devices  184 us (57%)
  Pallas kernels  43.5 us (14%)
  starting transfers between devices  42.9 us (13%)
  local copies, waits for them, and re-layouts  25.9 us (8%)
  other arithmetic  18.6 us (6%)
  between operations  3.74 us (1%)
    ppermute x28, waiting for transfers between devices, swap_tm(): return lax.ppermute(block, 'tm', [(i, i ^ mask) for i in range(n)])  169 us
    ppermute x28, starting transfers between devices, swap_tm(): return lax.ppermute(block, 'tm', [(i, i ^ mask) for i in range(n)])  30.9 us
    pallas_call x1, Pallas kernels, encoder_forward(): pl.pallas_call(forward_kernel, grid_spec=pltpu.PrefetchScalarGridSpec(num...  15 us
    pallas_call x2, Pallas kernels, encoder_backward(): pl.pallas_call(functools.partial(backward_kernel, n), grid_spec=pltpu.Pre...  13.1 us
    ppermute x5, starting transfers between devices, to_tm(): return lax.ppermute(block, ('tm', 'mp'), pairs)  11.5 us
    ppermute x5, waiting for transfers between devices, to_tm(): return lax.ppermute(block, ('tm', 'mp'), pairs)  8.84 us
    pallas_call x1, Pallas kernels, lower(): pl.pallas_call(functools.partial(lower_kernel, table), in_specs=[pl.Block...  7.09 us
    unnamed x48, local copies, waits for them, and re-layouts  6.89 us
  transfers between devices with their start and end apart: 42, of which 26 were waited for; matrix products, arithmetic and copies ran while one was open for 12% of the time, Pallas kernels for 9%

profile of v1, /device:TPU:0, one launch (start us, length us, event | category | flops | bytes accessed | tf_op | source)
XLA Modules:
  0.0 320.7 jit_solution(7204848420139512417)
XLA Ops:
  1.7 6.1 %collective-permute-start = (bf16[128,1024]{1,0:T(8,128)(2,1)S(1)}, bf16[128,1024]{1,0:T(8,128)(2,1)S(1)}, u32[]{:S(2)}, u32[]{:S(2)}) collective-permute-start(bf16[128,1024]{1,0:T(8,128)(2,1)S(1)} %constant_dynamic-slice_fusion.1), channel_id=1, source_target_pairs={{0,14},{1,15},{2,0},{3,1},{4,2},{5,3},{6,4},{7,5},{8,6},{9,7},{10,... | collective-permute-start | bytes 786440 | tf_op jit(solution)/shard_map/ppermute | solution.py:50
  15.4 4.7 %copy.28 = bf16[3,512,1024]{2,1,0:T(8,128)(2,1)} copy(bf16[3,512,1024]{1,2,0:T(8,128)(2,1)} %bitcast.110) | data formatting | bytes 6291456 | tf_op jit(solution)/shard_map/transpose | solution.py:429
  27.0 15.0 %encoder_forward.1 = (bf16[512,1024]{1,0:T(8,128)(2,1)S(1)}, bf16[3,512,512]{2,1,0:T(8,128)(2,1)S(1)}, bf16[4,2,2,256,256]{4,3,2,1,0:T(8,128)(2,1)}, bf16[192,512]{1,0:T(8,128)(2,1)S(1)}, f32[192,1024]{1,0:T(8,128)S(1)}) custom-call(s32[4]{0:T(128)S(1)} %pad_add_fusion.at, bf16[512,1024]{1,0:T(8,128)(2,1)S(1)} %fusion.1.x_ref, bf16[1536,1024]{1,0:T(8,128)(2,1)} %bitcast.105, ...), custom_call_target="tpu_custom_call" | custom-call | tf_op jit(solution)/shard_map/encoder_forward/pallas_call | solution.py:147
  45.7 3.9 %collective-permute-done.3 = bf16[64,512]{1,0:T(8,128)(2,1)S(1)} collective-permute-done((bf16[64,512]{1,0:T(8,128)(2,1)S(1)}, bf16[64,512]{1,0:T(8,128)(2,1)S(1)}, u32[]{:S(2)}, u32[]{:S(2)}) %collective-permute-start.3) | collective-permute-done | bytes 65568 | tf_op jit(solution)/shard_map/ppermute | solution.py:50
  49.6 2.7 collective-permute-done.4
  59.5 40.2 %collective-permute-done.5 = bf16[64,512]{1,0:T(8,128)(2,1)} collective-permute-done((bf16[64,512]{1,0:T(8,128)(2,1)}, bf16[64,512]{1,0:T(8,128)(2,1)}, u32[]{:S(2)}, u32[]{:S(2)}) %collective-permute-start.5) | collective-permute-done | bytes 65568 | tf_op jit(solution)/shard_map/ppermute | solution.py:36
  100.5 3.0 collective-permute-start.6
  111.0 4.2 %collective-permute-done.7 = bf16[2,2,64,512]{3,2,1,0:T(8,128)(2,1)S(1)} collective-permute-done((bf16[2,2,64,512]{3,2,1,0:T(8,128)(2,1)S(1)}, bf16[2,2,64,512]{3,2,1,0:T(8,128)(2,1)S(1)}, u32[]{:S(2)}, u32[]{:S(2)}) %collective-permute-start.7) | collective-permute-done | bytes 262176 | tf_op jit(solution)/shard_map/ppermute | solution.py:36
  116.0 5.2 %collective-permute-done.12 = bf16[2,4,128,512]{3,2,1,0:T(8,128)(2,1)S(1)} collective-permute-done((bf16[2,4,128,512]{3,2,1,0:T(8,128)(2,1)}, bf16[2,4,128,512]{3,2,1,0:T(8,128)(2,1)S(1)}, u32[]{:S(2)}, u32[]{:S(2)}) %collective-permute-start.12) | collective-permute-done | bytes 1048608 | tf_op jit(solution)/shard_map/ppermute | solution.py:36
  122.4 3.6 %gather_fusion = bf16[8,2,128,512]{3,2,1,0:T(8,128)(2,1)} fusion(bf16[2,8,128,512]{3,2,1,0:T(8,128)(2,1)} %constant_dynamic-update-slice_fusion, s32[1024]{0:T(1024)S(1)} %pad_clamp_fusion), kind=kCustom, calls=%fused_computation | custom fusion | bytes 4194336 | tf_op jit(solution)/shard_map/jit(_take)/gather | solution.py:411
  129.6 6.6 %lift.1 = (f32[512,1024]{1,0:T(8,128)S(1)}, bf16[512,1024]{1,0:T(8,128)(2,1)S(1)}, bf16[512,1024]{1,0:T(8,128)(2,1)S(1)}) custom-call(s32[4]{0:T(128)S(1)} %pad_add_fusion.at, bf16[512,512]{1,0:T(8,128)(2,1)} %bitcast.10.ta, bf16[512,512]{1,0:T(8,128)(2,1)} %collective-permute-done.8.tb, bf16[1024,1024]{1,0:T(8,128)(2,1)} %pad_maximum_fusion.w_ref, ...), custom_call_target="tpu_custom_call" | custom-call | tf_op jit(solution)/shard_map/lift/pallas_call | solution.py:318
  136.3 2.6 collective-permute-done.14
  143.0 10.5 %collective-permute-done.15 = bf16[2,128,1024]{2,1,0:T(8,128)(2,1)S(1)} collective-permute-done((bf16[2,128,1024]{2,1,0:T(8,128)(2,1)S(1)}, bf16[2,128,1024]{2,1,0:T(8,128)(2,1)S(1)}, u32[]{:S(2)}, u32[]{:S(2)}) %collective-permute-start.15) | collective-permute-done | bytes 524320 | tf_op jit(solution)/shard_map/ppermute | solution.py:36
  153.8 2.9 collective-permute-start.16
  157.0 11.1 %collective-permute-done.19 = f32[1,128]{1,0:T(1,128)S(1)} collective-permute-done((f32[1,128]{1,0:T(1,128)S(1)}, f32[1,128]{1,0:T(1,128)S(1)}, u32[]{:S(2)}, u32[]{:S(2)}) %collective-permute-start.19) | collective-permute-done | bytes 544 | tf_op jit(solution)/shard_map/ppermute | solution.py:36
  168.6 13.8 %collective-permute-done.20 = bf16[1,128,1024]{2,1,0:T(8,128)(2,1)S(1)} collective-permute-done((bf16[1,128,1024]{2,1,0:T(8,128)(2,1)S(1)}, bf16[1,128,1024]{2,1,0:T(8,128)(2,1)S(1)}, u32[]{:S(2)}, u32[]{:S(2)}) %collective-permute-start.20) | collective-permute-done | bytes 262176 | tf_op jit(solution)/shard_map/ppermute | solution.py:36
  182.6 13.7 %collective-permute-done.21 = bf16[2,128,1024]{2,1,0:T(8,128)(2,1)S(1)} collective-permute-done((bf16[2,128,1024]{2,1,0:T(8,128)(2,1)S(1)}, bf16[2,128,1024]{2,1,0:T(8,128)(2,1)S(1)}, u32[]{:S(2)}, u32[]{:S(2)}) %collective-permute-start.21) | collective-permute-done | bytes 524320 | tf_op jit(solution)/shard_map/ppermute | solution.py:36
  198.4 3.6 %collective-permute-done.24 = f32[1,2,128]{2,1,0:T(2,128)S(1)} collective-permute-done((f32[1,2,128]{2,1,0:T(2,128)S(1)}, f32[1,2,128]{2,1,0:T(2,128)S(1)}, u32[]{:S(2)}, u32[]{:S(2)}) %collective-permute-start.24) | collective-permute-done | bytes 1056 | tf_op jit(solution)/shard_map/ppermute | solution.py:36
  202.3 3.3 %collective-permute-done.25 = f32[2,2,128]{2,1,0:T(2,128)S(1)} collective-permute-done((f32[2,2,128]{2,1,0:T(2,128)S(1)}, f32[2,2,128]{2,1,0:T(2,128)S(1)}, u32[]{:S(2)}, u32[]{:S(2)}) %collective-permute-start.25) | collective-permute-done | bytes 2080 | tf_op jit(solution)/shard_map/ppermute | solution.py:36
  210.3 7.1 %lower.1 = (bf16[512,512]{1,0:T(8,128)(2,1)S(1)}, bf16[512,512]{1,0:T(8,128)(2,1)S(1)}) custom-call(s32[4]{0:T(128)S(1)} %pad_add_fusion.at, bf16[512,1024]{1,0:T(8,128)(2,1)} %bitcast.36.ca, bf16[512,1024]{1,0:T(8,128)(2,1)} %collective-permute-done.22.cb, bf16[512,2048]{1,0:T(8,128)(2,1)S(1)} %copy-done.2, bf16[512,2048]{1,0:T(8,128)(2,1)} %collective-permute-done.13.kvb, ...), custom_call_target="tpu_custom_call" | custom-call | tf_op jit(solution)/shard_map/lower/pallas_call | solution.py:360
  220.0 8.1 %collective-permute-done.27 = bf16[2,2,64,512]{3,2,1,0:T(8,128)(2,1)S(1)} collective-permute-done((bf16[2,2,64,512]{3,2,1,0:T(8,128)(2,1)S(1)}, bf16[2,2,64,512]{3,2,1,0:T(8,128)(2,1)S(1)}, u32[]{:S(2)}, u32[]{:S(2)}) %collective-permute-start.27) | collective-permute-done | bytes 262176 | tf_op jit(solution)/shard_map/ppermute | solution.py:36
  229.0 7.3 %collective-permute-done.28 = bf16[1,2,64,512]{3,2,1,0:T(8,128)(2,1)S(1)} collective-permute-done((bf16[1,2,64,512]{3,2,1,0:T(8,128)(2,1)S(1)}, bf16[1,2,64,512]{3,2,1,0:T(8,128)(2,1)S(1)}, u32[]{:S(2)}, u32[]{:S(2)}) %collective-permute-start.28) | collective-permute-done | bytes 131104 | tf_op jit(solution)/shard_map/ppermute | solution.py:36
  236.8 3.9 %collective-permute-done.29 = bf16[64,512]{1,0:T(8,128)(2,1)S(1)} collective-permute-done((bf16[64,512]{1,0:T(8,128)(2,1)S(1)}, bf16[64,512]{1,0:T(8,128)(2,1)S(1)}, u32[]{:S(2)}, u32[]{:S(2)}) %collective-permute-start.29) | collective-permute-done | bytes 65568 | tf_op jit(solution)/shard_map/ppermute | solution.py:36
  250.1 6.6 %encoder_backward.3 = (bf16[4,3,128,256]{3,2,1,0:T(8,128)(2,1)S(1)}, bf16[4,3,128,256]{3,2,1,0:T(8,128)(2,1)S(1)}) custom-call(s32[4]{0:T(128)S(1)} %pad_add_fusion.at, bf16[512,1024]{1,0:T(8,128)(2,1)S(1)} %get-tuple-element.30.n_ref, bf16[3,512,512]{2,1,0:T(8,128)(2,1)S(1)} %copy-done.5, bf16[4,2,2,256,256]{4,3,2,1,0:T(8,128)(2,1)} %get-tuple-element.32.probs, ...), custom_call_target="tpu_custom_call" | custom-call | tf_op jit(solution)/shard_map/encoder_backward/pallas_call | solution.py:255
  257.4 6.2 %collective-permute-done.39 = bf16[4,64,1024]{2,1,0:T(8,128)(2,1)S(1)} collective-permute-done((bf16[4,64,1024]{2,1,0:T(8,128)(2,1)S(1)}, bf16[4,64,1024]{2,1,0:T(8,128)(2,1)S(1)}, u32[]{:S(2)}, u32[]{:S(2)}) %collective-permute-start.39) | collective-permute-done | bytes 524320 | tf_op jit(solution)/shard_map/ppermute | solution.py:36
  264.2 6.6 %encoder_backward.2 = (bf16[4,3,128,256]{3,2,1,0:T(8,128)(2,1)S(1)}, bf16[4,3,128,256]{3,2,1,0:T(8,128)(2,1)S(1)}) custom-call(s32[4]{0:T(128)S(1)} %pad_add_fusion.at, bf16[512,1024]{1,0:T(8,128)(2,1)S(1)} %get-tuple-element.30.n_ref, bf16[3,512,512]{2,1,0:T(8,128)(2,1)S(1)} %copy-done.5, bf16[4,2,2,256,256]{4,3,2,1,0:T(8,128)(2,1)} %get-tuple-element.32.probs, ...), custom_call_target="tpu_custom_call" | custom-call | tf_op jit(solution)/shard_map/encoder_backward/pallas_call | solution.py:255
  273.0 4.5 %collective-permute-start.41 = (bf16[1,64,1024]{2,1,0:T(8,128)(2,1)S(1)}, bf16[1,64,1024]{2,1,0:T(8,128)(2,1)S(1)}, u32[]{:S(2)}, u32[]{:S(2)}) collective-permute-start(bf16[1,64,1024]{2,1,0:T(8,128)(2,1)S(1)} %slice.215), channel_id=1, source_target_pairs={{0,8},{2,10},{4,12},{6,14},{8,0},{10,2},{12,4},{14,6},{1,9},{3,11}... | collective-permute-start | bytes 393224 | tf_op jit(solution)/shard_map/ppermute | solution.py:36
  277.5 2.9 collective-permute-done.36
  281.1 14.6 %collective-permute-done.33 = bf16[4,3,128,256]{3,2,1,0:T(8,128)(2,1)S(1)} collective-permute-done((bf16[4,3,128,256]{3,2,1,0:T(8,128)(2,1)S(1)}, bf16[4,3,128,256]{3,2,1,0:T(8,128)(2,1)S(1)}, u32[]{:S(2)}, u32[]{:S(2)}) %collective-permute-start.33) | collective-permute-done | bytes 786464 | tf_op jit(solution)/shard_map/ppermute | solution.py:36
  296.9 3.6 %collective-permute-start.38 = (bf16[1,3,128,256]{3,2,1,0:T(8,128)(2,1)S(1)}, bf16[1,3,128,256]{3,2,1,0:T(8,128)(2,1)S(1)}, u32[]{:S(2)}, u32[]{:S(2)}) collective-permute-start(bf16[1,3,128,256]{3,2,1,0:T(8,128)(2,1)S(1)} %slice.211), channel_id=1, source_target_pairs={{0,8},{2,10},{4,12},{6,14},{8,0},{10,2},{12,4},{14,6},{1,9},{3,11}... | collective-permute-start | bytes 589832 | tf_op jit(solution)/shard_map/ppermute | solution.py:36
  300.5 9.3 %collective-permute-done.34 = bf16[2,3,128,256]{3,2,1,0:T(8,128)(2,1)S(1)} collective-permute-done((bf16[2,3,128,256]{3,2,1,0:T(8,128)(2,1)S(1)}, bf16[2,3,128,256]{3,2,1,0:T(8,128)(2,1)S(1)}, u32[]{:S(2)}, u32[]{:S(2)}) %collective-permute-start.34) | collective-permute-done | bytes 393248 | tf_op jit(solution)/shard_map/ppermute | solution.py:36
  310.8 8.8 %collective-permute-done.35 = bf16[1,3,128,256]{3,2,1,0:T(8,128)(2,1)S(1)} collective-permute-done((bf16[1,3,128,256]{3,2,1,0:T(8,128)(2,1)S(1)}, bf16[1,3,128,256]{3,2,1,0:T(8,128)(2,1)S(1)}, u32[]{:S(2)}, u32[]{:S(2)}) %collective-permute-start.35) | collective-permute-done | bytes 196640 | tf_op jit(solution)/shard_map/ppermute | solution.py:36
  (201 shorter events, 70.8 us)
Async XLA Ops:
  1.7 11.8 %collective-permute-start = (bf16[128,1024]{1,0:T(8,128)(2,1)S(1)}, bf16[128,1024]{1,0:T(8,128)(2,1)S(1)}, u32[]{:S(2)}, u32[]{:S(2)}) collective-permute-start(bf16[128,1024]{1,0:T(8,128)(2,1)S(1)} %constant_dynamic-slice_fusion.1), channel_id=1, source_target_pairs={{0,14},{1,15},{2,0},{3,1},{4,2},{5,3},{6,4},{7,5},{8,6},{9,7},{10,... | collective-permute-start | bytes 786440 | tf_op jit(solution)/shard_map/ppermute | solution.py:50
  13.5 7.4 %collective-permute-start.1 = (bf16[128,1024]{1,0:T(8,128)(2,1)S(1)}, bf16[128,1024]{1,0:T(8,128)(2,1)S(1)}, u32[]{:S(2)}, u32[]{:S(2)}) collective-permute-start(bf16[128,1024]{1,0:T(8,128)(2,1)S(1)} %collective-permute-done), channel_id=1, source_target_pairs={{0,1},{1,0},{2,3},{3,2},{4,5},{5,4},{6,7},{7,6},{8,9},{9,8},{10,11... | collective-permute-start | bytes 786440 | tf_op jit(solution)/shard_map/ppermute | solution.py:41
  22.4 30.7 %collective-permute-start.9 = (bf16[2,128,512]{2,1,0:T(8,128)(2,1)S(1)}, bf16[2,128,512]{2,1,0:T(8,128)(2,1)S(1)}, u32[]{:S(2)}, u32[]{:S(2)}) collective-permute-start(bf16[2,128,512]{2,1,0:T(8,128)(2,1)S(1)} %pad_maximum_fusion.6), channel_id=1, source_target_pairs={{0,8},{2,10},{4,12},{6,14},{8,0},{10,2},{12,4},{14,6},{1,9},{3,11}... | collective-permute-start | bytes 786440 | tf_op jit(solution)/shard_map/ppermute | solution.py:36
  22.8 30.3 %collective-permute-start.10 = (bf16[2,128,512]{2,1,0:T(8,128)(2,1)S(1)}, bf16[2,128,512]{2,1,0:T(8,128)(2,1)S(1)}, u32[]{:S(2)}, u32[]{:S(2)}) collective-permute-start(bf16[2,128,512]{2,1,0:T(8,128)(2,1)S(1)} %pad_maximum_fusion.7), channel_id=1, source_target_pairs={{0,4},{2,6},{4,0},{6,2},{8,12},{10,14},{12,8},{14,10},{1,5},{3,7},... | collective-permute-start | bytes 786440 | tf_op jit(solution)/shard_map/ppermute | solution.py:36
  24.5 28.6 %collective-permute-start.11 = (bf16[2,128,512]{2,1,0:T(8,128)(2,1)S(1)}, bf16[2,128,512]{2,1,0:T(8,128)(2,1)S(1)}, u32[]{:S(2)}, u32[]{:S(2)}) collective-permute-start(bf16[2,128,512]{2,1,0:T(8,128)(2,1)S(1)} %pad_maximum_fusion.8), channel_id=1, source_target_pairs={{0,12},{2,14},{4,8},{6,10},{8,4},{10,6},{12,0},{14,2},{1,13},{3,15... | collective-permute-start | bytes 786440 | tf_op jit(solution)/shard_map/ppermute | solution.py:36
  42.2 7.4 %collective-permute-start.3 = (bf16[64,512]{1,0:T(8,128)(2,1)S(1)}, bf16[64,512]{1,0:T(8,128)(2,1)S(1)}, u32[]{:S(2)}, u32[]{:S(2)}) collective-permute-start(bf16[64,512]{1,0:T(8,128)(2,1)S(1)} %get-tuple-element.57), channel_id=1, source_target_pairs={{0,2},{1,3},{2,4},{3,5},{4,6},{5,7},{6,8},{7,9},{8,10},{9,11},{10,... | collective-permute-start | bytes 196616 | tf_op jit(solution)/shard_map/ppermute | solution.py:50
  45.4 6.9 %collective-permute-start.4 = (bf16[64,512]{1,0:T(8,128)(2,1)S(1)}, bf16[64,512]{1,0:T(8,128)(2,1)S(1)}, u32[]{:S(2)}, u32[]{:S(2)}) collective-permute-start(bf16[64,512]{1,0:T(8,128)(2,1)S(1)} %get-tuple-element.58), channel_id=1, source_target_pairs={{0,3},{1,2},{2,5},{3,4},{4,7},{5,6},{6,9},{7,8},{8,11},{9,10},{10,... | collective-permute-start | bytes 196616 | tf_op jit(solution)/shard_map/ppermute | solution.py:50
  49.6 80.0 %collective-permute-start.13 = (bf16[512,2048]{1,0:T(8,128)(2,1)S(1)}, bf16[512,2048]{1,0:T(8,128)(2,1)}, u32[]{:S(2)}, u32[]{:S(2)}) collective-permute-start(bf16[512,2048]{1,0:T(8,128)(2,1)S(1)} %copy-done.1), channel_id=1, source_target_pairs={{0,2},{2,0},{4,6},{6,4},{8,10},{10,8},{12,14},{14,12},{1,3},{3,1},... | collective-permute-start | bytes 6291464 | tf_op jit(solution)/shard_map/ppermute | solution.py:36
  53.1 46.5 %collective-permute-start.5 = (bf16[64,512]{1,0:T(8,128)(2,1)}, bf16[64,512]{1,0:T(8,128)(2,1)}, u32[]{:S(2)}, u32[]{:S(2)}) collective-permute-start(bf16[64,512]{1,0:T(8,128)(2,1)} %get-tuple-element.62), channel_id=1, source_target_pairs={{0,2},{2,0},{4,6},{6,4},{8,10},{10,8},{12,14},{14,12},{1,3},{3,1},... | collective-permute-start | bytes 196616 | tf_op jit(solution)/shard_map/ppermute | solution.py:36
  57.5 63.8 %collective-permute-start.12 = (bf16[2,4,128,512]{3,2,1,0:T(8,128)(2,1)}, bf16[2,4,128,512]{3,2,1,0:T(8,128)(2,1)S(1)}, u32[]{:S(2)}, u32[]{:S(2)}) collective-permute-start(bf16[2,4,128,512]{3,2,1,0:T(8,128)(2,1)} %rev.3), channel_id=1, source_target_pairs={{0,2},{2,0},{4,6},{6,4},{8,10},{10,8},{12,14},{14,12},{1,3},{3,1},... | collective-permute-start | bytes 3145736 | tf_op jit(solution)/shard_map/ppermute | solution.py:36
  100.5 7.1 %collective-permute-start.6 = (bf16[1,2,64,512]{3,2,1,0:T(8,128)(2,1)S(1)}, bf16[1,2,64,512]{3,2,1,0:T(8,128)(2,1)S(1)}, u32[]{:S(2)}, u32[]{:S(2)}) collective-permute-start(bf16[1,2,64,512]{3,2,1,0:T(8,128)(2,1)S(1)} %maximum_bitcast_fusion.2), channel_id=1, source_target_pairs={{0,8},{2,10},{4,12},{6,14},{8,0},{10,2},{12,4},{14,6},{1,9},{3,11}... | collective-permute-start | bytes 393224 | tf_op jit(solution)/shard_map/ppermute | solution.py:36
  107.6 7.6 %collective-permute-start.7 = (bf16[2,2,64,512]{3,2,1,0:T(8,128)(2,1)S(1)}, bf16[2,2,64,512]{3,2,1,0:T(8,128)(2,1)S(1)}, u32[]{:S(2)}, u32[]{:S(2)}) collective-permute-start(bf16[2,2,64,512]{3,2,1,0:T(8,128)(2,1)S(1)} %pad_maximum_fusion.5), channel_id=1, source_target_pairs={{0,4},{2,6},{4,0},{6,2},{8,12},{10,14},{12,8},{14,10},{1,5},{3,7},... | collective-permute-start | bytes 786440 | tf_op jit(solution)/shard_map/ppermute | solution.py:36
  116.0 13.6 %collective-permute-start.8 = (bf16[512,512]{1,0:T(8,128)(2,1)}, bf16[512,512]{1,0:T(8,128)(2,1)}, u32[]{:S(2)}, u32[]{:S(2)}) collective-permute-start(bf16[512,512]{1,0:T(8,128)(2,1)} %bitcast.10.ta), channel_id=1, source_target_pairs={{0,1},{1,0},{2,3},{3,2},{4,5},{5,4},{6,7},{7,6},{8,9},{9,8},{10,11... | collective-permute-start | bytes 1572872 | tf_op jit(solution)/shard_map/ppermute | solution.py:41
  139.5 14.0 %collective-permute-start.15 = (bf16[2,128,1024]{2,1,0:T(8,128)(2,1)S(1)}, bf16[2,128,1024]{2,1,0:T(8,128)(2,1)S(1)}, u32[]{:S(2)}, u32[]{:S(2)}) collective-permute-start(bf16[2,128,1024]{2,1,0:T(8,128)(2,1)S(1)} %bitcast.119), channel_id=1, source_target_pairs={{0,4},{2,6},{4,0},{6,2},{8,12},{10,14},{12,8},{14,10},{1,5},{3,7},... | collective-permute-start | bytes 1572872 | tf_op jit(solution)/shard_map/ppermute | solution.py:36
  141.0 15.6 %collective-permute-start.18 = (f32[2,128]{1,0:T(2,128)S(1)}, f32[2,128]{1,0:T(2,128)S(1)}, u32[]{:S(2)}, u32[]{:S(2)}) collective-permute-start(f32[2,128]{1,0:T(2,128)S(1)} %slice.158), channel_id=1, source_target_pairs={{0,4},{2,6},{4,0},{6,2},{8,12},{10,14},{12,8},{14,10},{1,5},{3,7},... | collective-permute-start | bytes 3080 | tf_op jit(solution)/shard_map/ppermute | solution.py:36
  153.8 14.4 %collective-permute-start.16 = (bf16[1,128,1024]{2,1,0:T(8,128)(2,1)S(1)}, bf16[1,128,1024]{2,1,0:T(8,128)(2,1)S(1)}, u32[]{:S(2)}, u32[]{:S(2)}) collective-permute-start(bf16[1,128,1024]{2,1,0:T(8,128)(2,1)S(1)} %slice.194), channel_id=1, source_target_pairs={{0,8},{2,10},{4,12},{6,14},{8,0},{10,2},{12,4},{14,6},{1,9},{3,11}... | collective-permute-start | bytes 786440 | tf_op jit(solution)/shard_map/ppermute | solution.py:36
  156.7 11.4 %collective-permute-start.19 = (f32[1,128]{1,0:T(1,128)S(1)}, f32[1,128]{1,0:T(1,128)S(1)}, u32[]{:S(2)}, u32[]{:S(2)}) collective-permute-start(f32[1,128]{1,0:T(1,128)S(1)} %slice.160), channel_id=1, source_target_pairs={{0,8},{2,10},{4,12},{6,14},{8,0},{10,2},{12,4},{14,6},{1,9},{3,11}... | collective-permute-start | bytes 1544 | tf_op jit(solution)/shard_map/ppermute | solution.py:36
  168.5 13.9 %collective-permute-start.20 = (bf16[1,128,1024]{2,1,0:T(8,128)(2,1)S(1)}, bf16[1,128,1024]{2,1,0:T(8,128)(2,1)S(1)}, u32[]{:S(2)}, u32[]{:S(2)}) collective-permute-start(bf16[1,128,1024]{2,1,0:T(8,128)(2,1)S(1)} %bitcast.116), channel_id=1, source_target_pairs={{0,8},{2,10},{4,12},{6,14},{8,0},{10,2},{12,4},{14,6},{1,9},{3,11}... | collective-permute-start | bytes 786440 | tf_op jit(solution)/shard_map/ppermute | solution.py:36
  182.4 13.9 %collective-permute-start.21 = (bf16[2,128,1024]{2,1,0:T(8,128)(2,1)S(1)}, bf16[2,128,1024]{2,1,0:T(8,128)(2,1)S(1)}, u32[]{:S(2)}, u32[]{:S(2)}) collective-permute-start(bf16[2,128,1024]{2,1,0:T(8,128)(2,1)S(1)} %pad_maximum_fusion.4), channel_id=1, source_target_pairs={{0,4},{2,6},{4,0},{6,2},{8,12},{10,14},{12,8},{14,10},{1,5},{3,7},... | collective-permute-start | bytes 1572872 | tf_op jit(solution)/shard_map/ppermute | solution.py:36
  182.5 14.9 %collective-permute-start.23 = (f32[128]{0:T(128)S(1)}, f32[128]{0:T(128)S(1)}, u32[]{:S(2)}, u32[]{:S(2)}) collective-permute-start(f32[128]{0:T(128)S(1)} %get-tuple-element.69), channel_id=1, source_target_pairs={{0,1},{1,0},{2,3},{3,2},{4,5},{5,4},{6,7},{7,6},{8,9},{9,8},{10,11... | collective-permute-start | bytes 1544 | tf_op jit(solution)/shard_map/ppermute | solution.py:41
  197.4 11.9 %collective-permute-start.22 = (bf16[512,1024]{1,0:T(8,128)(2,1)}, bf16[512,1024]{1,0:T(8,128)(2,1)}, u32[]{:S(2)}, u32[]{:S(2)}) collective-permute-start(bf16[512,1024]{1,0:T(8,128)(2,1)} %bitcast.36.ca), channel_id=1, source_target_pairs={{0,1},{1,0},{2,3},{3,2},{4,5},{5,4},{6,7},{7,6},{8,9},{9,8},{10,11... | collective-permute-start | bytes 3145736 | tf_op jit(solution)/shard_map/ppermute | solution.py:41
  219.6 8.4 %collective-permute-start.27 = (bf16[2,2,64,512]{3,2,1,0:T(8,128)(2,1)S(1)}, bf16[2,2,64,512]{3,2,1,0:T(8,128)(2,1)S(1)}, u32[]{:S(2)}, u32[]{:S(2)}) collective-permute-start(bf16[2,2,64,512]{3,2,1,0:T(8,128)(2,1)S(1)} %bitcast.120), channel_id=1, source_target_pairs={{0,4},{2,6},{4,0},{6,2},{8,12},{10,14},{12,8},{14,10},{1,5},{3,7},... | collective-permute-start | bytes 786440 | tf_op jit(solution)/shard_map/ppermute | solution.py:36
  228.1 8.2 %collective-permute-start.28 = (bf16[1,2,64,512]{3,2,1,0:T(8,128)(2,1)S(1)}, bf16[1,2,64,512]{3,2,1,0:T(8,128)(2,1)S(1)}, u32[]{:S(2)}, u32[]{:S(2)}) collective-permute-start(bf16[1,2,64,512]{3,2,1,0:T(8,128)(2,1)S(1)} %slice.200), channel_id=1, source_target_pairs={{0,8},{2,10},{4,12},{6,14},{8,0},{10,2},{12,4},{14,6},{1,9},{3,11}... | collective-permute-start | bytes 393224 | tf_op jit(solution)/shard_map/ppermute | solution.py:36
  248.6 14.9 %collective-permute-start.39 = (bf16[4,64,1024]{2,1,0:T(8,128)(2,1)S(1)}, bf16[4,64,1024]{2,1,0:T(8,128)(2,1)S(1)}, u32[]{:S(2)}, u32[]{:S(2)}) collective-permute-start(bf16[4,64,1024]{2,1,0:T(8,128)(2,1)S(1)} %get-tuple-element.42), channel_id=1, source_target_pairs={{0,2},{2,0},{4,6},{6,4},{8,10},{10,8},{12,14},{14,12},{1,3},{3,1},... | collective-permute-start | bytes 1572872 | tf_op jit(solution)/shard_map/ppermute | solution.py:36
  256.7 23.7 %collective-permute-start.36 = (bf16[4,3,128,256]{3,2,1,0:T(8,128)(2,1)S(1)}, bf16[4,3,128,256]{3,2,1,0:T(8,128)(2,1)S(1)}, u32[]{:S(2)}, u32[]{:S(2)}) collective-permute-start(bf16[4,3,128,256]{3,2,1,0:T(8,128)(2,1)S(1)} %get-tuple-element.40), channel_id=1, source_target_pairs={{0,2},{2,0},{4,6},{6,4},{8,10},{10,8},{12,14},{14,12},{1,3},{3,1},... | collective-permute-start | bytes 2359304 | tf_op jit(solution)/shard_map/ppermute | solution.py:36
  263.8 9.2 %collective-permute-start.40 = (bf16[2,64,1024]{2,1,0:T(8,128)(2,1)S(1)}, bf16[2,64,1024]{2,1,0:T(8,128)(2,1)S(1)}, u32[]{:S(2)}, u32[]{:S(2)}) collective-permute-start(bf16[2,64,1024]{2,1,0:T(8,128)(2,1)S(1)} %slice.213), channel_id=1, source_target_pairs={{0,4},{2,6},{4,0},{6,2},{8,12},{10,14},{12,8},{14,10},{1,5},{3,7},... | collective-permute-start | bytes 786440 | tf_op jit(solution)/shard_map/ppermute | solution.py:36
  270.7 24.9 %collective-permute-start.33 = (bf16[4,3,128,256]{3,2,1,0:T(8,128)(2,1)S(1)}, bf16[4,3,128,256]{3,2,1,0:T(8,128)(2,1)S(1)}, u32[]{:S(2)}, u32[]{:S(2)}) collective-permute-start(bf16[4,3,128,256]{3,2,1,0:T(8,128)(2,1)S(1)} %get-tuple-element.38), channel_id=1, source_target_pairs={{0,2},{2,0},{4,6},{6,4},{8,10},{10,8},{12,14},{14,12},{1,3},{3,1},... | collective-permute-start | bytes 2359304 | tf_op jit(solution)/shard_map/ppermute | solution.py:36
  273.0 23.0 %collective-permute-start.41 = (bf16[1,64,1024]{2,1,0:T(8,128)(2,1)S(1)}, bf16[1,64,1024]{2,1,0:T(8,128)(2,1)S(1)}, u32[]{:S(2)}, u32[]{:S(2)}) collective-permute-start(bf16[1,64,1024]{2,1,0:T(8,128)(2,1)S(1)} %slice.215), channel_id=1, source_target_pairs={{0,8},{2,10},{4,12},{6,14},{8,0},{10,2},{12,4},{14,6},{1,9},{3,11}... | collective-permute-start | bytes 393224 | tf_op jit(solution)/shard_map/ppermute | solution.py:36
  280.7 16.1 %collective-permute-start.37 = (bf16[2,3,128,256]{3,2,1,0:T(8,128)(2,1)S(1)}, bf16[2,3,128,256]{3,2,1,0:T(8,128)(2,1)S(1)}, u32[]{:S(2)}, u32[]{:S(2)}) collective-permute-start(bf16[2,3,128,256]{3,2,1,0:T(8,128)(2,1)S(1)} %slice.209), channel_id=1, source_target_pairs={{0,4},{2,6},{4,0},{6,2},{8,12},{10,14},{12,8},{14,10},{1,5},{3,7},... | collective-permute-start | bytes 1179656 | tf_op jit(solution)/shard_map/ppermute | solution.py:36
  296.0 13.8 %collective-permute-start.34 = (bf16[2,3,128,256]{3,2,1,0:T(8,128)(2,1)S(1)}, bf16[2,3,128,256]{3,2,1,0:T(8,128)(2,1)S(1)}, u32[]{:S(2)}, u32[]{:S(2)}) collective-permute-start(bf16[2,3,128,256]{3,2,1,0:T(8,128)(2,1)S(1)} %slice.205), channel_id=1, source_target_pairs={{0,4},{2,6},{4,0},{6,2},{8,12},{10,14},{12,8},{14,10},{1,5},{3,7},... | collective-permute-start | bytes 1179656 | tf_op jit(solution)/shard_map/ppermute | solution.py:36
  296.9 13.9 %collective-permute-start.38 = (bf16[1,3,128,256]{3,2,1,0:T(8,128)(2,1)S(1)}, bf16[1,3,128,256]{3,2,1,0:T(8,128)(2,1)S(1)}, u32[]{:S(2)}, u32[]{:S(2)}) collective-permute-start(bf16[1,3,128,256]{3,2,1,0:T(8,128)(2,1)S(1)} %slice.211), channel_id=1, source_target_pairs={{0,8},{2,10},{4,12},{6,14},{8,0},{10,2},{12,4},{14,6},{1,9},{3,11}... | collective-permute-start | bytes 589832 | tf_op jit(solution)/shard_map/ppermute | solution.py:36
  309.9 9.7 %collective-permute-start.35 = (bf16[1,3,128,256]{3,2,1,0:T(8,128)(2,1)S(1)}, bf16[1,3,128,256]{3,2,1,0:T(8,128)(2,1)S(1)}, u32[]{:S(2)}, u32[]{:S(2)}) collective-permute-start(bf16[1,3,128,256]{3,2,1,0:T(8,128)(2,1)S(1)} %slice.207), channel_id=1, source_target_pairs={{0,8},{2,10},{4,12},{6,14},{8,0},{10,2},{12,4},{14,6},{1,9},{3,11}... | collective-permute-start | bytes 589832 | tf_op jit(solution)/shard_map/ppermute | solution.py:36
  (32 other events, 444.7 us)

commit v2 on v1

--- a/solution.py
+++ b/solution.py
@@ -17,6 +17,7 @@
 VMEM_LIMIT = 48 << 20
 SPLIT = 1
 CHUNK = 512
+LANES = 128
 
 
 def dot(a, b):
@@ -82,6 +83,16 @@
     return total[0]
 
 
+def scatter_last(blocks, masks):
+    low = blocks.astype(BF)
+    for i, mask in enumerate(masks):
+        half = low.shape[0] // 2
+        got = swap_tm(low[half:], mask)
+        if i + 1 == len(masks):
+            return low[0], got[0]
+        low = (low[:half].astype(F32) + got.astype(F32)).astype(BF)
+
+
 def scatter_pair(even, odd):
     total = even.astype(F32) + swap_tm(odd, 1).astype(F32)
     return scatter_halving(total, tm_bits()[1:], BF)
@@ -110,24 +121,34 @@
     base = normed[...]
     for i, w_ref in enumerate((wq_ref, wk_ref, wv_ref)):
         qkv[i] = dot_nt(base, w_ref[...]).astype(BF)
-    for w in range(rows // WINDOW):
-        span = pl.ds(w * WINDOW, WINDOW)
-        q, k, v = qkv[0, span, :], qkv[1, span, :], qkv[2, span, :]
-        square = (WINDOW, WINDOW)
-        key_at = lax.broadcasted_iota(jnp.int32, square, 0) + w * WINDOW
-        query_at = lax.broadcasted_iota(jnp.int32, square, 1) + w * WINDOW
-        allowed = (key_at >= border) == (query_at >= border)
-        attended = None
-        for h in range(cols // HEAD):
-            own = head_mask(k.shape, h)
-            scores = dot_nt(jnp.where(own, k, jnp.zeros_like(k)), q) * HEAD ** (-0.5)
-            scores = jnp.where(allowed, scores, -1e30)
-            terms = jnp.exp(scores - jnp.max(scores, axis=0, keepdims=True))
+    windows, heads = range(rows // WINDOW), range(cols // HEAD)
+    spans = [pl.ds(w * WINDOW, WINDOW) for w in windows]
+    own = [head_mask((WINDOW, cols), h) for h in heads]
+    scores = []
+    for w in windows:
+        q, k = qkv[0, spans[w], :], qkv[1, spans[w], :]
+        for h in heads:
+            scores.append(dot_nt(jnp.where(own[h], k, jnp.zeros_like(k)), q))
+    square = (WINDOW, WINDOW)
+    key_at = lax.broadcasted_iota(jnp.int32, square, 0)
+    query_at = lax.broadcasted_iota(jnp.int32, square, 1)
+    lows = []
+    for w in windows:
+        edge = border - w * WINDOW
+        allowed = (key_at >= edge) == (query_at >= edge)
+        for h in heads:
+            score = jnp.where(allowed, scores[w * len(heads) + h] * HEAD ** (-0.5), -1e30)
+            terms = jnp.exp(score - jnp.max(score, axis=0, keepdims=True))
             low = (terms * (1.0 / jnp.sum(terms, axis=0, keepdims=True))).astype(BF)
             probs[0, w, h] = low
-            part = dot_tn(low, v)
-            attended = part if attended is None else jnp.where(own, part, attended)
-        attn[span, :] = attended.astype(BF)
+            lows.append(low)
+    for w in windows:
+        v = qkv[2, spans[w], :]
+        attended = None
+        for h in heads:
+            part = dot_tn(lows[w * len(heads) + h], v)
+            attended = part if attended is None else jnp.where(own[h], part, attended)
+        attn[spans[w], :] = attended.astype(BF)
     tok_shape = (pooled.shape[0], rows)
     tok_of = (lax.broadcasted_iota(jnp.int32, tok_shape, 1) + shift) // POOL
     member = tok_of == lax.broadcasted_iota(jnp.int32, tok_shape, 0)
@@ -204,16 +225,11 @@
     )(at, d_ext, weight_out, pooled_attn)
 
 
-def backward_kernel(n, at, n_ref, qkv, probs, d_ref, even, odd, turned, grads):
+def backward_kernel(n, at, turned, qkv, probs, d_ref, even, odd, grads):
     shift, me = at[0], at[2]
-    rows = n_ref.shape[0]
+    rows = turned.shape[1]
     cols = d_ref.shape[1]
     block = even.shape[2]
-
-    @pl.when(pl.program_id(0) == 0)
-    def _():
-        turned[...] = n_ref[...].T
-
     tok_shape = (rows, d_ref.shape[0])
     tok_of = (lax.broadcasted_iota(jnp.int32, tok_shape, 0) + shift) // POOL
     member = tok_of == lax.broadcasted_iota(jnp.int32, tok_shape, 1)
@@ -245,8 +261,8 @@
                 ref[j, i] = term[:, i * cols : (i + 1) * cols]
 
 
-def encoder_backward(normed, qkv, probs, d_attn, at, n, first, count):
-    rows, width = normed.shape
+def encoder_backward(turned, qkv, probs, d_attn, at, n, first, count):
+    width, rows = turned.shape
     cols = 2 * HEAD
     windows = rows // WINDOW
     block = width // n
@@ -258,7 +274,7 @@
             num_scalar_prefetch=1,
             grid=(count,),
             in_specs=[
-                pl.BlockSpec((rows, width), lambda p, at: (0, 0)),
+                pl.BlockSpec((width, rows), lambda p, at: (0, 0)),
                 pl.BlockSpec((3, rows, cols), lambda p, at: (0, 0, p + first)),
                 pl.BlockSpec(
                     (1, windows, 2, WINDOW, WINDOW), lambda p, at: (p + first, 0, 0, 0, 0)
@@ -266,12 +282,12 @@
                 pl.BlockSpec((d_attn.shape[0], cols), lambda p, at: (0, p + first)),
             ],
             out_specs=[out, out],
-            scratch_shapes=[pltpu.VMEM((width, rows), BF), pltpu.VMEM((rows, 3 * cols), BF)],
+            scratch_shapes=[pltpu.VMEM((rows, 3 * cols), BF)],
         ),
         out_shape=[shape, shape],
         compiler_params=pltpu.CompilerParams(vmem_limit_bytes=VMEM_LIMIT),
         name="encoder_backward",
-    )(at, normed, qkv, probs, d_attn)
+    )(at, turned, qkv, probs, d_attn)
 
 
 def moves(order, piece):
@@ -289,82 +305,169 @@
     return [slice(r, min(r + CHUNK, rows)) for r in range(0, rows, CHUNK)]
 
 
-def lift_kernel(table, at, ta, tb, w_ref, gain, kva, kvb, lifted, send, keep, tok):
+def column_starts(order, at, block):
+    if order is None:
+        return None
+    me, group = at[2], at[4]
+    part = len(order) // 2
+    across = [
+        jnp.where(group == q, order[i], order[part + i]) | SPLIT
+        for q in range(2)
+        for i in range(part)
+    ]
+    return [pl.multiple_of((me ^ k) * block, block) for k in order + across]
+
+
+def weight_rows(order, here, got, other, bit):
+    flat = lambda w: w.reshape(-1, w.shape[-1])
+    across = bit if order is None else 1 - bit
+    parts = [flat(here[:, bit]), flat(got[:, across]), flat(other[:, across])]
+    return jnp.concatenate(parts, axis=0)
+
+
+def lift_kernel(table, order, at, ta, tb, here, got, other, gain, kva, kvb, lifted, send, keep, tok):
+    core, group = at[3], at[4]
     half = ta.shape[1]
     feats = kva.shape[0]
     cols = send.shape[1]
-    piece = ta.shape[0] // len(table) if table else 0
+    rows_all = ta.shape[0]
+    near = pl.ds(pl.multiple_of(core * half, half), half)
+    far = pl.ds(pl.multiple_of((1 - core) * half, half), half)
+    piece = rows_all // len(table) if table else 0
     for source_row, owner_row in table:
-        tok[owner_row : owner_row + piece, :half] = ta[source_row : source_row + piece]
-        tok[owner_row : owner_row + piece, half:] = tb[source_row : source_row + piece]
+        tok[owner_row : owner_row + piece, near] = ta[source_row : source_row + piece]
+        tok[owner_row : owner_row + piece, far] = tb[source_row : source_row + piece]
     if not table:
-        tok[:, :half] = ta[...]
-        tok[:, half:] = tb[...]
-    core = at[3]
-    for rows in chunks_of(tok.shape[0]):
-        product = dot(tok[rows], w_ref[...])
-        lifted[rows] = product
-        low = (product * gain[...]).astype(BF)
+        tok[:, near] = ta[...]
+        tok[:, far] = tb[...]
+    block = here.shape[2]
+    starts = column_starts(order, at, block)
+    for rows in chunks_of(rows_all):
+        x = tok[rows]
+        if starts:
+            x = jnp.concatenate([tok[rows, pl.ds(start, block)] for start in starts], axis=1)
+        lows = []
+        for bit in range(2):
+            span = slice(bit * feats, (bit + 1) * feats)
+            weight = weight_rows(order, here, got, other, bit)
+            product = dot(x, weight)
+            lifted[rows, span] = product
+            lows.append((product * gain[:, span]).astype(BF))
         for ref, side in ((send, 1 - core), (keep, core)):
             span = pl.ds(pl.multiple_of(side * cols, cols), cols)
-            part = dot(low[:, :feats], kva[:, span]) + dot(low[:, feats:], kvb[:, span])
+            part = dot(lows[0], kva[:, span]) + dot(lows[1], kvb[side ^ group])
             ref[rows] = part.astype(BF)
 
 
-def lift(table, at, ta, tb, weight, gain, kva, kvb):
+def lift(table, order, at, ta, tb, here, got, other, gain, kva, kvb):
     rows, half = ta.shape
-    cols = kva.shape[1] // 2
+    feats, cols = kva.shape[0], kva.shape[1] // 2
     whole = pl.BlockSpec(memory_space=pltpu.VMEM)
     return pl.pallas_call(
-        functools.partial(lift_kernel, table),
-        in_specs=[pl.BlockSpec(memory_space=pltpu.SMEM)] + [whole] * 6,
+        functools.partial(lift_kernel, table, order),
+        in_specs=[pl.BlockSpec(memory_space=pltpu.SMEM)] + [whole] * 8,
         out_specs=[whole] * 3,
         out_shape=[
-            jax.ShapeDtypeStruct((rows, weight.shape[1]), F32),
+            jax.ShapeDtypeStruct((rows, 2 * feats), F32),
             jax.ShapeDtypeStruct((rows, cols), BF),
             jax.ShapeDtypeStruct((rows, cols), BF),
         ],
         scratch_shapes=[pltpu.VMEM((rows, 2 * half), BF)],
         compiler_params=pltpu.CompilerParams(vmem_limit_bytes=VMEM_LIMIT),
         name="lift",
-    )(at, ta, tb, weight, gain, kva, kvb)
-
-
-def lower_kernel(table, at, ca, cb, kva, kvb, lifted, gain, inv, pull, w_ref, send, keep):
+    )(at, ta, tb, here, got, other, gain, kva, kvb)
+
+
+def two_parts(column):
+    high = column.astype(BF)
+    return high, (column - high.astype(F32)).astype(BF)
+
+
+def finish_kernel(mine, got, squares, d_kv, kv, load):
+    rows, cols = kv.shape
+    total = mine[...].astype(F32) + got[...].astype(F32)
+    mean = jnp.broadcast_to(squares[...], (rows, rows)).T[:, :1] * (1.0 / LLM_D)
+    inv = lax.rsqrt(mean + 1e-05)
+    low = (total * inv).astype(BF)
+    kv[...] = low
+    cot = (low.astype(F32) + d_kv[...].astype(F32)).astype(BF)
+    load[:, :cols] = cot
+    inner = jnp.sum(cot.astype(F32) * total, axis=1, keepdims=True)
+    lane = lax.broadcasted_iota(jnp.int32, (rows, load.shape[1] - cols), 1)
+    extra = jnp.zeros(lane.shape, F32)
+    for i, part in enumerate(two_parts(inv) + two_parts(inner)):
+        extra = jnp.where(lane == i, part.astype(F32), extra)
+    load[:, cols:] = extra.astype(BF)
+
+
+def finish(mine, got, squares, d_kv):
+    rows, cols = mine.shape
+    return pl.pallas_call(
+        finish_kernel,
+        out_shape=[
+            jax.ShapeDtypeStruct((rows, cols), BF),
+            jax.ShapeDtypeStruct((rows, cols + LANES), BF),
+        ],
+        compiler_params=pltpu.CompilerParams(vmem_limit_bytes=VMEM_LIMIT),
+        name="finish",
+    )(mine, got, squares, d_kv)
+
+
+def lower_kernel(table, order, at, ca, cb, here, got, other, gain, kva, kvb, lifted, send, keep, nat):
+    core, group = at[3], at[4]
     half = send.shape[1]
-    cols = ca.shape[1]
-    core = at[3]
-    own = pl.ds(pl.multiple_of(core * cols, cols), cols)
-    other = pl.ds(pl.multiple_of((1 - core) * cols, cols), cols)
+    feats = kva.shape[0]
+    cols = kva.shape[1] // 2
+    block = here.shape[2]
+    starts = column_starts(order, at, block)
+    near = pl.ds(pl.multiple_of(core * half, half), half)
+    far = pl.ds(pl.multiple_of((1 - core) * half, half), half)
     piece = ca.shape[0] // len(table) if table else 0
     for rows in chunks_of(ca.shape[0]):
-        parts = [
-            dot_nt(ca[rows], w[:, own]) + dot_nt(cb[rows], w[:, other]) for w in (kva, kvb)
-        ]
-        d_normed = jnp.concatenate(parts, axis=1)
-        d_lifted = inv[rows] * gain[...] * d_normed - lifted[rows] * pull[rows]
-        low = d_lifted.astype(BF)
-        for ref, w in ((send, w_ref[half:]), (keep, w_ref[:half])):
-            part = dot_nt(low, w).astype(BF)
-            if not table:
-                ref[rows] = part
-            for source_row, owner_row in table:
-                if rows.start <= owner_row < rows.stop:
-                    at_row = owner_row - rows.start
-                    ref[source_row : source_row + piece] = part[at_row : at_row + piece]
-
-
-def lower(table, at, ca, cb, kva, kvb, lifted, gain, inv, pull, weight):
+        extra = ca[rows, cols:].astype(F32)
+        extra_b = cb[rows, cols:].astype(F32)
+        inv = extra[:, 0:1] + extra[:, 1:2]
+        inner = extra[:, 2:3] + extra[:, 3:4] + extra_b[:, 2:3] + extra_b[:, 3:4]
+        pull = inv * inv * inv * inner * (1.0 / LLM_D)
+        cots = ((ca[rows, :cols], core), (cb[rows, :cols], 1 - core))
+        d_tok = None
+        for bit in range(2):
+            d_normed = None
+            for cot, side in cots:
+                span = pl.ds(pl.multiple_of(side * cols, cols), cols)
+                part = dot_nt(cot, kvb[side ^ group] if bit else kva[:, span])
+                d_normed = part if d_normed is None else d_normed + part
+            span = slice(bit * feats, (bit + 1) * feats)
+            low = (inv * gain[:, span] * d_normed - lifted[rows, span] * pull).astype(BF)
+            weight = weight_rows(order, here, got, other, bit)
+            part = dot_nt(low, weight)
+            d_tok = part if d_tok is None else d_tok + part
+        if not starts:
+            nat[rows] = d_tok.astype(BF)
+        for i, start in enumerate(starts or ()):
+            nat[rows, pl.ds(start, block)] = d_tok[:, i * block : (i + 1) * block].astype(BF)
+    for source_row, owner_row in table:
+        send[source_row : source_row + piece] = nat[owner_row : owner_row + piece, far]
+        keep[source_row : source_row + piece] = nat[owner_row : owner_row + piece, near]
+    if not table:
+        send[...] = nat[:, far]
+        keep[...] = nat[:, near]
+
+
+def lower(table, order, at, ca, cb, here, got, other, gain, kva, kvb, lifted):
+    rows = ca.shape[0]
+    width = 2 * here.shape[0] * here.shape[2]
     whole = pl.BlockSpec(memory_space=pltpu.VMEM)
-    out = jax.ShapeDtypeStruct((ca.shape[0], weight.shape[0] // 2), BF)
+    out = jax.ShapeDtypeStruct((rows, width // 2), BF)
     return pl.pallas_call(
-        functools.partial(lower_kernel, table),
+        functools.partial(lower_kernel, table, order),
         in_specs=[pl.BlockSpec(memory_space=pltpu.SMEM)] + [whole] * 9,
         out_specs=[whole] * 2,
         out_shape=[out] * 2,
+        scratch_shapes=[pltpu.VMEM((rows, width), BF)],
         compiler_params=pltpu.CompilerParams(vmem_limit_bytes=VMEM_LIMIT),
         name="lower",
-    )(at, ca, cb, kva, kvb, lifted, gain, inv, pull, weight)
+    )(at, ca, cb, here, got, other, gain, kva, kvb, lifted)
 
 
 def on_device(frames, weight_qkv, weight_out, proj_in, norm_gain, proj_kv, shifts, route, d_kv):
@@ -383,17 +486,13 @@
 
     part = lax.dynamic_slice_in_dim(frames, core * (WINDOW // 2), WINDOW // 2, 0)
     mine = to_tm(part, -1, False)
-    other = swap_mp(mine)
-    halo = jnp.where(
-        core == 0, jnp.concatenate([mine, other], 0), jnp.concatenate([other, mine], 0)
-    )
-    x_roll = lax.dynamic_slice_in_dim(jnp.concatenate([frames, halo], 0), shift, rows, 0)
-
-    proj_in, proj_kv, x_roll = lax.optimization_barrier((proj_in, proj_kv, x_roll))
-    kva, kvb = proj_kv, swap_tm(proj_kv, SPLIT)
+    w_t = jnp.transpose(weight_qkv, (1, 2, 0)).reshape(-1, width)
+    proj_in, proj_kv, w_t = lax.optimization_barrier((proj_in, proj_kv, w_t))
+
     masks = group_bits()
     order = offsets(masks)
     members = order + [k | SPLIT for k in order]
+    count = n // 2
     blocks = []
     for k in order:
         pair = [
@@ -402,14 +501,47 @@
         ]
         pair = jnp.stack(pair)
         blocks.append(swap_tm(pair, k) if k else pair)
-    here = jnp.stack(blocks, axis=1)
-    there = swap_tm(here[::-1], SPLIT)
-    lift_w = jnp.concatenate([here, there], axis=1)
-    natural = (jnp.arange(n, dtype=jnp.int32) + core * (n // 2)) % n
-    found = (natural ^ me)[:, None] == jnp.array(members, jnp.int32)[None, :]
-    place = jnp.sum(found * jnp.arange(n, dtype=jnp.int32)[None, :], axis=1)
-    lift_w = jnp.take(lift_w, place, axis=1).reshape(2, width, feats)
-    lift_w = jnp.concatenate([lift_w[0], lift_w[1]], axis=1)
+    here = jnp.stack(blocks)
+    group = lax.axis_index("groups")
+    if lax.axis_size("groups") == 2:
+        swap_groups = lambda block: lax.ppermute(block, "groups", [(0, 1), (1, 0)])
+        kv_near = swap_tm(lax.dynamic_slice_in_dim(proj_kv, group * kv_half, kv_half, 1), SPLIT)
+        kv_far = swap_groups(kv_near)
+        in_near = swap_tm(
+            lax.dynamic_slice_in_dim(here, group * (count // 2), count // 2, 0), SPLIT
+        )
+        in_far = swap_groups(in_near)
+    else:
+        group = group * 0
+        kv_near = swap_tm(proj_kv[:, :kv_half], SPLIT)
+        kv_far = swap_tm(proj_kv[:, kv_half:], SPLIT)
+        in_near = swap_tm(here[: count // 2], SPLIT)
+        in_far = swap_tm(here[count // 2 :], SPLIT)
+    kva, kvb = proj_kv, jnp.stack([kv_near, kv_far])
+    at_rows = order
+    if width // n % LANES:
+        stacked = jnp.concatenate([here, in_near[:, ::-1], in_far[:, ::-1]])
+        source = jnp.arange(n, dtype=jnp.int32) ^ me
+        found = source[:, None] == jnp.array(members, jnp.int32)[None, :]
+        place = jnp.sum(found * jnp.arange(n, dtype=jnp.int32)[None, :], axis=1)
+        stacked = jnp.take(stacked, place, axis=0)
+        here, in_near, in_far = jnp.split(stacked, [count, count + count // 2])
+        at_rows = None
+
+    other = swap_mp(mine)
+    halo = jnp.where(
+        core == 0, jnp.concatenate([mine, other], 0), jnp.concatenate([other, mine], 0)
+    )
+    x_roll = lax.dynamic_slice_in_dim(jnp.concatenate([frames, halo], 0), shift, rows, 0)
+
+    at = jnp.stack([shift, rows * n - shift - me * rows, me, core, group]).astype(jnp.int32)
+    normed, qkv, probs, pooled_attn, out_part = encoder_forward(
+        x_roll, w_t, weight_out, at, ext_tok
+    )
+    turned = normed.T
+    route, norm_gain, d_kv, pooled_attn = lax.optimization_barrier(
+        (route, norm_gain, d_kv, pooled_attn)
+    )
     gain = jnp.concatenate(
         [
             lax.dynamic_slice_in_dim(norm_gain, (me ^ bit) * feats, feats, 0)
@@ -424,13 +556,8 @@
         [k | bit for k in order for bit in (0, SPLIT)], jnp.int32
     )
     spread = jnp.kron(spread.astype(BF), jnp.eye(piece, dtype=BF))
-    d_kv = dot_tn(spread, d_kv)
-
-    w_t = jnp.transpose(weight_qkv, (1, 2, 0)).reshape(-1, width)
-    at = jnp.stack([shift, rows * n - shift - me * rows, me, core]).astype(jnp.int32)
-    normed, qkv, probs, pooled_attn, out_part = encoder_forward(
-        x_roll, w_t, weight_out, at, ext_tok
-    )
+    d_kv = dot_tn(spread, d_kv).astype(BF)
+
     out_low = out_part.astype(BF)
     low_own = lax.dynamic_slice_in_dim(out_low, core * half_w, half_w, 1)
     low_other = lax.dynamic_slice_in_dim(out_low, (1 - core) * half_w, half_w, 1)
@@ -450,7 +577,6 @@
     tail = tail_a.astype(F32) + tail_b.astype(F32)
     pooled = jnp.concatenate([pooled[:tail_tok] + tail, pooled[tail_tok:]], 0).astype(BF)
 
-    count = n // 2
     sorted_tok = dot(sort, pooled).astype(BF).reshape(2, count * piece, half_w)
     pair_tok = jnp.stack([sorted_tok[0], swap_tm(sorted_tok[1], SPLIT)])
     tok_half = gather_doubling(pair_tok, masks).reshape(-1, half_w)
@@ -463,24 +589,19 @@
         at_owner = source_rows[np.argsort(owner_rows)]
         tok_half, tok_other = tok_half[at_owner], tok_other[at_owner]
         table = []
-    lifted, kv_send, kv_keep = lift(table, at, tok_half, tok_other, lift_w, gain, kva, kvb)
+    lifted, kv_send, kv_keep = lift(
+        table, at_rows, at, tok_half, tok_other, here, in_near, in_far, gain, kva, kvb
+    )
     squares = jnp.sum(lifted * lifted, axis=-1).reshape(count, own_tok)
     square_sum = scatter_halving(squares + swap_mp(squares), masks, F32)
-    inv_rms = lax.rsqrt(square_sum / LLM_D + 1e-05)
     kv_part = kv_keep.astype(F32) + swap_mp(kv_send).astype(F32)
-    kv_sum = scatter_halving(kv_part.reshape(count, own_tok, kv_half), masks, BF)
-    kv_low = (kv_sum * inv_rms[:, None]).astype(BF)
-    total_cot = (kv_low.astype(F32) + d_kv).astype(BF)
+    kv_mine, kv_got = scatter_last(kv_part.reshape(count, own_tok, kv_half), masks)
+    kv_low, load = finish(kv_mine, kv_got, square_sum.reshape(1, own_tok), d_kv)
     kv = dot(spread, kv_low).astype(BF)
-    inner = jnp.sum(total_cot.astype(F32) * kv_sum, axis=-1)
-    inner = inner + swap_mp(inner)
-    stats = gather_doubling(jnp.stack([inv_rms, inner]), masks)
-    inv_all = stats[:, 0].reshape(-1, 1)
-    pull = inv_all**3 * stats[:, 1].reshape(-1, 1) / LLM_D
-    cot_half = gather_doubling(total_cot, masks).reshape(-1, kv_half)
+    cot_half = gather_doubling(load, masks).reshape(count * own_tok, -1)
     cot_other = swap_mp(cot_half)
     d_send, d_keep = lower(
-        table, at, cot_half, cot_other, kva, kvb, lifted, gain, inv_all, pull, lift_w
+        table, at_rows, at, cot_half, cot_other, here, in_near, in_far, gain, kva, kvb, lifted
     )
     if by_xla:
         at_source = owner_rows[np.argsort(source_rows)]
@@ -500,10 +621,11 @@
     )
     d_attn, out_even, out_odd = out_grad(d_ext, weight_out, pooled_attn, at, n)
     grad_out = scatter_pair(out_even, out_odd)
-    chunks, count = [], weight_out.shape[0] // (4 * HEAD)
-    for first in range(0, 2 * count, count):
-        even, odd = encoder_backward(normed, qkv, probs, d_attn, at, n, first, count)
+    chunks, first = [], 0
+    for pairs in (2, 1, 1):
+        even, odd = encoder_backward(turned, qkv, probs, d_attn, at, n, first, pairs)
         chunks.append(scatter_pair(even, odd))
+        first += pairs
     grad_qkv = jnp.transpose(jnp.concatenate(chunks, axis=-1), (1, 0, 2))
     return kv, grad_qkv, grad_out
 

time: 322 us -> 295 us (0.916)
  waiting for transfers between devices: 184 us -> 163 us
  starting transfers between devices: 42.9 us -> 51.3 us
  Pallas kernels: 43.5 us -> 38.1 us
  local copies, waits for them, and re-layouts: 25.9 us -> 21.1 us
  other arithmetic: 18.6 us -> 14.4 us
    ppermute x28 -> x29, waiting for transfers between devices: 169 us -> 137 us  [swap_tm(): return lax.ppermute(block, 'tm', [(i, i ^ mask) for i in range(n)])]
    ppermute x0 -> x2, waiting for transfers between devices: none -> 14.7 us  [on_device(): swap_groups = lambda block: lax.ppermute(block, 'groups', [(0, 1), (1, 0)])]
    ppermute x5, waiting for transfers between devices: 8.84 us -> 2.6 us  [to_tm(): return lax.ppermute(block, ('tm', 'mp'), pairs)]
    ppermute x5, starting transfers between devices: 11.5 us -> 15.2 us  [to_tm(): return lax.ppermute(block, ('tm', 'mp'), pairs)]
    gather x1 -> x0, local copies, waits for them, and re-layouts: 3.63 us -> none  [on_device(): lift_w = jnp.take(lift_w, place, axis=1).reshape(2, width, feats)]
    pallas_call x1, Pallas kernels: 15 us -> 11.8 us  [encoder_forward(): pl.pallas_call(forward_kernel, grid_spec=pltpu.PrefetchScalarGridSpec(num...]
    ppermute x9 -> x8, waiting for transfers between devices: 6.16 us -> 8.39 us  [swap_mp(): return lax.ppermute(block, 'mp', [(i, n - 1 - i) for i in range(n)])]
    unnamed x48 -> x41, local copies, waits for them, and re-layouts: 6.89 us -> 5.12 us
  transfers between devices with their start and end apart: 42 -> 44, of which waited for: 26 -> 27; matrix products, arithmetic and copies ran while one was open for 12% -> 10% of each run, Pallas kernels for 9% -> 7%
where the time goes in v2:
time: 295 us; the launch traced here: 294 us
  waiting for transfers between devices  163 us (55%)
  starting transfers between devices  51.3 us (17%)
  Pallas kernels  38.1 us (13%)
  local copies, waits for them, and re-layouts  21.1 us (7%)
  other arithmetic  14.4 us (5%)
  between operations  3.94 us (1%)
    ppermute x29, waiting for transfers between devices, swap_tm(): return lax.ppermute(block, 'tm', [(i, i ^ mask) for i in range(n)])  137 us
    ppermute x29, starting transfers between devices, swap_tm(): return lax.ppermute(block, 'tm', [(i, i ^ mask) for i in range(n)])  31.7 us
    ppermute x5, starting transfers between devices, to_tm(): return lax.ppermute(block, ('tm', 'mp'), pairs)  15.2 us
    ppermute x2, waiting for transfers between devices, on_device(): swap_groups = lambda block: lax.ppermute(block, 'groups', [(0, 1), (1, 0)])  14.7 us
    pallas_call x3, Pallas kernels, encoder_backward(): pl.pallas_call(functools.partial(backward_kernel, n), grid_spec=pltpu.Pre...  11.8 us
    pallas_call x1, Pallas kernels, encoder_forward(): pl.pallas_call(forward_kernel, grid_spec=pltpu.PrefetchScalarGridSpec(num...  11.8 us
    ppermute x8, waiting for transfers between devices, swap_mp(): return lax.ppermute(block, 'mp', [(i, n - 1 - i) for i in range(n)])  8.39 us
    pallas_call x1, Pallas kernels, lower(): pl.pallas_call(functools.partial(lower_kernel, table, order), in_specs=[p...  6.76 us
  transfers between devices with their start and end apart: 44, of which 27 were waited for; matrix products, arithmetic and copies ran while one was open for 10% of the time, Pallas kernels for 7%

profile of v2, /device:TPU:0, one launch (start us, length us, event | category | flops | bytes accessed | tf_op | source)
XLA Modules:
  0.0 294.3 jit_solution(10463898090553553391)
XLA Ops:
  2.4 6.0 %collective-permute-start = (bf16[128,1024]{1,0:T(8,128)(2,1)}, bf16[128,1024]{1,0:T(8,128)(2,1)}, u32[]{:S(2)}, u32[]{:S(2)}) collective-permute-start(bf16[128,1024]{1,0:T(8,128)(2,1)} %constant_dynamic-slice_fusion.4), channel_id=1, source_target_pairs={{0,14},{1,15},{2,0},{3,1},{4,2},{5,3},{6,4},{7,5},{8,6},{9,7},{10,... | collective-permute-start | bytes 786440 | tf_op jit(solution)/shard_map/ppermute | solution.py:51
  8.4 4.8 %copy.14 = bf16[3,512,1024]{2,1,0:T(8,128)(2,1)} copy(bf16[3,512,1024]{1,2,0:T(8,128)(2,1)} %bitcast.93) | data formatting | bytes 6291456 | tf_op jit(solution)/shard_map/transpose | solution.py:489
  15.1 3.4 %collective-permute-start.11 = (bf16[2,128,512]{2,1,0:T(8,128)(2,1)S(1)}, bf16[2,128,512]{2,1,0:T(8,128)(2,1)}, u32[]{:S(2)}, u32[]{:S(2)}) collective-permute-start(bf16[2,128,512]{2,1,0:T(8,128)(2,1)S(1)} %pad_maximum_fusion.8), channel_id=1, source_target_pairs={{0,12},{2,14},{4,8},{6,10},{8,4},{10,6},{12,0},{14,2},{1,13},{3,15... | collective-permute-start | bytes 786440 | tf_op jit(solution)/shard_map/ppermute | solution.py:37
  23.7 4.2 %collective-permute-done.9 = bf16[2,128,512]{2,1,0:T(8,128)(2,1)} collective-permute-done((bf16[2,128,512]{2,1,0:T(8,128)(2,1)S(1)}, bf16[2,128,512]{2,1,0:T(8,128)(2,1)}, u32[]{:S(2)}, u32[]{:S(2)}) %collective-permute-start.9) | collective-permute-done | bytes 262176 | tf_op jit(solution)/shard_map/ppermute | solution.py:37
  27.9 5.4 %collective-permute-done.10 = bf16[2,128,512]{2,1,0:T(8,128)(2,1)} collective-permute-done((bf16[2,128,512]{2,1,0:T(8,128)(2,1)S(1)}, bf16[2,128,512]{2,1,0:T(8,128)(2,1)}, u32[]{:S(2)}, u32[]{:S(2)}) %collective-permute-start.10) | collective-permute-done | bytes 262176 | tf_op jit(solution)/shard_map/ppermute | solution.py:37
  37.2 11.8 %encoder_forward.1 = (bf16[512,1024]{1,0:T(8,128)(2,1)S(1)}, bf16[3,512,512]{2,1,0:T(8,128)(2,1)S(1)}, bf16[4,2,2,256,256]{4,3,2,1,0:T(8,128)(2,1)}, bf16[192,512]{1,0:T(8,128)(2,1)S(1)}, f32[192,1024]{1,0:T(8,128)S(1)}) custom-call(s32[5]{0:T(128)S(1)} %stack.85.at, bf16[512,1024]{1,0:T(8,128)(2,1)S(1)} %fusion.x_ref, bf16[1536,1024]{1,0:T(8,128)(2,1)} %bitcast.90, ...), custom_call_target="tpu_custom_call" | custom-call | tf_op jit(solution)/shard_map/encoder_forward/pallas_call | solution.py:168
  53.3 5.8 %collective-permute-start.4 = (bf16[64,512]{1,0:T(8,128)(2,1)}, bf16[64,512]{1,0:T(8,128)(2,1)}, u32[]{:S(2)}, u32[]{:S(2)}) collective-permute-start(bf16[64,512]{1,0:T(8,128)(2,1)} %get-tuple-element.74), channel_id=1, source_target_pairs={{0,3},{1,2},{2,5},{3,4},{4,7},{5,6},{6,9},{7,8},{8,11},{9,10},{10,... | collective-permute-start | bytes 196616 | tf_op jit(solution)/shard_map/ppermute | solution.py:51
  72.1 6.1 %collective-permute-done.6 = bf16[1,2,64,512]{3,2,1,0:T(8,128)(2,1)S(1)} collective-permute-done((bf16[1,2,64,512]{3,2,1,0:T(8,128)(2,1)S(1)}, bf16[1,2,64,512]{3,2,1,0:T(8,128)(2,1)S(1)}, u32[]{:S(2)}, u32[]{:S(2)}) %collective-permute-start.6) | collective-permute-done | bytes 131104 | tf_op jit(solution)/shard_map/ppermute | solution.py:37
  81.7 3.0 %collective-permute-done.7 = bf16[2,2,64,512]{3,2,1,0:T(8,128)(2,1)S(1)} collective-permute-done((bf16[2,2,64,512]{3,2,1,0:T(8,128)(2,1)S(1)}, bf16[2,2,64,512]{3,2,1,0:T(8,128)(2,1)S(1)}, u32[]{:S(2)}, u32[]{:S(2)}) %collective-permute-start.7) | collective-permute-done | bytes 262176 | tf_op jit(solution)/shard_map/ppermute | solution.py:37
  85.6 7.8 %collective-permute-done.15 = bf16[512,1024]{1,0:T(8,128)(2,1)S(1)} collective-permute-done((bf16[512,1024]{1,0:T(8,128)(2,1)}, bf16[512,1024]{1,0:T(8,128)(2,1)S(1)}, u32[]{:S(2)}, u32[]{:S(2)}) %collective-permute-start.15) | collective-permute-done | bytes 1048608 | tf_op jit(solution)/shard_map/ppermute | solution.py:507
  93.4 2.7 pad_maximum_fusion.kvb
  96.1 6.9 %collective-permute-done.13.other = bf16[2,2,128,512]{3,2,1,0:T(8,128)(2,1)S(1)} collective-permute-done((bf16[2,2,128,512]{3,2,1,0:T(8,128)(2,1)S(1)}, bf16[2,2,128,512]{3,2,1,0:T(8,128)(2,1)S(1)}, u32[]{:S(2)}, u32[]{:S(2)}) %collective-permute-start.13) | collective-permute-done | bytes 524320 | tf_op jit(solution)/shard_map/ppermute | solution.py:507
  103.0 5.7 %lift.1 = (f32[512,1024]{1,0:T(8,128)}, bf16[512,1024]{1,0:T(8,128)(2,1)S(1)}, bf16[512,1024]{1,0:T(8,128)(2,1)S(1)}) custom-call(s32[5]{0:T(128)S(1)} %stack.85.at, bf16[512,512]{1,0:T(8,128)(2,1)S(1)} %bitcast.83, bf16[512,512]{1,0:T(8,128)(2,1)S(1)} %collective-permute-done.8.tb, bf16[4,2,128,512]{3,2,1,0:T(8,128)(2,1)S(1)} %pad_maximum_fusion.2.here, ...), custom_call_target="tpu_custom_call" | custom-call | tf_op jit(solution)/shard_map/lift/pallas_call | solution.py:366
  108.9 2.6 collective-permute-done.16
  117.4 10.4 %collective-permute-done.20 = f32[2,128]{1,0:T(2,128)S(1)} collective-permute-done((f32[2,128]{1,0:T(2,128)S(1)}, f32[2,128]{1,0:T(2,128)S(1)}, u32[]{:S(2)}, u32[]{:S(2)}) %collective-permute-start.20) | collective-permute-done | bytes 1056 | tf_op jit(solution)/shard_map/ppermute | solution.py:37
  132.4 12.6 %collective-permute-done.18 = bf16[1,128,1024]{2,1,0:T(8,128)(2,1)S(1)} collective-permute-done((bf16[1,128,1024]{2,1,0:T(8,128)(2,1)S(1)}, bf16[1,128,1024]{2,1,0:T(8,128)(2,1)S(1)}, u32[]{:S(2)}, u32[]{:S(2)}) %collective-permute-start.18) | collective-permute-done | bytes 262176 | tf_op jit(solution)/shard_map/ppermute | solution.py:37
  145.5 15.5 %collective-permute-done.22 = bf16[1,128,1152]{2,1,0:T(8,128)(2,1)S(1)} collective-permute-done((bf16[1,128,1152]{2,1,0:T(8,128)(2,1)S(1)}, bf16[1,128,1152]{2,1,0:T(8,128)(2,1)S(1)}, u32[]{:S(2)}, u32[]{:S(2)}) %collective-permute-start.22) | collective-permute-done | bytes 294944 | tf_op jit(solution)/shard_map/ppermute | solution.py:37
  161.1 15.2 %collective-permute-done.23 = bf16[2,128,1152]{2,1,0:T(8,128)(2,1)S(1)} collective-permute-done((bf16[2,128,1152]{2,1,0:T(8,128)(2,1)S(1)}, bf16[2,128,1152]{2,1,0:T(8,128)(2,1)S(1)}, u32[]{:S(2)}, u32[]{:S(2)}) %collective-permute-start.23) | collective-permute-done | bytes 589856 | tf_op jit(solution)/shard_map/ppermute | solution.py:37
  176.6 2.8 collective-permute-done.24.cb
  179.4 6.8 %lower.1 = (bf16[512,512]{1,0:T(8,128)(2,1)S(1)}, bf16[512,512]{1,0:T(8,128)(2,1)S(1)}) custom-call(s32[5]{0:T(128)S(1)} %stack.85.at, bf16[512,1152]{1,0:T(8,128)(2,1)S(1)} %bitcast.81, bf16[512,1152]{1,0:T(8,128)(2,1)S(1)} %collective-permute-done.24.cb, bf16[4,2,128,512]{3,2,1,0:T(8,128)(2,1)S(1)} %pad_maximum_fusion.2.here, ...), custom_call_target="tpu_custom_call" | custom-call | tf_op jit(solution)/shard_map/lower/pallas_call | solution.py:462
  188.7 8.1 %collective-permute-done.26 = bf16[2,2,64,512]{3,2,1,0:T(8,128)(2,1)S(1)} collective-permute-done((bf16[2,2,64,512]{3,2,1,0:T(8,128)(2,1)S(1)}, bf16[2,2,64,512]{3,2,1,0:T(8,128)(2,1)S(1)}, u32[]{:S(2)}, u32[]{:S(2)}) %collective-permute-start.26) | collective-permute-done | bytes 262176 | tf_op jit(solution)/shard_map/ppermute | solution.py:37
  197.5 7.5 %collective-permute-done.27 = bf16[1,2,64,512]{3,2,1,0:T(8,128)(2,1)S(1)} collective-permute-done((bf16[1,2,64,512]{3,2,1,0:T(8,128)(2,1)S(1)}, bf16[1,2,64,512]{3,2,1,0:T(8,128)(2,1)S(1)}, u32[]{:S(2)}, u32[]{:S(2)}) %collective-permute-start.27) | collective-permute-done | bytes 131104 | tf_op jit(solution)/shard_map/ppermute | solution.py:37
  205.8 3.6 %collective-permute-done.28 = bf16[64,512]{1,0:T(8,128)(2,1)S(1)} collective-permute-done((bf16[64,512]{1,0:T(8,128)(2,1)S(1)}, bf16[64,512]{1,0:T(8,128)(2,1)S(1)}, u32[]{:S(2)}, u32[]{:S(2)}) %collective-permute-start.28) | collective-permute-done | bytes 65568 | tf_op jit(solution)/shard_map/ppermute | solution.py:37
  221.3 2.8 encoder_backward.5
  225.5 2.8 encoder_backward.4
  231.3 6.3 %encoder_backward.3 = (bf16[4,3,128,256]{3,2,1,0:T(8,128)(2,1)S(1)}, bf16[4,3,128,256]{3,2,1,0:T(8,128)(2,1)S(1)}) custom-call(s32[5]{0:T(128)S(1)} %stack.85.at, bf16[1024,512]{1,0:T(8,128)(2,1)S(1)} %bitcast.79, bf16[3,512,512]{2,1,0:T(8,128)(2,1)S(1)} %copy-done.4, bf16[4,2,2,256,256]{4,3,2,1,0:T(8,128)(2,1)} %get-tuple-element.45.probs, ...), custom_call_target="tpu_custom_call" | custom-call | tf_op jit(solution)/shard_map/encoder_backward/pallas_call | solution.py:271
  239.0 16.9 %collective-permute-done.35 = bf16[4,3,128,128]{3,2,1,0:T(8,128)(2,1)S(1)} collective-permute-done((bf16[4,3,128,128]{3,2,1,0:T(8,128)(2,1)S(1)}, bf16[4,3,128,128]{3,2,1,0:T(8,128)(2,1)S(1)}, u32[]{:S(2)}, u32[]{:S(2)}) %collective-permute-start.35) | collective-permute-done | bytes 393248 | tf_op jit(solution)/shard_map/ppermute | solution.py:37
  260.0 4.9 %collective-permute-done.36 = bf16[2,3,128,128]{3,2,1,0:T(8,128)(2,1)S(1)} collective-permute-done((bf16[2,3,128,128]{3,2,1,0:T(8,128)(2,1)S(1)}, bf16[2,3,128,128]{3,2,1,0:T(8,128)(2,1)S(1)}, u32[]{:S(2)}, u32[]{:S(2)}) %collective-permute-start.36) | collective-permute-done | bytes 196640 | tf_op jit(solution)/shard_map/ppermute | solution.py:37
  266.4 4.3 %collective-permute-done.32 = bf16[4,3,128,256]{3,2,1,0:T(8,128)(2,1)S(1)} collective-permute-done((bf16[4,3,128,256]{3,2,1,0:T(8,128)(2,1)S(1)}, bf16[4,3,128,256]{3,2,1,0:T(8,128)(2,1)S(1)}, u32[]{:S(2)}, u32[]{:S(2)}) %collective-permute-start.32) | collective-permute-done | bytes 786464 | tf_op jit(solution)/shard_map/ppermute | solution.py:37
  271.9 3.0 %collective-permute-start.43 = (bf16[1,64,1024]{2,1,0:T(8,128)(2,1)S(1)}, bf16[1,64,1024]{2,1,0:T(8,128)(2,1)S(1)}, u32[]{:S(2)}, u32[]{:S(2)}) collective-permute-start(bf16[1,64,1024]{2,1,0:T(8,128)(2,1)S(1)} %slice.211), channel_id=1, source_target_pairs={{0,8},{2,10},{4,12},{6,14},{8,0},{10,2},{12,4},{14,6},{1,9},{3,11}... | collective-permute-start | bytes 393224 | tf_op jit(solution)/shard_map/ppermute | solution.py:37
  274.9 8.2 %collective-permute-done.33 = bf16[2,3,128,256]{3,2,1,0:T(8,128)(2,1)S(1)} collective-permute-done((bf16[2,3,128,256]{3,2,1,0:T(8,128)(2,1)S(1)}, bf16[2,3,128,256]{3,2,1,0:T(8,128)(2,1)S(1)}, u32[]{:S(2)}, u32[]{:S(2)}) %collective-permute-start.33) | collective-permute-done | bytes 393248 | tf_op jit(solution)/shard_map/ppermute | solution.py:37
  285.2 8.0 %collective-permute-done.34 = bf16[1,3,128,256]{3,2,1,0:T(8,128)(2,1)S(1)} collective-permute-done((bf16[1,3,128,256]{3,2,1,0:T(8,128)(2,1)S(1)}, bf16[1,3,128,256]{3,2,1,0:T(8,128)(2,1)S(1)}, u32[]{:S(2)}, u32[]{:S(2)}) %collective-permute-start.34) | collective-permute-done | bytes 196640 | tf_op jit(solution)/shard_map/ppermute | solution.py:37
  (187 shorter events, 74.5 us)
Async XLA Ops:
  2.4 17.4 %collective-permute-start = (bf16[128,1024]{1,0:T(8,128)(2,1)}, bf16[128,1024]{1,0:T(8,128)(2,1)}, u32[]{:S(2)}, u32[]{:S(2)}) collective-permute-start(bf16[128,1024]{1,0:T(8,128)(2,1)} %constant_dynamic-slice_fusion.4), channel_id=1, source_target_pairs={{0,14},{1,15},{2,0},{3,1},{4,2},{5,3},{6,4},{7,5},{8,6},{9,7},{10,... | collective-permute-start | bytes 786440 | tf_op jit(solution)/shard_map/ppermute | solution.py:51
  13.9 13.9 %collective-permute-start.9 = (bf16[2,128,512]{2,1,0:T(8,128)(2,1)S(1)}, bf16[2,128,512]{2,1,0:T(8,128)(2,1)}, u32[]{:S(2)}, u32[]{:S(2)}) collective-permute-start(bf16[2,128,512]{2,1,0:T(8,128)(2,1)S(1)} %pad_maximum_fusion.6), channel_id=1, source_target_pairs={{0,8},{2,10},{4,12},{6,14},{8,0},{10,2},{12,4},{14,6},{1,9},{3,11}... | collective-permute-start | bytes 786440 | tf_op jit(solution)/shard_map/ppermute | solution.py:37
  14.1 19.2 %collective-permute-start.10 = (bf16[2,128,512]{2,1,0:T(8,128)(2,1)S(1)}, bf16[2,128,512]{2,1,0:T(8,128)(2,1)}, u32[]{:S(2)}, u32[]{:S(2)}) collective-permute-start(bf16[2,128,512]{2,1,0:T(8,128)(2,1)S(1)} %pad_maximum_fusion.7), channel_id=1, source_target_pairs={{0,4},{2,6},{4,0},{6,2},{8,12},{10,14},{12,8},{14,10},{1,5},{3,7},... | collective-permute-start | bytes 786440 | tf_op jit(solution)/shard_map/ppermute | solution.py:37
  15.1 18.1 %collective-permute-start.11 = (bf16[2,128,512]{2,1,0:T(8,128)(2,1)S(1)}, bf16[2,128,512]{2,1,0:T(8,128)(2,1)}, u32[]{:S(2)}, u32[]{:S(2)}) collective-permute-start(bf16[2,128,512]{2,1,0:T(8,128)(2,1)S(1)} %pad_maximum_fusion.8), channel_id=1, source_target_pairs={{0,12},{2,14},{4,8},{6,10},{8,4},{10,6},{12,0},{14,2},{1,13},{3,15... | collective-permute-start | bytes 786440 | tf_op jit(solution)/shard_map/ppermute | solution.py:37
  19.7 47.4 %collective-permute-start.14 = (bf16[512,1024]{1,0:T(8,128)(2,1)}, bf16[512,1024]{1,0:T(8,128)(2,1)}, u32[]{:S(2)}, u32[]{:S(2)}) collective-permute-start(bf16[512,1024]{1,0:T(8,128)(2,1)} %constant_dynamic-slice_fusion.2), channel_id=1, source_target_pairs={{0,2},{2,0},{4,6},{6,4},{8,10},{10,8},{12,14},{14,12},{1,3},{3,1},... | collective-permute-start | bytes 3145736 | tf_op jit(solution)/shard_map/ppermute | solution.py:37
  19.7 14.8 %collective-permute-start.1 = (bf16[128,1024]{1,0:T(8,128)(2,1)}, bf16[128,1024]{1,0:T(8,128)(2,1)}, u32[]{:S(2)}, u32[]{:S(2)}) collective-permute-start(bf16[128,1024]{1,0:T(8,128)(2,1)} %collective-permute-done), channel_id=1, source_target_pairs={{0,1},{1,0},{2,3},{3,2},{4,5},{5,4},{6,7},{7,6},{8,9},{9,8},{10,11... | collective-permute-start | bytes 786440 | tf_op jit(solution)/shard_map/ppermute | solution.py:42
  53.3 10.5 %collective-permute-start.3 = (bf16[64,512]{1,0:T(8,128)(2,1)}, bf16[64,512]{1,0:T(8,128)(2,1)S(1)}, u32[]{:S(2)}, u32[]{:S(2)}) collective-permute-start(bf16[64,512]{1,0:T(8,128)(2,1)} %get-tuple-element.73), channel_id=1, source_target_pairs={{0,2},{1,3},{2,4},{3,5},{4,6},{5,7},{6,8},{7,9},{8,10},{9,11},{10,... | collective-permute-start | bytes 196616 | tf_op jit(solution)/shard_map/ppermute | solution.py:51
  53.3 10.5 %collective-permute-start.4 = (bf16[64,512]{1,0:T(8,128)(2,1)}, bf16[64,512]{1,0:T(8,128)(2,1)}, u32[]{:S(2)}, u32[]{:S(2)}) collective-permute-start(bf16[64,512]{1,0:T(8,128)(2,1)} %get-tuple-element.74), channel_id=1, source_target_pairs={{0,3},{1,2},{2,5},{3,4},{4,7},{5,6},{6,9},{7,8},{8,11},{9,10},{10,... | collective-permute-start | bytes 196616 | tf_op jit(solution)/shard_map/ppermute | solution.py:51
  65.6 14.6 %collective-permute-start.12 = (bf16[2,2,128,512]{3,2,1,0:T(8,128)(2,1)S(1)}, bf16[2,2,128,512]{3,2,1,0:T(8,128)(2,1)S(1)}, u32[]{:S(2)}, u32[]{:S(2)}) collective-permute-start(bf16[2,2,128,512]{3,2,1,0:T(8,128)(2,1)S(1)} %constant_dynamic-slice_fusion), channel_id=1, source_target_pairs={{0,2},{2,0},{4,6},{6,4},{8,10},{10,8},{12,14},{14,12},{1,3},{3,1},... | collective-permute-start | bytes 1572872 | tf_op jit(solution)/shard_map/ppermute | solution.py:37
  67.1 26.3 %collective-permute-start.15 = (bf16[512,1024]{1,0:T(8,128)(2,1)}, bf16[512,1024]{1,0:T(8,128)(2,1)S(1)}, u32[]{:S(2)}, u32[]{:S(2)}) collective-permute-start(bf16[512,1024]{1,0:T(8,128)(2,1)} %collective-permute-done.14), channel_id=1, source_target_pairs={{0,16},{16,0},{1,17},{17,1},{2,18},{18,2},{3,19},{19,3},{4,20},{20... | collective-permute-start | bytes 3145736 | tf_op jit(solution)/shard_map/ppermute | solution.py:507
  69.9 8.3 %collective-permute-start.6 = (bf16[1,2,64,512]{3,2,1,0:T(8,128)(2,1)S(1)}, bf16[1,2,64,512]{3,2,1,0:T(8,128)(2,1)S(1)}, u32[]{:S(2)}, u32[]{:S(2)}) collective-permute-start(bf16[1,2,64,512]{3,2,1,0:T(8,128)(2,1)S(1)} %maximum_bitcast_fusion.2), channel_id=1, source_target_pairs={{0,8},{2,10},{4,12},{6,14},{8,0},{10,2},{12,4},{14,6},{1,9},{3,11}... | collective-permute-start | bytes 393224 | tf_op jit(solution)/shard_map/ppermute | solution.py:37
  80.2 22.9 %collective-permute-start.13 = (bf16[2,2,128,512]{3,2,1,0:T(8,128)(2,1)S(1)}, bf16[2,2,128,512]{3,2,1,0:T(8,128)(2,1)S(1)}, u32[]{:S(2)}, u32[]{:S(2)}) collective-permute-start(bf16[2,2,128,512]{3,2,1,0:T(8,128)(2,1)S(1)} %collective-permute-done.12.got), channel_id=1, source_target_pairs={{0,16},{16,0},{1,17},{17,1},{2,18},{18,2},{3,19},{19,3},{4,20},{20... | collective-permute-start | bytes 1572872 | tf_op jit(solution)/shard_map/ppermute | solution.py:507
  84.7 18.3 %collective-permute-start.8 = (bf16[512,512]{1,0:T(8,128)(2,1)S(1)}, bf16[512,512]{1,0:T(8,128)(2,1)S(1)}, u32[]{:S(2)}, u32[]{:S(2)}) collective-permute-start(bf16[512,512]{1,0:T(8,128)(2,1)S(1)} %bitcast.82), channel_id=1, source_target_pairs={{0,1},{1,0},{2,3},{3,2},{4,5},{5,4},{6,7},{7,6},{8,9},{9,8},{10,11... | collective-permute-start | bytes 1572872 | tf_op jit(solution)/shard_map/ppermute | solution.py:42
  112.8 17.1 %collective-permute-start.17 = (bf16[2,128,1024]{2,1,0:T(8,128)(2,1)}, bf16[2,128,1024]{2,1,0:T(8,128)(2,1)}, u32[]{:S(2)}, u32[]{:S(2)}) collective-permute-start(bf16[2,128,1024]{2,1,0:T(8,128)(2,1)} %bitcast.28), channel_id=1, source_target_pairs={{0,4},{2,6},{4,0},{6,2},{8,12},{10,14},{12,8},{14,10},{1,5},{3,7},... | collective-permute-start | bytes 1572872 | tf_op jit(solution)/shard_map/ppermute | solution.py:37
  116.7 11.1 %collective-permute-start.20 = (f32[2,128]{1,0:T(2,128)S(1)}, f32[2,128]{1,0:T(2,128)S(1)}, u32[]{:S(2)}, u32[]{:S(2)}) collective-permute-start(f32[2,128]{1,0:T(2,128)S(1)} %slice.154), channel_id=1, source_target_pairs={{0,4},{2,6},{4,0},{6,2},{8,12},{10,14},{12,8},{14,10},{1,5},{3,7},... | collective-permute-start | bytes 3080 | tf_op jit(solution)/shard_map/ppermute | solution.py:37
  131.2 13.8 %collective-permute-start.18 = (bf16[1,128,1024]{2,1,0:T(8,128)(2,1)S(1)}, bf16[1,128,1024]{2,1,0:T(8,128)(2,1)S(1)}, u32[]{:S(2)}, u32[]{:S(2)}) collective-permute-start(bf16[1,128,1024]{2,1,0:T(8,128)(2,1)S(1)} %get-tuple-element.71), channel_id=1, source_target_pairs={{0,8},{2,10},{4,12},{6,14},{8,0},{10,2},{12,4},{14,6},{1,9},{3,11}... | collective-permute-start | bytes 786440 | tf_op jit(solution)/shard_map/ppermute | solution.py:37
  145.4 15.6 %collective-permute-start.22 = (bf16[1,128,1152]{2,1,0:T(8,128)(2,1)S(1)}, bf16[1,128,1152]{2,1,0:T(8,128)(2,1)S(1)}, u32[]{:S(2)}, u32[]{:S(2)}) collective-permute-start(bf16[1,128,1152]{2,1,0:T(8,128)(2,1)S(1)} %bitcast.84), channel_id=1, source_target_pairs={{0,8},{2,10},{4,12},{6,14},{8,0},{10,2},{12,4},{14,6},{1,9},{3,11}... | collective-permute-start | bytes 884744 | tf_op jit(solution)/shard_map/ppermute | solution.py:37
  161.0 15.3 %collective-permute-start.23 = (bf16[2,128,1152]{2,1,0:T(8,128)(2,1)S(1)}, bf16[2,128,1152]{2,1,0:T(8,128)(2,1)S(1)}, u32[]{:S(2)}, u32[]{:S(2)}) collective-permute-start(bf16[2,128,1152]{2,1,0:T(8,128)(2,1)S(1)} %pad_maximum_fusion.3), channel_id=1, source_target_pairs={{0,4},{2,6},{4,0},{6,2},{8,12},{10,14},{12,8},{14,10},{1,5},{3,7},... | collective-permute-start | bytes 1769480 | tf_op jit(solution)/shard_map/ppermute | solution.py:37
  188.3 8.4 %collective-permute-start.26 = (bf16[2,2,64,512]{3,2,1,0:T(8,128)(2,1)S(1)}, bf16[2,2,64,512]{3,2,1,0:T(8,128)(2,1)S(1)}, u32[]{:S(2)}, u32[]{:S(2)}) collective-permute-start(bf16[2,2,64,512]{3,2,1,0:T(8,128)(2,1)S(1)} %bitcast.97), channel_id=1, source_target_pairs={{0,4},{2,6},{4,0},{6,2},{8,12},{10,14},{12,8},{14,10},{1,5},{3,7},... | collective-permute-start | bytes 786440 | tf_op jit(solution)/shard_map/ppermute | solution.py:37
  196.8 8.2 %collective-permute-start.27 = (bf16[1,2,64,512]{3,2,1,0:T(8,128)(2,1)S(1)}, bf16[1,2,64,512]{3,2,1,0:T(8,128)(2,1)S(1)}, u32[]{:S(2)}, u32[]{:S(2)}) collective-permute-start(bf16[1,2,64,512]{3,2,1,0:T(8,128)(2,1)S(1)} %slice.192), channel_id=1, source_target_pairs={{0,8},{2,10},{4,12},{6,14},{8,0},{10,2},{12,4},{14,6},{1,9},{3,11}... | collective-permute-start | bytes 393224 | tf_op jit(solution)/shard_map/ppermute | solution.py:37
  224.1 14.2 %collective-permute-start.38 = (bf16[4,3,128,128]{3,2,1,0:T(8,128)(2,1)S(1)}, bf16[4,3,128,128]{3,2,1,0:T(8,128)(2,1)S(1)}, u32[]{:S(2)}, u32[]{:S(2)}) collective-permute-start(bf16[4,3,128,128]{3,2,1,0:T(8,128)(2,1)S(1)} %get-tuple-element.56), channel_id=1, source_target_pairs={{0,2},{2,0},{4,6},{6,4},{8,10},{10,8},{12,14},{14,12},{1,3},{3,1},... | collective-permute-start | bytes 1179656 | tf_op jit(solution)/shard_map/ppermute | solution.py:37
  228.3 28.3 %collective-permute-start.41 = (bf16[4,64,1024]{2,1,0:T(8,128)(2,1)S(1)}, bf16[4,64,1024]{2,1,0:T(8,128)(2,1)S(1)}, u32[]{:S(2)}, u32[]{:S(2)}) collective-permute-start(bf16[4,64,1024]{2,1,0:T(8,128)(2,1)S(1)} %get-tuple-element.58), channel_id=1, source_target_pairs={{0,2},{2,0},{4,6},{6,4},{8,10},{10,8},{12,14},{14,12},{1,3},{3,1},... | collective-permute-start | bytes 1572872 | tf_op jit(solution)/shard_map/ppermute | solution.py:37
  229.0 26.9 %collective-permute-start.35 = (bf16[4,3,128,128]{3,2,1,0:T(8,128)(2,1)S(1)}, bf16[4,3,128,128]{3,2,1,0:T(8,128)(2,1)S(1)}, u32[]{:S(2)}, u32[]{:S(2)}) collective-permute-start(bf16[4,3,128,128]{3,2,1,0:T(8,128)(2,1)S(1)} %get-tuple-element.54), channel_id=1, source_target_pairs={{0,2},{2,0},{4,6},{6,4},{8,10},{10,8},{12,14},{14,12},{1,3},{3,1},... | collective-permute-start | bytes 1179656 | tf_op jit(solution)/shard_map/ppermute | solution.py:37
  237.6 33.1 %collective-permute-start.32 = (bf16[4,3,128,256]{3,2,1,0:T(8,128)(2,1)S(1)}, bf16[4,3,128,256]{3,2,1,0:T(8,128)(2,1)S(1)}, u32[]{:S(2)}, u32[]{:S(2)}) collective-permute-start(bf16[4,3,128,256]{3,2,1,0:T(8,128)(2,1)S(1)} %get-tuple-element.52), channel_id=1, source_target_pairs={{0,2},{2,0},{4,6},{6,4},{8,10},{10,8},{12,14},{14,12},{1,3},{3,1},... | collective-permute-start | bytes 2359304 | tf_op jit(solution)/shard_map/ppermute | solution.py:37
  238.5 19.9 %collective-permute-start.39 = (bf16[2,3,128,128]{3,2,1,0:T(8,128)(2,1)S(1)}, bf16[2,3,128,128]{3,2,1,0:T(8,128)(2,1)S(1)}, u32[]{:S(2)}, u32[]{:S(2)}) collective-permute-start(bf16[2,3,128,128]{3,2,1,0:T(8,128)(2,1)S(1)} %slice.205), channel_id=1, source_target_pairs={{0,4},{2,6},{4,0},{6,2},{8,12},{10,14},{12,8},{14,10},{1,5},{3,7},... | collective-permute-start | bytes 589832 | tf_op jit(solution)/shard_map/ppermute | solution.py:37
  256.0 8.9 %collective-permute-start.36 = (bf16[2,3,128,128]{3,2,1,0:T(8,128)(2,1)S(1)}, bf16[2,3,128,128]{3,2,1,0:T(8,128)(2,1)S(1)}, u32[]{:S(2)}, u32[]{:S(2)}) collective-permute-start(bf16[2,3,128,128]{3,2,1,0:T(8,128)(2,1)S(1)} %slice.201), channel_id=1, source_target_pairs={{0,4},{2,6},{4,0},{6,2},{8,12},{10,14},{12,8},{14,10},{1,5},{3,7},... | collective-permute-start | bytes 589832 | tf_op jit(solution)/shard_map/ppermute | solution.py:37
  256.8 15.0 %collective-permute-start.42 = (bf16[2,64,1024]{2,1,0:T(8,128)(2,1)S(1)}, bf16[2,64,1024]{2,1,0:T(8,128)(2,1)S(1)}, u32[]{:S(2)}, u32[]{:S(2)}) collective-permute-start(bf16[2,64,1024]{2,1,0:T(8,128)(2,1)S(1)} %slice.209), channel_id=1, source_target_pairs={{0,4},{2,6},{4,0},{6,2},{8,12},{10,14},{12,8},{14,10},{1,5},{3,7},... | collective-permute-start | bytes 786440 | tf_op jit(solution)/shard_map/ppermute | solution.py:37
  258.5 7.9 %collective-permute-start.40 = (bf16[1,3,128,128]{3,2,1,0:T(8,128)(2,1)S(1)}, bf16[1,3,128,128]{3,2,1,0:T(8,128)(2,1)S(1)}, u32[]{:S(2)}, u32[]{:S(2)}) collective-permute-start(bf16[1,3,128,128]{3,2,1,0:T(8,128)(2,1)S(1)} %slice.207), channel_id=1, source_target_pairs={{0,8},{2,10},{4,12},{6,14},{8,0},{10,2},{12,4},{14,6},{1,9},{3,11}... | collective-permute-start | bytes 294920 | tf_op jit(solution)/shard_map/ppermute | solution.py:37
  265.0 6.7 %collective-permute-start.37 = (bf16[1,3,128,128]{3,2,1,0:T(8,128)(2,1)S(1)}, bf16[1,3,128,128]{3,2,1,0:T(8,128)(2,1)S(1)}, u32[]{:S(2)}, u32[]{:S(2)}) collective-permute-start(bf16[1,3,128,128]{3,2,1,0:T(8,128)(2,1)S(1)} %slice.203), channel_id=1, source_target_pairs={{0,8},{2,10},{4,12},{6,14},{8,0},{10,2},{12,4},{14,6},{1,9},{3,11}... | collective-permute-start | bytes 294920 | tf_op jit(solution)/shard_map/ppermute | solution.py:37
  271.0 12.0 %collective-permute-start.33 = (bf16[2,3,128,256]{3,2,1,0:T(8,128)(2,1)S(1)}, bf16[2,3,128,256]{3,2,1,0:T(8,128)(2,1)S(1)}, u32[]{:S(2)}, u32[]{:S(2)}) collective-permute-start(bf16[2,3,128,256]{3,2,1,0:T(8,128)(2,1)S(1)} %slice.197), channel_id=1, source_target_pairs={{0,4},{2,6},{4,0},{6,2},{8,12},{10,14},{12,8},{14,10},{1,5},{3,7},... | collective-permute-start | bytes 1179656 | tf_op jit(solution)/shard_map/ppermute | solution.py:37
  271.9 12.6 %collective-permute-start.43 = (bf16[1,64,1024]{2,1,0:T(8,128)(2,1)S(1)}, bf16[1,64,1024]{2,1,0:T(8,128)(2,1)S(1)}, u32[]{:S(2)}, u32[]{:S(2)}) collective-permute-start(bf16[1,64,1024]{2,1,0:T(8,128)(2,1)S(1)} %slice.211), channel_id=1, source_target_pairs={{0,8},{2,10},{4,12},{6,14},{8,0},{10,2},{12,4},{14,6},{1,9},{3,11}... | collective-permute-start | bytes 393224 | tf_op jit(solution)/shard_map/ppermute | solution.py:37
  283.2 10.1 %collective-permute-start.34 = (bf16[1,3,128,256]{3,2,1,0:T(8,128)(2,1)S(1)}, bf16[1,3,128,256]{3,2,1,0:T(8,128)(2,1)S(1)}, u32[]{:S(2)}, u32[]{:S(2)}) collective-permute-start(bf16[1,3,128,256]{3,2,1,0:T(8,128)(2,1)S(1)} %slice.199), channel_id=1, source_target_pairs={{0,8},{2,10},{4,12},{6,14},{8,0},{10,2},{12,4},{14,6},{1,9},{3,11}... | collective-permute-start | bytes 589832 | tf_op jit(solution)/shard_map/ppermute | solution.py:37
  (32 other events, 359.2 us)

commit v3 on v2

--- a/solution.py
+++ b/solution.py
@@ -93,13 +93,23 @@
         low = (low[:half].astype(F32) + got.astype(F32)).astype(BF)
 
 
-def scatter_pair(even, odd):
-    total = even.astype(F32) + swap_tm(odd, 1).astype(F32)
-    return scatter_halving(total, tm_bits()[1:], BF)
-
-
-def halving_order(n):
-    return offsets([1 << i for i in range(1, n.bit_length() - 1)])
+def scatter_chunks(chunks, lead):
+    sums = [lower for lower, _, _ in chunks]
+    sends = [upper for _, upper, _ in chunks]
+    for stage in range(len(chunks[0][2])):
+        for i, (_, _, masks) in enumerate(chunks):
+            total = sums[i].astype(F32) + swap_tm(sends[i], masks[stage]).astype(F32)
+            if total.shape[0] == 1:
+                sums[i] = total[0]
+                continue
+            low = total.astype(BF)
+            if i == lead:
+                done = low
+            if i + 1 == len(chunks):
+                low, done = lax.optimization_barrier((low, done))
+            half = low.shape[0] // 2
+            sums[i], sends[i] = low[:half], low[half:]
+    return sums
 
 
 def head_mask(shape, head):
@@ -198,24 +208,25 @@
     )(at, x_roll, w_t, w_t, w_t, weight_out)
 
 
-def out_grad_kernel(n, at, d_ref, wo_ref, pa_ref, d_attn, even, odd, turned):
+def out_grad_kernel(masks, at, d_ref, wo_ref, pa_ref, d_attn, even, odd, turned):
     me = at[2]
     block = even.shape[1]
     d_ext = d_ref[...]
     d_attn[...] = (dot_nt(d_ext, wo_ref[...]) * (1.0 / POOL)).astype(BF)
     turned[...] = pa_ref[...].T
-    for bit, ref in enumerate((even, odd)):
-        for j, k in enumerate(halving_order(n)):
+    for bit, ref in ((0, even), (masks[0], odd)):
+        for j, k in enumerate(offsets(masks[1:])):
             start = pl.multiple_of((me ^ (k | bit)) * block, block)
             ref[j] = dot(turned[pl.ds(start, block), :], d_ext).astype(BF)
 
 
-def out_grad(d_ext, weight_out, pooled_attn, at, n):
+def out_grad(d_ext, weight_out, pooled_attn, at, masks):
     heads_w, width = weight_out.shape
+    n = 2 ** len(masks)
     blocks = jax.ShapeDtypeStruct((n // 2, heads_w // n, width), BF)
     whole = pl.BlockSpec(memory_space=pltpu.VMEM)
     return pl.pallas_call(
-        functools.partial(out_grad_kernel, n),
+        functools.partial(out_grad_kernel, masks),
         in_specs=[pl.BlockSpec(memory_space=pltpu.SMEM), whole, whole, whole],
         out_specs=[whole] * 3,
         out_shape=[jax.ShapeDtypeStruct(pooled_attn.shape, BF), blocks, blocks],
@@ -225,7 +236,7 @@
     )(at, d_ext, weight_out, pooled_attn)
 
 
-def backward_kernel(n, at, turned, qkv, probs, d_ref, even, odd, grads):
+def backward_kernel(masks, at, turned, qkv, probs, d_ref, even, odd, grads):
     shift, me = at[0], at[2]
     rows = turned.shape[1]
     cols = d_ref.shape[1]
@@ -253,23 +264,24 @@
         for i in range(3):
             grads[span, i * cols : (i + 1) * cols] = sums[i].astype(BF)
     d_all = grads[...]
-    for bit, ref in enumerate((even, odd)):
-        for j, k in enumerate(halving_order(n)):
+    for bit, ref in ((0, even), (masks[0], odd)):
+        for j, k in enumerate(offsets(masks[1:])):
             start = pl.multiple_of((me ^ (k | bit)) * block, block)
             term = dot(turned[pl.ds(start, block), :], d_all).astype(BF)
             for i in range(3):
                 ref[j, i] = term[:, i * cols : (i + 1) * cols]
 
 
-def encoder_backward(turned, qkv, probs, d_attn, at, n, first, count):
+def encoder_backward(turned, qkv, probs, d_attn, at, masks, first, count):
     width, rows = turned.shape
+    n = 2 ** len(masks)
     cols = 2 * HEAD
     windows = rows // WINDOW
     block = width // n
     out = pl.BlockSpec((n // 2, 3, block, cols), lambda p, at: (0, 0, 0, p))
     shape = jax.ShapeDtypeStruct((n // 2, 3, block, cols * count), BF)
     return pl.pallas_call(
-        functools.partial(backward_kernel, n),
+        functools.partial(backward_kernel, masks),
         grid_spec=pltpu.PrefetchScalarGridSpec(
             num_scalar_prefetch=1,
             grid=(count,),
@@ -487,7 +499,13 @@
     part = lax.dynamic_slice_in_dim(frames, core * (WINDOW // 2), WINDOW // 2, 0)
     mine = to_tm(part, -1, False)
     w_t = jnp.transpose(weight_qkv, (1, 2, 0)).reshape(-1, width)
-    proj_in, proj_kv, w_t = lax.optimization_barrier((proj_in, proj_kv, w_t))
+    group = lax.axis_index("groups")
+    two_groups = lax.axis_size("groups") == 2
+    if not two_groups:
+        group = group * 0
+    proj_kv, part = lax.optimization_barrier((proj_kv, part))
+    kv_near = swap_tm(lax.dynamic_slice_in_dim(proj_kv, group * kv_half, kv_half, 1), SPLIT)
+    proj_in, w_t = lax.optimization_barrier((proj_in, w_t))
 
     masks = group_bits()
     order = offsets(masks)
@@ -501,32 +519,6 @@
         ]
         pair = jnp.stack(pair)
         blocks.append(swap_tm(pair, k) if k else pair)
-    here = jnp.stack(blocks)
-    group = lax.axis_index("groups")
-    if lax.axis_size("groups") == 2:
-        swap_groups = lambda block: lax.ppermute(block, "groups", [(0, 1), (1, 0)])
-        kv_near = swap_tm(lax.dynamic_slice_in_dim(proj_kv, group * kv_half, kv_half, 1), SPLIT)
-        kv_far = swap_groups(kv_near)
-        in_near = swap_tm(
-            lax.dynamic_slice_in_dim(here, group * (count // 2), count // 2, 0), SPLIT
-        )
-        in_far = swap_groups(in_near)
-    else:
-        group = group * 0
-        kv_near = swap_tm(proj_kv[:, :kv_half], SPLIT)
-        kv_far = swap_tm(proj_kv[:, kv_half:], SPLIT)
-        in_near = swap_tm(here[: count // 2], SPLIT)
-        in_far = swap_tm(here[count // 2 :], SPLIT)
-    kva, kvb = proj_kv, jnp.stack([kv_near, kv_far])
-    at_rows = order
-    if width // n % LANES:
-        stacked = jnp.concatenate([here, in_near[:, ::-1], in_far[:, ::-1]])
-        source = jnp.arange(n, dtype=jnp.int32) ^ me
-        found = source[:, None] == jnp.array(members, jnp.int32)[None, :]
-        place = jnp.sum(found * jnp.arange(n, dtype=jnp.int32)[None, :], axis=1)
-        stacked = jnp.take(stacked, place, axis=0)
-        here, in_near, in_far = jnp.split(stacked, [count, count + count // 2])
-        at_rows = None
 
     other = swap_mp(mine)
     halo = jnp.where(
@@ -538,6 +530,12 @@
     normed, qkv, probs, pooled_attn, out_part = encoder_forward(
         x_roll, w_t, weight_out, at, ext_tok
     )
+    out_part, kv_near = lax.optimization_barrier((out_part, kv_near))
+    swap_groups = lambda block: lax.ppermute(block, "groups", [(0, 1), (1, 0)])
+    if two_groups:
+        kv_far = swap_groups(kv_near)
+    else:
+        kv_far = swap_tm(proj_kv[:, kv_half:], SPLIT)
     turned = normed.T
     route, norm_gain, d_kv, pooled_attn = lax.optimization_barrier(
         (route, norm_gain, d_kv, pooled_attn)
@@ -564,6 +562,24 @@
     from_core = swap_mp(low_other[:own_tok])
     tail_a = to_tm(low_own[own_tok:], 1, False)
     tail_b = to_tm(low_other[own_tok:], 1, True)
+    tail_a, tail_b, from_core, blocks = lax.optimization_barrier(
+        (tail_a, tail_b, from_core, blocks)
+    )
+    here = jnp.stack(blocks)
+    in_near = swap_tm(
+        lax.dynamic_slice_in_dim(here, group * (count // 2), count // 2, 0), SPLIT
+    )
+    in_far = swap_groups(in_near) if two_groups else swap_tm(here[count // 2 :], SPLIT)
+    kva, kvb = proj_kv, jnp.stack([kv_near, kv_far])
+    at_rows = order
+    if width // n % LANES:
+        stacked = jnp.concatenate([here, in_near[:, ::-1], in_far[:, ::-1]])
+        source = jnp.arange(n, dtype=jnp.int32) ^ me
+        found = source[:, None] == jnp.array(members, jnp.int32)[None, :]
+        place = jnp.sum(found * jnp.arange(n, dtype=jnp.int32)[None, :], axis=1)
+        stacked = jnp.take(stacked, place, axis=0)
+        here, in_near, in_far = jnp.split(stacked, [count, count + count // 2])
+        at_rows = None
     own_pool = (
         jnp.arange(rows, dtype=jnp.int32)[None, :] // POOL
         == jnp.arange(own_tok, dtype=jnp.int32)[:, None]
@@ -619,13 +635,17 @@
     d_ext = jnp.where(
         core == 0, jnp.concatenate([left, right], 1), jnp.concatenate([right, left], 1)
     )
-    d_attn, out_even, out_odd = out_grad(d_ext, weight_out, pooled_attn, at, n)
-    grad_out = scatter_pair(out_even, out_odd)
-    chunks, first = [], 0
-    for pairs in (2, 1, 1):
-        even, odd = encoder_backward(turned, qkv, probs, d_attn, at, n, first, pairs)
-        chunks.append(scatter_pair(even, odd))
-        first += pairs
+    bits = tm_bits()
+    crossed = [bits[1], bits[0]] + bits[2:]
+    d_attn, out_even, out_odd = out_grad(d_ext, weight_out, pooled_attn, at, bits)
+    chunks = []
+    for pair, path in enumerate((bits, crossed, bits, bits)):
+        even, odd = encoder_backward(turned, qkv, probs, d_attn, at, path, pair, 1)
+        even, odd, at = lax.optimization_barrier((even, odd, at))
+        chunks.append((even, odd, path))
+    chunks.insert(2, (out_even, out_odd, bits))
+    chunks = scatter_chunks(chunks, 2)
+    grad_out = chunks.pop(2)
     grad_qkv = jnp.transpose(jnp.concatenate(chunks, axis=-1), (1, 0, 2))
     return kv, grad_qkv, grad_out
 

time: 295 us -> 278 us (0.942)
  waiting for transfers between devices: 163 us -> 156 us
  starting transfers between devices: 51.3 us -> 44.9 us
    ppermute x29 -> x32, waiting for transfers between devices: 137 us -> 130 us  [swap_tm(): return lax.ppermute(block, 'tm', [(i, i ^ mask) for i in range(n)])]
    ppermute x5, waiting for transfers between devices: 2.6 us -> 8.77 us  [to_tm(): return lax.ppermute(block, ('tm', 'mp'), pairs)]
    ppermute x2, waiting for transfers between devices: 14.7 us -> 9.22 us  [on_device(): swap_groups = lambda block: lax.ppermute(block, 'groups', [(0, 1), (1, 0)])]
    ppermute x5, starting transfers between devices: 15.2 us -> 11.7 us  [to_tm(): return lax.ppermute(block, ('tm', 'mp'), pairs)]
    ppermute x29 -> x32, starting transfers between devices: 31.7 us -> 29.2 us  [swap_tm(): return lax.ppermute(block, 'tm', [(i, i ^ mask) for i in range(n)])]
    pallas_call x4 -> x5, Pallas kernels: 13.4 us -> 12.6 us  [the longest x4 11.1 us: encoder_backward(): pl.pallas_call(functools.partial(backward_kernel, masks), grid_spec=pltpu...]
  transfers between devices with their start and end apart: 44 -> 47, of which waited for: 27 -> 27; matrix products, arithmetic and copies ran while one was open for 10% -> 9% of each run, Pallas kernels for 7% -> 7%
where the time goes in v3:
time: 278 us; the launch traced here: 277 us
  waiting for transfers between devices  156 us (56%)
  starting transfers between devices  44.9 us (16%)
  Pallas kernels  37.3 us (13%)
  local copies, waits for them, and re-layouts  18.5 us (7%)
  other arithmetic  14.1 us (5%)
  between operations  4.11 us (1%)
    ppermute x32, waiting for transfers between devices, swap_tm(): return lax.ppermute(block, 'tm', [(i, i ^ mask) for i in range(n)])  130 us
    ppermute x32, starting transfers between devices, swap_tm(): return lax.ppermute(block, 'tm', [(i, i ^ mask) for i in range(n)])  29.2 us
    pallas_call x1, Pallas kernels, encoder_forward(): pl.pallas_call(forward_kernel, grid_spec=pltpu.PrefetchScalarGridSpec(num...  11.8 us
    ppermute x5, starting transfers between devices, to_tm(): return lax.ppermute(block, ('tm', 'mp'), pairs)  11.7 us
    pallas_call x4, Pallas kernels, encoder_backward(): pl.pallas_call(functools.partial(backward_kernel, masks), grid_spec=pltpu...  11.1 us
    ppermute x2, waiting for transfers between devices, on_device(): swap_groups = lambda block: lax.ppermute(block, 'groups', [(0, 1), (1, 0)])  9.22 us
    ppermute x5, waiting for transfers between devices, to_tm(): return lax.ppermute(block, ('tm', 'mp'), pairs)  8.77 us
    ppermute x8, waiting for transfers between devices, swap_mp(): return lax.ppermute(block, 'mp', [(i, n - 1 - i) for i in range(n)])  8.28 us
  transfers between devices with their start and end apart: 47, of which 27 were waited for; matrix products, arithmetic and copies ran while one was open for 9% of the time, Pallas kernels for 7%

profile of v3, /device:TPU:0, one launch (start us, length us, event | category | flops | bytes accessed | tf_op | source)
XLA Modules:
  0.0 276.9 jit_solution(10857678514060092177)
XLA Ops:
  2.4 6.0 %collective-permute-start = (bf16[128,1024]{1,0:T(8,128)(2,1)}, bf16[128,1024]{1,0:T(8,128)(2,1)}, u32[]{:S(2)}, u32[]{:S(2)}) collective-permute-start(bf16[128,1024]{1,0:T(8,128)(2,1)} %constant_dynamic-slice_fusion.4), channel_id=1, source_target_pairs={{0,14},{1,15},{2,0},{3,1},{4,2},{5,3},{6,4},{7,5},{8,6},{9,7},{10,... | collective-permute-start | bytes 786440 | tf_op jit(solution)/shard_map/ppermute | solution.py:51
  9.8 4.8 %copy.14 = bf16[3,512,1024]{2,1,0:T(8,128)(2,1)} copy(bf16[3,512,1024]{1,2,0:T(8,128)(2,1)} %bitcast.95) | data formatting | bytes 6291456 | tf_op jit(solution)/shard_map/transpose | solution.py:501
  17.8 2.8 %collective-permute-start.8 = (bf16[2,128,512]{2,1,0:T(8,128)(2,1)}, bf16[2,128,512]{2,1,0:T(8,128)(2,1)}, u32[]{:S(2)}, u32[]{:S(2)}) collective-permute-start(bf16[2,128,512]{2,1,0:T(8,128)(2,1)} %pad_maximum_fusion.8), channel_id=1, source_target_pairs={{0,12},{2,14},{4,8},{6,10},{8,4},{10,6},{12,0},{14,2},{1,13},{3,15... | collective-permute-start | bytes 786440 | tf_op jit(solution)/shard_map/ppermute | solution.py:37
  27.4 11.8 %encoder_forward.1 = (bf16[512,1024]{1,0:T(8,128)(2,1)S(1)}, bf16[3,512,512]{2,1,0:T(8,128)(2,1)S(1)}, bf16[4,2,2,256,256]{4,3,2,1,0:T(8,128)(2,1)}, bf16[192,512]{1,0:T(8,128)(2,1)S(1)}, f32[192,1024]{1,0:T(8,128)S(1)}) custom-call(s32[5]{0:T(128)S(1)} %stack.85.at, bf16[512,1024]{1,0:T(8,128)(2,1)S(1)} %fusion.x_ref, bf16[1536,1024]{1,0:T(8,128)(2,1)} %bitcast.92, ...), custom_call_target="tpu_custom_call" | custom-call | tf_op jit(solution)/shard_map/encoder_forward/pallas_call | solution.py:178
  53.7 3.0 %collective-permute-done.9 = bf16[64,512]{1,0:T(8,128)(2,1)S(1)} collective-permute-done((bf16[64,512]{1,0:T(8,128)(2,1)S(1)}, bf16[64,512]{1,0:T(8,128)(2,1)S(1)}, u32[]{:S(2)}, u32[]{:S(2)}) %collective-permute-start.9) | collective-permute-done | bytes 65568 | tf_op jit(solution)/shard_map/ppermute | solution.py:37
  56.9 6.0 %collective-permute-done.10 = bf16[1,2,64,512]{3,2,1,0:T(8,128)(2,1)S(1)} collective-permute-done((bf16[1,2,64,512]{3,2,1,0:T(8,128)(2,1)S(1)}, bf16[1,2,64,512]{3,2,1,0:T(8,128)(2,1)S(1)}, u32[]{:S(2)}, u32[]{:S(2)}) %collective-permute-start.10) | collective-permute-done | bytes 131104 | tf_op jit(solution)/shard_map/ppermute | solution.py:37
  63.0 7.1 %collective-permute-done.11 = bf16[2,2,64,512]{3,2,1,0:T(8,128)(2,1)S(1)} collective-permute-done((bf16[2,2,64,512]{3,2,1,0:T(8,128)(2,1)S(1)}, bf16[2,2,64,512]{3,2,1,0:T(8,128)(2,1)S(1)}, u32[]{:S(2)}, u32[]{:S(2)}) %collective-permute-start.11) | collective-permute-done | bytes 262176 | tf_op jit(solution)/shard_map/ppermute | solution.py:37
  72.7 2.7 pad_maximum_fusion.kvb
  75.4 9.2 %collective-permute-done.14.other = bf16[2,2,128,512]{3,2,1,0:T(8,128)(2,1)S(1)} collective-permute-done((bf16[2,2,128,512]{3,2,1,0:T(8,128)(2,1)S(1)}, bf16[2,2,128,512]{3,2,1,0:T(8,128)(2,1)S(1)}, u32[]{:S(2)}, u32[]{:S(2)}) %collective-permute-start.14) | collective-permute-done | bytes 524320 | tf_op jit(solution)/shard_map/ppermute | solution.py:534
  84.6 5.7 %lift.1 = (f32[512,1024]{1,0:T(8,128)}, bf16[512,1024]{1,0:T(8,128)(2,1)S(1)}, bf16[512,1024]{1,0:T(8,128)(2,1)S(1)}) custom-call(s32[5]{0:T(128)S(1)} %stack.85.at, bf16[512,512]{1,0:T(8,128)(2,1)S(1)} %bitcast.85, bf16[512,512]{1,0:T(8,128)(2,1)S(1)} %collective-permute-done.12.tb, bf16[4,2,128,512]{3,2,1,0:T(8,128)(2,1)S(1)} %pad_maximum_fusion.2.here, ...), custom_call_target="tpu_custom_call" | custom-call | tf_op jit(solution)/shard_map/lift/pallas_call | solution.py:378
  90.4 2.6 collective-permute-done.16
  98.0 10.6 %collective-permute-done.20 = f32[2,128]{1,0:T(2,128)S(1)} collective-permute-done((f32[2,128]{1,0:T(2,128)S(1)}, f32[2,128]{1,0:T(2,128)S(1)}, u32[]{:S(2)}, u32[]{:S(2)}) %collective-permute-start.20) | collective-permute-done | bytes 1056 | tf_op jit(solution)/shard_map/ppermute | solution.py:37
  110.0 3.0 %collective-permute-start.18 = (bf16[1,128,1024]{2,1,0:T(8,128)(2,1)S(1)}, bf16[1,128,1024]{2,1,0:T(8,128)(2,1)S(1)}, u32[]{:S(2)}, u32[]{:S(2)}) collective-permute-start(bf16[1,128,1024]{2,1,0:T(8,128)(2,1)S(1)} %get-tuple-element.119), channel_id=1, source_target_pairs={{0,8},{2,10},{4,12},{6,14},{8,0},{10,2},{12,4},{14,6},{1,9},{3,11}... | collective-permute-start | bytes 786440 | tf_op jit(solution)/shard_map/ppermute | solution.py:37
  113.2 10.9 %collective-permute-done.18 = bf16[1,128,1024]{2,1,0:T(8,128)(2,1)S(1)} collective-permute-done((bf16[1,128,1024]{2,1,0:T(8,128)(2,1)S(1)}, bf16[1,128,1024]{2,1,0:T(8,128)(2,1)S(1)}, u32[]{:S(2)}, u32[]{:S(2)}) %collective-permute-start.18) | collective-permute-done | bytes 262176 | tf_op jit(solution)/shard_map/ppermute | solution.py:37
  124.6 14.6 %collective-permute-done.22 = bf16[1,128,1152]{2,1,0:T(8,128)(2,1)S(1)} collective-permute-done((bf16[1,128,1152]{2,1,0:T(8,128)(2,1)S(1)}, bf16[1,128,1152]{2,1,0:T(8,128)(2,1)S(1)}, u32[]{:S(2)}, u32[]{:S(2)}) %collective-permute-start.22) | collective-permute-done | bytes 294944 | tf_op jit(solution)/shard_map/ppermute | solution.py:37
  139.3 15.2 %collective-permute-done.23 = bf16[2,128,1152]{2,1,0:T(8,128)(2,1)S(1)} collective-permute-done((bf16[2,128,1152]{2,1,0:T(8,128)(2,1)S(1)}, bf16[2,128,1152]{2,1,0:T(8,128)(2,1)S(1)}, u32[]{:S(2)}, u32[]{:S(2)}) %collective-permute-start.23) | collective-permute-done | bytes 589856 | tf_op jit(solution)/shard_map/ppermute | solution.py:37
  154.8 2.8 %collective-permute-done.24.cb = bf16[512,1152]{1,0:T(8,128)(2,1)S(1)} collective-permute-done((bf16[512,1152]{1,0:T(8,128)(2,1)S(1)}, bf16[512,1152]{1,0:T(8,128)(2,1)S(1)}, u32[]{:S(2)}, u32[]{:S(2)}) %collective-permute-start.24) | collective-permute-done | bytes 1179680 | tf_op jit(solution)/shard_map/ppermute | solution.py:42
  157.6 6.8 %lower.1 = (bf16[512,512]{1,0:T(8,128)(2,1)S(1)}, bf16[512,512]{1,0:T(8,128)(2,1)S(1)}) custom-call(s32[5]{0:T(128)S(1)} %stack.85.at, bf16[512,1152]{1,0:T(8,128)(2,1)S(1)} %bitcast.83, bf16[512,1152]{1,0:T(8,128)(2,1)S(1)} %collective-permute-done.24.cb, bf16[4,2,128,512]{3,2,1,0:T(8,128)(2,1)S(1)} %pad_maximum_fusion.2.here, ...), custom_call_target="tpu_custom_call" | custom-call | tf_op jit(solution)/shard_map/lower/pallas_call | solution.py:474
  166.9 8.1 %collective-permute-done.26 = bf16[2,2,64,512]{3,2,1,0:T(8,128)(2,1)S(1)} collective-permute-done((bf16[2,2,64,512]{3,2,1,0:T(8,128)(2,1)S(1)}, bf16[2,2,64,512]{3,2,1,0:T(8,128)(2,1)S(1)}, u32[]{:S(2)}, u32[]{:S(2)}) %collective-permute-start.26) | collective-permute-done | bytes 262176 | tf_op jit(solution)/shard_map/ppermute | solution.py:37
  175.8 7.5 %collective-permute-done.27 = bf16[1,2,64,512]{3,2,1,0:T(8,128)(2,1)S(1)} collective-permute-done((bf16[1,2,64,512]{3,2,1,0:T(8,128)(2,1)S(1)}, bf16[1,2,64,512]{3,2,1,0:T(8,128)(2,1)S(1)}, u32[]{:S(2)}, u32[]{:S(2)}) %collective-permute-start.27) | collective-permute-done | bytes 131104 | tf_op jit(solution)/shard_map/ppermute | solution.py:37
  184.7 3.0 %collective-permute-done.28 = bf16[64,512]{1,0:T(8,128)(2,1)S(1)} collective-permute-done((bf16[64,512]{1,0:T(8,128)(2,1)S(1)}, bf16[64,512]{1,0:T(8,128)(2,1)S(1)}, u32[]{:S(2)}, u32[]{:S(2)}) %collective-permute-start.28) | collective-permute-done | bytes 65568 | tf_op jit(solution)/shard_map/ppermute | solution.py:37
  189.6 3.2 %collective-permute-start.31 = (bf16[64,512]{1,0:T(8,128)(2,1)S(1)}, bf16[64,512]{1,0:T(8,128)(2,1)S(1)}, u32[]{:S(2)}, u32[]{:S(2)}) collective-permute-start(bf16[64,512]{1,0:T(8,128)(2,1)S(1)} %slice.211), channel_id=1, source_target_pairs={{0,15},{1,14},{2,1},{3,0},{4,3},{5,2},{6,5},{7,4},{8,7},{9,6},{10,... | collective-permute-start | bytes 196616 | tf_op jit(solution)/shard_map/ppermute | solution.py:51
  201.0 2.8 encoder_backward.4
  204.4 2.8 encoder_backward.5
  209.7 2.8 encoder_backward.6
  212.4 2.8 encoder_backward.7
  220.3 23.7 %collective-permute-done.38 = bf16[4,3,128,128]{3,2,1,0:T(8,128)(2,1)S(1)} collective-permute-done((bf16[4,3,128,128]{3,2,1,0:T(8,128)(2,1)S(1)}, bf16[4,3,128,128]{3,2,1,0:T(8,128)(2,1)S(1)}, u32[]{:S(2)}, u32[]{:S(2)}) %collective-permute-start.38) | collective-permute-done | bytes 393248 | tf_op jit(solution)/shard_map/ppermute | solution.py:37
  246.8 3.3 %collective-permute-start.34 = (bf16[1,3,128,128]{3,2,1,0:T(8,128)(2,1)S(1)}, bf16[1,3,128,128]{3,2,1,0:T(8,128)(2,1)S(1)}, u32[]{:S(2)}, u32[]{:S(2)}) collective-permute-start(bf16[1,3,128,128]{3,2,1,0:T(8,128)(2,1)S(1)} %slice.215), channel_id=1, source_target_pairs={{0,8},{2,10},{4,12},{6,14},{8,0},{10,2},{12,4},{14,6},{1,9},{3,11}... | collective-permute-start | bytes 294920 | tf_op jit(solution)/shard_map/ppermute | solution.py:37
  250.3 6.7 %collective-permute-done.39 = bf16[2,3,128,128]{3,2,1,0:T(8,128)(2,1)S(1)} collective-permute-done((bf16[2,3,128,128]{3,2,1,0:T(8,128)(2,1)S(1)}, bf16[2,3,128,128]{3,2,1,0:T(8,128)(2,1)S(1)}, u32[]{:S(2)}, u32[]{:S(2)}) %collective-permute-start.39) | collective-permute-done | bytes 196640 | tf_op jit(solution)/shard_map/ppermute | solution.py:37
  262.4 3.4 %collective-permute-start.45 = (bf16[1,3,128,128]{3,2,1,0:T(8,128)(2,1)S(1)}, bf16[1,3,128,128]{3,2,1,0:T(8,128)(2,1)S(1)}, u32[]{:S(2)}, u32[]{:S(2)}) collective-permute-start(bf16[1,3,128,128]{3,2,1,0:T(8,128)(2,1)S(1)} %slice.194), channel_id=1, source_target_pairs={{0,8},{2,10},{4,12},{6,14},{8,0},{10,2},{12,4},{14,6},{1,9},{3,11}... | collective-permute-start | bytes 294920 | tf_op jit(solution)/shard_map/ppermute | solution.py:37
  265.8 3.6 %collective-permute-done.40 = bf16[1,3,128,128]{3,2,1,0:T(8,128)(2,1)S(1)} collective-permute-done((bf16[1,3,128,128]{3,2,1,0:T(8,128)(2,1)S(1)}, bf16[1,3,128,128]{3,2,1,0:T(8,128)(2,1)S(1)}, u32[]{:S(2)}, u32[]{:S(2)}) %collective-permute-start.40) | collective-permute-done | bytes 98336 | tf_op jit(solution)/shard_map/ppermute | solution.py:37
  269.6 4.4 %collective-permute-done.45 = bf16[1,3,128,128]{3,2,1,0:T(8,128)(2,1)S(1)} collective-permute-done((bf16[1,3,128,128]{3,2,1,0:T(8,128)(2,1)S(1)}, bf16[1,3,128,128]{3,2,1,0:T(8,128)(2,1)S(1)}, u32[]{:S(2)}, u32[]{:S(2)}) %collective-permute-start.45) | collective-permute-done | bytes 98336 | tf_op jit(solution)/shard_map/ppermute | solution.py:37
  (196 shorter events, 69.0 us)
Async XLA Ops:
  2.4 18.3 %collective-permute-start = (bf16[128,1024]{1,0:T(8,128)(2,1)}, bf16[128,1024]{1,0:T(8,128)(2,1)}, u32[]{:S(2)}, u32[]{:S(2)}) collective-permute-start(bf16[128,1024]{1,0:T(8,128)(2,1)} %constant_dynamic-slice_fusion.4), channel_id=1, source_target_pairs={{0,14},{1,15},{2,0},{3,1},{4,2},{5,3},{6,4},{7,5},{8,6},{9,7},{10,... | collective-permute-start | bytes 786440 | tf_op jit(solution)/shard_map/ppermute | solution.py:51
  9.7 33.2 %collective-permute-start.2 = (bf16[512,1024]{1,0:T(8,128)(2,1)S(1)}, bf16[512,1024]{1,0:T(8,128)(2,1)}, u32[]{:S(2)}, u32[]{:S(2)}) collective-permute-start(bf16[512,1024]{1,0:T(8,128)(2,1)S(1)} %constant_dynamic-slice_fusion.2), channel_id=1, source_target_pairs={{0,2},{2,0},{4,6},{6,4},{8,10},{10,8},{12,14},{14,12},{1,3},{3,1},... | collective-permute-start | bytes 3145736 | tf_op jit(solution)/shard_map/ppermute | solution.py:37
  14.8 30.5 %collective-permute-start.6 = (bf16[2,128,512]{2,1,0:T(8,128)(2,1)S(1)}, bf16[2,128,512]{2,1,0:T(8,128)(2,1)}, u32[]{:S(2)}, u32[]{:S(2)}) collective-permute-start(bf16[2,128,512]{2,1,0:T(8,128)(2,1)S(1)} %pad_maximum_fusion.6), channel_id=1, source_target_pairs={{0,8},{2,10},{4,12},{6,14},{8,0},{10,2},{12,4},{14,6},{1,9},{3,11}... | collective-permute-start | bytes 786440 | tf_op jit(solution)/shard_map/ppermute | solution.py:37
  15.6 30.2 %collective-permute-start.7 = (bf16[2,128,512]{2,1,0:T(8,128)(2,1)}, bf16[2,128,512]{2,1,0:T(8,128)(2,1)}, u32[]{:S(2)}, u32[]{:S(2)}) collective-permute-start(bf16[2,128,512]{2,1,0:T(8,128)(2,1)} %pad_maximum_fusion.7), channel_id=1, source_target_pairs={{0,4},{2,6},{4,0},{6,2},{8,12},{10,14},{12,8},{14,10},{1,5},{3,7},... | collective-permute-start | bytes 786440 | tf_op jit(solution)/shard_map/ppermute | solution.py:37
  17.8 29.5 %collective-permute-start.8 = (bf16[2,128,512]{2,1,0:T(8,128)(2,1)}, bf16[2,128,512]{2,1,0:T(8,128)(2,1)}, u32[]{:S(2)}, u32[]{:S(2)}) collective-permute-start(bf16[2,128,512]{2,1,0:T(8,128)(2,1)} %pad_maximum_fusion.8), channel_id=1, source_target_pairs={{0,12},{2,14},{4,8},{6,10},{8,4},{10,6},{12,0},{14,2},{1,13},{3,15... | collective-permute-start | bytes 786440 | tf_op jit(solution)/shard_map/ppermute | solution.py:37
  45.1 7.0 %collective-permute-start.3 = (bf16[64,512]{1,0:T(8,128)(2,1)S(1)}, bf16[64,512]{1,0:T(8,128)(2,1)S(1)}, u32[]{:S(2)}, u32[]{:S(2)}) collective-permute-start(bf16[64,512]{1,0:T(8,128)(2,1)S(1)} %get-tuple-element.122), channel_id=1, source_target_pairs={{0,2},{1,3},{2,4},{3,5},{4,6},{5,7},{6,8},{7,9},{8,10},{9,11},{10,... | collective-permute-start | bytes 196616 | tf_op jit(solution)/shard_map/ppermute | solution.py:51
  45.3 6.8 %collective-permute-start.5 = (bf16[128,512]{1,0:T(8,128)(2,1)S(1)}, bf16[128,512]{1,0:T(8,128)(2,1)S(1)}, u32[]{:S(2)}, u32[]{:S(2)}) collective-permute-start(bf16[128,512]{1,0:T(8,128)(2,1)S(1)} %constant_dynamic-slice_fusion.1), channel_id=1, source_target_pairs={{0,1},{1,0},{2,3},{3,2},{4,5},{5,4},{6,7},{7,6},{8,9},{9,8},{10,11... | collective-permute-start | bytes 393224 | tf_op jit(solution)/shard_map/ppermute | solution.py:42
  45.8 26.9 %collective-permute-start.15 = (bf16[512,1024]{1,0:T(8,128)(2,1)}, bf16[512,1024]{1,0:T(8,128)(2,1)S(1)}, u32[]{:S(2)}, u32[]{:S(2)}) collective-permute-start(bf16[512,1024]{1,0:T(8,128)(2,1)} %collective-permute-done.2), channel_id=1, source_target_pairs={{0,16},{16,0},{1,17},{17,1},{2,18},{18,2},{3,19},{19,3},{4,20},{20... | collective-permute-start | bytes 3145736 | tf_op jit(solution)/shard_map/ppermute | solution.py:534
  56.9 13.5 %collective-permute-start.13 = (bf16[2,2,128,512]{3,2,1,0:T(8,128)(2,1)S(1)}, bf16[2,2,128,512]{3,2,1,0:T(8,128)(2,1)S(1)}, u32[]{:S(2)}, u32[]{:S(2)}) collective-permute-start(bf16[2,2,128,512]{3,2,1,0:T(8,128)(2,1)S(1)} %constant_dynamic-slice_fusion), channel_id=1, source_target_pairs={{0,2},{2,0},{4,6},{6,4},{8,10},{10,8},{12,14},{14,12},{1,3},{3,1},... | collective-permute-start | bytes 1572872 | tf_op jit(solution)/shard_map/ppermute | solution.py:37
  63.0 7.2 %collective-permute-start.11 = (bf16[2,2,64,512]{3,2,1,0:T(8,128)(2,1)S(1)}, bf16[2,2,64,512]{3,2,1,0:T(8,128)(2,1)S(1)}, u32[]{:S(2)}, u32[]{:S(2)}) collective-permute-start(bf16[2,2,64,512]{3,2,1,0:T(8,128)(2,1)S(1)} %pad_maximum_fusion.9), channel_id=1, source_target_pairs={{0,4},{2,6},{4,0},{6,2},{8,12},{10,14},{12,8},{14,10},{1,5},{3,7},... | collective-permute-start | bytes 786440 | tf_op jit(solution)/shard_map/ppermute | solution.py:37
  70.3 14.3 %collective-permute-start.14 = (bf16[2,2,128,512]{3,2,1,0:T(8,128)(2,1)S(1)}, bf16[2,2,128,512]{3,2,1,0:T(8,128)(2,1)S(1)}, u32[]{:S(2)}, u32[]{:S(2)}) collective-permute-start(bf16[2,2,128,512]{3,2,1,0:T(8,128)(2,1)S(1)} %collective-permute-done.13.got), channel_id=1, source_target_pairs={{0,16},{16,0},{1,17},{17,1},{2,18},{18,2},{3,19},{19,3},{4,20},{20... | collective-permute-start | bytes 1572872 | tf_op jit(solution)/shard_map/ppermute | solution.py:534
  94.4 14.3 %collective-permute-start.17 = (bf16[2,128,1024]{2,1,0:T(8,128)(2,1)}, bf16[2,128,1024]{2,1,0:T(8,128)(2,1)}, u32[]{:S(2)}, u32[]{:S(2)}) collective-permute-start(bf16[2,128,1024]{2,1,0:T(8,128)(2,1)} %bitcast.28), channel_id=1, source_target_pairs={{0,4},{2,6},{4,0},{6,2},{8,12},{10,14},{12,8},{14,10},{1,5},{3,7},... | collective-permute-start | bytes 1572872 | tf_op jit(solution)/shard_map/ppermute | solution.py:37
  96.3 12.3 %collective-permute-start.20 = (f32[2,128]{1,0:T(2,128)S(1)}, f32[2,128]{1,0:T(2,128)S(1)}, u32[]{:S(2)}, u32[]{:S(2)}) collective-permute-start(f32[2,128]{1,0:T(2,128)S(1)} %slice.166), channel_id=1, source_target_pairs={{0,4},{2,6},{4,0},{6,2},{8,12},{10,14},{12,8},{14,10},{1,5},{3,7},... | collective-permute-start | bytes 3080 | tf_op jit(solution)/shard_map/ppermute | solution.py:37
  110.0 14.2 %collective-permute-start.18 = (bf16[1,128,1024]{2,1,0:T(8,128)(2,1)S(1)}, bf16[1,128,1024]{2,1,0:T(8,128)(2,1)S(1)}, u32[]{:S(2)}, u32[]{:S(2)}) collective-permute-start(bf16[1,128,1024]{2,1,0:T(8,128)(2,1)S(1)} %get-tuple-element.119), channel_id=1, source_target_pairs={{0,8},{2,10},{4,12},{6,14},{8,0},{10,2},{12,4},{14,6},{1,9},{3,11}... | collective-permute-start | bytes 786440 | tf_op jit(solution)/shard_map/ppermute | solution.py:37
  124.5 14.6 %collective-permute-start.22 = (bf16[1,128,1152]{2,1,0:T(8,128)(2,1)S(1)}, bf16[1,128,1152]{2,1,0:T(8,128)(2,1)S(1)}, u32[]{:S(2)}, u32[]{:S(2)}) collective-permute-start(bf16[1,128,1152]{2,1,0:T(8,128)(2,1)S(1)} %bitcast.86), channel_id=1, source_target_pairs={{0,8},{2,10},{4,12},{6,14},{8,0},{10,2},{12,4},{14,6},{1,9},{3,11}... | collective-permute-start | bytes 884744 | tf_op jit(solution)/shard_map/ppermute | solution.py:37
  139.2 15.3 %collective-permute-start.23 = (bf16[2,128,1152]{2,1,0:T(8,128)(2,1)S(1)}, bf16[2,128,1152]{2,1,0:T(8,128)(2,1)S(1)}, u32[]{:S(2)}, u32[]{:S(2)}) collective-permute-start(bf16[2,128,1152]{2,1,0:T(8,128)(2,1)S(1)} %pad_maximum_fusion.3), channel_id=1, source_target_pairs={{0,4},{2,6},{4,0},{6,2},{8,12},{10,14},{12,8},{14,10},{1,5},{3,7},... | collective-permute-start | bytes 1769480 | tf_op jit(solution)/shard_map/ppermute | solution.py:37
  166.6 8.4 %collective-permute-start.26 = (bf16[2,2,64,512]{3,2,1,0:T(8,128)(2,1)S(1)}, bf16[2,2,64,512]{3,2,1,0:T(8,128)(2,1)S(1)}, u32[]{:S(2)}, u32[]{:S(2)}) collective-permute-start(bf16[2,2,64,512]{3,2,1,0:T(8,128)(2,1)S(1)} %bitcast.100), channel_id=1, source_target_pairs={{0,4},{2,6},{4,0},{6,2},{8,12},{10,14},{12,8},{14,10},{1,5},{3,7},... | collective-permute-start | bytes 786440 | tf_op jit(solution)/shard_map/ppermute | solution.py:37
  175.1 8.2 %collective-permute-start.27 = (bf16[1,2,64,512]{3,2,1,0:T(8,128)(2,1)S(1)}, bf16[1,2,64,512]{3,2,1,0:T(8,128)(2,1)S(1)}, u32[]{:S(2)}, u32[]{:S(2)}) collective-permute-start(bf16[1,2,64,512]{3,2,1,0:T(8,128)(2,1)S(1)} %slice.208), channel_id=1, source_target_pairs={{0,8},{2,10},{4,12},{6,14},{8,0},{10,2},{12,4},{14,6},{1,9},{3,11}... | collective-permute-start | bytes 393224 | tf_op jit(solution)/shard_map/ppermute | solution.py:37
  203.8 13.5 %collective-permute-start.32 = (bf16[4,3,128,128]{3,2,1,0:T(8,128)(2,1)S(1)}, bf16[4,3,128,128]{3,2,1,0:T(8,128)(2,1)S(1)}, u32[]{:S(2)}, u32[]{:S(2)}) collective-permute-start(bf16[4,3,128,128]{3,2,1,0:T(8,128)(2,1)S(1)} %get-tuple-element.87), channel_id=1, source_target_pairs={{0,2},{2,0},{4,6},{6,4},{8,10},{10,8},{12,14},{14,12},{1,3},{3,1},... | collective-permute-start | bytes 1179656 | tf_op jit(solution)/shard_map/ppermute | solution.py:37
  207.2 12.3 %collective-permute-start.35 = (bf16[4,3,128,128]{3,2,1,0:T(8,128)(2,1)S(1)}, bf16[4,3,128,128]{3,2,1,0:T(8,128)(2,1)S(1)}, u32[]{:S(2)}, u32[]{:S(2)}) collective-permute-start(bf16[4,3,128,128]{3,2,1,0:T(8,128)(2,1)S(1)} %get-tuple-element.92), channel_id=1, source_target_pairs={{0,4},{2,6},{4,0},{6,2},{8,12},{10,14},{12,8},{14,10},{1,5},{3,7},... | collective-permute-start | bytes 1179656 | tf_op jit(solution)/shard_map/ppermute | solution.py:37
  208.2 36.1 %collective-permute-start.42 = (bf16[4,64,1024]{2,1,0:T(8,128)(2,1)S(1)}, bf16[4,64,1024]{2,1,0:T(8,128)(2,1)S(1)}, u32[]{:S(2)}, u32[]{:S(2)}) collective-permute-start(bf16[4,64,1024]{2,1,0:T(8,128)(2,1)S(1)} %get-tuple-element.104), channel_id=1, source_target_pairs={{0,2},{2,0},{4,6},{6,4},{8,10},{10,8},{12,14},{14,12},{1,3},{3,1},... | collective-permute-start | bytes 1572872 | tf_op jit(solution)/shard_map/ppermute | solution.py:37
  215.2 29.0 %collective-permute-start.41 = (bf16[4,3,128,128]{3,2,1,0:T(8,128)(2,1)S(1)}, bf16[4,3,128,128]{3,2,1,0:T(8,128)(2,1)S(1)}, u32[]{:S(2)}, u32[]{:S(2)}) collective-permute-start(bf16[4,3,128,128]{3,2,1,0:T(8,128)(2,1)S(1)} %get-tuple-element.102), channel_id=1, source_target_pairs={{0,2},{2,0},{4,6},{6,4},{8,10},{10,8},{12,14},{14,12},{1,3},{3,1},... | collective-permute-start | bytes 1179656 | tf_op jit(solution)/shard_map/ppermute | solution.py:37
  215.8 28.1 %collective-permute-start.38 = (bf16[4,3,128,128]{3,2,1,0:T(8,128)(2,1)S(1)}, bf16[4,3,128,128]{3,2,1,0:T(8,128)(2,1)S(1)}, u32[]{:S(2)}, u32[]{:S(2)}) collective-permute-start(bf16[4,3,128,128]{3,2,1,0:T(8,128)(2,1)S(1)} %get-tuple-element.97), channel_id=1, source_target_pairs={{0,2},{2,0},{4,6},{6,4},{8,10},{10,8},{12,14},{14,12},{1,3},{3,1},... | collective-permute-start | bytes 1179656 | tf_op jit(solution)/shard_map/ppermute | solution.py:37
  217.4 29.3 %collective-permute-start.33 = (bf16[2,3,128,128]{3,2,1,0:T(8,128)(2,1)S(1)}, bf16[2,3,128,128]{3,2,1,0:T(8,128)(2,1)S(1)}, u32[]{:S(2)}, u32[]{:S(2)}) collective-permute-start(bf16[2,3,128,128]{3,2,1,0:T(8,128)(2,1)S(1)} %slice.213), channel_id=1, source_target_pairs={{0,4},{2,6},{4,0},{6,2},{8,12},{10,14},{12,8},{14,10},{1,5},{3,7},... | collective-permute-start | bytes 589832 | tf_op jit(solution)/shard_map/ppermute | solution.py:37
  219.7 30.4 %collective-permute-start.36 = (bf16[2,3,128,128]{3,2,1,0:T(8,128)(2,1)S(1)}, bf16[2,3,128,128]{3,2,1,0:T(8,128)(2,1)S(1)}, u32[]{:S(2)}, u32[]{:S(2)}) collective-permute-start(bf16[2,3,128,128]{3,2,1,0:T(8,128)(2,1)S(1)} %slice.217), channel_id=1, source_target_pairs={{0,2},{2,0},{4,6},{6,4},{8,10},{10,8},{12,14},{14,12},{1,3},{3,1},... | collective-permute-start | bytes 589832 | tf_op jit(solution)/shard_map/ppermute | solution.py:37
  244.1 12.9 %collective-permute-start.39 = (bf16[2,3,128,128]{3,2,1,0:T(8,128)(2,1)S(1)}, bf16[2,3,128,128]{3,2,1,0:T(8,128)(2,1)S(1)}, u32[]{:S(2)}, u32[]{:S(2)}) collective-permute-start(bf16[2,3,128,128]{3,2,1,0:T(8,128)(2,1)S(1)} %slice.221), channel_id=1, source_target_pairs={{0,4},{2,6},{4,0},{6,2},{8,12},{10,14},{12,8},{14,10},{1,5},{3,7},... | collective-permute-start | bytes 589832 | tf_op jit(solution)/shard_map/ppermute | solution.py:37
  244.5 17.7 %collective-permute-start.44 = (bf16[2,64,1024]{2,1,0:T(8,128)(2,1)S(1)}, bf16[2,64,1024]{2,1,0:T(8,128)(2,1)S(1)}, u32[]{:S(2)}, u32[]{:S(2)}) collective-permute-start(bf16[2,64,1024]{2,1,0:T(8,128)(2,1)S(1)} %slice.225), channel_id=1, source_target_pairs={{0,4},{2,6},{4,0},{6,2},{8,12},{10,14},{12,8},{14,10},{1,5},{3,7},... | collective-permute-start | bytes 786440 | tf_op jit(solution)/shard_map/ppermute | solution.py:37
  246.6 15.6 %collective-permute-start.43 = (bf16[2,3,128,128]{3,2,1,0:T(8,128)(2,1)S(1)}, bf16[2,3,128,128]{3,2,1,0:T(8,128)(2,1)S(1)}, u32[]{:S(2)}, u32[]{:S(2)}) collective-permute-start(bf16[2,3,128,128]{3,2,1,0:T(8,128)(2,1)S(1)} %slice.190), channel_id=1, source_target_pairs={{0,4},{2,6},{4,0},{6,2},{8,12},{10,14},{12,8},{14,10},{1,5},{3,7},... | collective-permute-start | bytes 589832 | tf_op jit(solution)/shard_map/ppermute | solution.py:37
  246.8 11.9 %collective-permute-start.34 = (bf16[1,3,128,128]{3,2,1,0:T(8,128)(2,1)S(1)}, bf16[1,3,128,128]{3,2,1,0:T(8,128)(2,1)S(1)}, u32[]{:S(2)}, u32[]{:S(2)}) collective-permute-start(bf16[1,3,128,128]{3,2,1,0:T(8,128)(2,1)S(1)} %slice.215), channel_id=1, source_target_pairs={{0,8},{2,10},{4,12},{6,14},{8,0},{10,2},{12,4},{14,6},{1,9},{3,11}... | collective-permute-start | bytes 294920 | tf_op jit(solution)/shard_map/ppermute | solution.py:37
  250.2 9.5 %collective-permute-start.37 = (bf16[1,3,128,128]{3,2,1,0:T(8,128)(2,1)S(1)}, bf16[1,3,128,128]{3,2,1,0:T(8,128)(2,1)S(1)}, u32[]{:S(2)}, u32[]{:S(2)}) collective-permute-start(bf16[1,3,128,128]{3,2,1,0:T(8,128)(2,1)S(1)} %slice.219), channel_id=1, source_target_pairs={{0,8},{2,10},{4,12},{6,14},{8,0},{10,2},{12,4},{14,6},{1,9},{3,11}... | collective-permute-start | bytes 294920 | tf_op jit(solution)/shard_map/ppermute | solution.py:37
  257.1 12.4 %collective-permute-start.40 = (bf16[1,3,128,128]{3,2,1,0:T(8,128)(2,1)S(1)}, bf16[1,3,128,128]{3,2,1,0:T(8,128)(2,1)S(1)}, u32[]{:S(2)}, u32[]{:S(2)}) collective-permute-start(bf16[1,3,128,128]{3,2,1,0:T(8,128)(2,1)S(1)} %slice.223), channel_id=1, source_target_pairs={{0,8},{2,10},{4,12},{6,14},{8,0},{10,2},{12,4},{14,6},{1,9},{3,11}... | collective-permute-start | bytes 294920 | tf_op jit(solution)/shard_map/ppermute | solution.py:37
  262.4 11.6 %collective-permute-start.45 = (bf16[1,3,128,128]{3,2,1,0:T(8,128)(2,1)S(1)}, bf16[1,3,128,128]{3,2,1,0:T(8,128)(2,1)S(1)}, u32[]{:S(2)}, u32[]{:S(2)}) collective-permute-start(bf16[1,3,128,128]{3,2,1,0:T(8,128)(2,1)S(1)} %slice.194), channel_id=1, source_target_pairs={{0,8},{2,10},{4,12},{6,14},{8,0},{10,2},{12,4},{14,6},{1,9},{3,11}... | collective-permute-start | bytes 294920 | tf_op jit(solution)/shard_map/ppermute | solution.py:37
  (33 other events, 312.7 us)

commit v4 on v3

--- a/solution.py
+++ b/solution.py
@@ -93,22 +93,23 @@
         low = (low[:half].astype(F32) + got.astype(F32)).astype(BF)
 
 
-def scatter_chunks(chunks, lead):
+def scatter_chunks(chunks):
     sums = [lower for lower, _, _ in chunks]
     sends = [upper for _, upper, _ in chunks]
-    for stage in range(len(chunks[0][2])):
-        for i, (_, _, masks) in enumerate(chunks):
-            total = sums[i].astype(F32) + swap_tm(sends[i], masks[stage]).astype(F32)
-            if total.shape[0] == 1:
-                sums[i] = total[0]
-                continue
-            low = total.astype(BF)
-            if i == lead:
-                done = low
-            if i + 1 == len(chunks):
-                low, done = lax.optimization_barrier((low, done))
-            half = low.shape[0] // 2
-            sums[i], sends[i] = low[:half], low[half:]
+    stages = len(chunks[0][2])
+    steps = [(i + 1.5 * t, -t, i) for i in range(len(chunks)) for t in range(stages)]
+    last = None
+    for _, t, i in sorted(steps):
+        got = swap_tm(sends[i], chunks[i][2][-t])
+        if last is not None:
+            got, _ = lax.optimization_barrier((got, last))
+        total = sums[i].astype(F32) + got.astype(F32)
+        if total.shape[0] == 1:
+            sums[i] = total[0]
+            continue
+        low = last = total.astype(BF)
+        half = low.shape[0] // 2
+        sums[i], sends[i] = low[:half], low[half:]
     return sums
 
 
@@ -197,10 +198,10 @@
             scratch_shapes=[pltpu.VMEM((rows, cols), BF)],
         ),
         out_shape=[
-            jax.ShapeDtypeStruct((rows, width), BF),
-            jax.ShapeDtypeStruct((3, rows, heads_w), BF),
-            jax.ShapeDtypeStruct((pairs, windows, 2, WINDOW, WINDOW), BF),
-            jax.ShapeDtypeStruct((ext_tok, heads_w), BF),
+            pltpu.HBM((rows, width), BF),
+            pltpu.HBM((3, rows, heads_w), BF),
+            pltpu.HBM((pairs, windows, 2, WINDOW, WINDOW), BF),
+            pltpu.HBM((ext_tok, heads_w), BF),
             jax.ShapeDtypeStruct((ext_tok, width), F32),
         ],
         compiler_params=pltpu.CompilerParams(vmem_limit_bytes=VMEM_LIMIT),
@@ -504,7 +505,8 @@
     if not two_groups:
         group = group * 0
     proj_kv, part = lax.optimization_barrier((proj_kv, part))
-    kv_near = swap_tm(lax.dynamic_slice_in_dim(proj_kv, group * kv_half, kv_half, 1), SPLIT)
+    kv_cut = lax.dynamic_slice_in_dim(proj_kv, group * kv_half, kv_half, 1)
+    kv_near = [swap_tm(part, SPLIT) for part in jnp.split(kv_cut, 2)]
     proj_in, w_t = lax.optimization_barrier((proj_in, w_t))
 
     masks = group_bits()
@@ -526,16 +528,24 @@
     )
     x_roll = lax.dynamic_slice_in_dim(jnp.concatenate([frames, halo], 0), shift, rows, 0)
 
+    swap_groups = lambda block: lax.ppermute(block, "groups", [(0, 1), (1, 0)])
+    x_roll, kv_near[0] = lax.optimization_barrier((x_roll, kv_near[0]))
+    kv_far = [swap_groups(kv_near[0])] if two_groups else []
     at = jnp.stack([shift, rows * n - shift - me * rows, me, core, group]).astype(jnp.int32)
     normed, qkv, probs, pooled_attn, out_part = encoder_forward(
         x_roll, w_t, weight_out, at, ext_tok
     )
-    out_part, kv_near = lax.optimization_barrier((out_part, kv_near))
-    swap_groups = lambda block: lax.ppermute(block, "groups", [(0, 1), (1, 0)])
+    out_part, kv_near, blocks, kv_far = lax.optimization_barrier(
+        (out_part, kv_near, blocks, kv_far)
+    )
     if two_groups:
-        kv_far = swap_groups(kv_near)
+        kv_far.append(swap_groups(kv_near[1]))
     else:
-        kv_far = swap_tm(proj_kv[:, kv_half:], SPLIT)
+        kv_far.append(swap_tm(proj_kv[:, kv_half:], SPLIT))
+    here = jnp.stack(blocks)
+    in_near = swap_tm(
+        lax.dynamic_slice_in_dim(here, group * (count // 2), count // 2, 0), SPLIT
+    )
     turned = normed.T
     route, norm_gain, d_kv, pooled_attn = lax.optimization_barrier(
         (route, norm_gain, d_kv, pooled_attn)
@@ -562,15 +572,26 @@
     from_core = swap_mp(low_other[:own_tok])
     tail_a = to_tm(low_own[own_tok:], 1, False)
     tail_b = to_tm(low_other[own_tok:], 1, True)
-    tail_a, tail_b, from_core, blocks = lax.optimization_barrier(
-        (tail_a, tail_b, from_core, blocks)
-    )
-    here = jnp.stack(blocks)
-    in_near = swap_tm(
-        lax.dynamic_slice_in_dim(here, group * (count // 2), count // 2, 0), SPLIT
-    )
+    own_pool = (
+        jnp.arange(rows, dtype=jnp.int32)[None, :] // POOL
+        == jnp.arange(own_tok, dtype=jnp.int32)[:, None]
+    ).astype(BF) * (1.0 / POOL)
+    x_mean = dot(own_pool, lax.dynamic_slice_in_dim(frames, core * half_w, half_w, 1))
+    pooled = (
+        x_mean
+        + lax.dynamic_slice_in_dim(out_part, core * half_w, half_w, 1)[:own_tok]
+        + from_core.astype(F32)
+    )
+    tail = tail_a.astype(F32) + tail_b.astype(F32)
+    pooled = jnp.concatenate([pooled[:tail_tok] + tail, pooled[tail_tok:]], 0).astype(BF)
+
+    sorted_tok = dot(sort, pooled).astype(BF).reshape(2, count * piece, half_w)
+    pair_tok = jnp.stack([sorted_tok[0], swap_tm(sorted_tok[1], SPLIT)])
+    pair_tok, in_near, kv_far = lax.optimization_barrier((pair_tok, in_near, kv_far))
+    tok_half = gather_doubling(pair_tok, masks).reshape(-1, half_w)
     in_far = swap_groups(in_near) if two_groups else swap_tm(here[count // 2 :], SPLIT)
-    kva, kvb = proj_kv, jnp.stack([kv_near, kv_far])
+    kva = proj_kv
+    kvb = jnp.stack([jnp.concatenate(kv_near), jnp.concatenate(kv_far)])
     at_rows = order
     if width // n % LANES:
         stacked = jnp.concatenate([here, in_near[:, ::-1], in_far[:, ::-1]])
@@ -580,22 +601,6 @@
         stacked = jnp.take(stacked, place, axis=0)
         here, in_near, in_far = jnp.split(stacked, [count, count + count // 2])
         at_rows = None
-    own_pool = (
-        jnp.arange(rows, dtype=jnp.int32)[None, :] // POOL
-        == jnp.arange(own_tok, dtype=jnp.int32)[:, None]
-    ).astype(BF) * (1.0 / POOL)
-    x_mean = dot(own_pool, lax.dynamic_slice_in_dim(frames, core * half_w, half_w, 1))
-    pooled = (
-        x_mean
-        + lax.dynamic_slice_in_dim(out_part, core * half_w, half_w, 1)[:own_tok]
-        + from_core.astype(F32)
-    )
-    tail = tail_a.astype(F32) + tail_b.astype(F32)
-    pooled = jnp.concatenate([pooled[:tail_tok] + tail, pooled[tail_tok:]], 0).astype(BF)
-
-    sorted_tok = dot(sort, pooled).astype(BF).reshape(2, count * piece, half_w)
-    pair_tok = jnp.stack([sorted_tok[0], swap_tm(sorted_tok[1], SPLIT)])
-    tok_half = gather_doubling(pair_tok, masks).reshape(-1, half_w)
     tok_other = swap_mp(tok_half)
     table = list(moves(order, piece))
     source_rows = np.concatenate([np.arange(r, r + piece) for r, _ in table])
@@ -611,6 +616,7 @@
     squares = jnp.sum(lifted * lifted, axis=-1).reshape(count, own_tok)
     square_sum = scatter_halving(squares + swap_mp(squares), masks, F32)
     kv_part = kv_keep.astype(F32) + swap_mp(kv_send).astype(F32)
+    kv_part, turned = lax.optimization_barrier((kv_part, turned))
     kv_mine, kv_got = scatter_last(kv_part.reshape(count, own_tok, kv_half), masks)
     kv_low, load = finish(kv_mine, kv_got, square_sum.reshape(1, own_tok), d_kv)
     kv = dot(spread, kv_low).astype(BF)
@@ -644,7 +650,7 @@
         even, odd, at = lax.optimization_barrier((even, odd, at))
         chunks.append((even, odd, path))
     chunks.insert(2, (out_even, out_odd, bits))
-    chunks = scatter_chunks(chunks, 2)
+    chunks = scatter_chunks(chunks)
     grad_out = chunks.pop(2)
     grad_qkv = jnp.transpose(jnp.concatenate(chunks, axis=-1), (1, 0, 2))
     return kv, grad_qkv, grad_out

time: 278 us -> 291 us (1.047)
  other arithmetic: 14.1 us -> 22.6 us
  starting transfers between devices: 44.9 us -> 52.4 us
    ppermute x32 -> x33, waiting for transfers between devices: 130 us -> 143 us  [swap_tm(): return lax.ppermute(block, 'tm', [(i, i ^ mask) for i in range(n)])]
    ppermute x32 -> x33, starting transfers between devices: 29.2 us -> 36.5 us  [swap_tm(): return lax.ppermute(block, 'tm', [(i, i ^ mask) for i in range(n)])]
    ppermute x2 -> x3, waiting for transfers between devices: 9.22 us -> 2.4 us  [on_device(): swap_groups = lambda block: lax.ppermute(block, 'groups', [(0, 1), (1, 0)])]
    ppermute x5, waiting for transfers between devices: 8.77 us -> 2.47 us  [to_tm(): return lax.ppermute(block, ('tm', 'mp'), pairs)]
    another operation x4, other arithmetic: 1.51 us -> 4.99 us  [on_device(): pair = jnp.stack(pair)]
    unnamed x37 -> x33, local copies, waits for them, and re-layouts: 5.34 us -> 2.01 us
  transfers between devices with their start and end apart: 47 -> 49, of which waited for: 27 -> 27; matrix products, arithmetic and copies ran while one was open for 9% -> 11% of each run, Pallas kernels for 7% -> 6%
where the time goes in v4:
time: 291 us; the launch traced here: 290 us
  waiting for transfers between devices  155 us (53%)
  starting transfers between devices  52.4 us (18%)
  Pallas kernels  35.9 us (12%)
  other arithmetic  22.6 us (8%)
  local copies, waits for them, and re-layouts  17.6 us (6%)
  between operations  4.09 us (1%)
    ppermute x33, waiting for transfers between devices, swap_tm(): return lax.ppermute(block, 'tm', [(i, i ^ mask) for i in range(n)])  143 us
    ppermute x33, starting transfers between devices, swap_tm(): return lax.ppermute(block, 'tm', [(i, i ^ mask) for i in range(n)])  36.5 us
    ppermute x5, starting transfers between devices, to_tm(): return lax.ppermute(block, ('tm', 'mp'), pairs)  11.2 us
    pallas_call x4, Pallas kernels, encoder_backward(): pl.pallas_call(functools.partial(backward_kernel, masks), grid_spec=pltpu...  11 us
    pallas_call x1, Pallas kernels, encoder_forward(): pl.pallas_call(forward_kernel, grid_spec=pltpu.PrefetchScalarGridSpec(num...  10.3 us
    ppermute x8, waiting for transfers between devices, swap_mp(): return lax.ppermute(block, 'mp', [(i, n - 1 - i) for i in range(n)])  7.26 us
    pallas_call x1, Pallas kernels, lower(): pl.pallas_call(functools.partial(lower_kernel, table, order), in_specs=[p...  6.76 us
  transfers between devices with their start and end apart: 49, of which 27 were waited for; matrix products, arithmetic and copies ran while one was open for 11% of the time, Pallas kernels for 6%

profile of v4, /device:TPU:0, one launch (start us, length us, event | category | flops | bytes accessed | tf_op | source)
XLA Modules:
  0.0 290.3 jit_solution(15809616804521480430)
XLA Ops:
  2.4 6.0 %collective-permute-start = (bf16[128,1024]{1,0:T(8,128)(2,1)}, bf16[128,1024]{1,0:T(8,128)(2,1)}, u32[]{:S(2)}, u32[]{:S(2)}) collective-permute-start(bf16[128,1024]{1,0:T(8,128)(2,1)} %constant_dynamic-slice_fusion.4), channel_id=1, source_target_pairs={{0,14},{1,15},{2,0},{3,1},{4,2},{5,3},{6,4},{7,5},{8,6},{9,7},{10,... | collective-permute-start | bytes 786440 | tf_op jit(solution)/shard_map/ppermute | solution.py:51
  8.4 2.2 fusion.33
  12.6 3.2 %copy.14 = bf16[3,512,1024]{2,1,0:T(8,128)(2,1)S(1)} copy(bf16[3,512,1024]{1,2,0:T(8,128)(2,1)} %bitcast.96) | data formatting | bytes 6291456 | tf_op jit(solution)/shard_map/transpose | solution.py:502
  15.9 2.1 dynamic-slice_bitcast_fusion.1
  28.0 3.4 %collective-permute-start.6 = (bf16[2,128,512]{2,1,0:T(8,128)(2,1)}, bf16[2,128,512]{2,1,0:T(8,128)(2,1)}, u32[]{:S(2)}, u32[]{:S(2)}) collective-permute-start(bf16[2,128,512]{2,1,0:T(8,128)(2,1)} %pad_maximum_fusion.8), channel_id=1, source_target_pairs={{0,12},{2,14},{4,8},{6,10},{8,4},{10,6},{12,0},{14,2},{1,13},{3,15... | collective-permute-start | bytes 786440 | tf_op jit(solution)/shard_map/ppermute | solution.py:37
  37.0 10.3 %encoder_forward.1 = (bf16[512,1024]{1,0:T(8,128)(2,1)}, bf16[3,512,512]{2,1,0:T(8,128)(2,1)}, bf16[4,2,2,256,256]{4,3,2,1,0:T(8,128)(2,1)}, bf16[192,512]{1,0:T(8,128)(2,1)}, f32[192,1024]{1,0:T(8,128)S(1)}) custom-call(s32[5]{0:T(128)S(1)} %stack.85.at, bf16[512,1024]{1,0:T(8,128)(2,1)S(1)} %fusion.x_ref, bf16[1536,1024]{1,0:T(8,128)(2,1)S(1)} %bitcast.79, ...), custom_call_target="tpu_custom_call" | custom-call | tf_op jit(solution)/shard_map/encoder_forward/pallas_call | solution.py:179
  54.9 2.5 collective-permute-start.12
  60.3 12.9 %collective-permute-done.11 = bf16[64,512]{1,0:T(8,128)(2,1)S(1)} collective-permute-done((bf16[64,512]{1,0:T(8,128)(2,1)S(1)}, bf16[64,512]{1,0:T(8,128)(2,1)S(1)}, u32[]{:S(2)}, u32[]{:S(2)}) %collective-permute-start.11) | collective-permute-done | bytes 65568 | tf_op jit(solution)/shard_map/ppermute | solution.py:37
  75.3 6.2 %collective-permute-done.14 = bf16[1,2,64,512]{3,2,1,0:T(8,128)(2,1)S(1)} collective-permute-done((bf16[1,2,64,512]{3,2,1,0:T(8,128)(2,1)S(1)}, bf16[1,2,64,512]{3,2,1,0:T(8,128)(2,1)S(1)}, u32[]{:S(2)}, u32[]{:S(2)}) %collective-permute-start.14) | collective-permute-done | bytes 131104 | tf_op jit(solution)/shard_map/ppermute | solution.py:37
  83.1 6.6 %collective-permute-done.15 = bf16[2,2,64,512]{3,2,1,0:T(8,128)(2,1)S(1)} collective-permute-done((bf16[2,2,64,512]{3,2,1,0:T(8,128)(2,1)S(1)}, bf16[2,2,64,512]{3,2,1,0:T(8,128)(2,1)S(1)}, u32[]{:S(2)}, u32[]{:S(2)}) %collective-permute-start.15) | collective-permute-done | bytes 262176 | tf_op jit(solution)/shard_map/ppermute | solution.py:37
  93.9 2.4 collective-permute-done.17.other
  96.3 5.8 %lift.1 = (f32[512,1024]{1,0:T(8,128)}, bf16[512,1024]{1,0:T(8,128)(2,1)}, bf16[512,1024]{1,0:T(8,128)(2,1)S(1)}) custom-call(s32[5]{0:T(128)S(1)} %stack.85.at, bf16[512,512]{1,0:T(8,128)(2,1)S(1)} %bitcast.89, bf16[512,512]{1,0:T(8,128)(2,1)S(1)} %collective-permute-done.16.tb, bf16[4,2,128,512]{3,2,1,0:T(8,128)(2,1)S(1)} %pad_maximum_fusion.2.here, ...), custom_call_target="tpu_custom_call" | custom-call | tf_op jit(solution)/shard_map/lift/pallas_call | solution.py:379
  113.9 9.6 %collective-permute-done.22 = f32[2,128]{1,0:T(2,128)S(1)} collective-permute-done((f32[2,128]{1,0:T(2,128)S(1)}, f32[2,128]{1,0:T(2,128)S(1)}, u32[]{:S(2)}, u32[]{:S(2)}) %collective-permute-start.22) | collective-permute-done | bytes 1056 | tf_op jit(solution)/shard_map/ppermute | solution.py:37
  123.6 2.3 collective-permute-start.23
  128.3 12.6 %collective-permute-done.20 = bf16[1,128,1024]{2,1,0:T(8,128)(2,1)S(1)} collective-permute-done((bf16[1,128,1024]{2,1,0:T(8,128)(2,1)S(1)}, bf16[1,128,1024]{2,1,0:T(8,128)(2,1)S(1)}, u32[]{:S(2)}, u32[]{:S(2)}) %collective-permute-start.20) | collective-permute-done | bytes 262176 | tf_op jit(solution)/shard_map/ppermute | solution.py:37
  141.4 15.3 %collective-permute-done.24 = bf16[1,128,1152]{2,1,0:T(8,128)(2,1)S(1)} collective-permute-done((bf16[1,128,1152]{2,1,0:T(8,128)(2,1)S(1)}, bf16[1,128,1152]{2,1,0:T(8,128)(2,1)S(1)}, u32[]{:S(2)}, u32[]{:S(2)}) %collective-permute-start.24) | collective-permute-done | bytes 294944 | tf_op jit(solution)/shard_map/ppermute | solution.py:37
  156.8 15.2 %collective-permute-done.25 = bf16[2,128,1152]{2,1,0:T(8,128)(2,1)S(1)} collective-permute-done((bf16[2,128,1152]{2,1,0:T(8,128)(2,1)S(1)}, bf16[2,128,1152]{2,1,0:T(8,128)(2,1)S(1)}, u32[]{:S(2)}, u32[]{:S(2)}) %collective-permute-start.25) | collective-permute-done | bytes 589856 | tf_op jit(solution)/shard_map/ppermute | solution.py:37
  172.3 2.8 collective-permute-done.26.cb
  175.1 6.8 %lower.1 = (bf16[512,512]{1,0:T(8,128)(2,1)S(1)}, bf16[512,512]{1,0:T(8,128)(2,1)S(1)}) custom-call(s32[5]{0:T(128)S(1)} %stack.85.at, bf16[512,1152]{1,0:T(8,128)(2,1)S(1)} %bitcast.87, bf16[512,1152]{1,0:T(8,128)(2,1)S(1)} %collective-permute-done.26.cb, bf16[4,2,128,512]{3,2,1,0:T(8,128)(2,1)S(1)} %pad_maximum_fusion.2.here, ...), custom_call_target="tpu_custom_call" | custom-call | tf_op jit(solution)/shard_map/lower/pallas_call | solution.py:475
  184.4 8.1 %collective-permute-done.28 = bf16[2,2,64,512]{3,2,1,0:T(8,128)(2,1)S(1)} collective-permute-done((bf16[2,2,64,512]{3,2,1,0:T(8,128)(2,1)S(1)}, bf16[2,2,64,512]{3,2,1,0:T(8,128)(2,1)S(1)}, u32[]{:S(2)}, u32[]{:S(2)}) %collective-permute-start.28) | collective-permute-done | bytes 262176 | tf_op jit(solution)/shard_map/ppermute | solution.py:37
  193.5 7.3 %collective-permute-done.29 = bf16[1,2,64,512]{3,2,1,0:T(8,128)(2,1)S(1)} collective-permute-done((bf16[1,2,64,512]{3,2,1,0:T(8,128)(2,1)S(1)}, bf16[1,2,64,512]{3,2,1,0:T(8,128)(2,1)S(1)}, u32[]{:S(2)}, u32[]{:S(2)}) %collective-permute-start.29) | collective-permute-done | bytes 131104 | tf_op jit(solution)/shard_map/ppermute | solution.py:37
  200.9 4.3 %collective-permute-done.30 = bf16[64,512]{1,0:T(8,128)(2,1)S(1)} collective-permute-done((bf16[64,512]{1,0:T(8,128)(2,1)S(1)}, bf16[64,512]{1,0:T(8,128)(2,1)S(1)}, u32[]{:S(2)}, u32[]{:S(2)}) %collective-permute-start.30) | collective-permute-done | bytes 65568 | tf_op jit(solution)/shard_map/ppermute | solution.py:37
  213.1 2.8 encoder_backward.4
  217.3 2.8 encoder_backward.5
  221.7 2.8 encoder_backward.6
  224.5 2.8 encoder_backward.7
  235.3 3.9 %collective-permute-done.39 = bf16[4,64,1024]{2,1,0:T(8,128)(2,1)S(1)} collective-permute-done((bf16[4,64,1024]{2,1,0:T(8,128)(2,1)S(1)}, bf16[4,64,1024]{2,1,0:T(8,128)(2,1)S(1)}, u32[]{:S(2)}, u32[]{:S(2)}) %collective-permute-start.39) | collective-permute-done | bytes 524320 | tf_op jit(solution)/shard_map/ppermute | solution.py:37
  240.6 17.8 %collective-permute-done.38 = bf16[2,3,128,128]{3,2,1,0:T(8,128)(2,1)S(1)} collective-permute-done((bf16[2,3,128,128]{3,2,1,0:T(8,128)(2,1)S(1)}, bf16[2,3,128,128]{3,2,1,0:T(8,128)(2,1)S(1)}, u32[]{:S(2)}, u32[]{:S(2)}) %collective-permute-start.38) | collective-permute-done | bytes 196640 | tf_op jit(solution)/shard_map/ppermute | solution.py:37
  259.9 2.5 collective-permute-start.41
  262.7 7.3 %collective-permute-done.41 = bf16[2,64,1024]{2,1,0:T(8,128)(2,1)S(1)} collective-permute-done((bf16[2,64,1024]{2,1,0:T(8,128)(2,1)S(1)}, bf16[2,64,1024]{2,1,0:T(8,128)(2,1)S(1)}, u32[]{:S(2)}, u32[]{:S(2)}) %collective-permute-start.41) | collective-permute-done | bytes 262176 | tf_op jit(solution)/shard_map/ppermute | solution.py:37
  279.7 3.0 %collective-permute-done.46 = bf16[2,3,128,128]{3,2,1,0:T(8,128)(2,1)S(1)} collective-permute-done((bf16[2,3,128,128]{3,2,1,0:T(8,128)(2,1)S(1)}, bf16[2,3,128,128]{3,2,1,0:T(8,128)(2,1)S(1)}, u32[]{:S(2)}, u32[]{:S(2)}) %collective-permute-start.46) | collective-permute-done | bytes 196640 | tf_op jit(solution)/shard_map/ppermute | solution.py:37
  284.0 5.3 %collective-permute-done.47 = bf16[1,3,128,128]{3,2,1,0:T(8,128)(2,1)S(1)} collective-permute-done((bf16[1,3,128,128]{3,2,1,0:T(8,128)(2,1)S(1)}, bf16[1,3,128,128]{3,2,1,0:T(8,128)(2,1)S(1)}, u32[]{:S(2)}, u32[]{:S(2)}) %collective-permute-start.47) | collective-permute-done | bytes 98336 | tf_op jit(solution)/shard_map/ppermute | solution.py:37
  (197 shorter events, 87.6 us)
Async XLA Ops:
  2.4 18.1 %collective-permute-start = (bf16[128,1024]{1,0:T(8,128)(2,1)}, bf16[128,1024]{1,0:T(8,128)(2,1)}, u32[]{:S(2)}, u32[]{:S(2)}) collective-permute-start(bf16[128,1024]{1,0:T(8,128)(2,1)} %constant_dynamic-slice_fusion.4), channel_id=1, source_target_pairs={{0,14},{1,15},{2,0},{3,1},{4,2},{5,3},{6,4},{7,5},{8,6},{9,7},{10,... | collective-permute-start | bytes 786440 | tf_op jit(solution)/shard_map/ppermute | solution.py:51
  10.6 39.4 %collective-permute-start.3 = (bf16[256,1024]{1,0:T(8,128)(2,1)}, bf16[256,1024]{1,0:T(8,128)(2,1)}, u32[]{:S(2)}, u32[]{:S(2)}) collective-permute-start(bf16[256,1024]{1,0:T(8,128)(2,1)} %get-tuple-element.145), channel_id=1, source_target_pairs={{0,2},{2,0},{4,6},{6,4},{8,10},{10,8},{12,14},{14,12},{1,3},{3,1},... | collective-permute-start | bytes 1572872 | tf_op jit(solution)/shard_map/ppermute | solution.py:37
  10.6 24.9 %collective-permute-start.2 = (bf16[256,1024]{1,0:T(8,128)(2,1)}, bf16[256,1024]{1,0:T(8,128)(2,1)}, u32[]{:S(2)}, u32[]{:S(2)}) collective-permute-start(bf16[256,1024]{1,0:T(8,128)(2,1)} %get-tuple-element.146), channel_id=1, source_target_pairs={{0,2},{2,0},{4,6},{6,4},{8,10},{10,8},{12,14},{14,12},{1,3},{3,1},... | collective-permute-start | bytes 1572872 | tf_op jit(solution)/shard_map/ppermute | solution.py:37
  18.8 31.2 %collective-permute-start.4 = (bf16[2,128,512]{2,1,0:T(8,128)(2,1)}, bf16[2,128,512]{2,1,0:T(8,128)(2,1)}, u32[]{:S(2)}, u32[]{:S(2)}) collective-permute-start(bf16[2,128,512]{2,1,0:T(8,128)(2,1)} %pad_maximum_fusion.6), channel_id=1, source_target_pairs={{0,8},{2,10},{4,12},{6,14},{8,0},{10,2},{12,4},{14,6},{1,9},{3,11}... | collective-permute-start | bytes 786440 | tf_op jit(solution)/shard_map/ppermute | solution.py:37
  19.5 30.5 %collective-permute-start.5 = (bf16[2,128,512]{2,1,0:T(8,128)(2,1)}, bf16[2,128,512]{2,1,0:T(8,128)(2,1)}, u32[]{:S(2)}, u32[]{:S(2)}) collective-permute-start(bf16[2,128,512]{2,1,0:T(8,128)(2,1)} %pad_maximum_fusion.7), channel_id=1, source_target_pairs={{0,4},{2,6},{4,0},{6,2},{8,12},{10,14},{12,8},{14,10},{1,5},{3,7},... | collective-permute-start | bytes 786440 | tf_op jit(solution)/shard_map/ppermute | solution.py:37
  28.0 22.0 %collective-permute-start.6 = (bf16[2,128,512]{2,1,0:T(8,128)(2,1)}, bf16[2,128,512]{2,1,0:T(8,128)(2,1)}, u32[]{:S(2)}, u32[]{:S(2)}) collective-permute-start(bf16[2,128,512]{2,1,0:T(8,128)(2,1)} %pad_maximum_fusion.8), channel_id=1, source_target_pairs={{0,12},{2,14},{4,8},{6,10},{8,4},{10,6},{12,0},{14,2},{1,13},{3,15... | collective-permute-start | bytes 786440 | tf_op jit(solution)/shard_map/ppermute | solution.py:37
  35.5 14.5 %collective-permute-start.7 = (bf16[256,1024]{1,0:T(8,128)(2,1)}, bf16[256,1024]{1,0:T(8,128)(2,1)}, u32[]{:S(2)}, u32[]{:S(2)}) collective-permute-start(bf16[256,1024]{1,0:T(8,128)(2,1)} %collective-permute-done.2), channel_id=1, source_target_pairs={{0,16},{16,0},{1,17},{17,1},{2,18},{18,2},{3,19},{19,3},{4,20},{20... | collective-permute-start | bytes 1572872 | tf_op jit(solution)/shard_map/ppermute | solution.py:531
  51.3 8.7 %collective-permute-start.9 = (bf16[64,512]{1,0:T(8,128)(2,1)S(1)}, bf16[64,512]{1,0:T(8,128)(2,1)S(1)}, u32[]{:S(2)}, u32[]{:S(2)}) collective-permute-start(bf16[64,512]{1,0:T(8,128)(2,1)S(1)} %get-tuple-element.161), channel_id=1, source_target_pairs={{0,2},{1,3},{2,4},{3,5},{4,6},{5,7},{6,8},{7,9},{8,10},{9,11},{10,... | collective-permute-start | bytes 196616 | tf_op jit(solution)/shard_map/ppermute | solution.py:51
  54.9 18.4 %collective-permute-start.12 = (bf16[2,2,128,512]{3,2,1,0:T(8,128)(2,1)S(1)}, bf16[2,2,128,512]{3,2,1,0:T(8,128)(2,1)S(1)}, u32[]{:S(2)}, u32[]{:S(2)}) collective-permute-start(bf16[2,2,128,512]{3,2,1,0:T(8,128)(2,1)S(1)} %constant_dynamic-slice_fusion), channel_id=1, source_target_pairs={{0,2},{2,0},{4,6},{6,4},{8,10},{10,8},{12,14},{14,12},{1,3},{3,1},... | collective-permute-start | bytes 1572872 | tf_op jit(solution)/shard_map/ppermute | solution.py:37
  57.4 15.9 %collective-permute-start.13 = (bf16[256,1024]{1,0:T(8,128)(2,1)}, bf16[256,1024]{1,0:T(8,128)(2,1)S(1)}, u32[]{:S(2)}, u32[]{:S(2)}) collective-permute-start(bf16[256,1024]{1,0:T(8,128)(2,1)} %collective-permute-done.3), channel_id=1, source_target_pairs={{0,16},{16,0},{1,17},{17,1},{2,18},{18,2},{3,19},{19,3},{4,20},{20... | collective-permute-start | bytes 1572872 | tf_op jit(solution)/shard_map/ppermute | solution.py:531
  60.2 13.0 %collective-permute-start.11 = (bf16[64,512]{1,0:T(8,128)(2,1)S(1)}, bf16[64,512]{1,0:T(8,128)(2,1)S(1)}, u32[]{:S(2)}, u32[]{:S(2)}) collective-permute-start(bf16[64,512]{1,0:T(8,128)(2,1)S(1)} %get-tuple-element.166), channel_id=1, source_target_pairs={{0,2},{2,0},{4,6},{6,4},{8,10},{10,8},{12,14},{14,12},{1,3},{3,1},... | collective-permute-start | bytes 196616 | tf_op jit(solution)/shard_map/ppermute | solution.py:37
  81.5 8.3 %collective-permute-start.15 = (bf16[2,2,64,512]{3,2,1,0:T(8,128)(2,1)S(1)}, bf16[2,2,64,512]{3,2,1,0:T(8,128)(2,1)S(1)}, u32[]{:S(2)}, u32[]{:S(2)}) collective-permute-start(bf16[2,2,64,512]{3,2,1,0:T(8,128)(2,1)S(1)} %pad_maximum_fusion.9), channel_id=1, source_target_pairs={{0,4},{2,6},{4,0},{6,2},{8,12},{10,14},{12,8},{14,10},{1,5},{3,7},... | collective-permute-start | bytes 786440 | tf_op jit(solution)/shard_map/ppermute | solution.py:37
  82.4 13.9 %collective-permute-start.17 = (bf16[2,2,128,512]{3,2,1,0:T(8,128)(2,1)S(1)}, bf16[2,2,128,512]{3,2,1,0:T(8,128)(2,1)S(1)}, u32[]{:S(2)}, u32[]{:S(2)}) collective-permute-start(bf16[2,2,128,512]{3,2,1,0:T(8,128)(2,1)S(1)} %collective-permute-done.12.got), channel_id=1, source_target_pairs={{0,16},{16,0},{1,17},{17,1},{2,18},{18,2},{3,19},{19,3},{4,20},{20... | collective-permute-start | bytes 1572872 | tf_op jit(solution)/shard_map/ppermute | solution.py:531
  109.3 16.6 %collective-permute-start.19 = (bf16[2,128,1024]{2,1,0:T(8,128)(2,1)}, bf16[2,128,1024]{2,1,0:T(8,128)(2,1)}, u32[]{:S(2)}, u32[]{:S(2)}) collective-permute-start(bf16[2,128,1024]{2,1,0:T(8,128)(2,1)} %bitcast.29), channel_id=1, source_target_pairs={{0,4},{2,6},{4,0},{6,2},{8,12},{10,14},{12,8},{14,10},{1,5},{3,7},... | collective-permute-start | bytes 1572872 | tf_op jit(solution)/shard_map/ppermute | solution.py:37
  112.4 11.1 %collective-permute-start.22 = (f32[2,128]{1,0:T(2,128)S(1)}, f32[2,128]{1,0:T(2,128)S(1)}, u32[]{:S(2)}, u32[]{:S(2)}) collective-permute-start(f32[2,128]{1,0:T(2,128)S(1)} %slice.166), channel_id=1, source_target_pairs={{0,4},{2,6},{4,0},{6,2},{8,12},{10,14},{12,8},{14,10},{1,5},{3,7},... | collective-permute-start | bytes 3080 | tf_op jit(solution)/shard_map/ppermute | solution.py:37
  127.3 13.6 %collective-permute-start.20 = (bf16[1,128,1024]{2,1,0:T(8,128)(2,1)S(1)}, bf16[1,128,1024]{2,1,0:T(8,128)(2,1)S(1)}, u32[]{:S(2)}, u32[]{:S(2)}) collective-permute-start(bf16[1,128,1024]{2,1,0:T(8,128)(2,1)S(1)} %get-tuple-element.159), channel_id=1, source_target_pairs={{0,8},{2,10},{4,12},{6,14},{8,0},{10,2},{12,4},{14,6},{1,9},{3,11}... | collective-permute-start | bytes 786440 | tf_op jit(solution)/shard_map/ppermute | solution.py:37
  141.3 15.3 %collective-permute-start.24 = (bf16[1,128,1152]{2,1,0:T(8,128)(2,1)S(1)}, bf16[1,128,1152]{2,1,0:T(8,128)(2,1)S(1)}, u32[]{:S(2)}, u32[]{:S(2)}) collective-permute-start(bf16[1,128,1152]{2,1,0:T(8,128)(2,1)S(1)} %bitcast.90), channel_id=1, source_target_pairs={{0,8},{2,10},{4,12},{6,14},{8,0},{10,2},{12,4},{14,6},{1,9},{3,11}... | collective-permute-start | bytes 884744 | tf_op jit(solution)/shard_map/ppermute | solution.py:37
  156.7 15.3 %collective-permute-start.25 = (bf16[2,128,1152]{2,1,0:T(8,128)(2,1)S(1)}, bf16[2,128,1152]{2,1,0:T(8,128)(2,1)S(1)}, u32[]{:S(2)}, u32[]{:S(2)}) collective-permute-start(bf16[2,128,1152]{2,1,0:T(8,128)(2,1)S(1)} %pad_maximum_fusion.3), channel_id=1, source_target_pairs={{0,4},{2,6},{4,0},{6,2},{8,12},{10,14},{12,8},{14,10},{1,5},{3,7},... | collective-permute-start | bytes 1769480 | tf_op jit(solution)/shard_map/ppermute | solution.py:37
  184.0 8.4 %collective-permute-start.28 = (bf16[2,2,64,512]{3,2,1,0:T(8,128)(2,1)S(1)}, bf16[2,2,64,512]{3,2,1,0:T(8,128)(2,1)S(1)}, u32[]{:S(2)}, u32[]{:S(2)}) collective-permute-start(bf16[2,2,64,512]{3,2,1,0:T(8,128)(2,1)S(1)} %bitcast.103), channel_id=1, source_target_pairs={{0,4},{2,6},{4,0},{6,2},{8,12},{10,14},{12,8},{14,10},{1,5},{3,7},... | collective-permute-start | bytes 786440 | tf_op jit(solution)/shard_map/ppermute | solution.py:37
  192.6 8.2 %collective-permute-start.29 = (bf16[1,2,64,512]{3,2,1,0:T(8,128)(2,1)S(1)}, bf16[1,2,64,512]{3,2,1,0:T(8,128)(2,1)S(1)}, u32[]{:S(2)}, u32[]{:S(2)}) collective-permute-start(bf16[1,2,64,512]{3,2,1,0:T(8,128)(2,1)S(1)} %slice.208), channel_id=1, source_target_pairs={{0,8},{2,10},{4,12},{6,14},{8,0},{10,2},{12,4},{14,6},{1,9},{3,11}... | collective-permute-start | bytes 393224 | tf_op jit(solution)/shard_map/ppermute | solution.py:37
  215.8 13.5 %collective-permute-start.34 = (bf16[4,3,128,128]{3,2,1,0:T(8,128)(2,1)S(1)}, bf16[4,3,128,128]{3,2,1,0:T(8,128)(2,1)S(1)}, u32[]{:S(2)}, u32[]{:S(2)}) collective-permute-start(bf16[4,3,128,128]{3,2,1,0:T(8,128)(2,1)S(1)} %get-tuple-element.113), channel_id=1, source_target_pairs={{0,2},{2,0},{4,6},{6,4},{8,10},{10,8},{12,14},{14,12},{1,3},{3,1},... | collective-permute-start | bytes 1179656 | tf_op jit(solution)/shard_map/ppermute | solution.py:37
  220.1 11.5 %collective-permute-start.36 = (bf16[4,3,128,128]{3,2,1,0:T(8,128)(2,1)S(1)}, bf16[4,3,128,128]{3,2,1,0:T(8,128)(2,1)S(1)}, u32[]{:S(2)}, u32[]{:S(2)}) collective-permute-start(bf16[4,3,128,128]{3,2,1,0:T(8,128)(2,1)S(1)} %get-tuple-element.118), channel_id=1, source_target_pairs={{0,4},{2,6},{4,0},{6,2},{8,12},{10,14},{12,8},{14,10},{1,5},{3,7},... | collective-permute-start | bytes 1179656 | tf_op jit(solution)/shard_map/ppermute | solution.py:37
  221.1 18.1 %collective-permute-start.39 = (bf16[4,64,1024]{2,1,0:T(8,128)(2,1)S(1)}, bf16[4,64,1024]{2,1,0:T(8,128)(2,1)S(1)}, u32[]{:S(2)}, u32[]{:S(2)}) collective-permute-start(bf16[4,64,1024]{2,1,0:T(8,128)(2,1)S(1)} %get-tuple-element.122), channel_id=1, source_target_pairs={{0,2},{2,0},{4,6},{6,4},{8,10},{10,8},{12,14},{14,12},{1,3},{3,1},... | collective-permute-start | bytes 1572872 | tf_op jit(solution)/shard_map/ppermute | solution.py:37
  227.2 42.8 %collective-permute-start.44 = (bf16[4,3,128,128]{3,2,1,0:T(8,128)(2,1)S(1)}, bf16[4,3,128,128]{3,2,1,0:T(8,128)(2,1)S(1)}, u32[]{:S(2)}, u32[]{:S(2)}) collective-permute-start(bf16[4,3,128,128]{3,2,1,0:T(8,128)(2,1)S(1)} %get-tuple-element.138), channel_id=1, source_target_pairs={{0,2},{2,0},{4,6},{6,4},{8,10},{10,8},{12,14},{14,12},{1,3},{3,1},... | collective-permute-start | bytes 1179656 | tf_op jit(solution)/shard_map/ppermute | solution.py:37
  228.7 33.7 %collective-permute-start.42 = (bf16[4,3,128,128]{3,2,1,0:T(8,128)(2,1)S(1)}, bf16[4,3,128,128]{3,2,1,0:T(8,128)(2,1)S(1)}, u32[]{:S(2)}, u32[]{:S(2)}) collective-permute-start(bf16[4,3,128,128]{3,2,1,0:T(8,128)(2,1)S(1)} %get-tuple-element.130), channel_id=1, source_target_pairs={{0,2},{2,0},{4,6},{6,4},{8,10},{10,8},{12,14},{14,12},{1,3},{3,1},... | collective-permute-start | bytes 1179656 | tf_op jit(solution)/shard_map/ppermute | solution.py:37
  231.7 26.6 %collective-permute-start.38 = (bf16[2,3,128,128]{3,2,1,0:T(8,128)(2,1)S(1)}, bf16[2,3,128,128]{3,2,1,0:T(8,128)(2,1)S(1)}, u32[]{:S(2)}, u32[]{:S(2)}) collective-permute-start(bf16[2,3,128,128]{3,2,1,0:T(8,128)(2,1)S(1)} %slice.217), channel_id=1, source_target_pairs={{0,2},{2,0},{4,6},{6,4},{8,10},{10,8},{12,14},{14,12},{1,3},{3,1},... | collective-permute-start | bytes 589832 | tf_op jit(solution)/shard_map/ppermute | solution.py:37
  239.2 23.4 %collective-permute-start.37 = (bf16[1,3,128,128]{3,2,1,0:T(8,128)(2,1)S(1)}, bf16[1,3,128,128]{3,2,1,0:T(8,128)(2,1)S(1)}, u32[]{:S(2)}, u32[]{:S(2)}) collective-permute-start(bf16[1,3,128,128]{3,2,1,0:T(8,128)(2,1)S(1)} %slice.215), channel_id=1, source_target_pairs={{0,8},{2,10},{4,12},{6,14},{8,0},{10,2},{12,4},{14,6},{1,9},{3,11}... | collective-permute-start | bytes 294920 | tf_op jit(solution)/shard_map/ppermute | solution.py:37
  258.4 11.6 %collective-permute-start.40 = (bf16[1,3,128,128]{3,2,1,0:T(8,128)(2,1)S(1)}, bf16[1,3,128,128]{3,2,1,0:T(8,128)(2,1)S(1)}, u32[]{:S(2)}, u32[]{:S(2)}) collective-permute-start(bf16[1,3,128,128]{3,2,1,0:T(8,128)(2,1)S(1)} %slice.219), channel_id=1, source_target_pairs={{0,8},{2,10},{4,12},{6,14},{8,0},{10,2},{12,4},{14,6},{1,9},{3,11}... | collective-permute-start | bytes 294920 | tf_op jit(solution)/shard_map/ppermute | solution.py:37
  259.9 10.1 %collective-permute-start.41 = (bf16[2,64,1024]{2,1,0:T(8,128)(2,1)S(1)}, bf16[2,64,1024]{2,1,0:T(8,128)(2,1)S(1)}, u32[]{:S(2)}, u32[]{:S(2)}) collective-permute-start(bf16[2,64,1024]{2,1,0:T(8,128)(2,1)S(1)} %slice.221), channel_id=1, source_target_pairs={{0,4},{2,6},{4,0},{6,2},{8,12},{10,14},{12,8},{14,10},{1,5},{3,7},... | collective-permute-start | bytes 786440 | tf_op jit(solution)/shard_map/ppermute | solution.py:37
  262.5 11.1 %collective-permute-start.43 = (bf16[2,3,128,128]{3,2,1,0:T(8,128)(2,1)S(1)}, bf16[2,3,128,128]{3,2,1,0:T(8,128)(2,1)S(1)}, u32[]{:S(2)}, u32[]{:S(2)}) collective-permute-start(bf16[2,3,128,128]{3,2,1,0:T(8,128)(2,1)S(1)} %slice.223), channel_id=1, source_target_pairs={{0,4},{2,6},{4,0},{6,2},{8,12},{10,14},{12,8},{14,10},{1,5},{3,7},... | collective-permute-start | bytes 589832 | tf_op jit(solution)/shard_map/ppermute | solution.py:37
  270.0 8.9 %collective-permute-start.48 = (bf16[1,64,1024]{2,1,0:T(8,128)(2,1)S(1)}, bf16[1,64,1024]{2,1,0:T(8,128)(2,1)S(1)}, u32[]{:S(2)}, u32[]{:S(2)}) collective-permute-start(bf16[1,64,1024]{2,1,0:T(8,128)(2,1)S(1)} %slice.231), channel_id=1, source_target_pairs={{0,8},{2,10},{4,12},{6,14},{8,0},{10,2},{12,4},{14,6},{1,9},{3,11}... | collective-permute-start | bytes 393224 | tf_op jit(solution)/shard_map/ppermute | solution.py:37
  273.7 9.0 %collective-permute-start.45 = (bf16[1,3,128,128]{3,2,1,0:T(8,128)(2,1)S(1)}, bf16[1,3,128,128]{3,2,1,0:T(8,128)(2,1)S(1)}, u32[]{:S(2)}, u32[]{:S(2)}) collective-permute-start(bf16[1,3,128,128]{3,2,1,0:T(8,128)(2,1)S(1)} %slice.225), channel_id=1, source_target_pairs={{0,8},{2,10},{4,12},{6,14},{8,0},{10,2},{12,4},{14,6},{1,9},{3,11}... | collective-permute-start | bytes 294920 | tf_op jit(solution)/shard_map/ppermute | solution.py:37
  (33 other events, 398.0 us)

commit v5 on v4

--- a/solution.py
+++ b/solution.py
@@ -83,26 +83,40 @@
     return total[0]
 
 
-def scatter_last(blocks, masks):
-    low = blocks.astype(BF)
-    for i, mask in enumerate(masks):
-        half = low.shape[0] // 2
-        got = swap_tm(low[half:], mask)
-        if i + 1 == len(masks):
-            return low[0], got[0]
-        low = (low[:half].astype(F32) + got.astype(F32)).astype(BF)
-
-
-def scatter_chunks(chunks):
+def in_turn(got, last):
+    return got if last is None else lax.optimization_barrier((got, last))[0]
+
+
+def scatter_last(parts, masks):
+    lows, pairs, last = list(parts), [], None
+    for mask in masks:
+        for i, low in enumerate(lows):
+            half = low.shape[0] // 2
+            got = in_turn(swap_tm(low[half:], mask), last)
+            if mask == masks[-1]:
+                pairs.append((low[0], got[0]))
+                last = got
+                continue
+            lows[i] = last = (low[:half].astype(F32) + got.astype(F32)).astype(BF)
+    return pairs
+
+
+def gather_parts(parts, masks):
+    parts, last = [part[None] for part in parts], None
+    for mask in reversed(masks):
+        for i, part in enumerate(parts):
+            got = in_turn(swap_tm(part, mask), last)
+            parts[i] = last = jnp.concatenate([part, got], axis=0)
+    return parts
+
+
+def scatter_chunks(chunks, steps):
     sums = [lower for lower, _, _ in chunks]
     sends = [upper for _, upper, _ in chunks]
-    stages = len(chunks[0][2])
-    steps = [(i + 1.5 * t, -t, i) for i in range(len(chunks)) for t in range(stages)]
-    last = None
-    for _, t, i in sorted(steps):
-        got = swap_tm(sends[i], chunks[i][2][-t])
-        if last is not None:
-            got, _ = lax.optimization_barrier((got, last))
+    stage, last = [0] * len(chunks), None
+    for i in steps:
+        got = in_turn(swap_tm(sends[i], chunks[i][2][stage[i]]), last)
+        stage[i] += 1
         total = sums[i].astype(F32) + got.astype(F32)
         if total.shape[0] == 1:
             sums[i] = total[0]
@@ -117,8 +131,9 @@
     return lax.broadcasted_iota(jnp.int32, shape, 1) // HEAD == head
 
 
-def forward_kernel(at, x_ref, wq_ref, wk_ref, wv_ref, wo_ref, normed, qkv, probs, pooled, out, attn):
-    shift, border = at[0], at[1]
+def forward_kernel(at, x_ref, wq_ref, wk_ref, wv_ref, wo_ref, *refs):
+    normed, qkv, probs, pooled, own_near, own_far, tail_near, tail_far, attn, out = refs
+    shift, border, core = at[0], at[1], at[3]
     rows = x_ref.shape[0]
     cols = wq_ref.shape[0]
 
@@ -168,6 +183,16 @@
     pooled[...] = low
     out[...] += dot(low, wo_ref[...])
 
+    @pl.when(pl.program_id(0) == pl.num_programs(0) - 1)
+    def _():
+        count, half = own_near.shape
+        near = pl.ds(pl.multiple_of(core * half, half), half)
+        far = pl.ds(pl.multiple_of((1 - core) * half, half), half)
+        own_near[...] = out[:count, near]
+        own_far[...] = out[:count, far].astype(BF)
+        tail_near[...] = out[count:, near].astype(BF)
+        tail_far[...] = out[count:, far].astype(BF)
+
 
 def encoder_forward(x_roll, w_t, weight_out, at, ext_tok):
     rows, width = x_roll.shape
@@ -176,6 +201,8 @@
     pairs = heads_w // cols
     windows = rows // WINDOW
     weight = lambda i: pl.BlockSpec((cols, width), lambda p, at: (i * pairs + p, 0))
+    own_tok = rows // POOL
+    piece = lambda count: pl.BlockSpec((count, width // 2), lambda p, at: (0, 0))
     return pl.pallas_call(
         forward_kernel,
         grid_spec=pltpu.PrefetchScalarGridSpec(
@@ -193,16 +220,22 @@
                 pl.BlockSpec((3, rows, cols), lambda p, at: (0, 0, p)),
                 pl.BlockSpec((1, windows, 2, WINDOW, WINDOW), lambda p, at: (p, 0, 0, 0, 0)),
                 pl.BlockSpec((ext_tok, cols), lambda p, at: (0, p)),
-                pl.BlockSpec((ext_tok, width), lambda p, at: (0, 0)),
+                piece(own_tok),
+                piece(own_tok),
+                piece(ext_tok - own_tok),
+                piece(ext_tok - own_tok),
             ],
-            scratch_shapes=[pltpu.VMEM((rows, cols), BF)],
+            scratch_shapes=[pltpu.VMEM((rows, cols), BF), pltpu.VMEM((ext_tok, width), F32)],
         ),
         out_shape=[
             pltpu.HBM((rows, width), BF),
             pltpu.HBM((3, rows, heads_w), BF),
             pltpu.HBM((pairs, windows, 2, WINDOW, WINDOW), BF),
             pltpu.HBM((ext_tok, heads_w), BF),
-            jax.ShapeDtypeStruct((ext_tok, width), F32),
+            jax.ShapeDtypeStruct((own_tok, width // 2), F32),
+            jax.ShapeDtypeStruct((own_tok, width // 2), BF),
+            jax.ShapeDtypeStruct((ext_tok - own_tok, width // 2), BF),
+            jax.ShapeDtypeStruct((ext_tok - own_tok, width // 2), BF),
         ],
         compiler_params=pltpu.CompilerParams(vmem_limit_bytes=VMEM_LIMIT),
         name="encoder_forward",
@@ -321,74 +354,67 @@
 def column_starts(order, at, block):
     if order is None:
         return None
-    me, group = at[2], at[4]
-    part = len(order) // 2
-    across = [
-        jnp.where(group == q, order[i], order[part + i]) | SPLIT
-        for q in range(2)
-        for i in range(part)
-    ]
-    return [pl.multiple_of((me ^ k) * block, block) for k in order + across]
-
-
-def weight_rows(order, here, got, other, bit):
-    flat = lambda w: w.reshape(-1, w.shape[-1])
-    across = bit if order is None else 1 - bit
-    parts = [flat(here[:, bit]), flat(got[:, across]), flat(other[:, across])]
-    return jnp.concatenate(parts, axis=0)
-
-
-def lift_kernel(table, order, at, ta, tb, here, got, other, gain, kva, kvb, lifted, send, keep, tok):
+    offset = [k | bit for bit in (0, SPLIT) for k in order]
+    return [pl.multiple_of((at[2] ^ k) * block, block) for k in offset]
+
+
+def weight_rows(here, there):
+    return jnp.concatenate([w[...].reshape(-1, w.shape[-1]) for w in (here, there)], axis=0)
+
+
+def both(index, size):
+    return (
+        pl.ds(pl.multiple_of(index * size, size), size),
+        pl.ds(pl.multiple_of((1 - index) * size, size), size),
+    )
+
+
+def lift_kernel(table, order, at, ta, tb, here, there, gain, kva, kvb, *refs):
+    lifted, send, keep, tok, low = refs
     core, group = at[3], at[4]
-    half = ta.shape[1]
-    feats = kva.shape[0]
-    cols = send.shape[1]
-    rows_all = ta.shape[0]
-    near = pl.ds(pl.multiple_of(core * half, half), half)
-    far = pl.ds(pl.multiple_of((1 - core) * half, half), half)
-    piece = rows_all // len(table) if table else 0
+    feats, cols = kva.shape[0], send.shape[1]
+    near, far = both(core, ta.shape[1])
+    mine, across = both(at[2] % 2, feats)
+    piece = ta.shape[0] // len(table) if table else 0
     for source_row, owner_row in table:
         tok[owner_row : owner_row + piece, near] = ta[source_row : source_row + piece]
         tok[owner_row : owner_row + piece, far] = tb[source_row : source_row + piece]
     if not table:
         tok[:, near] = ta[...]
         tok[:, far] = tb[...]
-    block = here.shape[2]
+    block = here.shape[1]
     starts = column_starts(order, at, block)
-    for rows in chunks_of(rows_all):
+    weight = weight_rows(here, there)
+    for rows in chunks_of(tok.shape[0]):
         x = tok[rows]
         if starts:
             x = jnp.concatenate([tok[rows, pl.ds(start, block)] for start in starts], axis=1)
-        lows = []
-        for bit in range(2):
-            span = slice(bit * feats, (bit + 1) * feats)
-            weight = weight_rows(order, here, got, other, bit)
-            product = dot(x, weight)
-            lifted[rows, span] = product
-            lows.append((product * gain[:, span]).astype(BF))
+        product = dot(x, weight)
+        lifted[rows] = product
+        low[rows] = (product * gain[...]).astype(BF)
         for ref, side in ((send, 1 - core), (keep, core)):
             span = pl.ds(pl.multiple_of(side * cols, cols), cols)
-            part = dot(lows[0], kva[:, span]) + dot(lows[1], kvb[side ^ group])
+            part = dot(low[rows, mine], kva[:, span]) + dot(low[rows, across], kvb[side ^ group])
             ref[rows] = part.astype(BF)
 
 
-def lift(table, order, at, ta, tb, here, got, other, gain, kva, kvb):
+def lift(table, order, at, ta, tb, here, there, gain, kva, kvb):
     rows, half = ta.shape
     feats, cols = kva.shape[0], kva.shape[1] // 2
     whole = pl.BlockSpec(memory_space=pltpu.VMEM)
     return pl.pallas_call(
         functools.partial(lift_kernel, table, order),
-        in_specs=[pl.BlockSpec(memory_space=pltpu.SMEM)] + [whole] * 8,
+        in_specs=[pl.BlockSpec(memory_space=pltpu.SMEM)] + [whole] * 7,
         out_specs=[whole] * 3,
         out_shape=[
             jax.ShapeDtypeStruct((rows, 2 * feats), F32),
             jax.ShapeDtypeStruct((rows, cols), BF),
             jax.ShapeDtypeStruct((rows, cols), BF),
         ],
-        scratch_shapes=[pltpu.VMEM((rows, 2 * half), BF)],
+        scratch_shapes=[pltpu.VMEM((rows, 2 * half), BF), pltpu.VMEM((rows, 2 * feats), BF)],
         compiler_params=pltpu.CompilerParams(vmem_limit_bytes=VMEM_LIMIT),
         name="lift",
-    )(at, ta, tb, here, got, other, gain, kva, kvb)
+    )(at, ta, tb, here, there, gain, kva, kvb)
 
 
 def two_parts(column):
@@ -396,8 +422,9 @@
     return high, (column - high.astype(F32)).astype(BF)
 
 
-def finish_kernel(mine, got, squares, d_kv, kv, load):
-    rows, cols = kv.shape
+def finish_kernel(mine, got, squares, d_kv, *refs):
+    rows, cols = mine.shape
+    kv, load, inner = refs[-3:]
     total = mine[...].astype(F32) + got[...].astype(F32)
     mean = jnp.broadcast_to(squares[...], (rows, rows)).T[:, :1] * (1.0 / LLM_D)
     inv = lax.rsqrt(mean + 1e-05)
@@ -405,60 +432,67 @@
     kv[...] = low
     cot = (low.astype(F32) + d_kv[...].astype(F32)).astype(BF)
     load[:, :cols] = cot
-    inner = jnp.sum(cot.astype(F32) * total, axis=1, keepdims=True)
-    lane = lax.broadcasted_iota(jnp.int32, (rows, load.shape[1] - cols), 1)
-    extra = jnp.zeros(lane.shape, F32)
-    for i, part in enumerate(two_parts(inv) + two_parts(inner)):
-        extra = jnp.where(lane == i, part.astype(F32), extra)
-    load[:, cols:] = extra.astype(BF)
-
-
-def finish(mine, got, squares, d_kv):
+    pull = jnp.sum(cot.astype(F32) * total, axis=1, keepdims=True)
+    if len(refs) == 4:
+        pull += refs[0][...]
+        lane = lax.broadcasted_iota(jnp.int32, (rows, load.shape[1] - cols), 1)
+        extra = jnp.zeros(lane.shape, F32)
+        for i, part in enumerate(two_parts(inv) + two_parts(pull)):
+            extra = jnp.where(lane == i, part.astype(F32), extra)
+        load[:, cols:] = extra.astype(BF)
+    inner[...] = pull
+
+
+def finish(mine, got, squares, d_kv, *inner):
     rows, cols = mine.shape
     return pl.pallas_call(
         finish_kernel,
         out_shape=[
             jax.ShapeDtypeStruct((rows, cols), BF),
-            jax.ShapeDtypeStruct((rows, cols + LANES), BF),
+            jax.ShapeDtypeStruct((rows, cols + LANES * len(inner)), BF),
+            jax.ShapeDtypeStruct((rows, 1), F32),
         ],
         compiler_params=pltpu.CompilerParams(vmem_limit_bytes=VMEM_LIMIT),
         name="finish",
-    )(mine, got, squares, d_kv)
-
-
-def lower_kernel(table, order, at, ca, cb, here, got, other, gain, kva, kvb, lifted, send, keep, nat):
+    )(mine, got, squares, d_kv, *inner)
+
+
+def lower_kernel(table, order, at, ca0, ca1, cb0, cb1, here, there, gain, kva, kvb, *refs):
+    lifted, send, keep, nat, low = refs
     core, group = at[3], at[4]
-    half = send.shape[1]
-    feats = kva.shape[0]
+    feats, half = kva.shape[0], send.shape[1]
     cols = kva.shape[1] // 2
-    block = here.shape[2]
+    near, far = both(core, half)
+    mine, across = both(at[2] % 2, feats)
+    block = here.shape[1]
     starts = column_starts(order, at, block)
-    near = pl.ds(pl.multiple_of(core * half, half), half)
-    far = pl.ds(pl.multiple_of((1 - core) * half, half), half)
-    piece = ca.shape[0] // len(table) if table else 0
-    for rows in chunks_of(ca.shape[0]):
-        extra = ca[rows, cols:].astype(F32)
-        extra_b = cb[rows, cols:].astype(F32)
+    weight = weight_rows(here, there)
+    part_cols = ca0.shape[1]
+    piece = ca0.shape[0] // len(table) if table else 0
+    for rows in chunks_of(ca0.shape[0]):
+        extra = ca1[rows, part_cols:].astype(F32)
+        extra_b = cb1[rows, part_cols:].astype(F32)
         inv = extra[:, 0:1] + extra[:, 1:2]
         inner = extra[:, 2:3] + extra[:, 3:4] + extra_b[:, 2:3] + extra_b[:, 3:4]
         pull = inv * inv * inv * inner * (1.0 / LLM_D)
-        cots = ((ca[rows, :cols], core), (cb[rows, :cols], 1 - core))
-        d_tok = None
-        for bit in range(2):
+        cots = [
+            (jnp.concatenate([c0[rows], c1[rows, :part_cols]], axis=1), side)
+            for c0, c1, side in ((ca0, ca1, core), (cb0, cb1, 1 - core))
+        ]
+        for is_mine, span in ((True, mine), (False, across)):
             d_normed = None
             for cot, side in cots:
-                span = pl.ds(pl.multiple_of(side * cols, cols), cols)
-                part = dot_nt(cot, kvb[side ^ group] if bit else kva[:, span])
+                at_side = pl.ds(pl.multiple_of(side * cols, cols), cols)
+                part = dot_nt(cot, kva[:, at_side] if is_mine else kvb[side ^ group])
                 d_normed = part if d_normed is None else d_normed + part
-            span = slice(bit * feats, (bit + 1) * feats)
-            low = (inv * gain[:, span] * d_normed - lifted[rows, span] * pull).astype(BF)
-            weight = weight_rows(order, here, got, other, bit)
-            part = dot_nt(low, weight)
-            d_tok = part if d_tok is None else d_tok + part
+            low[rows, span] = (
+                inv * gain[:, span] * d_normed - lifted[rows, span] * pull
+            ).astype(BF)
+        d_tok = dot_nt(low[rows], weight).astype(BF)
         if not starts:
-            nat[rows] = d_tok.astype(BF)
+            nat[rows] = d_tok
         for i, start in enumerate(starts or ()):
-            nat[rows, pl.ds(start, block)] = d_tok[:, i * block : (i + 1) * block].astype(BF)
+            nat[rows, pl.ds(start, block)] = d_tok[:, i * block : (i + 1) * block]
     for source_row, owner_row in table:
         send[source_row : source_row + piece] = nat[owner_row : owner_row + piece, far]
         keep[source_row : source_row + piece] = nat[owner_row : owner_row + piece, near]
@@ -467,20 +501,20 @@
         keep[...] = nat[:, near]
 
 
-def lower(table, order, at, ca, cb, here, got, other, gain, kva, kvb, lifted):
-    rows = ca.shape[0]
-    width = 2 * here.shape[0] * here.shape[2]
+def lower(table, order, at, cots, here, there, gain, kva, kvb, lifted):
+    rows, width = cots[0].shape[0], lifted.shape[1]
+    tok_width = 2 * here.shape[0] * here.shape[1]
     whole = pl.BlockSpec(memory_space=pltpu.VMEM)
-    out = jax.ShapeDtypeStruct((rows, width // 2), BF)
+    out = jax.ShapeDtypeStruct((rows, tok_width // 2), BF)
     return pl.pallas_call(
         functools.partial(lower_kernel, table, order),
-        in_specs=[pl.BlockSpec(memory_space=pltpu.SMEM)] + [whole] * 9,
+        in_specs=[pl.BlockSpec(memory_space=pltpu.SMEM)] + [whole] * 10,
         out_specs=[whole] * 2,
         out_shape=[out] * 2,
-        scratch_shapes=[pltpu.VMEM((rows, width), BF)],
+        scratch_shapes=[pltpu.VMEM((rows, tok_width), BF), pltpu.VMEM((rows, width), BF)],
         compiler_params=pltpu.CompilerParams(vmem_limit_bytes=VMEM_LIMIT),
         name="lower",
-    )(at, ca, cb, here, got, other, gain, kva, kvb, lifted)
+    )(at, *cots, here, there, gain, kva, kvb, lifted)
 
 
 def on_device(frames, weight_qkv, weight_out, proj_in, norm_gain, proj_kv, shifts, route, d_kv):
@@ -505,8 +539,7 @@
     if not two_groups:
         group = group * 0
     proj_kv, part = lax.optimization_barrier((proj_kv, part))
-    kv_cut = lax.dynamic_slice_in_dim(proj_kv, group * kv_half, kv_half, 1)
-    kv_near = [swap_tm(part, SPLIT) for part in jnp.split(kv_cut, 2)]
+    kv_near = swap_tm(lax.dynamic_slice_in_dim(proj_kv, group * kv_half, kv_half, 1), SPLIT)
     proj_in, w_t = lax.optimization_barrier((proj_in, w_t))
 
     masks = group_bits()
@@ -515,11 +548,7 @@
     count = n // 2
     blocks = []
     for k in order:
-        pair = [
-            lax.dynamic_slice_in_dim(proj_in, (me ^ k ^ bit) * feats, feats, 1)
-            for bit in (0, SPLIT)
-        ]
-        pair = jnp.stack(pair)
+        pair = lax.dynamic_slice_in_dim(proj_in, (me ^ k) // 2 * 2 * feats, 2 * feats, 1)
         blocks.append(swap_tm(pair, k) if k else pair)
 
     other = swap_mp(mine)
@@ -528,34 +557,22 @@
     )
     x_roll = lax.dynamic_slice_in_dim(jnp.concatenate([frames, halo], 0), shift, rows, 0)
 
+    at = jnp.stack([shift, rows * n - shift - me * rows, me, core, group]).astype(jnp.int32)
+    normed, qkv, probs, pooled_attn, own_near, own_far, tail_near, tail_far = encoder_forward(
+        x_roll, w_t, weight_out, at, ext_tok
+    )
+    own_far, kv_near = lax.optimization_barrier((own_far, kv_near))
     swap_groups = lambda block: lax.ppermute(block, "groups", [(0, 1), (1, 0)])
-    x_roll, kv_near[0] = lax.optimization_barrier((x_roll, kv_near[0]))
-    kv_far = [swap_groups(kv_near[0])] if two_groups else []
-    at = jnp.stack([shift, rows * n - shift - me * rows, me, core, group]).astype(jnp.int32)
-    normed, qkv, probs, pooled_attn, out_part = encoder_forward(
-        x_roll, w_t, weight_out, at, ext_tok
-    )
-    out_part, kv_near, blocks, kv_far = lax.optimization_barrier(
-        (out_part, kv_near, blocks, kv_far)
-    )
     if two_groups:
-        kv_far.append(swap_groups(kv_near[1]))
+        kv_far = swap_groups(kv_near)
     else:
-        kv_far.append(swap_tm(proj_kv[:, kv_half:], SPLIT))
-    here = jnp.stack(blocks)
-    in_near = swap_tm(
-        lax.dynamic_slice_in_dim(here, group * (count // 2), count // 2, 0), SPLIT
-    )
+        kv_far = swap_tm(proj_kv[:, kv_half:], SPLIT)
     turned = normed.T
     route, norm_gain, d_kv, pooled_attn = lax.optimization_barrier(
         (route, norm_gain, d_kv, pooled_attn)
     )
-    gain = jnp.concatenate(
-        [
-            lax.dynamic_slice_in_dim(norm_gain, (me ^ bit) * feats, feats, 0)
-            for bit in (0, SPLIT)
-        ]
-    ).reshape(1, -1)
+    gain = lax.dynamic_slice_in_dim(norm_gain, me // 2 * 2 * feats, 2 * feats, 0)
+    gain = gain.reshape(1, -1)
     owner_at = (lax.dynamic_index_in_dim(route, me, 0, keepdims=False) ^ me)[None, :]
     sort = owner_at == jnp.array(members, jnp.int32)[:, None]
     sort = jnp.kron(sort.astype(BF), jnp.eye(piece, dtype=BF))
@@ -566,41 +583,42 @@
     spread = jnp.kron(spread.astype(BF), jnp.eye(piece, dtype=BF))
     d_kv = dot_tn(spread, d_kv).astype(BF)
 
-    out_low = out_part.astype(BF)
-    low_own = lax.dynamic_slice_in_dim(out_low, core * half_w, half_w, 1)
-    low_other = lax.dynamic_slice_in_dim(out_low, (1 - core) * half_w, half_w, 1)
-    from_core = swap_mp(low_other[:own_tok])
-    tail_a = to_tm(low_own[own_tok:], 1, False)
-    tail_b = to_tm(low_other[own_tok:], 1, True)
+    from_core = swap_mp(own_far)
+    tail_a = to_tm(tail_near, 1, False)
+    tail_b = to_tm(tail_far, 1, True)
+    tail_a, tail_b, from_core, blocks = lax.optimization_barrier(
+        (tail_a, tail_b, from_core, blocks)
+    )
     own_pool = (
         jnp.arange(rows, dtype=jnp.int32)[None, :] // POOL
         == jnp.arange(own_tok, dtype=jnp.int32)[:, None]
     ).astype(BF) * (1.0 / POOL)
     x_mean = dot(own_pool, lax.dynamic_slice_in_dim(frames, core * half_w, half_w, 1))
-    pooled = (
-        x_mean
-        + lax.dynamic_slice_in_dim(out_part, core * half_w, half_w, 1)[:own_tok]
-        + from_core.astype(F32)
-    )
+    pooled = x_mean + own_near + from_core.astype(F32)
     tail = tail_a.astype(F32) + tail_b.astype(F32)
     pooled = jnp.concatenate([pooled[:tail_tok] + tail, pooled[tail_tok:]], 0).astype(BF)
 
     sorted_tok = dot(sort, pooled).astype(BF).reshape(2, count * piece, half_w)
-    pair_tok = jnp.stack([sorted_tok[0], swap_tm(sorted_tok[1], SPLIT)])
-    pair_tok, in_near, kv_far = lax.optimization_barrier((pair_tok, in_near, kv_far))
-    tok_half = gather_doubling(pair_tok, masks).reshape(-1, half_w)
-    in_far = swap_groups(in_near) if two_groups else swap_tm(here[count // 2 :], SPLIT)
-    kva = proj_kv
-    kvb = jnp.stack([jnp.concatenate(kv_near), jnp.concatenate(kv_far)])
+    handed = swap_tm(sorted_tok[1], SPLIT)
+    here = jnp.stack(blocks)
+    handed, here = lax.optimization_barrier((handed, here))
+    there = swap_tm(here, SPLIT)
+    pair_tok = jnp.stack([sorted_tok[0], handed])
+    tok_half = gather_doubling(pair_tok, masks[-1:])
+    tok_half, kv_far = lax.optimization_barrier((tok_half, kv_far))
+    kva, kvb = proj_kv, jnp.stack([kv_near, kv_far])
     at_rows = order
     if width // n % LANES:
-        stacked = jnp.concatenate([here, in_near[:, ::-1], in_far[:, ::-1]])
+        stacked = jnp.concatenate([here, there])
         source = jnp.arange(n, dtype=jnp.int32) ^ me
         found = source[:, None] == jnp.array(members, jnp.int32)[None, :]
         place = jnp.sum(found * jnp.arange(n, dtype=jnp.int32)[None, :], axis=1)
         stacked = jnp.take(stacked, place, axis=0)
-        here, in_near, in_far = jnp.split(stacked, [count, count + count // 2])
+        here, there = jnp.split(stacked, 2)
         at_rows = None
+    for mask in reversed(masks[:-1]):
+        tok_half = jnp.concatenate([tok_half, swap_tm(tok_half, mask)], axis=0)
+    tok_half = tok_half.reshape(-1, half_w)
     tok_other = swap_mp(tok_half)
     table = list(moves(order, piece))
     source_rows = np.concatenate([np.arange(r, r + piece) for r, _ in table])
@@ -611,19 +629,24 @@
         tok_half, tok_other = tok_half[at_owner], tok_other[at_owner]
         table = []
     lifted, kv_send, kv_keep = lift(
-        table, at_rows, at, tok_half, tok_other, here, in_near, in_far, gain, kva, kvb
+        table, at_rows, at, tok_half, tok_other, here, there, gain, kva, kvb
     )
     squares = jnp.sum(lifted * lifted, axis=-1).reshape(count, own_tok)
     square_sum = scatter_halving(squares + swap_mp(squares), masks, F32)
-    kv_part = kv_keep.astype(F32) + swap_mp(kv_send).astype(F32)
+    kv_part = (kv_keep.astype(F32) + swap_mp(kv_send).astype(F32)).astype(BF)
     kv_part, turned = lax.optimization_barrier((kv_part, turned))
-    kv_mine, kv_got = scatter_last(kv_part.reshape(count, own_tok, kv_half), masks)
-    kv_low, load = finish(kv_mine, kv_got, square_sum.reshape(1, own_tok), d_kv)
-    kv = dot(spread, kv_low).astype(BF)
-    cot_half = gather_doubling(load, masks).reshape(count * own_tok, -1)
-    cot_other = swap_mp(cot_half)
+    kv_parts = jnp.split(kv_part.reshape(count, own_tok, kv_half), 2, axis=2)
+    (mine_a, got_a), (mine_b, got_b) = scatter_last(kv_parts, masks)
+    square_sum = square_sum.reshape(1, own_tok)
+    d_kv_a, d_kv_b = jnp.split(d_kv, 2, axis=1)
+    kv_a, load_a, inner = finish(mine_a, got_a, square_sum, d_kv_a)
+    kv_b, load_b, _ = finish(mine_b, got_b, square_sum, d_kv_b, inner)
+    kv = dot(spread, jnp.concatenate([kv_a, kv_b], axis=1)).astype(BF)
+    loads = gather_parts([load_a, load_b], masks)
+    loads = [load.reshape(count * own_tok, -1) for load in loads]
+    cots = loads + [swap_mp(load) for load in loads]
     d_send, d_keep = lower(
-        table, at_rows, at, cot_half, cot_other, here, in_near, in_far, gain, kva, kvb, lifted
+        table, at_rows, at, cots, here, there, gain, kva, kvb, lifted
     )
     if by_xla:
         at_source = owner_rows[np.argsort(source_rows)]
@@ -645,13 +668,16 @@
     crossed = [bits[1], bits[0]] + bits[2:]
     d_attn, out_even, out_odd = out_grad(d_ext, weight_out, pooled_attn, at, bits)
     chunks = []
-    for pair, path in enumerate((bits, crossed, bits, bits)):
+    for pair, path in enumerate((bits, bits, bits, crossed)):
         even, odd = encoder_backward(turned, qkv, probs, d_attn, at, path, pair, 1)
         even, odd, at = lax.optimization_barrier((even, odd, at))
         chunks.append((even, odd, path))
-    chunks.insert(2, (out_even, out_odd, bits))
-    chunks = scatter_chunks(chunks)
-    grad_out = chunks.pop(2)
+    chunks.append((out_even, out_odd, bits))
+    steps = list(range(len(chunks))) * len(bits)
+    if len(bits) == 3:
+        steps = [0, 0, 1, 3, 0, 1, 4, 1, 4, 2, 3, 4, 2, 3, 2]
+    chunks = scatter_chunks(chunks, steps)
+    grad_out = chunks.pop()
     grad_qkv = jnp.transpose(jnp.concatenate(chunks, axis=-1), (1, 0, 2))
     return kv, grad_qkv, grad_out
 

time: 291 us -> 262 us (0.900)
  waiting for transfers between devices: 155 us -> 133 us
  other arithmetic: 22.6 us -> 16.5 us
    ppermute x33 -> x36, waiting for transfers between devices: 143 us -> 113 us  [swap_tm(): return lax.ppermute(block, 'tm', [(i, i ^ mask) for i in range(n)])]
    another operation x10 -> x3, other arithmetic: 8.99 us -> 2.83 us  [the longest x1 2.78 us: on_device(): kva, kvb = (proj_kv, jnp.stack([kv_near, kv_far]))]
    ppermute x5, waiting for transfers between devices: 2.47 us -> 8.13 us  [to_tm(): return lax.ppermute(block, ('tm', 'mp'), pairs)]
    ppermute x3 -> x1, waiting for transfers between devices: 2.4 us -> 7.64 us  [on_device(): swap_groups = lambda block: lax.ppermute(block, 'groups', [(0, 1), (1, 0)])]
    dynamic_slice x2 -> x3, local copies, waits for them, and re-layouts: 0.89 us -> 5.15 us  [the longest x1 2.27 us: on_device(): lax.dynamic_slice_in_dim(proj_kv, group * kv_half, kv_half, 1)]
    ppermute x8 -> x9, waiting for transfers between devices: 7.26 us -> 4.13 us  [swap_mp(): return lax.ppermute(block, 'mp', [(i, n - 1 - i) for i in range(n)])]
    ppermute x33 -> x36, starting transfers between devices: 36.5 us -> 36.3 us  [swap_tm(): return lax.ppermute(block, 'tm', [(i, i ^ mask) for i in range(n)])]
  transfers between devices with their start and end apart: 49 -> 51, of which waited for: 27 -> 28; matrix products, arithmetic and copies ran while one was open for 11% -> 12% of each run, Pallas kernels for 6% -> 8%
where the time goes in v5:
time: 262 us
  waiting for transfers between devices  133 us (51%)
  starting transfers between devices  50.2 us (19%)
  Pallas kernels  37.8 us (14%)
  other arithmetic  16.5 us (6%)
  local copies, waits for them, and re-layouts  16.3 us (6%)
  between operations  4.06 us (2%)
  matrix products  3.6 us (1%)
    ppermute x36, waiting for transfers between devices, swap_tm(): return lax.ppermute(block, 'tm', [(i, i ^ mask) for i in range(n)])  113 us
    ppermute x36, starting transfers between devices, swap_tm(): return lax.ppermute(block, 'tm', [(i, i ^ mask) for i in range(n)])  36.3 us
    pallas_call x4, Pallas kernels, encoder_backward(): pl.pallas_call(functools.partial(backward_kernel, masks), grid_spec=pltpu...  11 us
    pallas_call x1, Pallas kernels, encoder_forward(): pl.pallas_call(forward_kernel, grid_spec=pltpu.PrefetchScalarGridSpec(num...  11 us
    ppermute x5, starting transfers between devices, to_tm(): return lax.ppermute(block, ('tm', 'mp'), pairs)  10.7 us
    ppermute x5, waiting for transfers between devices, to_tm(): return lax.ppermute(block, ('tm', 'mp'), pairs)  8.13 us
    ppermute x1, waiting for transfers between devices, on_device(): swap_groups = lambda block: lax.ppermute(block, 'groups', [(0, 1), (1, 0)])  7.64 us
    pallas_call x1, Pallas kernels, lower(): pl.pallas_call(functools.partial(lower_kernel, table, order), in_specs=[p...  6.88 us
  transfers between devices with their start and end apart: 51, of which 28 were waited for; matrix products, arithmetic and copies ran while one was open for 12% of the time, Pallas kernels for 8%

profile of v5, /device:TPU:0, one launch (start us, length us, event | category | flops | bytes accessed | tf_op | source)
XLA Modules:
  0.0 261.6 jit_solution(13807900532482312022)
XLA Ops:
  2.4 6.0 %collective-permute-start = (bf16[128,1024]{1,0:T(8,128)(2,1)}, bf16[128,1024]{1,0:T(8,128)(2,1)}, u32[]{:S(2)}, u32[]{:S(2)}) collective-permute-start(bf16[128,1024]{1,0:T(8,128)(2,1)} %constant_dynamic-slice_fusion.6), channel_id=1, source_target_pairs={{0,14},{1,15},{2,0},{3,1},{4,2},{5,3},{6,4},{7,5},{8,6},{9,7},{10,... | collective-permute-start | bytes 786440 | tf_op jit(solution)/shard_map/ppermute | solution.py:51
  10.6 3.2 %copy.14 = bf16[3,512,1024]{2,1,0:T(8,128)(2,1)S(1)} copy(bf16[3,512,1024]{1,2,0:T(8,128)(2,1)} %bitcast.90) | data formatting | bytes 6291456 | tf_op jit(solution)/shard_map/transpose | solution.py:536
  17.1 3.3 %collective-permute-start.6 = (bf16[128,1024]{1,0:T(8,128)(2,1)}, bf16[128,1024]{1,0:T(8,128)(2,1)}, u32[]{:S(2)}, u32[]{:S(2)}) collective-permute-start(bf16[128,1024]{1,0:T(8,128)(2,1)} %get-tuple-element.171), channel_id=1, source_target_pairs={{0,8},{2,10},{4,12},{6,14},{8,0},{10,2},{12,4},{14,6},{1,9},{3,11}... | collective-permute-start | bytes 786440 | tf_op jit(solution)/shard_map/ppermute | solution.py:37
  27.9 11.0 %encoder_forward.1 = (bf16[512,1024]{1,0:T(8,128)(2,1)}, bf16[3,512,512]{2,1,0:T(8,128)(2,1)}, bf16[4,2,2,256,256]{4,3,2,1,0:T(8,128)(2,1)}, bf16[192,512]{1,0:T...) custom-call(s32[5]{0:T(128)S(1)} %stack.49.at, ...), custom_call_target="tpu_custom_call" | custom-call | tf_op jit(solution)/shard_map/encoder_forward/pallas_call | solution.py:206
  52.6 3.0 %collective-permute-done.9 = bf16[64,512]{1,0:T(8,128)(2,1)S(1)} collective-permute-done((bf16[64,512]{1,0:T(8,128)(2,1)S(1)}, bf16[64,512]{1,0:T(8,128)(2,1)S(1)}, u32[]{:S(2)}, u32[]{:S(2)}) %collective-permute-start.9) | collective-permute-done | bytes 65568 | tf_op jit(solution)/shard_map/ppermute | solution.py:37
  55.9 6.1 %collective-permute-done.10 = bf16[1,2,64,512]{3,2,1,0:T(8,128)(2,1)S(1)} collective-permute-done((bf16[1,2,64,512]{3,2,1,0:T(8,128)(2,1)S(1)}, bf16[1,2,64,512]{3,2,1,0:T(8,128)(2,1)S(1)}, u32[]{:S(2)}, u32[]{:S(2)}) %collective-permute-start.10) | collective-permute-done | bytes 131104 | tf_op jit(solution)/shard_map/ppermute | solution.py:37
  62.0 7.6 %collective-permute-done.11 = bf16[512,1024]{1,0:T(8,128)(2,1)S(1)} collective-permute-done((bf16[512,1024]{1,0:T(8,128)(2,1)}, bf16[512,1024]{1,0:T(8,128)(2,1)S(1)}, u32[]{:S(2)}, u32[]{:S(2)}) %collective-permute-start.11) | collective-permute-done | bytes 1048608 | tf_op jit(solution)/shard_map/ppermute | solution.py:565
  69.7 7.8 %collective-permute-done.12 = bf16[2,2,64,512]{3,2,1,0:T(8,128)(2,1)S(1)} collective-permute-done((bf16[2,2,64,512]{3,2,1,0:T(8,128)(2,1)S(1)}, bf16[2,2,64,512]{3,2,1,0:T(8,128)(2,1)S(1)}, u32[]{:S(2)}, u32[]{:S(2)}) %collective-permute-start.12) | collective-permute-done | bytes 262176 | tf_op jit(solution)/shard_map/ppermute | solution.py:37
  78.3 2.8 %pad_maximum_fusion.kvb = bf16[2,512,1024]{2,1,0:T(8,128)(2,1)} fusion(bf16[1,512,1024]{2,1,0:T(8,128)(2,1)S(1)} %bitcast.92, bf16[1,512,1024]{2,1,0:T(8,128)(2,1)} %bitcast.17), kind=kLoop, calls=%fused_computation | loop fusion | flops 1048576 | bytes 4194304 | tf_op jit(solution)/shard_map/stack | solution.py:609
  81.1 6.0 %lift.1 = (f32[512,1024]{1,0:T(8,128)}, bf16[512,1024]{1,0:T(8,128)(2,1)}, bf16[512,1024]{1,0:T(8,128)(2,1)S(1)}) custom-call(s32[5]{0:T(128)S(1)} %stack.49.at, bf16[512,512]{1,0:T(8,128)(2,1)S(1)} %bitcast.76, bf16[512,512]{1,0:T(8,128)(2,1)S(1)} %collective-permute-done.13.tb, bf16[4,128,1024]{2,1,0:T(8,128)(2,1)S(1)} %pad_maximum_fusion.1.here, ...), custom_call_target="tpu_custom_call" | custom-call | tf_op jit(solution)/shard_map/lift/pallas_call | solution.py:405
  101.8 4.0 %collective-permute-done.16 = bf16[2,128,512]{2,1,0:T(8,128)(2,1)S(1)} collective-permute-done((bf16[2,128,512]{2,1,0:T(8,128)(2,1)S(1)}, bf16[2,128,512]{2,1,0:T(8,128)(2,1)S(1)}, u32[]{:S(2)}, u32[]{:S(2)}) %collective-permute-start.16) | collective-permute-done | bytes 262176 | tf_op jit(solution)/shard_map/ppermute | solution.py:37
  105.9 3.1 %collective-permute-start.17 = (bf16[1,128,512]{2,1,0:T(8,128)(2,1)S(1)}, bf16[1,128,512]{2,1,0:T(8,128)(2,1)S(1)}, u32[]{:S(2)}, u32[]{:S(2)}) collective-permute-start(bf16[1,128,512]{2,1,0:T(8,128)(2,1)S(1)} %get-tuple-element.178), channel_id=1, source_target_pairs={{0,8},{2,10},{4,12},{6,14},{8,0},{10,2},{12,4},{14,6},{1,9},{3,11}... | collective-permute-start | bytes 393224 | tf_op jit(solution)/shard_map/ppermute | solution.py:37
  109.0 4.5 %collective-permute-done.18 = bf16[2,128,512]{2,1,0:T(8,128)(2,1)S(1)} collective-permute-done((bf16[2,128,512]{2,1,0:T(8,128)(2,1)S(1)}, bf16[2,128,512]{2,1,0:T(8,128)(2,1)S(1)}, u32[]{:S(2)}, u32[]{:S(2)}) %collective-permute-start.18) | collective-permute-done | bytes 262176 | tf_op jit(solution)/shard_map/ppermute | solution.py:37
  117.0 7.9 %collective-permute-done.22 = bf16[1,128,512]{2,1,0:T(8,128)(2,1)S(1)} collective-permute-done((bf16[1,128,512]{2,1,0:T(8,128)(2,1)S(1)}, bf16[1,128,512]{2,1,0:T(8,128)(2,1)S(1)}, u32[]{:S(2)}, u32[]{:S(2)}) %collective-permute-start.22) | collective-permute-done | bytes 131104 | tf_op jit(solution)/shard_map/ppermute | solution.py:37
  125.8 3.6 %collective-permute-done.23 = bf16[1,128,512]{2,1,0:T(8,128)(2,1)S(1)} collective-permute-done((bf16[1,128,512]{2,1,0:T(8,128)(2,1)S(1)}, bf16[1,128,512]{2,1,0:T(8,128)(2,1)S(1)}, u32[]{:S(2)}, u32[]{:S(2)}) %collective-permute-start.23) | collective-permute-done | bytes 131104 | tf_op jit(solution)/shard_map/ppermute | solution.py:37
  129.6 5.2 %collective-permute-done.25 = bf16[1,128,640]{2,1,0:T(8,128)(2,1)S(1)} collective-permute-done((bf16[1,128,640]{2,1,0:T(8,128)(2,1)S(1)}, bf16[1,128,640]{2,1,0:T(8,128)(2,1)S(1)}, u32[]{:S(2)}, u32[]{:S(2)}) %collective-permute-start.25) | collective-permute-done | bytes 163872 | tf_op jit(solution)/shard_map/ppermute | solution.py:37
  134.8 5.5 %collective-permute-done.24 = bf16[2,128,512]{2,1,0:T(8,128)(2,1)S(1)} collective-permute-done((bf16[2,128,512]{2,1,0:T(8,128)(2,1)S(1)}, bf16[2,128,512]{2,1,0:T(8,128)(2,1)S(1)}, u32[]{:S(2)}, u32[]{:S(2)}) %collective-permute-start.24) | collective-permute-done | bytes 262176 | tf_op jit(solution)/shard_map/ppermute | solution.py:37
  140.4 6.7 %collective-permute-done.26 = bf16[2,128,640]{2,1,0:T(8,128)(2,1)S(1)} collective-permute-done((bf16[2,128,640]{2,1,0:T(8,128)(2,1)S(1)}, bf16[2,128,640]{2,1,0:T(8,128)(2,1)S(1)}, u32[]{:S(2)}, u32[]{:S(2)}) %collective-permute-start.26) | collective-permute-done | bytes 327712 | tf_op jit(solution)/shard_map/ppermute | solution.py:37
  150.1 6.9 %lower.1 = (bf16[512,512]{1,0:T(8,128)(2,1)S(1)}, bf16[512,512]{1,0:T(8,128)(2,1)S(1)}) custom-call(s32[5]{0:T(128)S(1)} %stack.49.at, bf16[512,512]{1,0:T(8,128)(2,1)S(1)} %bitcast.74, bf16[512,640]{1,0:T(8,128)(2,1)S(1)} %bitcast.72, bf16[512,512]{1,0:T(8,128)(2,1)S(1)} %collective-permute-done.27.cb0, bf16[512,640]{1,0:T(8,128)(2,1)S(1)} %collective-permute-done.28.cb1, ...), custom_call_target="tpu_custom_call" | custom-call | tf_op jit(solution)/shard_map/lower/pallas_call | solution.py:509
  159.3 8.3 %collective-permute-done.30 = bf16[2,2,64,512]{3,2,1,0:T(8,128)(2,1)S(1)} collective-permute-done((bf16[2,2,64,512]{3,2,1,0:T(8,128)(2,1)S(1)}, bf16[2,2,64,512]{3,2,1,0:T(8,128)(2,1)S(1)}, u32[]{:S(2)}, u32[]{:S(2)}) %collective-permute-start.30) | collective-permute-done | bytes 262176 | tf_op jit(solution)/shard_map/ppermute | solution.py:37
  167.8 8.4 %collective-permute-done.31 = bf16[1,2,64,512]{3,2,1,0:T(8,128)(2,1)S(1)} collective-permute-done((bf16[1,2,64,512]{3,2,1,0:T(8,128)(2,1)S(1)}, bf16[1,2,64,512]{3,2,1,0:T(8,128)(2,1)S(1)}, u32[]{:S(2)}, u32[]{:S(2)}) %collective-permute-start.31) | collective-permute-done | bytes 131104 | tf_op jit(solution)/shard_map/ppermute | solution.py:37
  177.2 3.4 %collective-permute-done.32 = bf16[64,512]{1,0:T(8,128)(2,1)S(1)} collective-permute-done((bf16[64,512]{1,0:T(8,128)(2,1)S(1)}, bf16[64,512]{1,0:T(8,128)(2,1)S(1)}, u32[]{:S(2)}, u32[]{:S(2)}) %collective-permute-start.32) | collective-permute-done | bytes 65568 | tf_op jit(solution)/shard_map/ppermute | solution.py:37
  189.0 2.8 %encoder_backward.4 = (bf16[4,3,128,128]{3,2,1,0:T(8,128)(2,1)S(1)}, bf16[4,3,128,128]{3,2,1,0:T(8,128)(2,1)S(1)}) custom-call(s32[5]{0:T(128)S(1)} %stack.49.at, bf16[1024,512]{1,0:T(8,128)(2,1)S(1)} %bitcast.67, bf16[3,512,512]{2,1,0:T(8,128)(2,1)S(1)} %copy-done.2, bf16[4,2,2,256,256]{4,3,2,1,0:T(8,128)(2,1)S(1)} %copy-done.1, ...), custom_call_target="tpu_custom_call" | custom-call | tf_op jit(solution)/shard_map/encoder_backward/pallas_call | solution.py:317
  193.1 2.8 %encoder_backward.5 = (bf16[4,3,128,128]{3,2,1,0:T(8,128)(2,1)S(1)}, bf16[4,3,128,128]{3,2,1,0:T(8,128)(2,1)S(1)}) custom-call(s32[5]{0:T(128)S(1)} %stack.49.at, bf16[1024,512]{1,0:T(8,128)(2,1)S(1)} %bitcast.68, bf16[3,512,512]{2,1,0:T(8,128)(2,1)S(1)} %copy-done.2, bf16[4,2,2,256,256]{4,3,2,1,0:T(8,128)(2,1)S(1)} %copy-done.1, ...), custom_call_target="tpu_custom_call" | custom-call | tf_op jit(solution)/shard_map/encoder_backward/pallas_call | solution.py:317
  196.7 7.2 %collective-permute-done.36 = bf16[4,3,128,128]{3,2,1,0:T(8,128)(2,1)S(1)} collective-permute-done((bf16[4,3,128,128]{3,2,1,0:T(8,128)(2,1)S(1)}, bf16[4,3,128,128]{3,2,1,0:T(8,128)(2,1)S(1)}, u32[]{:S(2)}, u32[]{:S(2)}) %collective-permute-start.36) | collective-permute-done | bytes 393248 | tf_op jit(solution)/shard_map/ppermute | solution.py:37
  218.3 5.8 %collective-permute-done.39 = bf16[4,3,128,128]{3,2,1,0:T(8,128)(2,1)S(1)} collective-permute-done((bf16[4,3,128,128]{3,2,1,0:T(8,128)(2,1)S(1)}, bf16[4,3,128,128]{3,2,1,0:T(8,128)(2,1)S(1)}, u32[]{:S(2)}, u32[]{:S(2)}) %collective-permute-start.39) | collective-permute-done | bytes 393248 | tf_op jit(solution)/shard_map/ppermute | solution.py:37
  226.3 5.4 %collective-permute-start.42 = (bf16[1,3,128,128]{3,2,1,0:T(8,128)(2,1)S(1)}, bf16[1,3,128,128]{3,2,1,0:T(8,128)(2,1)S(1)}, u32[]{:S(2)}, u32[]{:S(2)}) collective-permute-start(bf16[1,3,128,128]{3,2,1,0:T(8,128)(2,1)S(1)} %slice.222), channel_id=1, source_target_pairs={{0,8},{2,10},{4,12},{6,14},{8,0},{10,2},{12,4},{14,6},{1,9},{3,11}... | collective-permute-start | bytes 294920 | tf_op jit(solution)/shard_map/ppermute | solution.py:37
  232.0 2.8 %collective-permute-done.42 = bf16[1,3,128,128]{3,2,1,0:T(8,128)(2,1)S(1)} collective-permute-done((bf16[1,3,128,128]{3,2,1,0:T(8,128)(2,1)S(1)}, bf16[1,3,128,128]{3,2,1,0:T(8,128)(2,1)S(1)}, u32[]{:S(2)}, u32[]{:S(2)}) %collective-permute-start.42) | collective-permute-done | bytes 98336 | tf_op jit(solution)/shard_map/ppermute | solution.py:37
  234.8 7.6 %collective-permute-done.45 = bf16[2,64,1024]{2,1,0:T(8,128)(2,1)S(1)} collective-permute-done((bf16[2,64,1024]{2,1,0:T(8,128)(2,1)S(1)}, bf16[2,64,1024]{2,1,0:T(8,128)(2,1)S(1)}, u32[]{:S(2)}, u32[]{:S(2)}) %collective-permute-start.45) | collective-permute-done | bytes 262176 | tf_op jit(solution)/shard_map/ppermute | solution.py:37
  242.8 3.0 %collective-permute-start.49 = (bf16[1,3,128,128]{3,2,1,0:T(8,128)(2,1)S(1)}, bf16[1,3,128,128]{3,2,1,0:T(8,128)(2,1)S(1)}, u32[]{:S(2)}, u32[]{:S(2)}) collective-permute-start(bf16[1,3,128,128]{3,2,1,0:T(8,128)(2,1)S(1)} %slice.232), channel_id=1, source_target_pairs={{0,8},{2,10},{4,12},{6,14},{8,0},{10,2},{12,4},{14,6},{1,9},{3,11}... | collective-permute-start | bytes 294920 | tf_op jit(solution)/shard_map/ppermute | solution.py:37
  245.8 6.3 %collective-permute-done.50 = bf16[1,64,1024]{2,1,0:T(8,128)(2,1)S(1)} collective-permute-done((bf16[1,64,1024]{2,1,0:T(8,128)(2,1)S(1)}, bf16[1,64,1024]{2,1,0:T(8,128)(2,1)S(1)}, u32[]{:S(2)}, u32[]{:S(2)}) %collective-permute-start.50) | collective-permute-done | bytes 131104 | tf_op jit(solution)/shard_map/ppermute | solution.py:37
  255.1 5.5 %collective-permute-done.48 = bf16[1,3,128,128]{3,2,1,0:T(8,128)(2,1)S(1)} collective-permute-done((bf16[1,3,128,128]{3,2,1,0:T(8,128)(2,1)S(1)}, bf16[1,3,128,128]{3,2,1,0:T(8,128)(2,1)S(1)}, u32[]{:S(2)}, u32[]{:S(2)}) %collective-permute-start.48) | collective-permute-done | bytes 98336 | tf_op jit(solution)/shard_map/ppermute | solution.py:37
  (194 shorter events, 84.1 us)
Async XLA Ops:
  2.4 18.1 %collective-permute-start = (bf16[128,1024]{1,0:T(8,128)(2,1)}, bf16[128,1024]{1,0:T(8,128)(2,1)}, u32[]{:S(2)}, u32[]{:S(2)}) collective-permute-start(bf16[128,1024]{1,0:T(8,128)(2,1)} %constant_dynamic-slice_fusion.6), channel_id=1, source_target_pairs={{0,14},{1,15},{2,0},{3,1},{4,2},{5,3},{6,4},{7,5},{8,6},{9,7},{10,... | collective-permute-start | bytes 786440 | tf_op jit(solution)/shard_map/ppermute | solution.py:51
  10.6 31.9 %collective-permute-start.4 = (bf16[512,1024]{1,0:T(8,128)(2,1)}, bf16[512,1024]{1,0:T(8,128)(2,1)}, u32[]{:S(2)}, u32[]{:S(2)}) collective-permute-start(bf16[512,1024]{1,0:T(8,128)(2,1)} %constant_dynamic-slice_fusion.4), channel_id=1, source_target_pairs={{0,2},{2,0},{4,6},{6,4},{8,10},{10,8},{12,14},{14,12},{1,3},{3,1},... | collective-permute-start | bytes 3145736 | tf_op jit(solution)/shard_map/ppermute | solution.py:37
  16.0 26.8 %collective-permute-start.8 = (bf16[128,1024]{1,0:T(8,128)(2,1)}, bf16[128,1024]{1,0:T(8,128)(2,1)}, u32[]{:S(2)}, u32[]{:S(2)}) collective-permute-start(bf16[128,1024]{1,0:T(8,128)(2,1)} %get-tuple-element.169), channel_id=1, source_target_pairs={{0,12},{2,14},{4,8},{6,10},{8,4},{10,6},{12,0},{14,2},{1,13},{3,15... | collective-permute-start | bytes 786440 | tf_op jit(solution)/shard_map/ppermute | solution.py:37
  17.1 26.9 %collective-permute-start.7 = (bf16[128,1024]{1,0:T(8,128)(2,1)}, bf16[128,1024]{1,0:T(8,128)(2,1)}, u32[]{:S(2)}, u32[]{:S(2)}) collective-permute-start(bf16[128,1024]{1,0:T(8,128)(2,1)} %get-tuple-element.170), channel_id=1, source_target_pairs={{0,4},{2,6},{4,0},{6,2},{8,12},{10,14},{12,8},{14,10},{1,5},{3,7},... | collective-permute-start | bytes 786440 | tf_op jit(solution)/shard_map/ppermute | solution.py:37
  17.1 28.4 %collective-permute-start.6 = (bf16[128,1024]{1,0:T(8,128)(2,1)}, bf16[128,1024]{1,0:T(8,128)(2,1)}, u32[]{:S(2)}, u32[]{:S(2)}) collective-permute-start(bf16[128,1024]{1,0:T(8,128)(2,1)} %get-tuple-element.171), channel_id=1, source_target_pairs={{0,8},{2,10},{4,12},{6,14},{8,0},{10,2},{12,4},{14,6},{1,9},{3,11}... | collective-permute-start | bytes 786440 | tf_op jit(solution)/shard_map/ppermute | solution.py:37
  44.0 25.7 %collective-permute-start.11 = (bf16[512,1024]{1,0:T(8,128)(2,1)}, bf16[512,1024]{1,0:T(8,128)(2,1)S(1)}, u32[]{:S(2)}, u32[]{:S(2)}) collective-permute-start(bf16[512,1024]{1,0:T(8,128)(2,1)} %collective-permute-done.4), channel_id=1, source_target_pairs={{0,16},{16,0},{1,17},{17,1},{2,18},{18,2},{3,19},{19,3},{4,20},{20... | collective-permute-start | bytes 3145736 | tf_op jit(solution)/shard_map/ppermute | solution.py:565
  55.7 25.3 %collective-permute-start.14 = (bf16[4,128,1024]{2,1,0:T(8,128)(2,1)S(1)}, bf16[4,128,1024]{2,1,0:T(8,128)(2,1)S(1)}, u32[]{:S(2)}, u32[]{:S(2)}) collective-permute-start(bf16[4,128,1024]{2,1,0:T(8,128)(2,1)S(1)} %pad_maximum_fusion.1.here), channel_id=1, source_target_pairs={{0,2},{2,0},{4,6},{6,4},{8,10},{10,8},{12,14},{14,12},{1,3},{3,1},... | collective-permute-start | bytes 3145736 | tf_op jit(solution)/shard_map/ppermute | solution.py:37
  96.6 9.2 %collective-permute-start.16 = (bf16[2,128,512]{2,1,0:T(8,128)(2,1)S(1)}, bf16[2,128,512]{2,1,0:T(8,128)(2,1)S(1)}, u32[]{:S(2)}, u32[]{:S(2)}) collective-permute-start(bf16[2,128,512]{2,1,0:T(8,128)(2,1)S(1)} %get-tuple-element.167), channel_id=1, source_target_pairs={{0,4},{2,6},{4,0},{6,2},{8,12},{10,14},{12,8},{14,10},{1,5},{3,7},... | collective-permute-start | bytes 786440 | tf_op jit(solution)/shard_map/ppermute | solution.py:37
  98.4 16.2 %collective-permute-start.21 = (f32[1,128]{1,0:T(1,128)S(1)}, f32[1,128]{1,0:T(1,128)S(1)}, u32[]{:S(2)}, u32[]{:S(2)}) collective-permute-start(f32[1,128]{1,0:T(1,128)S(1)} %slice.165), channel_id=1, source_target_pairs={{0,8},{2,10},{4,12},{6,14},{8,0},{10,2},{12,4},{14,6},{1,9},{3,11}... | collective-permute-start | bytes 1544 | tf_op jit(solution)/shard_map/ppermute | solution.py:37
  100.1 13.4 %collective-permute-start.18 = (bf16[2,128,512]{2,1,0:T(8,128)(2,1)S(1)}, bf16[2,128,512]{2,1,0:T(8,128)(2,1)S(1)}, u32[]{:S(2)}, u32[]{:S(2)}) collective-permute-start(bf16[2,128,512]{2,1,0:T(8,128)(2,1)S(1)} %get-tuple-element.168), channel_id=1, source_target_pairs={{0,4},{2,6},{4,0},{6,2},{8,12},{10,14},{12,8},{14,10},{1,5},{3,7},... | collective-permute-start | bytes 786440 | tf_op jit(solution)/shard_map/ppermute | solution.py:37
  105.9 8.7 %collective-permute-start.17 = (bf16[1,128,512]{2,1,0:T(8,128)(2,1)S(1)}, bf16[1,128,512]{2,1,0:T(8,128)(2,1)S(1)}, u32[]{:S(2)}, u32[]{:S(2)}) collective-permute-start(bf16[1,128,512]{2,1,0:T(8,128)(2,1)S(1)} %get-tuple-element.178), channel_id=1, source_target_pairs={{0,8},{2,10},{4,12},{6,14},{8,0},{10,2},{12,4},{14,6},{1,9},{3,11}... | collective-permute-start | bytes 393224 | tf_op jit(solution)/shard_map/ppermute | solution.py:37
  113.6 11.3 %collective-permute-start.22 = (bf16[1,128,512]{2,1,0:T(8,128)(2,1)S(1)}, bf16[1,128,512]{2,1,0:T(8,128)(2,1)S(1)}, u32[]{:S(2)}, u32[]{:S(2)}) collective-permute-start(bf16[1,128,512]{2,1,0:T(8,128)(2,1)S(1)} %get-tuple-element.179), channel_id=1, source_target_pairs={{0,8},{2,10},{4,12},{6,14},{8,0},{10,2},{12,4},{14,6},{1,9},{3,11}... | collective-permute-start | bytes 393224 | tf_op jit(solution)/shard_map/ppermute | solution.py:37
  114.9 14.5 %collective-permute-start.23 = (bf16[1,128,512]{2,1,0:T(8,128)(2,1)S(1)}, bf16[1,128,512]{2,1,0:T(8,128)(2,1)S(1)}, u32[]{:S(2)}, u32[]{:S(2)}) collective-permute-start(bf16[1,128,512]{2,1,0:T(8,128)(2,1)S(1)} %bitcast.80), channel_id=1, source_target_pairs={{0,8},{2,10},{4,12},{6,14},{8,0},{10,2},{12,4},{14,6},{1,9},{3,11}... | collective-permute-start | bytes 393224 | tf_op jit(solution)/shard_map/ppermute | solution.py:37
  125.8 8.9 %collective-permute-start.25 = (bf16[1,128,640]{2,1,0:T(8,128)(2,1)S(1)}, bf16[1,128,640]{2,1,0:T(8,128)(2,1)S(1)}, u32[]{:S(2)}, u32[]{:S(2)}) collective-permute-start(bf16[1,128,640]{2,1,0:T(8,128)(2,1)S(1)} %bitcast.77), channel_id=1, source_target_pairs={{0,8},{2,10},{4,12},{6,14},{8,0},{10,2},{12,4},{14,6},{1,9},{3,11}... | collective-permute-start | bytes 491528 | tf_op jit(solution)/shard_map/ppermute | solution.py:37
  129.5 10.9 %collective-permute-start.24 = (bf16[2,128,512]{2,1,0:T(8,128)(2,1)S(1)}, bf16[2,128,512]{2,1,0:T(8,128)(2,1)S(1)}, u32[]{:S(2)}, u32[]{:S(2)}) collective-permute-start(bf16[2,128,512]{2,1,0:T(8,128)(2,1)S(1)} %pad_maximum_fusion.7), channel_id=1, source_target_pairs={{0,4},{2,6},{4,0},{6,2},{8,12},{10,14},{12,8},{14,10},{1,5},{3,7},... | collective-permute-start | bytes 786440 | tf_op jit(solution)/shard_map/ppermute | solution.py:37
  134.8 12.4 %collective-permute-start.26 = (bf16[2,128,640]{2,1,0:T(8,128)(2,1)S(1)}, bf16[2,128,640]{2,1,0:T(8,128)(2,1)S(1)}, u32[]{:S(2)}, u32[]{:S(2)}) collective-permute-start(bf16[2,128,640]{2,1,0:T(8,128)(2,1)S(1)} %pad_maximum_fusion.5), channel_id=1, source_target_pairs={{0,4},{2,6},{4,0},{6,2},{8,12},{10,14},{12,8},{14,10},{1,5},{3,7},... | collective-permute-start | bytes 983048 | tf_op jit(solution)/shard_map/ppermute | solution.py:37
  159.2 8.4 %collective-permute-start.30 = (bf16[2,2,64,512]{3,2,1,0:T(8,128)(2,1)S(1)}, bf16[2,2,64,512]{3,2,1,0:T(8,128)(2,1)S(1)}, u32[]{:S(2)}, u32[]{:S(2)}) collective-permute-start(bf16[2,2,64,512]{3,2,1,0:T(8,128)(2,1)S(1)} %bitcast.94), channel_id=1, source_target_pairs={{0,4},{2,6},{4,0},{6,2},{8,12},{10,14},{12,8},{14,10},{1,5},{3,7},... | collective-permute-start | bytes 786440 | tf_op jit(solution)/shard_map/ppermute | solution.py:37
  167.7 8.5 %collective-permute-start.31 = (bf16[1,2,64,512]{3,2,1,0:T(8,128)(2,1)S(1)}, bf16[1,2,64,512]{3,2,1,0:T(8,128)(2,1)S(1)}, u32[]{:S(2)}, u32[]{:S(2)}) collective-permute-start(bf16[1,2,64,512]{3,2,1,0:T(8,128)(2,1)S(1)} %slice.211), channel_id=1, source_target_pairs={{0,8},{2,10},{4,12},{6,14},{8,0},{10,2},{12,4},{14,6},{1,9},{3,11}... | collective-permute-start | bytes 393224 | tf_op jit(solution)/shard_map/ppermute | solution.py:37
  191.8 12.1 %collective-permute-start.36 = (bf16[4,3,128,128]{3,2,1,0:T(8,128)(2,1)S(1)}, bf16[4,3,128,128]{3,2,1,0:T(8,128)(2,1)S(1)}, u32[]{:S(2)}, u32[]{:S(2)}) collective-permute-start(bf16[4,3,128,128]{3,2,1,0:T(8,128)(2,1)S(1)} %get-tuple-element.135), channel_id=1, source_target_pairs={{0,2},{2,0},{4,6},{6,4},{8,10},{10,8},{12,14},{14,12},{1,3},{3,1},... | collective-permute-start | bytes 1179656 | tf_op jit(solution)/shard_map/ppermute | solution.py:37
  195.9 20.3 %collective-permute-start.40 = (bf16[4,3,128,128]{3,2,1,0:T(8,128)(2,1)S(1)}, bf16[4,3,128,128]{3,2,1,0:T(8,128)(2,1)S(1)}, u32[]{:S(2)}, u32[]{:S(2)}) collective-permute-start(bf16[4,3,128,128]{3,2,1,0:T(8,128)(2,1)S(1)} %get-tuple-element.149), channel_id=1, source_target_pairs={{0,2},{2,0},{4,6},{6,4},{8,10},{10,8},{12,14},{14,12},{1,3},{3,1},... | collective-permute-start | bytes 1179656 | tf_op jit(solution)/shard_map/ppermute | solution.py:37
  204.1 10.6 %collective-permute-start.37 = (bf16[2,3,128,128]{3,2,1,0:T(8,128)(2,1)S(1)}, bf16[2,3,128,128]{3,2,1,0:T(8,128)(2,1)S(1)}, u32[]{:S(2)}, u32[]{:S(2)}) collective-permute-start(bf16[2,3,128,128]{3,2,1,0:T(8,128)(2,1)S(1)} %slice.216), channel_id=1, source_target_pairs={{0,4},{2,6},{4,0},{6,2},{8,12},{10,14},{12,8},{14,10},{1,5},{3,7},... | collective-permute-start | bytes 589832 | tf_op jit(solution)/shard_map/ppermute | solution.py:37
  205.4 20.9 %collective-permute-start.43 = (bf16[4,64,1024]{2,1,0:T(8,128)(2,1)S(1)}, bf16[4,64,1024]{2,1,0:T(8,128)(2,1)S(1)}, u32[]{:S(2)}, u32[]{:S(2)}) collective-permute-start(bf16[4,64,1024]{2,1,0:T(8,128)(2,1)S(1)} %get-tuple-element.155), channel_id=1, source_target_pairs={{0,2},{2,0},{4,6},{6,4},{8,10},{10,8},{12,14},{14,12},{1,3},{3,1},... | collective-permute-start | bytes 1572872 | tf_op jit(solution)/shard_map/ppermute | solution.py:37
  211.8 12.3 %collective-permute-start.39 = (bf16[4,3,128,128]{3,2,1,0:T(8,128)(2,1)S(1)}, bf16[4,3,128,128]{3,2,1,0:T(8,128)(2,1)S(1)}, u32[]{:S(2)}, u32[]{:S(2)}) collective-permute-start(bf16[4,3,128,128]{3,2,1,0:T(8,128)(2,1)S(1)} %get-tuple-element.147), channel_id=1, source_target_pairs={{0,4},{2,6},{4,0},{6,2},{8,12},{10,14},{12,8},{14,10},{1,5},{3,7},... | collective-permute-start | bytes 1179656 | tf_op jit(solution)/shard_map/ppermute | solution.py:37
  213.9 28.7 %collective-permute-start.44 = (bf16[4,3,128,128]{3,2,1,0:T(8,128)(2,1)S(1)}, bf16[4,3,128,128]{3,2,1,0:T(8,128)(2,1)S(1)}, u32[]{:S(2)}, u32[]{:S(2)}) collective-permute-start(bf16[4,3,128,128]{3,2,1,0:T(8,128)(2,1)S(1)} %get-tuple-element.159), channel_id=1, source_target_pairs={{0,2},{2,0},{4,6},{6,4},{8,10},{10,8},{12,14},{14,12},{1,3},{3,1},... | collective-permute-start | bytes 1179656 | tf_op jit(solution)/shard_map/ppermute | solution.py:37
  214.8 9.8 %collective-permute-start.38 = (bf16[1,3,128,128]{3,2,1,0:T(8,128)(2,1)S(1)}, bf16[1,3,128,128]{3,2,1,0:T(8,128)(2,1)S(1)}, u32[]{:S(2)}, u32[]{:S(2)}) collective-permute-start(bf16[1,3,128,128]{3,2,1,0:T(8,128)(2,1)S(1)} %slice.218), channel_id=1, source_target_pairs={{0,8},{2,10},{4,12},{6,14},{8,0},{10,2},{12,4},{14,6},{1,9},{3,11}... | collective-permute-start | bytes 294920 | tf_op jit(solution)/shard_map/ppermute | solution.py:37
  216.3 9.9 %collective-permute-start.41 = (bf16[2,3,128,128]{3,2,1,0:T(8,128)(2,1)S(1)}, bf16[2,3,128,128]{3,2,1,0:T(8,128)(2,1)S(1)}, u32[]{:S(2)}, u32[]{:S(2)}) collective-permute-start(bf16[2,3,128,128]{3,2,1,0:T(8,128)(2,1)S(1)} %slice.220), channel_id=1, source_target_pairs={{0,4},{2,6},{4,0},{6,2},{8,12},{10,14},{12,8},{14,10},{1,5},{3,7},... | collective-permute-start | bytes 589832 | tf_op jit(solution)/shard_map/ppermute | solution.py:37
  224.2 18.5 %collective-permute-start.47 = (bf16[2,3,128,128]{3,2,1,0:T(8,128)(2,1)S(1)}, bf16[2,3,128,128]{3,2,1,0:T(8,128)(2,1)S(1)}, u32[]{:S(2)}, u32[]{:S(2)}) collective-permute-start(bf16[2,3,128,128]{3,2,1,0:T(8,128)(2,1)S(1)} %slice.228), channel_id=1, source_target_pairs={{0,2},{2,0},{4,6},{6,4},{8,10},{10,8},{12,14},{14,12},{1,3},{3,1},... | collective-permute-start | bytes 589832 | tf_op jit(solution)/shard_map/ppermute | solution.py:37
  226.3 8.5 %collective-permute-start.42 = (bf16[1,3,128,128]{3,2,1,0:T(8,128)(2,1)S(1)}, bf16[1,3,128,128]{3,2,1,0:T(8,128)(2,1)S(1)}, u32[]{:S(2)}, u32[]{:S(2)}) collective-permute-start(bf16[1,3,128,128]{3,2,1,0:T(8,128)(2,1)S(1)} %slice.222), channel_id=1, source_target_pairs={{0,8},{2,10},{4,12},{6,14},{8,0},{10,2},{12,4},{14,6},{1,9},{3,11}... | collective-permute-start | bytes 294920 | tf_op jit(solution)/shard_map/ppermute | solution.py:37
  231.9 10.6 %collective-permute-start.45 = (bf16[2,64,1024]{2,1,0:T(8,128)(2,1)S(1)}, bf16[2,64,1024]{2,1,0:T(8,128)(2,1)S(1)}, u32[]{:S(2)}, u32[]{:S(2)}) collective-permute-start(bf16[2,64,1024]{2,1,0:T(8,128)(2,1)S(1)} %slice.224), channel_id=1, source_target_pairs={{0,4},{2,6},{4,0},{6,2},{8,12},{10,14},{12,8},{14,10},{1,5},{3,7},... | collective-permute-start | bytes 786440 | tf_op jit(solution)/shard_map/ppermute | solution.py:37
  242.5 9.6 %collective-permute-start.50 = (bf16[1,64,1024]{2,1,0:T(8,128)(2,1)S(1)}, bf16[1,64,1024]{2,1,0:T(8,128)(2,1)S(1)}, u32[]{:S(2)}, u32[]{:S(2)}) collective-permute-start(bf16[1,64,1024]{2,1,0:T(8,128)(2,1)S(1)} %slice.234), channel_id=1, source_target_pairs={{0,8},{2,10},{4,12},{6,14},{8,0},{10,2},{12,4},{14,6},{1,9},{3,11}... | collective-permute-start | bytes 393224 | tf_op jit(solution)/shard_map/ppermute | solution.py:37
  242.8 12.1 %collective-permute-start.49 = (bf16[1,3,128,128]{3,2,1,0:T(8,128)(2,1)S(1)}, bf16[1,3,128,128]{3,2,1,0:T(8,128)(2,1)S(1)}, u32[]{:S(2)}, u32[]{:S(2)}) collective-permute-start(bf16[1,3,128,128]{3,2,1,0:T(8,128)(2,1)S(1)} %slice.232), channel_id=1, source_target_pairs={{0,8},{2,10},{4,12},{6,14},{8,0},{10,2},{12,4},{14,6},{1,9},{3,11}... | collective-permute-start | bytes 294920 | tf_op jit(solution)/shard_map/ppermute | solution.py:37
  245.8 9.1 %collective-permute-start.46 = (bf16[2,3,128,128]{3,2,1,0:T(8,128)(2,1)S(1)}, bf16[2,3,128,128]{3,2,1,0:T(8,128)(2,1)S(1)}, u32[]{:S(2)}, u32[]{:S(2)}) collective-permute-start(bf16[2,3,128,128]{3,2,1,0:T(8,128)(2,1)S(1)} %slice.226), channel_id=1, source_target_pairs={{0,4},{2,6},{4,0},{6,2},{8,12},{10,14},{12,8},{14,10},{1,5},{3,7},... | collective-permute-start | bytes 589832 | tf_op jit(solution)/shard_map/ppermute | solution.py:37
  (34 other events, 366.4 us)

commit v6 on v5

--- a/solution.py
+++ b/solution.py
@@ -110,10 +110,10 @@
     return parts
 
 
-def scatter_chunks(chunks, steps):
+def scatter_chunks(chunks, steps, last):
     sums = [lower for lower, _, _ in chunks]
     sends = [upper for _, upper, _ in chunks]
-    stage, last = [0] * len(chunks), None
+    stage = [0] * len(chunks)
     for i in steps:
         got = in_turn(swap_tm(sends[i], chunks[i][2][stage[i]]), last)
         stage[i] += 1
@@ -369,12 +369,18 @@
     )
 
 
+def kv_columns(low, at, kva, kvb, side, rows):
+    feats, cols = kva.shape[0], kvb.shape[2]
+    mine, across = both(at[2] % 2, feats)
+    span = pl.ds(pl.multiple_of(side * cols, cols), cols)
+    part = dot(low[rows, mine], kva[:, span]) + dot(low[rows, across], kvb[side ^ at[4]])
+    return part.astype(BF)
+
+
 def lift_kernel(table, order, at, ta, tb, here, there, gain, kva, kvb, *refs):
-    lifted, send, keep, tok, low = refs
-    core, group = at[3], at[4]
-    feats, cols = kva.shape[0], send.shape[1]
+    lifted, squares, low, send, tok = refs
+    core = at[3]
     near, far = both(core, ta.shape[1])
-    mine, across = both(at[2] % 2, feats)
     piece = ta.shape[0] // len(table) if table else 0
     for source_row, owner_row in table:
         tok[owner_row : owner_row + piece, near] = ta[source_row : source_row + piece]
@@ -385,36 +391,57 @@
     block = here.shape[1]
     starts = column_starts(order, at, block)
     weight = weight_rows(here, there)
+    group_rows = squares.shape[1]
     for rows in chunks_of(tok.shape[0]):
         x = tok[rows]
         if starts:
             x = jnp.concatenate([tok[rows, pl.ds(start, block)] for start in starts], axis=1)
         product = dot(x, weight)
-        lifted[rows] = product
+        lifted[rows] = product.astype(BF)
         low[rows] = (product * gain[...]).astype(BF)
-        for ref, side in ((send, 1 - core), (keep, core)):
-            span = pl.ds(pl.multiple_of(side * cols, cols), cols)
-            part = dot(low[rows, mine], kva[:, span]) + dot(low[rows, across], kvb[side ^ group])
-            ref[rows] = part.astype(BF)
-
-
-def lift(table, order, at, ta, tb, here, there, gain, kva, kvb):
+        sums = jnp.sum(product * product, axis=1, keepdims=True)
+        for first in range(0, rows.stop - rows.start, group_rows):
+            column = sums[first : first + group_rows]
+            owner = (rows.start + first) // group_rows
+            squares[owner : owner + 1] = jnp.broadcast_to(column, (group_rows,) * 2).T[:1]
+        send[rows] = kv_columns(low, at, kva, kvb, 1 - core, rows)
+
+
+def lift(table, order, at, own_tok, ta, tb, here, there, gain, kva, kvb):
     rows, half = ta.shape
     feats, cols = kva.shape[0], kva.shape[1] // 2
     whole = pl.BlockSpec(memory_space=pltpu.VMEM)
     return pl.pallas_call(
         functools.partial(lift_kernel, table, order),
         in_specs=[pl.BlockSpec(memory_space=pltpu.SMEM)] + [whole] * 7,
-        out_specs=[whole] * 3,
+        out_specs=[whole] * 4,
         out_shape=[
-            jax.ShapeDtypeStruct((rows, 2 * feats), F32),
-            jax.ShapeDtypeStruct((rows, cols), BF),
+            jax.ShapeDtypeStruct((rows, 2 * feats), BF),
+            jax.ShapeDtypeStruct((rows // own_tok, own_tok), F32),
+            jax.ShapeDtypeStruct((rows, 2 * feats), BF),
             jax.ShapeDtypeStruct((rows, cols), BF),
         ],
-        scratch_shapes=[pltpu.VMEM((rows, 2 * half), BF), pltpu.VMEM((rows, 2 * feats), BF)],
+        scratch_shapes=[pltpu.VMEM((rows, 2 * half), BF)],
         compiler_params=pltpu.CompilerParams(vmem_limit_bytes=VMEM_LIMIT),
         name="lift",
     )(at, ta, tb, here, there, gain, kva, kvb)
+
+
+def keep_kernel(at, low, kva, kvb, keep):
+    for rows in chunks_of(low.shape[0]):
+        keep[rows] = kv_columns(low, at, kva, kvb, at[3], rows)
+
+
+def keep_columns(at, low, kva, kvb):
+    whole = pl.BlockSpec(memory_space=pltpu.VMEM)
+    return pl.pallas_call(
+        keep_kernel,
+        in_specs=[pl.BlockSpec(memory_space=pltpu.SMEM)] + [whole] * 3,
+        out_specs=whole,
+        out_shape=jax.ShapeDtypeStruct((low.shape[0], kva.shape[1] // 2), BF),
+        compiler_params=pltpu.CompilerParams(vmem_limit_bytes=VMEM_LIMIT),
+        name="keep_columns",
+    )(at, low, kva, kvb)
 
 
 def two_parts(column):
@@ -486,7 +513,7 @@
                 part = dot_nt(cot, kva[:, at_side] if is_mine else kvb[side ^ group])
                 d_normed = part if d_normed is None else d_normed + part
             low[rows, span] = (
-                inv * gain[:, span] * d_normed - lifted[rows, span] * pull
+                inv * gain[:, span] * d_normed - lifted[rows, span].astype(F32) * pull
             ).astype(BF)
         d_tok = dot_nt(low[rows], weight).astype(BF)
         if not starts:
@@ -605,7 +632,7 @@
     there = swap_tm(here, SPLIT)
     pair_tok = jnp.stack([sorted_tok[0], handed])
     tok_half = gather_doubling(pair_tok, masks[-1:])
-    tok_half, kv_far = lax.optimization_barrier((tok_half, kv_far))
+    tok_half, turned, d_kv = lax.optimization_barrier((tok_half, turned, d_kv))
     kva, kvb = proj_kv, jnp.stack([kv_near, kv_far])
     at_rows = order
     if width // n % LANES:
@@ -628,13 +655,13 @@
         at_owner = source_rows[np.argsort(owner_rows)]
         tok_half, tok_other = tok_half[at_owner], tok_other[at_owner]
         table = []
-    lifted, kv_send, kv_keep = lift(
-        table, at_rows, at, tok_half, tok_other, here, there, gain, kva, kvb
-    )
-    squares = jnp.sum(lifted * lifted, axis=-1).reshape(count, own_tok)
+    lifted, squares, scaled, kv_send = lift(
+        table, at_rows, at, own_tok, tok_half, tok_other, here, there, gain, kva, kvb
+    )
+    kv_got = swap_mp(kv_send)
+    kv_keep = keep_columns(at, scaled, kva, kvb)
     square_sum = scatter_halving(squares + swap_mp(squares), masks, F32)
-    kv_part = (kv_keep.astype(F32) + swap_mp(kv_send).astype(F32)).astype(BF)
-    kv_part, turned = lax.optimization_barrier((kv_part, turned))
+    kv_part = (kv_keep.astype(F32) + kv_got.astype(F32)).astype(BF)
     kv_parts = jnp.split(kv_part.reshape(count, own_tok, kv_half), 2, axis=2)
     (mine_a, got_a), (mine_b, got_b) = scatter_last(kv_parts, masks)
     square_sum = square_sum.reshape(1, own_tok)
@@ -676,7 +703,7 @@
     steps = list(range(len(chunks))) * len(bits)
     if len(bits) == 3:
         steps = [0, 0, 1, 3, 0, 1, 4, 1, 4, 2, 3, 4, 2, 3, 2]
-    chunks = scatter_chunks(chunks, steps)
+    chunks = scatter_chunks(chunks, steps, even)
     grad_out = chunks.pop()
     grad_qkv = jnp.transpose(jnp.concatenate(chunks, axis=-1), (1, 0, 2))
     return kv, grad_qkv, grad_out

time: 262 us -> 247 us (0.943)
  waiting for transfers between devices: 133 us -> 112 us
  starting transfers between devices: 50.2 us -> 56.6 us
  other arithmetic: 16.5 us -> 13.7 us
    ppermute x36, waiting for transfers between devices: 113 us -> 100 us  [swap_tm(): return lax.ppermute(block, 'tm', [(i, i ^ mask) for i in range(n)])]
    ppermute x1, waiting for transfers between devices: 7.64 us -> 0.01 us  [on_device(): swap_groups = lambda block: lax.ppermute(block, 'groups', [(0, 1), (1, 0)])]
    ppermute x36, starting transfers between devices: 36.3 us -> 40 us  [swap_tm(): return lax.ppermute(block, 'tm', [(i, i ^ mask) for i in range(n)])]
    pallas_call x0 -> x1, Pallas kernels: none -> 2.85 us  [keep_columns(): pl.pallas_call(keep_kernel, in_specs=[pl.BlockSpec(memory_space=pltpu.SME...]
    ppermute x5, starting transfers between devices: 10.7 us -> 13.4 us  [to_tm(): return lax.ppermute(block, ('tm', 'mp'), pairs)]
  transfers between devices with their start and end apart: 51 -> 51, of which waited for: 28 -> 31; matrix products, arithmetic and copies ran while one was open for 12% -> 11% of each run, Pallas kernels for 8% -> 10%
where the time goes in v6:
time: 247 us; the launch traced here: 246 us
  waiting for transfers between devices  112 us (45%)
  starting transfers between devices  56.6 us (23%)
  Pallas kernels  39.4 us (16%)
  local copies, waits for them, and re-layouts  16.2 us (7%)
  other arithmetic  13.7 us (6%)
  between operations  4.1 us (2%)
  matrix products  3.59 us (1%)
    ppermute x36, waiting for transfers between devices, swap_tm(): return lax.ppermute(block, 'tm', [(i, i ^ mask) for i in range(n)])  100 us
    ppermute x36, starting transfers between devices, swap_tm(): return lax.ppermute(block, 'tm', [(i, i ^ mask) for i in range(n)])  40 us
    ppermute x5, starting transfers between devices, to_tm(): return lax.ppermute(block, ('tm', 'mp'), pairs)  13.4 us
    pallas_call x1, Pallas kernels, encoder_forward(): pl.pallas_call(forward_kernel, grid_spec=pltpu.PrefetchScalarGridSpec(num...  11.1 us
    pallas_call x4, Pallas kernels, encoder_backward(): pl.pallas_call(functools.partial(backward_kernel, masks), grid_spec=pltpu...  11 us
    ppermute x5, waiting for transfers between devices, to_tm(): return lax.ppermute(block, ('tm', 'mp'), pairs)  7.99 us
    pallas_call x1, Pallas kernels, lower(): pl.pallas_call(functools.partial(lower_kernel, table, order), in_specs=[p...  6.42 us
    pallas_call x1, Pallas kernels, lift(): pl.pallas_call(functools.partial(lift_kernel, table, order), in_specs=[pl...  5.22 us
  transfers between devices with their start and end apart: 51, of which 31 were waited for; matrix products, arithmetic and copies ran while one was open for 11% of the time, Pallas kernels for 10%

profile of v6, /device:TPU:0, one launch (start us, length us, event | category | flops | bytes accessed | tf_op | source)
XLA Modules:
  0.0 246.1 jit_solution(7946347070902476010)
XLA Ops:
  2.4 6.0 %collective-permute-start = (bf16[128,1024]{1,0:T(8,128)(2,1)}, bf16[128,1024]{1,0:T(8,128)(2,1)}, u32[]{:S(2)}, u32[]{:S(2)}) collective-permute-start(bf16[128,1024]{1,0:T(8,128)(2,1)} %constant_dynamic-slice_fusion.6), channel_id=1, source_target_pairs={{0,14},{1,15},{2,0},{3,1},{4,2},{5,3},{6,4},{7,5},{8,6},{9,7},{10,... | collective-permute-start | bytes 786440 | tf_op jit(solution)/shard_map/ppermute | solution.py:51
  10.7 3.2 %copy.14 = bf16[3,512,1024]{2,1,0:T(8,128)(2,1)S(1)} copy(bf16[3,512,1024]{1,2,0:T(8,128)(2,1)} %bitcast.88) | data formatting | bytes 6291456 | tf_op jit(solution)/shard_map/transpose | solution.py:563
  17.1 3.3 %collective-permute-start.6 = (bf16[128,1024]{1,0:T(8,128)(2,1)}, bf16[128,1024]{1,0:T(8,128)(2,1)}, u32[]{:S(2)}, u32[]{:S(2)}) collective-permute-start(bf16[128,1024]{1,0:T(8,128)(2,1)} %get-tuple-element.173), channel_id=1, source_target_pairs={{0,8},{2,10},{4,12},{6,14},{8,0},{10,2},{12,4},{14,6},{1,9},{3,11}... | collective-permute-start | bytes 786440 | tf_op jit(solution)/shard_map/ppermute | solution.py:37
  28.0 11.1 %encoder_forward.1 = (bf16[512,1024]{1,0:T(8,128)(2,1)}, bf16[3,512,512]{2,1,0:T(8,128)(2,1)}, bf16[4,2,2,256,256]{4,3,2,1,0:T(8,128)(2,1)}, bf16[192,512]{1,0:T...) custom-call(s32[5]{0:T(128)S(1)} %stack.49.at, ...), custom_call_target="tpu_custom_call" | custom-call | tf_op jit(solution)/shard_map/encoder_forward/pallas_call | solution.py:206
  52.8 3.0 %collective-permute-done.9 = bf16[64,512]{1,0:T(8,128)(2,1)S(1)} collective-permute-done((bf16[64,512]{1,0:T(8,128)(2,1)S(1)}, bf16[64,512]{1,0:T(8,128)(2,1)S(1)}, u32[]{:S(2)}, u32[]{:S(2)}) %collective-permute-start.9) | collective-permute-done | bytes 65568 | tf_op jit(solution)/shard_map/ppermute | solution.py:37
  58.5 3.7 %collective-permute-done.10 = bf16[1,2,64,512]{3,2,1,0:T(8,128)(2,1)} collective-permute-done((bf16[1,2,64,512]{3,2,1,0:T(8,128)(2,1)S(1)}, bf16[1,2,64,512]{3,2,1,0:T(8,128)(2,1)}, u32[]{:S(2)}, u32[]{:S(2)}) %collective-permute-start.10) | collective-permute-done | bytes 131104 | tf_op jit(solution)/shard_map/ppermute | solution.py:37
  63.3 7.3 %collective-permute-done.11 = bf16[2,2,64,512]{3,2,1,0:T(8,128)(2,1)S(1)} collective-permute-done((bf16[2,2,64,512]{3,2,1,0:T(8,128)(2,1)S(1)}, bf16[2,2,64,512]{3,2,1,0:T(8,128)(2,1)S(1)}, u32[]{:S(2)}, u32[]{:S(2)}) %collective-permute-start.11) | collective-permute-done | bytes 262176 | tf_op jit(solution)/shard_map/ppermute | solution.py:37
  71.4 3.1 %pad_maximum_fusion.kvb = bf16[2,512,1024]{2,1,0:T(8,128)(2,1)} fusion(bf16[1,512,1024]{2,1,0:T(8,128)(2,1)} %bitcast.19, bf16[1,512,1024]{2,1,0:T(8,128)(2,1)} %bitcast.18), kind=kLoop, calls=%fused_computation | loop fusion | flops 1048576 | bytes 4194304 | tf_op jit(solution)/shard_map/stack | solution.py:636
  74.5 5.8 %collective-permute-done.13.there = bf16[4,128,1024]{2,1,0:T(8,128)(2,1)S(1)} collective-permute-done((bf16[4,128,1024]{2,1,0:T(8,128)(2,1)S(1)}, bf16[4,128,1024]{2,1,0:T(8,128)(2,1)S(1)}, u32[]{:S(2)}, u32[]{:S(2)}) %collective-permute-start.13) | collective-permute-done | bytes 1048608 | tf_op jit(solution)/shard_map/ppermute | solution.py:37
  81.3 5.2 %lift.1 = (bf16[512,1024]{1,0:T(8,128)(2,1)S(1)}, f32[4,128]{1,0:T(4,128)S(1)}, bf16[512,1024]{1,0:T(8,128)(2,1)S(1)}, bf16[512,1024]{1,0:T(8,128)(2,1)S(1)}) custom-call(s32[5]{0:T(128)S(1)} %stack.49.at, bf16[512,512]{1,0:T(8,128)(2,1)S(1)} %bitcast.74, bf16[512,512]{1,0:T(8,128)(2,1)S(1)} %collective-permute-done.12.tb, ...), custom_call_target="tpu_custom_call" | custom-call | tf_op jit(solution)/shard_map/lift/pallas_call | solution.py:414
  88.1 2.9 %keep_columns.1 = bf16[512,1024]{1,0:T(8,128)(2,1)S(1)} custom-call(s32[5]{0:T(128)S(1)} %stack.49.at, bf16[512,1024]{1,0:T(8,128)(2,1)S(1)} %get-tuple-element.110.low, bf16[512,2048]{1,0:T(8,128)(2,1)S(1)} %copy-done.2, bf16[2,512,1024]{2,1,0:T(8,128)(2,1)} %pad_maximum_fusion.kvb), custom_call_target="tpu_custom_call" | custom-call | tf_op jit(solution)/shard_map/keep_columns/pallas_call | solution.py:437
  97.2 3.6 %collective-permute-done.16 = bf16[2,128,512]{2,1,0:T(8,128)(2,1)S(1)} collective-permute-done((bf16[2,128,512]{2,1,0:T(8,128)(2,1)S(1)}, bf16[2,128,512]{2,1,0:T(8,128)(2,1)S(1)}, u32[]{:S(2)}, u32[]{:S(2)}) %collective-permute-start.16) | collective-permute-done | bytes 262176 | tf_op jit(solution)/shard_map/ppermute | solution.py:37
  103.5 4.7 %collective-permute-done.18 = bf16[2,128,512]{2,1,0:T(8,128)(2,1)S(1)} collective-permute-done((bf16[2,128,512]{2,1,0:T(8,128)(2,1)S(1)}, bf16[2,128,512]{2,1,0:T(8,128)(2,1)S(1)}, u32[]{:S(2)}, u32[]{:S(2)}) %collective-permute-start.18) | collective-permute-done | bytes 262176 | tf_op jit(solution)/shard_map/ppermute | solution.py:37
  111.7 8.2 %collective-permute-done.22 = bf16[1,128,512]{2,1,0:T(8,128)(2,1)S(1)} collective-permute-done((bf16[1,128,512]{2,1,0:T(8,128)(2,1)S(1)}, bf16[1,128,512]{2,1,0:T(8,128)(2,1)S(1)}, u32[]{:S(2)}, u32[]{:S(2)}) %collective-permute-start.22) | collective-permute-done | bytes 131104 | tf_op jit(solution)/shard_map/ppermute | solution.py:37
  123.7 5.1 %collective-permute-done.25 = bf16[1,128,640]{2,1,0:T(8,128)(2,1)S(1)} collective-permute-done((bf16[1,128,640]{2,1,0:T(8,128)(2,1)S(1)}, bf16[1,128,640]{2,1,0:T(8,128)(2,1)S(1)}, u32[]{:S(2)}, u32[]{:S(2)}) %collective-permute-start.25) | collective-permute-done | bytes 163872 | tf_op jit(solution)/shard_map/ppermute | solution.py:37
  128.9 3.7 %collective-permute-done.24 = bf16[2,128,512]{2,1,0:T(8,128)(2,1)S(1)} collective-permute-done((bf16[2,128,512]{2,1,0:T(8,128)(2,1)S(1)}, bf16[2,128,512]{2,1,0:T(8,128)(2,1)S(1)}, u32[]{:S(2)}, u32[]{:S(2)}) %collective-permute-start.24) | collective-permute-done | bytes 262176 | tf_op jit(solution)/shard_map/ppermute | solution.py:37
  132.7 5.9 %collective-permute-done.26 = bf16[2,128,640]{2,1,0:T(8,128)(2,1)S(1)} collective-permute-done((bf16[2,128,640]{2,1,0:T(8,128)(2,1)S(1)}, bf16[2,128,640]{2,1,0:T(8,128)(2,1)S(1)}, u32[]{:S(2)}, u32[]{:S(2)}) %collective-permute-start.26) | collective-permute-done | bytes 327712 | tf_op jit(solution)/shard_map/ppermute | solution.py:37
  141.6 6.4 %lower.1 = (bf16[512,512]{1,0:T(8,128)(2,1)S(1)}, bf16[512,512]{1,0:T(8,128)(2,1)S(1)}) custom-call(s32[5]{0:T(128)S(1)} %stack.49.at, bf16[512,512]{1,0:T(8,128)(2,1)S(1)} %bitcast.72, bf16[512,640]{1,0:T(8,128)(2,1)S(1)} %bitcast.70, bf16[512,512]{1,0:T(8,128)(2,1)S(1)} %collective-permute-done.27.cb0, bf16[512,640]{1,0:T(8,128)(2,1)S(1)} %collective-permute-done.28.cb1, ...), custom_call_target="tpu_custom_call" | custom-call | tf_op jit(solution)/shard_map/lower/pallas_call | solution.py:536
  150.5 8.2 %collective-permute-done.30 = bf16[2,2,64,512]{3,2,1,0:T(8,128)(2,1)S(1)} collective-permute-done((bf16[2,2,64,512]{3,2,1,0:T(8,128)(2,1)S(1)}, bf16[2,2,64,512]{3,2,1,0:T(8,128)(2,1)S(1)}, u32[]{:S(2)}, u32[]{:S(2)}) %collective-permute-start.30) | collective-permute-done | bytes 262176 | tf_op jit(solution)/shard_map/ppermute | solution.py:37
  158.8 3.3 %collective-permute-start.31 = (bf16[1,2,64,512]{3,2,1,0:T(8,128)(2,1)S(1)}, bf16[1,2,64,512]{3,2,1,0:T(8,128)(2,1)S(1)}, u32[]{:S(2)}, u32[]{:S(2)}) collective-permute-start(bf16[1,2,64,512]{3,2,1,0:T(8,128)(2,1)S(1)} %slice.211), channel_id=1, source_target_pairs={{0,8},{2,10},{4,12},{6,14},{8,0},{10,2},{12,4},{14,6},{1,9},{3,11}... | collective-permute-start | bytes 393224 | tf_op jit(solution)/shard_map/ppermute | solution.py:37
  162.0 6.1 %collective-permute-done.31 = bf16[1,2,64,512]{3,2,1,0:T(8,128)(2,1)S(1)} collective-permute-done((bf16[1,2,64,512]{3,2,1,0:T(8,128)(2,1)S(1)}, bf16[1,2,64,512]{3,2,1,0:T(8,128)(2,1)S(1)}, u32[]{:S(2)}, u32[]{:S(2)}) %collective-permute-start.31) | collective-permute-done | bytes 131104 | tf_op jit(solution)/shard_map/ppermute | solution.py:37
  169.4 3.1 %collective-permute-done.32 = bf16[64,512]{1,0:T(8,128)(2,1)S(1)} collective-permute-done((bf16[64,512]{1,0:T(8,128)(2,1)S(1)}, bf16[64,512]{1,0:T(8,128)(2,1)S(1)}, u32[]{:S(2)}, u32[]{:S(2)}) %collective-permute-start.32) | collective-permute-done | bytes 65568 | tf_op jit(solution)/shard_map/ppermute | solution.py:37
  172.8 4.2 %collective-permute-start.35 = (bf16[64,512]{1,0:T(8,128)(2,1)S(1)}, bf16[64,512]{1,0:T(8,128)(2,1)S(1)}, u32[]{:S(2)}, u32[]{:S(2)}) collective-permute-start(bf16[64,512]{1,0:T(8,128)(2,1)S(1)} %slice.214), channel_id=1, source_target_pairs={{0,15},{1,14},{2,1},{3,0},{4,3},{5,2},{6,5},{7,4},{8,7},{9,6},{10,... | collective-permute-start | bytes 196616 | tf_op jit(solution)/shard_map/ppermute | solution.py:51
  183.0 2.8 %encoder_backward.4 = (bf16[4,3,128,128]{3,2,1,0:T(8,128)(2,1)S(1)}, bf16[4,3,128,128]{3,2,1,0:T(8,128)(2,1)S(1)}) custom-call(s32[5]{0:T(128)S(1)} %stack.49.at, bf16[1024,512]{1,0:T(8,128)(2,1)S(1)} %bitcast.65, bf16[3,512,512]{2,1,0:T(8,128)(2,1)S(1)} %copy-done.3, bf16[4,2,2,256,256]{4,3,2,1,0:T(8,128)(2,1)S(1)} %copy-done.1, ...), custom_call_target="tpu_custom_call" | custom-call | tf_op jit(solution)/shard_map/encoder_backward/pallas_call | solution.py:317
  185.9 2.8 %encoder_backward.5 = (bf16[4,3,128,128]{3,2,1,0:T(8,128)(2,1)S(1)}, bf16[4,3,128,128]{3,2,1,0:T(8,128)(2,1)S(1)}) custom-call(s32[5]{0:T(128)S(1)} %stack.49.at, bf16[1024,512]{1,0:T(8,128)(2,1)S(1)} %bitcast.66, bf16[3,512,512]{2,1,0:T(8,128)(2,1)S(1)} %copy-done.3, bf16[4,2,2,256,256]{4,3,2,1,0:T(8,128)(2,1)S(1)} %copy-done.1, ...), custom_call_target="tpu_custom_call" | custom-call | tf_op jit(solution)/shard_map/encoder_backward/pallas_call | solution.py:317
  193.5 2.8 %encoder_backward.7 = (bf16[4,3,128,128]{3,2,1,0:T(8,128)(2,1)S(1)}, bf16[4,3,128,128]{3,2,1,0:T(8,128)(2,1)S(1)}) custom-call(s32[5]{0:T(128)S(1)} %stack.49.at, bf16[1024,512]{1,0:T(8,128)(2,1)S(1)} %bitcast.68, bf16[3,512,512]{2,1,0:T(8,128)(2,1)S(1)} %copy-done.3, bf16[4,2,2,256,256]{4,3,2,1,0:T(8,128)(2,1)S(1)} %copy-done.1, ...), custom_call_target="tpu_custom_call" | custom-call | tf_op jit(solution)/shard_map/encoder_backward/pallas_call | solution.py:317
  203.1 3.8 %collective-permute-done.37 = bf16[2,3,128,128]{3,2,1,0:T(8,128)(2,1)S(1)} collective-permute-done((bf16[2,3,128,128]{3,2,1,0:T(8,128)(2,1)S(1)}, bf16[2,3,128,128]{3,2,1,0:T(8,128)(2,1)S(1)}, u32[]{:S(2)}, u32[]{:S(2)}) %collective-permute-start.37) | collective-permute-done | bytes 196640 | tf_op jit(solution)/shard_map/ppermute | solution.py:37
  209.8 4.5 %collective-permute-done.39 = bf16[4,3,128,128]{3,2,1,0:T(8,128)(2,1)S(1)} collective-permute-done((bf16[4,3,128,128]{3,2,1,0:T(8,128)(2,1)S(1)}, bf16[4,3,128,128]{3,2,1,0:T(8,128)(2,1)S(1)}, u32[]{:S(2)}, u32[]{:S(2)}) %collective-permute-start.39) | collective-permute-done | bytes 393248 | tf_op jit(solution)/shard_map/ppermute | solution.py:37
  224.1 3.7 %collective-permute-done.45 = bf16[2,64,1024]{2,1,0:T(8,128)(2,1)S(1)} collective-permute-done((bf16[2,64,1024]{2,1,0:T(8,128)(2,1)S(1)}, bf16[2,64,1024]{2,1,0:T(8,128)(2,1)S(1)}, u32[]{:S(2)}, u32[]{:S(2)}) %collective-permute-start.45) | collective-permute-done | bytes 262176 | tf_op jit(solution)/shard_map/ppermute | solution.py:37
  228.2 3.0 %collective-permute-start.49 = (bf16[1,3,128,128]{3,2,1,0:T(8,128)(2,1)S(1)}, bf16[1,3,128,128]{3,2,1,0:T(8,128)(2,1)S(1)}, u32[]{:S(2)}, u32[]{:S(2)}) collective-permute-start(bf16[1,3,128,128]{3,2,1,0:T(8,128)(2,1)S(1)} %slice.232), channel_id=1, source_target_pairs={{0,8},{2,10},{4,12},{6,14},{8,0},{10,2},{12,4},{14,6},{1,9},{3,11}... | collective-permute-start | bytes 294920 | tf_op jit(solution)/shard_map/ppermute | solution.py:37
  232.4 3.6 %collective-permute-done.50 = bf16[1,64,1024]{2,1,0:T(8,128)(2,1)S(1)} collective-permute-done((bf16[1,64,1024]{2,1,0:T(8,128)(2,1)S(1)}, bf16[1,64,1024]{2,1,0:T(8,128)(2,1)S(1)}, u32[]{:S(2)}, u32[]{:S(2)}) %collective-permute-start.50) | collective-permute-done | bytes 131104 | tf_op jit(solution)/shard_map/ppermute | solution.py:37
  240.2 5.0 %collective-permute-done.48 = bf16[1,3,128,128]{3,2,1,0:T(8,128)(2,1)S(1)} collective-permute-done((bf16[1,3,128,128]{3,2,1,0:T(8,128)(2,1)S(1)}, bf16[1,3,128,128]{3,2,1,0:T(8,128)(2,1)S(1)}, u32[]{:S(2)}, u32[]{:S(2)}) %collective-permute-start.48) | collective-permute-done | bytes 98336 | tf_op jit(solution)/shard_map/ppermute | solution.py:37
  (204 shorter events, 93.0 us)
Async XLA Ops:
  2.4 18.1 %collective-permute-start = (bf16[128,1024]{1,0:T(8,128)(2,1)}, bf16[128,1024]{1,0:T(8,128)(2,1)}, u32[]{:S(2)}, u32[]{:S(2)}) collective-permute-start(bf16[128,1024]{1,0:T(8,128)(2,1)} %constant_dynamic-slice_fusion.6), channel_id=1, source_target_pairs={{0,14},{1,15},{2,0},{3,1},{4,2},{5,3},{6,4},{7,5},{8,6},{9,7},{10,... | collective-permute-start | bytes 786440 | tf_op jit(solution)/shard_map/ppermute | solution.py:51
  10.7 31.9 %collective-permute-start.4 = (bf16[512,1024]{1,0:T(8,128)(2,1)}, bf16[512,1024]{1,0:T(8,128)(2,1)}, u32[]{:S(2)}, u32[]{:S(2)}) collective-permute-start(bf16[512,1024]{1,0:T(8,128)(2,1)} %constant_dynamic-slice_fusion.4), channel_id=1, source_target_pairs={{0,2},{2,0},{4,6},{6,4},{8,10},{10,8},{12,14},{14,12},{1,3},{3,1},... | collective-permute-start | bytes 3145736 | tf_op jit(solution)/shard_map/ppermute | solution.py:37
  16.1 26.9 %collective-permute-start.8 = (bf16[128,1024]{1,0:T(8,128)(2,1)}, bf16[128,1024]{1,0:T(8,128)(2,1)}, u32[]{:S(2)}, u32[]{:S(2)}) collective-permute-start(bf16[128,1024]{1,0:T(8,128)(2,1)} %get-tuple-element.171), channel_id=1, source_target_pairs={{0,12},{2,14},{4,8},{6,10},{8,4},{10,6},{12,0},{14,2},{1,13},{3,15... | collective-permute-start | bytes 786440 | tf_op jit(solution)/shard_map/ppermute | solution.py:37
  17.1 26.5 %collective-permute-start.7 = (bf16[128,1024]{1,0:T(8,128)(2,1)}, bf16[128,1024]{1,0:T(8,128)(2,1)}, u32[]{:S(2)}, u32[]{:S(2)}) collective-permute-start(bf16[128,1024]{1,0:T(8,128)(2,1)} %get-tuple-element.172), channel_id=1, source_target_pairs={{0,4},{2,6},{4,0},{6,2},{8,12},{10,14},{12,8},{14,10},{1,5},{3,7},... | collective-permute-start | bytes 786440 | tf_op jit(solution)/shard_map/ppermute | solution.py:37
  17.1 28.1 %collective-permute-start.6 = (bf16[128,1024]{1,0:T(8,128)(2,1)}, bf16[128,1024]{1,0:T(8,128)(2,1)}, u32[]{:S(2)}, u32[]{:S(2)}) collective-permute-start(bf16[128,1024]{1,0:T(8,128)(2,1)} %get-tuple-element.173), channel_id=1, source_target_pairs={{0,8},{2,10},{4,12},{6,14},{8,0},{10,2},{12,4},{14,6},{1,9},{3,11}... | collective-permute-start | bytes 786440 | tf_op jit(solution)/shard_map/ppermute | solution.py:37
  39.8 7.4 %collective-permute-start.2 = (bf16[64,512]{1,0:T(8,128)(2,1)}, bf16[64,512]{1,0:T(8,128)(2,1)S(1)}, u32[]{:S(2)}, u32[]{:S(2)}) collective-permute-start(bf16[64,512]{1,0:T(8,128)(2,1)} %get-tuple-element.90), channel_id=1, source_target_pairs={{0,2},{1,3},{2,4},{3,5},{4,6},{5,7},{6,8},{7,9},{8,10},{9,11},{10,... | collective-permute-start | bytes 196616 | tf_op jit(solution)/shard_map/ppermute | solution.py:51
  43.6 27.7 %collective-permute-start.14 = (bf16[512,1024]{1,0:T(8,128)(2,1)}, bf16[512,1024]{1,0:T(8,128)(2,1)}, u32[]{:S(2)}, u32[]{:S(2)}) collective-permute-start(bf16[512,1024]{1,0:T(8,128)(2,1)} %collective-permute-done.4), channel_id=1, source_target_pairs={{0,16},{16,0},{1,17},{17,1},{2,18},{18,2},{3,19},{19,3},{4,20},{20... | collective-permute-start | bytes 3145736 | tf_op jit(solution)/shard_map/ppermute | solution.py:592
  55.8 24.5 %collective-permute-start.13 = (bf16[4,128,1024]{2,1,0:T(8,128)(2,1)S(1)}, bf16[4,128,1024]{2,1,0:T(8,128)(2,1)S(1)}, u32[]{:S(2)}, u32[]{:S(2)}) collective-permute-start(bf16[4,128,1024]{2,1,0:T(8,128)(2,1)S(1)} %pad_maximum_fusion.1.here), channel_id=1, source_target_pairs={{0,2},{2,0},{4,6},{6,4},{8,10},{10,8},{12,14},{14,12},{1,3},{3,1},... | collective-permute-start | bytes 3145736 | tf_op jit(solution)/shard_map/ppermute | solution.py:37
  91.5 9.3 %collective-permute-start.16 = (bf16[2,128,512]{2,1,0:T(8,128)(2,1)S(1)}, bf16[2,128,512]{2,1,0:T(8,128)(2,1)S(1)}, u32[]{:S(2)}, u32[]{:S(2)}) collective-permute-start(bf16[2,128,512]{2,1,0:T(8,128)(2,1)S(1)} %get-tuple-element.169), channel_id=1, source_target_pairs={{0,4},{2,6},{4,0},{6,2},{8,12},{10,14},{12,8},{14,10},{1,5},{3,7},... | collective-permute-start | bytes 786440 | tf_op jit(solution)/shard_map/ppermute | solution.py:37
  94.6 14.7 %collective-permute-start.21 = (f32[1,128]{1,0:T(1,128)S(1)}, f32[1,128]{1,0:T(1,128)S(1)}, u32[]{:S(2)}, u32[]{:S(2)}) collective-permute-start(f32[1,128]{1,0:T(1,128)S(1)} %slice.165), channel_id=1, source_target_pairs={{0,8},{2,10},{4,12},{6,14},{8,0},{10,2},{12,4},{14,6},{1,9},{3,11}... | collective-permute-start | bytes 1544 | tf_op jit(solution)/shard_map/ppermute | solution.py:37
  97.2 11.1 %collective-permute-start.18 = (bf16[2,128,512]{2,1,0:T(8,128)(2,1)S(1)}, bf16[2,128,512]{2,1,0:T(8,128)(2,1)S(1)}, u32[]{:S(2)}, u32[]{:S(2)}) collective-permute-start(bf16[2,128,512]{2,1,0:T(8,128)(2,1)S(1)} %get-tuple-element.170), channel_id=1, source_target_pairs={{0,4},{2,6},{4,0},{6,2},{8,12},{10,14},{12,8},{14,10},{1,5},{3,7},... | collective-permute-start | bytes 786440 | tf_op jit(solution)/shard_map/ppermute | solution.py:37
  100.9 8.5 %collective-permute-start.17 = (bf16[1,128,512]{2,1,0:T(8,128)(2,1)S(1)}, bf16[1,128,512]{2,1,0:T(8,128)(2,1)S(1)}, u32[]{:S(2)}, u32[]{:S(2)}) collective-permute-start(bf16[1,128,512]{2,1,0:T(8,128)(2,1)S(1)} %get-tuple-element.180), channel_id=1, source_target_pairs={{0,8},{2,10},{4,12},{6,14},{8,0},{10,2},{12,4},{14,6},{1,9},{3,11}... | collective-permute-start | bytes 393224 | tf_op jit(solution)/shard_map/ppermute | solution.py:37
  108.3 11.6 %collective-permute-start.22 = (bf16[1,128,512]{2,1,0:T(8,128)(2,1)S(1)}, bf16[1,128,512]{2,1,0:T(8,128)(2,1)S(1)}, u32[]{:S(2)}, u32[]{:S(2)}) collective-permute-start(bf16[1,128,512]{2,1,0:T(8,128)(2,1)S(1)} %get-tuple-element.181), channel_id=1, source_target_pairs={{0,8},{2,10},{4,12},{6,14},{8,0},{10,2},{12,4},{14,6},{1,9},{3,11}... | collective-permute-start | bytes 393224 | tf_op jit(solution)/shard_map/ppermute | solution.py:37
  109.6 12.7 %collective-permute-start.23 = (bf16[1,128,512]{2,1,0:T(8,128)(2,1)S(1)}, bf16[1,128,512]{2,1,0:T(8,128)(2,1)S(1)}, u32[]{:S(2)}, u32[]{:S(2)}) collective-permute-start(bf16[1,128,512]{2,1,0:T(8,128)(2,1)S(1)} %bitcast.78), channel_id=1, source_target_pairs={{0,8},{2,10},{4,12},{6,14},{8,0},{10,2},{12,4},{14,6},{1,9},{3,11}... | collective-permute-start | bytes 393224 | tf_op jit(solution)/shard_map/ppermute | solution.py:37
  120.9 7.9 %collective-permute-start.25 = (bf16[1,128,640]{2,1,0:T(8,128)(2,1)S(1)}, bf16[1,128,640]{2,1,0:T(8,128)(2,1)S(1)}, u32[]{:S(2)}, u32[]{:S(2)}) collective-permute-start(bf16[1,128,640]{2,1,0:T(8,128)(2,1)S(1)} %bitcast.75), channel_id=1, source_target_pairs={{0,8},{2,10},{4,12},{6,14},{8,0},{10,2},{12,4},{14,6},{1,9},{3,11}... | collective-permute-start | bytes 491528 | tf_op jit(solution)/shard_map/ppermute | solution.py:37
  122.4 10.2 %collective-permute-start.24 = (bf16[2,128,512]{2,1,0:T(8,128)(2,1)S(1)}, bf16[2,128,512]{2,1,0:T(8,128)(2,1)S(1)}, u32[]{:S(2)}, u32[]{:S(2)}) collective-permute-start(bf16[2,128,512]{2,1,0:T(8,128)(2,1)S(1)} %pad_maximum_fusion.7), channel_id=1, source_target_pairs={{0,4},{2,6},{4,0},{6,2},{8,12},{10,14},{12,8},{14,10},{1,5},{3,7},... | collective-permute-start | bytes 786440 | tf_op jit(solution)/shard_map/ppermute | solution.py:37
  128.8 9.8 %collective-permute-start.26 = (bf16[2,128,640]{2,1,0:T(8,128)(2,1)S(1)}, bf16[2,128,640]{2,1,0:T(8,128)(2,1)S(1)}, u32[]{:S(2)}, u32[]{:S(2)}) collective-permute-start(bf16[2,128,640]{2,1,0:T(8,128)(2,1)S(1)} %pad_maximum_fusion.5), channel_id=1, source_target_pairs={{0,4},{2,6},{4,0},{6,2},{8,12},{10,14},{12,8},{14,10},{1,5},{3,7},... | collective-permute-start | bytes 983048 | tf_op jit(solution)/shard_map/ppermute | solution.py:37
  150.3 8.4 %collective-permute-start.30 = (bf16[2,2,64,512]{3,2,1,0:T(8,128)(2,1)S(1)}, bf16[2,2,64,512]{3,2,1,0:T(8,128)(2,1)S(1)}, u32[]{:S(2)}, u32[]{:S(2)}) collective-permute-start(bf16[2,2,64,512]{3,2,1,0:T(8,128)(2,1)S(1)} %bitcast.91), channel_id=1, source_target_pairs={{0,4},{2,6},{4,0},{6,2},{8,12},{10,14},{12,8},{14,10},{1,5},{3,7},... | collective-permute-start | bytes 786440 | tf_op jit(solution)/shard_map/ppermute | solution.py:37
  158.8 9.4 %collective-permute-start.31 = (bf16[1,2,64,512]{3,2,1,0:T(8,128)(2,1)S(1)}, bf16[1,2,64,512]{3,2,1,0:T(8,128)(2,1)S(1)}, u32[]{:S(2)}, u32[]{:S(2)}) collective-permute-start(bf16[1,2,64,512]{3,2,1,0:T(8,128)(2,1)S(1)} %slice.211), channel_id=1, source_target_pairs={{0,8},{2,10},{4,12},{6,14},{8,0},{10,2},{12,4},{14,6},{1,9},{3,11}... | collective-permute-start | bytes 393224 | tf_op jit(solution)/shard_map/ppermute | solution.py:37
  185.8 12.1 %collective-permute-start.36 = (bf16[4,3,128,128]{3,2,1,0:T(8,128)(2,1)S(1)}, bf16[4,3,128,128]{3,2,1,0:T(8,128)(2,1)S(1)}, u32[]{:S(2)}, u32[]{:S(2)}) collective-permute-start(bf16[4,3,128,128]{3,2,1,0:T(8,128)(2,1)S(1)} %get-tuple-element.136), channel_id=1, source_target_pairs={{0,2},{2,0},{4,6},{6,4},{8,10},{10,8},{12,14},{14,12},{1,3},{3,1},... | collective-permute-start | bytes 1179656 | tf_op jit(solution)/shard_map/ppermute | solution.py:37
  188.7 18.3 %collective-permute-start.40 = (bf16[4,3,128,128]{3,2,1,0:T(8,128)(2,1)S(1)}, bf16[4,3,128,128]{3,2,1,0:T(8,128)(2,1)S(1)}, u32[]{:S(2)}, u32[]{:S(2)}) collective-permute-start(bf16[4,3,128,128]{3,2,1,0:T(8,128)(2,1)S(1)} %get-tuple-element.151), channel_id=1, source_target_pairs={{0,2},{2,0},{4,6},{6,4},{8,10},{10,8},{12,14},{14,12},{1,3},{3,1},... | collective-permute-start | bytes 1179656 | tf_op jit(solution)/shard_map/ppermute | solution.py:37
  198.1 8.9 %collective-permute-start.37 = (bf16[2,3,128,128]{3,2,1,0:T(8,128)(2,1)S(1)}, bf16[2,3,128,128]{3,2,1,0:T(8,128)(2,1)S(1)}, u32[]{:S(2)}, u32[]{:S(2)}) collective-permute-start(bf16[2,3,128,128]{3,2,1,0:T(8,128)(2,1)S(1)} %slice.216), channel_id=1, source_target_pairs={{0,4},{2,6},{4,0},{6,2},{8,12},{10,14},{12,8},{14,10},{1,5},{3,7},... | collective-permute-start | bytes 589832 | tf_op jit(solution)/shard_map/ppermute | solution.py:37
  199.1 18.5 %collective-permute-start.43 = (bf16[4,64,1024]{2,1,0:T(8,128)(2,1)S(1)}, bf16[4,64,1024]{2,1,0:T(8,128)(2,1)S(1)}, u32[]{:S(2)}, u32[]{:S(2)}) collective-permute-start(bf16[4,64,1024]{2,1,0:T(8,128)(2,1)S(1)} %get-tuple-element.157), channel_id=1, source_target_pairs={{0,2},{2,0},{4,6},{6,4},{8,10},{10,8},{12,14},{14,12},{1,3},{3,1},... | collective-permute-start | bytes 1572872 | tf_op jit(solution)/shard_map/ppermute | solution.py:37
  199.2 15.1 %collective-permute-start.39 = (bf16[4,3,128,128]{3,2,1,0:T(8,128)(2,1)S(1)}, bf16[4,3,128,128]{3,2,1,0:T(8,128)(2,1)S(1)}, u32[]{:S(2)}, u32[]{:S(2)}) collective-permute-start(bf16[4,3,128,128]{3,2,1,0:T(8,128)(2,1)S(1)} %get-tuple-element.149), channel_id=1, source_target_pairs={{0,4},{2,6},{4,0},{6,2},{8,12},{10,14},{12,8},{14,10},{1,5},{3,7},... | collective-permute-start | bytes 1179656 | tf_op jit(solution)/shard_map/ppermute | solution.py:37
  201.1 26.9 %collective-permute-start.44 = (bf16[4,3,128,128]{3,2,1,0:T(8,128)(2,1)S(1)}, bf16[4,3,128,128]{3,2,1,0:T(8,128)(2,1)S(1)}, u32[]{:S(2)}, u32[]{:S(2)}) collective-permute-start(bf16[4,3,128,128]{3,2,1,0:T(8,128)(2,1)S(1)} %get-tuple-element.161), channel_id=1, source_target_pairs={{0,2},{2,0},{4,6},{6,4},{8,10},{10,8},{12,14},{14,12},{1,3},{3,1},... | collective-permute-start | bytes 1179656 | tf_op jit(solution)/shard_map/ppermute | solution.py:37
  207.0 8.0 %collective-permute-start.38 = (bf16[1,3,128,128]{3,2,1,0:T(8,128)(2,1)S(1)}, bf16[1,3,128,128]{3,2,1,0:T(8,128)(2,1)S(1)}, u32[]{:S(2)}, u32[]{:S(2)}) collective-permute-start(bf16[1,3,128,128]{3,2,1,0:T(8,128)(2,1)S(1)} %slice.218), channel_id=1, source_target_pairs={{0,8},{2,10},{4,12},{6,14},{8,0},{10,2},{12,4},{14,6},{1,9},{3,11}... | collective-permute-start | bytes 294920 | tf_op jit(solution)/shard_map/ppermute | solution.py:37
  207.2 9.2 %collective-permute-start.41 = (bf16[2,3,128,128]{3,2,1,0:T(8,128)(2,1)S(1)}, bf16[2,3,128,128]{3,2,1,0:T(8,128)(2,1)S(1)}, u32[]{:S(2)}, u32[]{:S(2)}) collective-permute-start(bf16[2,3,128,128]{3,2,1,0:T(8,128)(2,1)S(1)} %slice.220), channel_id=1, source_target_pairs={{0,4},{2,6},{4,0},{6,2},{8,12},{10,14},{12,8},{14,10},{1,5},{3,7},... | collective-permute-start | bytes 589832 | tf_op jit(solution)/shard_map/ppermute | solution.py:37
  214.4 13.7 %collective-permute-start.47 = (bf16[2,3,128,128]{3,2,1,0:T(8,128)(2,1)S(1)}, bf16[2,3,128,128]{3,2,1,0:T(8,128)(2,1)S(1)}, u32[]{:S(2)}, u32[]{:S(2)}) collective-permute-start(bf16[2,3,128,128]{3,2,1,0:T(8,128)(2,1)S(1)} %slice.228), channel_id=1, source_target_pairs={{0,2},{2,0},{4,6},{6,4},{8,10},{10,8},{12,14},{14,12},{1,3},{3,1},... | collective-permute-start | bytes 589832 | tf_op jit(solution)/shard_map/ppermute | solution.py:37
  220.4 7.4 %collective-permute-start.45 = (bf16[2,64,1024]{2,1,0:T(8,128)(2,1)S(1)}, bf16[2,64,1024]{2,1,0:T(8,128)(2,1)S(1)}, u32[]{:S(2)}, u32[]{:S(2)}) collective-permute-start(bf16[2,64,1024]{2,1,0:T(8,128)(2,1)S(1)} %slice.224), channel_id=1, source_target_pairs={{0,4},{2,6},{4,0},{6,2},{8,12},{10,14},{12,8},{14,10},{1,5},{3,7},... | collective-permute-start | bytes 786440 | tf_op jit(solution)/shard_map/ppermute | solution.py:37
  227.9 8.2 %collective-permute-start.50 = (bf16[1,64,1024]{2,1,0:T(8,128)(2,1)S(1)}, bf16[1,64,1024]{2,1,0:T(8,128)(2,1)S(1)}, u32[]{:S(2)}, u32[]{:S(2)}) collective-permute-start(bf16[1,64,1024]{2,1,0:T(8,128)(2,1)S(1)} %slice.234), channel_id=1, source_target_pairs={{0,8},{2,10},{4,12},{6,14},{8,0},{10,2},{12,4},{14,6},{1,9},{3,11}... | collective-permute-start | bytes 393224 | tf_op jit(solution)/shard_map/ppermute | solution.py:37
  228.2 10.5 %collective-permute-start.49 = (bf16[1,3,128,128]{3,2,1,0:T(8,128)(2,1)S(1)}, bf16[1,3,128,128]{3,2,1,0:T(8,128)(2,1)S(1)}, u32[]{:S(2)}, u32[]{:S(2)}) collective-permute-start(bf16[1,3,128,128]{3,2,1,0:T(8,128)(2,1)S(1)} %slice.232), channel_id=1, source_target_pairs={{0,8},{2,10},{4,12},{6,14},{8,0},{10,2},{12,4},{14,6},{1,9},{3,11}... | collective-permute-start | bytes 294920 | tf_op jit(solution)/shard_map/ppermute | solution.py:37
  231.2 7.5 %collective-permute-start.46 = (bf16[2,3,128,128]{3,2,1,0:T(8,128)(2,1)S(1)}, bf16[2,3,128,128]{3,2,1,0:T(8,128)(2,1)S(1)}, u32[]{:S(2)}, u32[]{:S(2)}) collective-permute-start(bf16[2,3,128,128]{3,2,1,0:T(8,128)(2,1)S(1)} %slice.226), channel_id=1, source_target_pairs={{0,4},{2,6},{4,0},{6,2},{8,12},{10,14},{12,8},{14,10},{1,5},{3,7},... | collective-permute-start | bytes 589832 | tf_op jit(solution)/shard_map/ppermute | solution.py:37
  (39 other events, 401.9 us)

commit v7 on v6

--- a/solution.py
+++ b/solution.py
@@ -358,8 +358,8 @@
     return [pl.multiple_of((at[2] ^ k) * block, block) for k in offset]
 
 
-def weight_rows(here, there):
-    return jnp.concatenate([w[...].reshape(-1, w.shape[-1]) for w in (here, there)], axis=0)
+def weight_rows(blocks):
+    return jnp.concatenate([block[...] for block in blocks], axis=0)
 
 
 def both(index, size):
@@ -369,16 +369,20 @@
     )
 
 
-def kv_columns(low, at, kva, kvb, side, rows):
-    feats, cols = kva.shape[0], kvb.shape[2]
+def kv_columns(low, at, kva, near, far, side, rows, out):
+    feats, cols = kva.shape[0], near.shape[1]
     mine, across = both(at[2] % 2, feats)
     span = pl.ds(pl.multiple_of(side * cols, cols), cols)
-    part = dot(low[rows, mine], kva[:, span]) + dot(low[rows, across], kvb[side ^ at[4]])
-    return part.astype(BF)
-
-
-def lift_kernel(table, order, at, ta, tb, here, there, gain, kva, kvb, *refs):
-    lifted, squares, low, send, tok = refs
+    for place, part in enumerate((near, far)):
+
+        @pl.when(side ^ at[4] == place)
+        def _():
+            total = dot(low[rows, mine], kva[:, span]) + dot(low[rows, across], part[...])
+            out[rows] = total.astype(BF)
+
+
+def lift_kernel(table, order, at, ta, tb, gain, kva, kv_near, kv_far, *refs):
+    blocks, (lifted, squares, low, send, tok) = refs[:-5], refs[-5:]
     core = at[3]
     near, far = both(core, ta.shape[1])
     piece = ta.shape[0] // len(table) if table else 0
@@ -388,9 +392,9 @@
     if not table:
         tok[:, near] = ta[...]
         tok[:, far] = tb[...]
-    block = here.shape[1]
+    block = blocks[0].shape[0]
     starts = column_starts(order, at, block)
-    weight = weight_rows(here, there)
+    weight = weight_rows(blocks)
     group_rows = squares.shape[1]
     for rows in chunks_of(tok.shape[0]):
         x = tok[rows]
@@ -404,16 +408,16 @@
             column = sums[first : first + group_rows]
             owner = (rows.start + first) // group_rows
             squares[owner : owner + 1] = jnp.broadcast_to(column, (group_rows,) * 2).T[:1]
-        send[rows] = kv_columns(low, at, kva, kvb, 1 - core, rows)
-
-
-def lift(table, order, at, own_tok, ta, tb, here, there, gain, kva, kvb):
+        kv_columns(low, at, kva, kv_near, kv_far, 1 - core, rows, send)
+
+
+def lift(table, order, at, own_tok, ta, tb, gain, kvs, blocks):
     rows, half = ta.shape
-    feats, cols = kva.shape[0], kva.shape[1] // 2
+    feats, cols = kvs[0].shape[0], kvs[0].shape[1] // 2
     whole = pl.BlockSpec(memory_space=pltpu.VMEM)
     return pl.pallas_call(
         functools.partial(lift_kernel, table, order),
-        in_specs=[pl.BlockSpec(memory_space=pltpu.SMEM)] + [whole] * 7,
+        in_specs=[pl.BlockSpec(memory_space=pltpu.SMEM)] + [whole] * (6 + len(blocks)),
         out_specs=[whole] * 4,
         out_shape=[
             jax.ShapeDtypeStruct((rows, 2 * feats), BF),
@@ -424,24 +428,24 @@
         scratch_shapes=[pltpu.VMEM((rows, 2 * half), BF)],
         compiler_params=pltpu.CompilerParams(vmem_limit_bytes=VMEM_LIMIT),
         name="lift",
-    )(at, ta, tb, here, there, gain, kva, kvb)
-
-
-def keep_kernel(at, low, kva, kvb, keep):
+    )(at, ta, tb, gain, *kvs, *blocks)
+
+
+def keep_kernel(at, low, kva, kv_near, kv_far, keep):
     for rows in chunks_of(low.shape[0]):
-        keep[rows] = kv_columns(low, at, kva, kvb, at[3], rows)
-
-
-def keep_columns(at, low, kva, kvb):
+        kv_columns(low, at, kva, kv_near, kv_far, at[3], rows, keep)
+
+
+def keep_columns(at, low, kvs):
     whole = pl.BlockSpec(memory_space=pltpu.VMEM)
     return pl.pallas_call(
         keep_kernel,
-        in_specs=[pl.BlockSpec(memory_space=pltpu.SMEM)] + [whole] * 3,
+        in_specs=[pl.BlockSpec(memory_space=pltpu.SMEM)] + [whole] * 4,
         out_specs=whole,
-        out_shape=jax.ShapeDtypeStruct((low.shape[0], kva.shape[1] // 2), BF),
+        out_shape=jax.ShapeDtypeStruct((low.shape[0], kvs[0].shape[1] // 2), BF),
         compiler_params=pltpu.CompilerParams(vmem_limit_bytes=VMEM_LIMIT),
         name="keep_columns",
-    )(at, low, kva, kvb)
+    )(at, low, *kvs)
 
 
 def two_parts(column):
@@ -484,16 +488,16 @@
     )(mine, got, squares, d_kv, *inner)
 
 
-def lower_kernel(table, order, at, ca0, ca1, cb0, cb1, here, there, gain, kva, kvb, *refs):
-    lifted, send, keep, nat, low = refs
+def lower_kernel(table, order, at, ca0, ca1, cb0, cb1, gain, lifted, kva, kv_near, kv_far, *refs):
+    blocks, (send, keep, nat, low) = refs[:-4], refs[-4:]
     core, group = at[3], at[4]
     feats, half = kva.shape[0], send.shape[1]
     cols = kva.shape[1] // 2
     near, far = both(core, half)
     mine, across = both(at[2] % 2, feats)
-    block = here.shape[1]
+    block = blocks[0].shape[0]
     starts = column_starts(order, at, block)
-    weight = weight_rows(here, there)
+    weight = weight_rows(blocks)
     part_cols = ca0.shape[1]
     piece = ca0.shape[0] // len(table) if table else 0
     for rows in chunks_of(ca0.shape[0]):
@@ -502,19 +506,22 @@
         inv = extra[:, 0:1] + extra[:, 1:2]
         inner = extra[:, 2:3] + extra[:, 3:4] + extra_b[:, 2:3] + extra_b[:, 3:4]
         pull = inv * inv * inv * inner * (1.0 / LLM_D)
-        cots = [
-            (jnp.concatenate([c0[rows], c1[rows, :part_cols]], axis=1), side)
-            for c0, c1, side in ((ca0, ca1, core), (cb0, cb1, 1 - core))
-        ]
-        for is_mine, span in ((True, mine), (False, across)):
-            d_normed = None
-            for cot, side in cots:
-                at_side = pl.ds(pl.multiple_of(side * cols, cols), cols)
-                part = dot_nt(cot, kva[:, at_side] if is_mine else kvb[side ^ group])
-                d_normed = part if d_normed is None else d_normed + part
-            low[rows, span] = (
-                inv * gain[:, span] * d_normed - lifted[rows, span].astype(F32) * pull
-            ).astype(BF)
+        cot_a = lambda: jnp.concatenate([ca0[rows], ca1[rows, :part_cols]], axis=1)
+        cot_b = lambda: jnp.concatenate([cb0[rows], cb1[rows, :part_cols]], axis=1)
+
+        def put(span, weight_a, weight_b):
+            d_normed = dot_nt(cot_a(), weight_a) + dot_nt(cot_b(), weight_b)
+            scaled = inv * gain[:, span] * d_normed
+            low[rows, span] = (scaled - lifted[rows, span].astype(F32) * pull).astype(BF)
+
+        own_cols, other_cols = both(core, cols)
+        put(mine, kva[:, own_cols], kva[:, other_cols])
+        for place, pair in enumerate(((kv_near, kv_far), (kv_far, kv_near))):
+
+            @pl.when(core ^ group == place)
+            def _():
+                put(across, pair[0][...], pair[1][...])
+
         d_tok = dot_nt(low[rows], weight).astype(BF)
         if not starts:
             nat[rows] = d_tok
@@ -528,20 +535,20 @@
         keep[...] = nat[:, near]
 
 
-def lower(table, order, at, cots, here, there, gain, kva, kvb, lifted):
+def lower(table, order, at, cots, gain, lifted, kvs, blocks):
     rows, width = cots[0].shape[0], lifted.shape[1]
-    tok_width = 2 * here.shape[0] * here.shape[1]
+    tok_width = len(blocks) * blocks[0].shape[0]
     whole = pl.BlockSpec(memory_space=pltpu.VMEM)
     out = jax.ShapeDtypeStruct((rows, tok_width // 2), BF)
     return pl.pallas_call(
         functools.partial(lower_kernel, table, order),
-        in_specs=[pl.BlockSpec(memory_space=pltpu.SMEM)] + [whole] * 10,
+        in_specs=[pl.BlockSpec(memory_space=pltpu.SMEM)] + [whole] * (9 + len(blocks)),
         out_specs=[whole] * 2,
         out_shape=[out] * 2,
         scratch_shapes=[pltpu.VMEM((rows, tok_width), BF), pltpu.VMEM((rows, width), BF)],
         compiler_params=pltpu.CompilerParams(vmem_limit_bytes=VMEM_LIMIT),
         name="lower",
-    )(at, *cots, here, there, gain, kva, kvb, lifted)
+    )(at, *cots, gain, lifted, *kvs, *blocks)
 
 
 def on_device(frames, weight_qkv, weight_out, proj_in, norm_gain, proj_kv, shifts, route, d_kv):
@@ -577,6 +584,7 @@
     for k in order:
         pair = lax.dynamic_slice_in_dim(proj_in, (me ^ k) // 2 * 2 * feats, 2 * feats, 1)
         blocks.append(swap_tm(pair, k) if k else pair)
+    across = [swap_tm(blocks[0], SPLIT)]
 
     other = swap_mp(mine)
     halo = jnp.where(
@@ -588,7 +596,10 @@
     normed, qkv, probs, pooled_attn, own_near, own_far, tail_near, tail_far = encoder_forward(
         x_roll, w_t, weight_out, at, ext_tok
     )
-    own_far, kv_near = lax.optimization_barrier((own_far, kv_near))
+    own_far, kv_near, across, blocks[1:-1] = lax.optimization_barrier(
+        (own_far, kv_near, across, blocks[1:-1])
+    )
+    across += [swap_tm(block, SPLIT) for block in blocks[1:-1]]
     swap_groups = lambda block: lax.ppermute(block, "groups", [(0, 1), (1, 0)])
     if two_groups:
         kv_far = swap_groups(kv_near)
@@ -613,9 +624,6 @@
     from_core = swap_mp(own_far)
     tail_a = to_tm(tail_near, 1, False)
     tail_b = to_tm(tail_far, 1, True)
-    tail_a, tail_b, from_core, blocks = lax.optimization_barrier(
-        (tail_a, tail_b, from_core, blocks)
-    )
     own_pool = (
         jnp.arange(rows, dtype=jnp.int32)[None, :] // POOL
         == jnp.arange(own_tok, dtype=jnp.int32)[:, None]
@@ -627,25 +635,25 @@
 
     sorted_tok = dot(sort, pooled).astype(BF).reshape(2, count * piece, half_w)
     handed = swap_tm(sorted_tok[1], SPLIT)
-    here = jnp.stack(blocks)
-    handed, here = lax.optimization_barrier((handed, here))
-    there = swap_tm(here, SPLIT)
+    handed, across, blocks[-1] = lax.optimization_barrier((handed, across, blocks[-1]))
+    last_across = swap_tm(blocks[-1], SPLIT)
     pair_tok = jnp.stack([sorted_tok[0], handed])
     tok_half = gather_doubling(pair_tok, masks[-1:])
-    tok_half, turned, d_kv = lax.optimization_barrier((tok_half, turned, d_kv))
-    kva, kvb = proj_kv, jnp.stack([kv_near, kv_far])
+    tok_half, turned, d_kv, last_across = lax.optimization_barrier(
+        (tok_half, turned, d_kv, last_across)
+    )
+    blocks += across + [last_across]
     at_rows = order
     if width // n % LANES:
-        stacked = jnp.concatenate([here, there])
         source = jnp.arange(n, dtype=jnp.int32) ^ me
         found = source[:, None] == jnp.array(members, jnp.int32)[None, :]
         place = jnp.sum(found * jnp.arange(n, dtype=jnp.int32)[None, :], axis=1)
-        stacked = jnp.take(stacked, place, axis=0)
-        here, there = jnp.split(stacked, 2)
+        blocks = list(jnp.take(jnp.stack(blocks), place, axis=0))
         at_rows = None
     for mask in reversed(masks[:-1]):
         tok_half = jnp.concatenate([tok_half, swap_tm(tok_half, mask)], axis=0)
-    tok_half = tok_half.reshape(-1, half_w)
+    tok_half, kv_far = lax.optimization_barrier((tok_half.reshape(-1, half_w), kv_far))
+    kvs = (proj_kv, kv_near, kv_far)
     tok_other = swap_mp(tok_half)
     table = list(moves(order, piece))
     source_rows = np.concatenate([np.arange(r, r + piece) for r, _ in table])
@@ -656,10 +664,10 @@
         tok_half, tok_other = tok_half[at_owner], tok_other[at_owner]
         table = []
     lifted, squares, scaled, kv_send = lift(
-        table, at_rows, at, own_tok, tok_half, tok_other, here, there, gain, kva, kvb
+        table, at_rows, at, own_tok, tok_half, tok_other, gain, kvs, blocks
     )
     kv_got = swap_mp(kv_send)
-    kv_keep = keep_columns(at, scaled, kva, kvb)
+    kv_keep = keep_columns(at, scaled, kvs)
     square_sum = scatter_halving(squares + swap_mp(squares), masks, F32)
     kv_part = (kv_keep.astype(F32) + kv_got.astype(F32)).astype(BF)
     kv_parts = jnp.split(kv_part.reshape(count, own_tok, kv_half), 2, axis=2)
@@ -672,9 +680,7 @@
     loads = gather_parts([load_a, load_b], masks)
     loads = [load.reshape(count * own_tok, -1) for load in loads]
     cots = loads + [swap_mp(load) for load in loads]
-    d_send, d_keep = lower(
-        table, at_rows, at, cots, here, there, gain, kva, kvb, lifted
-    )
+    d_send, d_keep = lower(table, at_rows, at, cots, gain, lifted, kvs, blocks)
     if by_xla:
         at_source = owner_rows[np.argsort(source_rows)]
         d_send, d_keep = d_send[at_source], d_keep[at_source]
@@ -702,7 +708,7 @@
     chunks.append((out_even, out_odd, bits))
     steps = list(range(len(chunks))) * len(bits)
     if len(bits) == 3:
-        steps = [0, 0, 1, 3, 0, 1, 4, 1, 4, 2, 3, 4, 2, 3, 2]
+        steps = [0, 0, 1, 3, 0, 1, 4, 2, 1, 4, 3, 2, 4, 3, 2]
     chunks = scatter_chunks(chunks, steps, even)
     grad_out = chunks.pop()
     grad_qkv = jnp.transpose(jnp.concatenate(chunks, axis=-1), (1, 0, 2))

time: 247 us -> 251 us (1.016)
  starting transfers between devices: 56.6 us -> 63.1 us
  other arithmetic: 13.7 us -> 9.2 us
    ppermute x36 -> x39, starting transfers between devices: 40 us -> 47.5 us  [swap_tm(): return lax.ppermute(block, 'tm', [(i, i ^ mask) for i in range(n)])]
    another operation x4 -> x2, other arithmetic: 4.43 us -> 0.06 us  [the longest x1 3.13 us: on_device(): kva, kvb = (proj_kv, jnp.stack([kv_near, kv_far]))]
    ppermute x5, waiting for transfers between devices: 7.99 us -> 4.09 us  [to_tm(): return lax.ppermute(block, ('tm', 'mp'), pairs)]
    ppermute x36 -> x39, waiting for transfers between devices: 100 us -> 101 us  [swap_tm(): return lax.ppermute(block, 'tm', [(i, i ^ mask) for i in range(n)])]
  transfers between devices with their start and end apart: 51 -> 54, of which waited for: 31 -> 32; matrix products, arithmetic and copies ran while one was open for 11% -> 9% of each run, Pallas kernels for 10% -> 10%
where the time goes in v7:
time: 251 us; the launch traced here: 250 us
  waiting for transfers between devices  111 us (44%)
  starting transfers between devices  63.1 us (25%)
  Pallas kernels  41.5 us (17%)
  local copies, waits for them, and re-layouts  17.9 us (7%)
  other arithmetic  9.2 us (4%)
  between operations  4.08 us (2%)
  matrix products  2.88 us (1%)
    ppermute x39, waiting for transfers between devices, swap_tm(): return lax.ppermute(block, 'tm', [(i, i ^ mask) for i in range(n)])  101 us
    ppermute x39, starting transfers between devices, swap_tm(): return lax.ppermute(block, 'tm', [(i, i ^ mask) for i in range(n)])  47.5 us
    ppermute x5, starting transfers between devices, to_tm(): return lax.ppermute(block, ('tm', 'mp'), pairs)  12.1 us
    pallas_call x1, Pallas kernels, encoder_forward(): pl.pallas_call(forward_kernel, grid_spec=pltpu.PrefetchScalarGridSpec(num...  11.1 us
    pallas_call x4, Pallas kernels, encoder_backward(): pl.pallas_call(functools.partial(backward_kernel, masks), grid_spec=pltpu...  11 us
    pallas_call x1, Pallas kernels, lower(): pl.pallas_call(functools.partial(lower_kernel, table, order), in_specs=[p...  7.01 us
    pallas_call x1, Pallas kernels, lift(): pl.pallas_call(functools.partial(lift_kernel, table, order), in_specs=[pl...  6.25 us
    ppermute x9, waiting for transfers between devices, swap_mp(): return lax.ppermute(block, 'mp', [(i, n - 1 - i) for i in range(n)])  5.83 us
  transfers between devices with their start and end apart: 54, of which 32 were waited for; matrix products, arithmetic and copies ran while one was open for 9% of the time, Pallas kernels for 10%

profile of v7, /device:TPU:0, one launch (start us, length us, event | category | flops | bytes accessed | tf_op | source)
XLA Modules:
  0.0 249.7 jit_solution(5729408806914981223)
XLA Ops:
  2.4 6.0 %collective-permute-start = (bf16[128,1024]{1,0:T(8,128)(2,1)}, bf16[128,1024]{1,0:T(8,128)(2,1)}, u32[]{:S(2)}, u32[]{:S(2)}) collective-permute-start(bf16[128,1024]{1,0:T(8,128)(2,1)} %constant_dynamic-slice_fusion.6), channel_id=1, source_target_pairs={{0,14},{1,15},{2,0},{3,1},{4,2},{5,3},{6,4},{7,5},{8,6},{9,7},{10,... | collective-permute-start | bytes 786440 | tf_op jit(solution)/shard_map/ppermute | solution.py:51
  10.7 3.2 %copy.14 = bf16[3,512,1024]{2,1,0:T(8,128)(2,1)S(1)} copy(bf16[3,512,1024]{1,2,0:T(8,128)(2,1)} %bitcast.82) | data formatting | bytes 6291456 | tf_op jit(solution)/shard_map/transpose | solution.py:570
  17.2 3.3 %collective-permute-start.4 = (bf16[128,1024]{1,0:T(8,128)(2,1)}, bf16[128,1024]{1,0:T(8,128)(2,1)}, u32[]{:S(2)}, u32[]{:S(2)}) collective-permute-start(bf16[128,1024]{1,0:T(8,128)(2,1)} %get-tuple-element.177), channel_id=1, source_target_pairs={{0,8},{2,10},{4,12},{6,14},{8,0},{10,2},{12,4},{14,6},{1,9},{3,11}... | collective-permute-start | bytes 786440 | tf_op jit(solution)/shard_map/ppermute | solution.py:37
  30.1 11.1 %encoder_forward.1 = (bf16[512,1024]{1,0:T(8,128)(2,1)}, bf16[3,512,512]{2,1,0:T(8,128)(2,1)}, bf16[4,2,2,256,256]{4,3,2,1,0:T(8,128)(2,1)}, bf16[192,512]{1,0:T...) custom-call(s32[5]{0:T(128)S(1)} %stack.25.at, ...), custom_call_target="tpu_custom_call" | custom-call | tf_op jit(solution)/shard_map/encoder_forward/pallas_call | solution.py:206
  54.7 9.0 %collective-permute-done.9 = bf16[64,512]{1,0:T(8,128)(2,1)} collective-permute-done((bf16[64,512]{1,0:T(8,128)(2,1)}, bf16[64,512]{1,0:T(8,128)(2,1)}, u32[]{:S(2)}, u32[]{:S(2)}) %collective-permute-start.9) | collective-permute-done | bytes 65568 | tf_op jit(solution)/shard_map/ppermute | solution.py:37
  64.9 6.5 %collective-permute-done.13 = bf16[1,2,64,512]{3,2,1,0:T(8,128)(2,1)S(1)} collective-permute-done((bf16[1,2,64,512]{3,2,1,0:T(8,128)(2,1)S(1)}, bf16[1,2,64,512]{3,2,1,0:T(8,128)(2,1)S(1)}, u32[]{:S(2)}, u32[]{:S(2)}) %collective-permute-start.13) | collective-permute-done | bytes 131104 | tf_op jit(solution)/shard_map/ppermute | solution.py:37
  73.3 6.6 %collective-permute-done.15 = bf16[2,2,64,512]{3,2,1,0:T(8,128)(2,1)S(1)} collective-permute-done((bf16[2,2,64,512]{3,2,1,0:T(8,128)(2,1)S(1)}, bf16[2,2,64,512]{3,2,1,0:T(8,128)(2,1)S(1)}, u32[]{:S(2)}, u32[]{:S(2)}) %collective-permute-start.15) | collective-permute-done | bytes 262176 | tf_op jit(solution)/shard_map/ppermute | solution.py:37
  82.0 6.2 %lift.1 = (bf16[512,1024]{1,0:T(8,128)(2,1)S(1)}, f32[4,128]{1,0:T(4,128)S(1)}, bf16[512,1024]{1,0:T(8,128)(2,1)S(1)}, bf16[512,1024]{1,0:T(8,128)(2,1)}) custom-call(s32[5]{0:T(128)S(1)} %stack.25.at, bf16[512,512]{1,0:T(8,128)(2,1)S(1)} %bitcast.68, bf16[512,512]{1,0:T(8,128)(2,1)S(1)} %collective-permute-done.17.tb, f32[1,1024]{1,0:T(1,128)S(1)} %bitcast.77, ...), custom_call_target="tpu_custom_call" | custom-call | tf_op jit(solution)/shard_map/lift/pallas_call | solution.py:418
  91.0 3.3 %keep_columns.1 = bf16[512,1024]{1,0:T(8,128)(2,1)S(1)} custom-call(s32[5]{0:T(128)S(1)} %stack.25.at, bf16[512,1024]{1,0:T(8,128)(2,1)S(1)} %get-tuple-element.114.low, bf16[512,2048]{1,0:T(8,128)(2,1)} %kva.2, bf16[512,1024]{1,0:T(8,128)(2,1)} %collective-permute-done.2.kv_near, bf16[512,1024]{1,0:T(8,128)(2,1)S(1)} %copy-done.4), custom_call_target="tpu_custom_call" | custom-call | tf_op jit(solution)/shard_map/keep_columns/pallas_call | solution.py:441
  100.5 3.9 %collective-permute-done.19 = bf16[2,128,512]{2,1,0:T(8,128)(2,1)S(1)} collective-permute-done((bf16[2,128,512]{2,1,0:T(8,128)(2,1)S(1)}, bf16[2,128,512]{2,1,0:T(8,128)(2,1)S(1)}, u32[]{:S(2)}, u32[]{:S(2)}) %collective-permute-start.19) | collective-permute-done | bytes 262176 | tf_op jit(solution)/shard_map/ppermute | solution.py:37
  106.8 4.9 %collective-permute-done.21 = bf16[2,128,512]{2,1,0:T(8,128)(2,1)S(1)} collective-permute-done((bf16[2,128,512]{2,1,0:T(8,128)(2,1)S(1)}, bf16[2,128,512]{2,1,0:T(8,128)(2,1)S(1)}, u32[]{:S(2)}, u32[]{:S(2)}) %collective-permute-start.21) | collective-permute-done | bytes 262176 | tf_op jit(solution)/shard_map/ppermute | solution.py:37
  115.2 6.7 %collective-permute-done.25 = bf16[1,128,512]{2,1,0:T(8,128)(2,1)S(1)} collective-permute-done((bf16[1,128,512]{2,1,0:T(8,128)(2,1)S(1)}, bf16[1,128,512]{2,1,0:T(8,128)(2,1)S(1)}, u32[]{:S(2)}, u32[]{:S(2)}) %collective-permute-start.25) | collective-permute-done | bytes 131104 | tf_op jit(solution)/shard_map/ppermute | solution.py:37
  123.5 5.4 %collective-permute-start.27 = (bf16[2,128,512]{2,1,0:T(8,128)(2,1)S(1)}, bf16[2,128,512]{2,1,0:T(8,128)(2,1)S(1)}, u32[]{:S(2)}, u32[]{:S(2)}) collective-permute-start(bf16[2,128,512]{2,1,0:T(8,128)(2,1)S(1)} %pad_maximum_fusion.5), channel_id=1, source_target_pairs={{0,4},{2,6},{4,0},{6,2},{8,12},{10,14},{12,8},{14,10},{1,5},{3,7},... | collective-permute-start | bytes 786440 | tf_op jit(solution)/shard_map/ppermute | solution.py:37
  128.9 3.6 %collective-permute-done.28 = bf16[1,128,640]{2,1,0:T(8,128)(2,1)S(1)} collective-permute-done((bf16[1,128,640]{2,1,0:T(8,128)(2,1)S(1)}, bf16[1,128,640]{2,1,0:T(8,128)(2,1)S(1)}, u32[]{:S(2)}, u32[]{:S(2)}) %collective-permute-start.28) | collective-permute-done | bytes 163872 | tf_op jit(solution)/shard_map/ppermute | solution.py:37
  135.4 6.7 %collective-permute-done.29 = bf16[2,128,640]{2,1,0:T(8,128)(2,1)S(1)} collective-permute-done((bf16[2,128,640]{2,1,0:T(8,128)(2,1)S(1)}, bf16[2,128,640]{2,1,0:T(8,128)(2,1)S(1)}, u32[]{:S(2)}, u32[]{:S(2)}) %collective-permute-start.29) | collective-permute-done | bytes 327712 | tf_op jit(solution)/shard_map/ppermute | solution.py:37
  145.1 7.0 %lower.1 = (bf16[512,512]{1,0:T(8,128)(2,1)S(1)}, bf16[512,512]{1,0:T(8,128)(2,1)S(1)}) custom-call(s32[5]{0:T(128)S(1)} %stack.25.at, bf16[512,512]{1,0:T(8,128)(2,1)S(1)} %bitcast.66, bf16[512,640]{1,0:T(8,128)(2,1)S(1)} %bitcast.64, bf16[512,512]{1,0:T(8,128)(2,1)S(1)} %collective-permute-done.30.cb0, bf16[512,640]{1,0:T(8,128)(2,1)S(1)} %collective-permute-done.31.cb1, ...), custom_call_target="tpu_custom_call" | custom-call | tf_op jit(solution)/shard_map/lower/pallas_call | solution.py:543
  154.6 8.2 %collective-permute-done.33 = bf16[2,2,64,512]{3,2,1,0:T(8,128)(2,1)S(1)} collective-permute-done((bf16[2,2,64,512]{3,2,1,0:T(8,128)(2,1)S(1)}, bf16[2,2,64,512]{3,2,1,0:T(8,128)(2,1)S(1)}, u32[]{:S(2)}, u32[]{:S(2)}) %collective-permute-start.33) | collective-permute-done | bytes 262176 | tf_op jit(solution)/shard_map/ppermute | solution.py:37
  162.9 3.8 %collective-permute-start.34 = (bf16[1,2,64,512]{3,2,1,0:T(8,128)(2,1)S(1)}, bf16[1,2,64,512]{3,2,1,0:T(8,128)(2,1)S(1)}, u32[]{:S(2)}, u32[]{:S(2)}) collective-permute-start(bf16[1,2,64,512]{3,2,1,0:T(8,128)(2,1)S(1)} %slice.211), channel_id=1, source_target_pairs={{0,8},{2,10},{4,12},{6,14},{8,0},{10,2},{12,4},{14,6},{1,9},{3,11}... | collective-permute-start | bytes 393224 | tf_op jit(solution)/shard_map/ppermute | solution.py:37
  166.6 6.1 %collective-permute-done.34 = bf16[1,2,64,512]{3,2,1,0:T(8,128)(2,1)S(1)} collective-permute-done((bf16[1,2,64,512]{3,2,1,0:T(8,128)(2,1)S(1)}, bf16[1,2,64,512]{3,2,1,0:T(8,128)(2,1)S(1)}, u32[]{:S(2)}, u32[]{:S(2)}) %collective-permute-start.34) | collective-permute-done | bytes 131104 | tf_op jit(solution)/shard_map/ppermute | solution.py:37
  172.9 4.2 %collective-permute-done.35 = bf16[64,512]{1,0:T(8,128)(2,1)S(1)} collective-permute-done((bf16[64,512]{1,0:T(8,128)(2,1)S(1)}, bf16[64,512]{1,0:T(8,128)(2,1)S(1)}, u32[]{:S(2)}, u32[]{:S(2)}) %collective-permute-start.35) | collective-permute-done | bytes 65568 | tf_op jit(solution)/shard_map/ppermute | solution.py:37
  177.4 3.0 %collective-permute-start.38 = (bf16[64,512]{1,0:T(8,128)(2,1)S(1)}, bf16[64,512]{1,0:T(8,128)(2,1)S(1)}, u32[]{:S(2)}, u32[]{:S(2)}) collective-permute-start(bf16[64,512]{1,0:T(8,128)(2,1)S(1)} %slice.214), channel_id=1, source_target_pairs={{0,15},{1,14},{2,1},{3,0},{4,3},{5,2},{6,5},{7,4},{8,7},{9,6},{10,... | collective-permute-start | bytes 196616 | tf_op jit(solution)/shard_map/ppermute | solution.py:51
  186.5 2.8 %encoder_backward.4 = (bf16[4,3,128,128]{3,2,1,0:T(8,128)(2,1)S(1)}, bf16[4,3,128,128]{3,2,1,0:T(8,128)(2,1)S(1)}) custom-call(s32[5]{0:T(128)S(1)} %stack.25.at, bf16[1024,512]{1,0:T(8,128)(2,1)S(1)} %bitcast.59, bf16[3,512,512]{2,1,0:T(8,128)(2,1)S(1)} %copy-done.2, bf16[4,2,2,256,256]{4,3,2,1,0:T(8,128)(2,1)S(1)} %copy-done.1, ...), custom_call_target="tpu_custom_call" | custom-call | tf_op jit(solution)/shard_map/encoder_backward/pallas_call | solution.py:317
  189.3 2.8 %encoder_backward.5 = (bf16[4,3,128,128]{3,2,1,0:T(8,128)(2,1)S(1)}, bf16[4,3,128,128]{3,2,1,0:T(8,128)(2,1)S(1)}) custom-call(s32[5]{0:T(128)S(1)} %stack.25.at, bf16[1024,512]{1,0:T(8,128)(2,1)S(1)} %bitcast.60, bf16[3,512,512]{2,1,0:T(8,128)(2,1)S(1)} %copy-done.2, bf16[4,2,2,256,256]{4,3,2,1,0:T(8,128)(2,1)S(1)} %copy-done.1, ...), custom_call_target="tpu_custom_call" | custom-call | tf_op jit(solution)/shard_map/encoder_backward/pallas_call | solution.py:317
  194.2 2.8 %encoder_backward.6 = (bf16[4,3,128,128]{3,2,1,0:T(8,128)(2,1)S(1)}, bf16[4,3,128,128]{3,2,1,0:T(8,128)(2,1)S(1)}) custom-call(s32[5]{0:T(128)S(1)} %stack.25.at, bf16[1024,512]{1,0:T(8,128)(2,1)S(1)} %bitcast.61, bf16[3,512,512]{2,1,0:T(8,128)(2,1)S(1)} %copy-done.2, bf16[4,2,2,256,256]{4,3,2,1,0:T(8,128)(2,1)S(1)} %copy-done.1, ...), custom_call_target="tpu_custom_call" | custom-call | tf_op jit(solution)/shard_map/encoder_backward/pallas_call | solution.py:317
  197.0 2.8 %encoder_backward.7 = (bf16[4,3,128,128]{3,2,1,0:T(8,128)(2,1)S(1)}, bf16[4,3,128,128]{3,2,1,0:T(8,128)(2,1)S(1)}) custom-call(s32[5]{0:T(128)S(1)} %stack.25.at, bf16[1024,512]{1,0:T(8,128)(2,1)S(1)} %bitcast.62, bf16[3,512,512]{2,1,0:T(8,128)(2,1)S(1)} %copy-done.2, bf16[4,2,2,256,256]{4,3,2,1,0:T(8,128)(2,1)S(1)} %copy-done.1, ...), custom_call_target="tpu_custom_call" | custom-call | tf_op jit(solution)/shard_map/encoder_backward/pallas_call | solution.py:317
  206.6 2.8 %collective-permute-done.40 = bf16[2,3,128,128]{3,2,1,0:T(8,128)(2,1)S(1)} collective-permute-done((bf16[2,3,128,128]{3,2,1,0:T(8,128)(2,1)S(1)}, bf16[2,3,128,128]{3,2,1,0:T(8,128)(2,1)S(1)}, u32[]{:S(2)}, u32[]{:S(2)}) %collective-permute-start.40) | collective-permute-done | bytes 196640 | tf_op jit(solution)/shard_map/ppermute | solution.py:37
  213.8 3.9 %collective-permute-done.42 = bf16[4,3,128,128]{3,2,1,0:T(8,128)(2,1)S(1)} collective-permute-done((bf16[4,3,128,128]{3,2,1,0:T(8,128)(2,1)S(1)}, bf16[4,3,128,128]{3,2,1,0:T(8,128)(2,1)S(1)}, u32[]{:S(2)}, u32[]{:S(2)}) %collective-permute-start.42) | collective-permute-done | bytes 393248 | tf_op jit(solution)/shard_map/ppermute | solution.py:37
  221.0 4.5 %collective-permute-start.45 = (bf16[1,3,128,128]{3,2,1,0:T(8,128)(2,1)S(1)}, bf16[1,3,128,128]{3,2,1,0:T(8,128)(2,1)S(1)}, u32[]{:S(2)}, u32[]{:S(2)}) collective-permute-start(bf16[1,3,128,128]{3,2,1,0:T(8,128)(2,1)S(1)} %slice.222), channel_id=1, source_target_pairs={{0,8},{2,10},{4,12},{6,14},{8,0},{10,2},{12,4},{14,6},{1,9},{3,11}... | collective-permute-start | bytes 294920 | tf_op jit(solution)/shard_map/ppermute | solution.py:37
  225.8 3.6 %collective-permute-done.46 = bf16[4,3,128,128]{3,2,1,0:T(8,128)(2,1)S(1)} collective-permute-done((bf16[4,3,128,128]{3,2,1,0:T(8,128)(2,1)S(1)}, bf16[4,3,128,128]{3,2,1,0:T(8,128)(2,1)S(1)}, u32[]{:S(2)}, u32[]{:S(2)}) %collective-permute-start.46) | collective-permute-done | bytes 393248 | tf_op jit(solution)/shard_map/ppermute | solution.py:37
  229.7 4.9 %collective-permute-done.50 = bf16[2,64,1024]{2,1,0:T(8,128)(2,1)S(1)} collective-permute-done((bf16[2,64,1024]{2,1,0:T(8,128)(2,1)S(1)}, bf16[2,64,1024]{2,1,0:T(8,128)(2,1)S(1)}, u32[]{:S(2)}, u32[]{:S(2)}) %collective-permute-start.50) | collective-permute-done | bytes 262176 | tf_op jit(solution)/shard_map/ppermute | solution.py:37
  234.9 2.9 %collective-permute-start.53 = (bf16[1,64,1024]{2,1,0:T(8,128)(2,1)S(1)}, bf16[1,64,1024]{2,1,0:T(8,128)(2,1)S(1)}, u32[]{:S(2)}, u32[]{:S(2)}) collective-permute-start(bf16[1,64,1024]{2,1,0:T(8,128)(2,1)S(1)} %slice.234), channel_id=1, source_target_pairs={{0,8},{2,10},{4,12},{6,14},{8,0},{10,2},{12,4},{14,6},{1,9},{3,11}... | collective-permute-start | bytes 393224 | tf_op jit(solution)/shard_map/ppermute | solution.py:37
  239.0 6.6 %collective-permute-done.52 = bf16[1,3,128,128]{3,2,1,0:T(8,128)(2,1)S(1)} collective-permute-done((bf16[1,3,128,128]{3,2,1,0:T(8,128)(2,1)S(1)}, bf16[1,3,128,128]{3,2,1,0:T(8,128)(2,1)S(1)}, u32[]{:S(2)}, u32[]{:S(2)}) %collective-permute-start.52) | collective-permute-done | bytes 98336 | tf_op jit(solution)/shard_map/ppermute | solution.py:37
  (204 shorter events, 86.7 us)
Async XLA Ops:
  2.4 18.1 %collective-permute-start = (bf16[128,1024]{1,0:T(8,128)(2,1)}, bf16[128,1024]{1,0:T(8,128)(2,1)}, u32[]{:S(2)}, u32[]{:S(2)}) collective-permute-start(bf16[128,1024]{1,0:T(8,128)(2,1)} %constant_dynamic-slice_fusion.6), channel_id=1, source_target_pairs={{0,14},{1,15},{2,0},{3,1},{4,2},{5,3},{6,4},{7,5},{8,6},{9,7},{10,... | collective-permute-start | bytes 786440 | tf_op jit(solution)/shard_map/ppermute | solution.py:51
  10.7 33.7 %collective-permute-start.2 = (bf16[512,1024]{1,0:T(8,128)(2,1)}, bf16[512,1024]{1,0:T(8,128)(2,1)}, u32[]{:S(2)}, u32[]{:S(2)}) collective-permute-start(bf16[512,1024]{1,0:T(8,128)(2,1)} %constant_dynamic-slice_fusion.4), channel_id=1, source_target_pairs={{0,2},{2,0},{4,6},{6,4},{8,10},{10,8},{12,14},{14,12},{1,3},{3,1},... | collective-permute-start | bytes 3145736 | tf_op jit(solution)/shard_map/ppermute | solution.py:37
  16.1 38.6 %collective-permute-start.12 = (bf16[128,1024]{1,0:T(8,128)(2,1)}, bf16[128,1024]{1,0:T(8,128)(2,1)}, u32[]{:S(2)}, u32[]{:S(2)}) collective-permute-start(bf16[128,1024]{1,0:T(8,128)(2,1)} %get-tuple-element.175), channel_id=1, source_target_pairs={{0,12},{2,14},{4,8},{6,10},{8,4},{10,6},{12,0},{14,2},{1,13},{3,15... | collective-permute-start | bytes 786440 | tf_op jit(solution)/shard_map/ppermute | solution.py:37
  17.2 25.5 %collective-permute-start.5 = (bf16[128,1024]{1,0:T(8,128)(2,1)}, bf16[128,1024]{1,0:T(8,128)(2,1)}, u32[]{:S(2)}, u32[]{:S(2)}) collective-permute-start(bf16[128,1024]{1,0:T(8,128)(2,1)} %get-tuple-element.176), channel_id=1, source_target_pairs={{0,4},{2,6},{4,0},{6,2},{8,12},{10,14},{12,8},{14,10},{1,5},{3,7},... | collective-permute-start | bytes 786440 | tf_op jit(solution)/shard_map/ppermute | solution.py:37
  17.2 25.5 %collective-permute-start.4 = (bf16[128,1024]{1,0:T(8,128)(2,1)}, bf16[128,1024]{1,0:T(8,128)(2,1)}, u32[]{:S(2)}, u32[]{:S(2)}) collective-permute-start(bf16[128,1024]{1,0:T(8,128)(2,1)} %get-tuple-element.177), channel_id=1, source_target_pairs={{0,8},{2,10},{4,12},{6,14},{8,0},{10,2},{12,4},{14,6},{1,9},{3,11}... | collective-permute-start | bytes 786440 | tf_op jit(solution)/shard_map/ppermute | solution.py:37
  24.4 19.3 %collective-permute-start.3 = (bf16[128,1024]{1,0:T(8,128)(2,1)}, bf16[128,1024]{1,0:T(8,128)(2,1)S(1)}, u32[]{:S(2)}, u32[]{:S(2)}) collective-permute-start(bf16[128,1024]{1,0:T(8,128)(2,1)} %get-tuple-element.178.refs_0_), channel_id=1, source_target_pairs={{0,2},{2,0},{4,6},{6,4},{8,10},{10,8},{12,14},{14,12},{1,3},{3,1},... | collective-permute-start | bytes 786440 | tf_op jit(solution)/shard_map/ppermute | solution.py:37
  42.7 9.4 %collective-permute-start.8 = (bf16[64,512]{1,0:T(8,128)(2,1)}, bf16[64,512]{1,0:T(8,128)(2,1)S(1)}, u32[]{:S(2)}, u32[]{:S(2)}) collective-permute-start(bf16[64,512]{1,0:T(8,128)(2,1)} %get-tuple-element.97), channel_id=1, source_target_pairs={{0,3},{1,2},{2,5},{3,4},{4,7},{5,6},{6,9},{7,8},{8,11},{9,10},{10,... | collective-permute-start | bytes 196616 | tf_op jit(solution)/shard_map/ppermute | solution.py:51
  45.2 18.4 %collective-permute-start.10 = (bf16[128,1024]{1,0:T(8,128)(2,1)}, bf16[128,1024]{1,0:T(8,128)(2,1)S(1)}, u32[]{:S(2)}, u32[]{:S(2)}) collective-permute-start(bf16[128,1024]{1,0:T(8,128)(2,1)} %collective-permute-done.4.refs_1_), channel_id=1, source_target_pairs={{0,2},{2,0},{4,6},{6,4},{8,10},{10,8},{12,14},{14,12},{1,3},{3,1},... | collective-permute-start | bytes 786440 | tf_op jit(solution)/shard_map/ppermute | solution.py:37
  45.9 17.8 %collective-permute-start.11 = (bf16[128,1024]{1,0:T(8,128)(2,1)}, bf16[128,1024]{1,0:T(8,128)(2,1)S(1)}, u32[]{:S(2)}, u32[]{:S(2)}) collective-permute-start(bf16[128,1024]{1,0:T(8,128)(2,1)} %collective-permute-done.5.refs_2_), channel_id=1, source_target_pairs={{0,2},{2,0},{4,6},{6,4},{8,10},{10,8},{12,14},{14,12},{1,3},{3,1},... | collective-permute-start | bytes 786440 | tf_op jit(solution)/shard_map/ppermute | solution.py:37
  50.5 29.5 %collective-permute-start.16 = (bf16[512,1024]{1,0:T(8,128)(2,1)}, bf16[512,1024]{1,0:T(8,128)(2,1)S(1)}, u32[]{:S(2)}, u32[]{:S(2)}) collective-permute-start(bf16[512,1024]{1,0:T(8,128)(2,1)} %collective-permute-done.2.kv_near), channel_id=1, source_target_pairs={{0,16},{16,0},{1,17},{17,1},{2,18},{18,2},{3,19},{19,3},{4,20},{20... | collective-permute-start | bytes 3145736 | tf_op jit(solution)/shard_map/ppermute | solution.py:603
  52.9 10.8 %collective-permute-start.9 = (bf16[64,512]{1,0:T(8,128)(2,1)}, bf16[64,512]{1,0:T(8,128)(2,1)}, u32[]{:S(2)}, u32[]{:S(2)}) collective-permute-start(bf16[64,512]{1,0:T(8,128)(2,1)} %get-tuple-element.190), channel_id=1, source_target_pairs={{0,2},{2,0},{4,6},{6,4},{8,10},{10,8},{12,14},{14,12},{1,3},{3,1},... | collective-permute-start | bytes 196616 | tf_op jit(solution)/shard_map/ppermute | solution.py:37
  95.2 9.3 %collective-permute-start.19 = (bf16[2,128,512]{2,1,0:T(8,128)(2,1)S(1)}, bf16[2,128,512]{2,1,0:T(8,128)(2,1)S(1)}, u32[]{:S(2)}, u32[]{:S(2)}) collective-permute-start(bf16[2,128,512]{2,1,0:T(8,128)(2,1)S(1)} %get-tuple-element.173), channel_id=1, source_target_pairs={{0,4},{2,6},{4,0},{6,2},{8,12},{10,14},{12,8},{14,10},{1,5},{3,7},... | collective-permute-start | bytes 786440 | tf_op jit(solution)/shard_map/ppermute | solution.py:37
  98.0 14.7 %collective-permute-start.24 = (f32[1,128]{1,0:T(1,128)S(1)}, f32[1,128]{1,0:T(1,128)S(1)}, u32[]{:S(2)}, u32[]{:S(2)}) collective-permute-start(f32[1,128]{1,0:T(1,128)S(1)} %slice.165), channel_id=1, source_target_pairs={{0,8},{2,10},{4,12},{6,14},{8,0},{10,2},{12,4},{14,6},{1,9},{3,11}... | collective-permute-start | bytes 1544 | tf_op jit(solution)/shard_map/ppermute | solution.py:37
  100.2 11.5 %collective-permute-start.21 = (bf16[2,128,512]{2,1,0:T(8,128)(2,1)S(1)}, bf16[2,128,512]{2,1,0:T(8,128)(2,1)S(1)}, u32[]{:S(2)}, u32[]{:S(2)}) collective-permute-start(bf16[2,128,512]{2,1,0:T(8,128)(2,1)S(1)} %get-tuple-element.174), channel_id=1, source_target_pairs={{0,4},{2,6},{4,0},{6,2},{8,12},{10,14},{12,8},{14,10},{1,5},{3,7},... | collective-permute-start | bytes 786440 | tf_op jit(solution)/shard_map/ppermute | solution.py:37
  111.9 10.0 %collective-permute-start.25 = (bf16[1,128,512]{2,1,0:T(8,128)(2,1)S(1)}, bf16[1,128,512]{2,1,0:T(8,128)(2,1)S(1)}, u32[]{:S(2)}, u32[]{:S(2)}) collective-permute-start(bf16[1,128,512]{2,1,0:T(8,128)(2,1)S(1)} %get-tuple-element.185), channel_id=1, source_target_pairs={{0,8},{2,10},{4,12},{6,14},{8,0},{10,2},{12,4},{14,6},{1,9},{3,11}... | collective-permute-start | bytes 393224 | tf_op jit(solution)/shard_map/ppermute | solution.py:37
  113.0 10.5 %collective-permute-start.26 = (bf16[1,128,512]{2,1,0:T(8,128)(2,1)S(1)}, bf16[1,128,512]{2,1,0:T(8,128)(2,1)S(1)}, u32[]{:S(2)}, u32[]{:S(2)}) collective-permute-start(bf16[1,128,512]{2,1,0:T(8,128)(2,1)S(1)} %bitcast.72), channel_id=1, source_target_pairs={{0,8},{2,10},{4,12},{6,14},{8,0},{10,2},{12,4},{14,6},{1,9},{3,11}... | collective-permute-start | bytes 393224 | tf_op jit(solution)/shard_map/ppermute | solution.py:37
  122.8 9.7 %collective-permute-start.28 = (bf16[1,128,640]{2,1,0:T(8,128)(2,1)S(1)}, bf16[1,128,640]{2,1,0:T(8,128)(2,1)S(1)}, u32[]{:S(2)}, u32[]{:S(2)}) collective-permute-start(bf16[1,128,640]{2,1,0:T(8,128)(2,1)S(1)} %bitcast.69), channel_id=1, source_target_pairs={{0,8},{2,10},{4,12},{6,14},{8,0},{10,2},{12,4},{14,6},{1,9},{3,11}... | collective-permute-start | bytes 491528 | tf_op jit(solution)/shard_map/ppermute | solution.py:37
  123.5 11.9 %collective-permute-start.27 = (bf16[2,128,512]{2,1,0:T(8,128)(2,1)S(1)}, bf16[2,128,512]{2,1,0:T(8,128)(2,1)S(1)}, u32[]{:S(2)}, u32[]{:S(2)}) collective-permute-start(bf16[2,128,512]{2,1,0:T(8,128)(2,1)S(1)} %pad_maximum_fusion.5), channel_id=1, source_target_pairs={{0,4},{2,6},{4,0},{6,2},{8,12},{10,14},{12,8},{14,10},{1,5},{3,7},... | collective-permute-start | bytes 786440 | tf_op jit(solution)/shard_map/ppermute | solution.py:37
  132.6 9.6 %collective-permute-start.29 = (bf16[2,128,640]{2,1,0:T(8,128)(2,1)S(1)}, bf16[2,128,640]{2,1,0:T(8,128)(2,1)S(1)}, u32[]{:S(2)}, u32[]{:S(2)}) collective-permute-start(bf16[2,128,640]{2,1,0:T(8,128)(2,1)S(1)} %pad_maximum_fusion.3), channel_id=1, source_target_pairs={{0,4},{2,6},{4,0},{6,2},{8,12},{10,14},{12,8},{14,10},{1,5},{3,7},... | collective-permute-start | bytes 983048 | tf_op jit(solution)/shard_map/ppermute | solution.py:37
  162.9 9.9 %collective-permute-start.34 = (bf16[1,2,64,512]{3,2,1,0:T(8,128)(2,1)S(1)}, bf16[1,2,64,512]{3,2,1,0:T(8,128)(2,1)S(1)}, u32[]{:S(2)}, u32[]{:S(2)}) collective-permute-start(bf16[1,2,64,512]{3,2,1,0:T(8,128)(2,1)S(1)} %slice.211), channel_id=1, source_target_pairs={{0,8},{2,10},{4,12},{6,14},{8,0},{10,2},{12,4},{14,6},{1,9},{3,11}... | collective-permute-start | bytes 393224 | tf_op jit(solution)/shard_map/ppermute | solution.py:37
  189.3 12.1 %collective-permute-start.39 = (bf16[4,3,128,128]{3,2,1,0:T(8,128)(2,1)S(1)}, bf16[4,3,128,128]{3,2,1,0:T(8,128)(2,1)S(1)}, u32[]{:S(2)}, u32[]{:S(2)}) collective-permute-start(bf16[4,3,128,128]{3,2,1,0:T(8,128)(2,1)S(1)} %get-tuple-element.140), channel_id=1, source_target_pairs={{0,2},{2,0},{4,6},{6,4},{8,10},{10,8},{12,14},{14,12},{1,3},{3,1},... | collective-permute-start | bytes 1179656 | tf_op jit(solution)/shard_map/ppermute | solution.py:37
  192.1 17.7 %collective-permute-start.43 = (bf16[4,3,128,128]{3,2,1,0:T(8,128)(2,1)S(1)}, bf16[4,3,128,128]{3,2,1,0:T(8,128)(2,1)S(1)}, u32[]{:S(2)}, u32[]{:S(2)}) collective-permute-start(bf16[4,3,128,128]{3,2,1,0:T(8,128)(2,1)S(1)} %get-tuple-element.155), channel_id=1, source_target_pairs={{0,2},{2,0},{4,6},{6,4},{8,10},{10,8},{12,14},{14,12},{1,3},{3,1},... | collective-permute-start | bytes 1179656 | tf_op jit(solution)/shard_map/ppermute | solution.py:37
  202.5 18.5 %collective-permute-start.47 = (bf16[4,64,1024]{2,1,0:T(8,128)(2,1)S(1)}, bf16[4,64,1024]{2,1,0:T(8,128)(2,1)S(1)}, u32[]{:S(2)}, u32[]{:S(2)}) collective-permute-start(bf16[4,64,1024]{2,1,0:T(8,128)(2,1)S(1)} %get-tuple-element.163), channel_id=1, source_target_pairs={{0,2},{2,0},{4,6},{6,4},{8,10},{10,8},{12,14},{14,12},{1,3},{3,1},... | collective-permute-start | bytes 1572872 | tf_op jit(solution)/shard_map/ppermute | solution.py:37
  203.2 14.6 %collective-permute-start.42 = (bf16[4,3,128,128]{3,2,1,0:T(8,128)(2,1)S(1)}, bf16[4,3,128,128]{3,2,1,0:T(8,128)(2,1)S(1)}, u32[]{:S(2)}, u32[]{:S(2)}) collective-permute-start(bf16[4,3,128,128]{3,2,1,0:T(8,128)(2,1)S(1)} %get-tuple-element.153), channel_id=1, source_target_pairs={{0,4},{2,6},{4,0},{6,2},{8,12},{10,14},{12,8},{14,10},{1,5},{3,7},... | collective-permute-start | bytes 1179656 | tf_op jit(solution)/shard_map/ppermute | solution.py:37
  204.5 24.9 %collective-permute-start.46 = (bf16[4,3,128,128]{3,2,1,0:T(8,128)(2,1)S(1)}, bf16[4,3,128,128]{3,2,1,0:T(8,128)(2,1)S(1)}, u32[]{:S(2)}, u32[]{:S(2)}) collective-permute-start(bf16[4,3,128,128]{3,2,1,0:T(8,128)(2,1)S(1)} %get-tuple-element.161), channel_id=1, source_target_pairs={{0,2},{2,0},{4,6},{6,4},{8,10},{10,8},{12,14},{14,12},{1,3},{3,1},... | collective-permute-start | bytes 1179656 | tf_op jit(solution)/shard_map/ppermute | solution.py:37
  209.8 8.7 %collective-permute-start.41 = (bf16[1,3,128,128]{3,2,1,0:T(8,128)(2,1)S(1)}, bf16[1,3,128,128]{3,2,1,0:T(8,128)(2,1)S(1)}, u32[]{:S(2)}, u32[]{:S(2)}) collective-permute-start(bf16[1,3,128,128]{3,2,1,0:T(8,128)(2,1)S(1)} %slice.218), channel_id=1, source_target_pairs={{0,8},{2,10},{4,12},{6,14},{8,0},{10,2},{12,4},{14,6},{1,9},{3,11}... | collective-permute-start | bytes 294920 | tf_op jit(solution)/shard_map/ppermute | solution.py:37
  217.9 16.8 %collective-permute-start.49 = (bf16[2,3,128,128]{3,2,1,0:T(8,128)(2,1)S(1)}, bf16[2,3,128,128]{3,2,1,0:T(8,128)(2,1)S(1)}, u32[]{:S(2)}, u32[]{:S(2)}) collective-permute-start(bf16[2,3,128,128]{3,2,1,0:T(8,128)(2,1)S(1)} %slice.226), channel_id=1, source_target_pairs={{0,2},{2,0},{4,6},{6,4},{8,10},{10,8},{12,14},{14,12},{1,3},{3,1},... | collective-permute-start | bytes 589832 | tf_op jit(solution)/shard_map/ppermute | solution.py:37
  221.0 8.6 %collective-permute-start.45 = (bf16[1,3,128,128]{3,2,1,0:T(8,128)(2,1)S(1)}, bf16[1,3,128,128]{3,2,1,0:T(8,128)(2,1)S(1)}, u32[]{:S(2)}, u32[]{:S(2)}) collective-permute-start(bf16[1,3,128,128]{3,2,1,0:T(8,128)(2,1)S(1)} %slice.222), channel_id=1, source_target_pairs={{0,8},{2,10},{4,12},{6,14},{8,0},{10,2},{12,4},{14,6},{1,9},{3,11}... | collective-permute-start | bytes 294920 | tf_op jit(solution)/shard_map/ppermute | solution.py:37
  225.8 8.8 %collective-permute-start.50 = (bf16[2,64,1024]{2,1,0:T(8,128)(2,1)S(1)}, bf16[2,64,1024]{2,1,0:T(8,128)(2,1)S(1)}, u32[]{:S(2)}, u32[]{:S(2)}) collective-permute-start(bf16[2,64,1024]{2,1,0:T(8,128)(2,1)S(1)} %slice.228), channel_id=1, source_target_pairs={{0,4},{2,6},{4,0},{6,2},{8,12},{10,14},{12,8},{14,10},{1,5},{3,7},... | collective-permute-start | bytes 786440 | tf_op jit(solution)/shard_map/ppermute | solution.py:37
  234.8 10.8 %collective-permute-start.52 = (bf16[1,3,128,128]{3,2,1,0:T(8,128)(2,1)S(1)}, bf16[1,3,128,128]{3,2,1,0:T(8,128)(2,1)S(1)}, u32[]{:S(2)}, u32[]{:S(2)}) collective-permute-start(bf16[1,3,128,128]{3,2,1,0:T(8,128)(2,1)S(1)} %slice.232), channel_id=1, source_target_pairs={{0,8},{2,10},{4,12},{6,14},{8,0},{10,2},{12,4},{14,6},{1,9},{3,11}... | collective-permute-start | bytes 294920 | tf_op jit(solution)/shard_map/ppermute | solution.py:37
  234.9 14.1 %collective-permute-start.53 = (bf16[1,64,1024]{2,1,0:T(8,128)(2,1)S(1)}, bf16[1,64,1024]{2,1,0:T(8,128)(2,1)S(1)}, u32[]{:S(2)}, u32[]{:S(2)}) collective-permute-start(bf16[1,64,1024]{2,1,0:T(8,128)(2,1)S(1)} %slice.234), channel_id=1, source_target_pairs={{0,8},{2,10},{4,12},{6,14},{8,0},{10,2},{12,4},{14,6},{1,9},{3,11}... | collective-permute-start | bytes 393224 | tf_op jit(solution)/shard_map/ppermute | solution.py:37
  238.2 9.8 %collective-permute-start.51 = (bf16[1,3,128,128]{3,2,1,0:T(8,128)(2,1)S(1)}, bf16[1,3,128,128]{3,2,1,0:T(8,128)(2,1)S(1)}, u32[]{:S(2)}, u32[]{:S(2)}) collective-permute-start(bf16[1,3,128,128]{3,2,1,0:T(8,128)(2,1)S(1)} %slice.230), channel_id=1, source_target_pairs={{0,8},{2,10},{4,12},{6,14},{8,0},{10,2},{12,4},{14,6},{1,9},{3,11}... | collective-permute-start | bytes 294920 | tf_op jit(solution)/shard_map/ppermute | solution.py:37
  (40 other events, 423.6 us)

commit v8 on v7

--- a/solution.py
+++ b/solution.py
@@ -359,7 +359,7 @@
 
 
 def weight_rows(blocks):
-    return jnp.concatenate([block[...] for block in blocks], axis=0)
+    return jnp.concatenate([b[...].reshape(-1, b.shape[-1]) for b in blocks], axis=0)
 
 
 def both(index, size):
@@ -537,7 +537,7 @@
 
 def lower(table, order, at, cots, gain, lifted, kvs, blocks):
     rows, width = cots[0].shape[0], lifted.shape[1]
-    tok_width = len(blocks) * blocks[0].shape[0]
+    tok_width = sum(block.size for block in blocks) // width
     whole = pl.BlockSpec(memory_space=pltpu.VMEM)
     out = jax.ShapeDtypeStruct((rows, tok_width // 2), BF)
     return pl.pallas_call(
@@ -584,7 +584,6 @@
     for k in order:
         pair = lax.dynamic_slice_in_dim(proj_in, (me ^ k) // 2 * 2 * feats, 2 * feats, 1)
         blocks.append(swap_tm(pair, k) if k else pair)
-    across = [swap_tm(blocks[0], SPLIT)]
 
     other = swap_mp(mine)
     halo = jnp.where(
@@ -596,10 +595,8 @@
     normed, qkv, probs, pooled_attn, own_near, own_far, tail_near, tail_far = encoder_forward(
         x_roll, w_t, weight_out, at, ext_tok
     )
-    own_far, kv_near, across, blocks[1:-1] = lax.optimization_barrier(
-        (own_far, kv_near, across, blocks[1:-1])
-    )
-    across += [swap_tm(block, SPLIT) for block in blocks[1:-1]]
+    own_far, kv_near, blocks[0] = lax.optimization_barrier((own_far, kv_near, blocks[0]))
+    across = [swap_tm(blocks[0], SPLIT)]
     swap_groups = lambda block: lax.ppermute(block, "groups", [(0, 1), (1, 0)])
     if two_groups:
         kv_far = swap_groups(kv_near)
@@ -635,26 +632,25 @@
 
     sorted_tok = dot(sort, pooled).astype(BF).reshape(2, count * piece, half_w)
     handed = swap_tm(sorted_tok[1], SPLIT)
-    handed, across, blocks[-1] = lax.optimization_barrier((handed, across, blocks[-1]))
-    last_across = swap_tm(blocks[-1], SPLIT)
+    handed, across, blocks[1:] = lax.optimization_barrier((handed, across, blocks[1:]))
+    across.append(swap_tm(jnp.stack(blocks[1:]), SPLIT))
     pair_tok = jnp.stack([sorted_tok[0], handed])
     tok_half = gather_doubling(pair_tok, masks[-1:])
-    tok_half, turned, d_kv, last_across = lax.optimization_barrier(
-        (tok_half, turned, d_kv, last_across)
-    )
-    blocks += across + [last_across]
+    tok_half, turned, d_kv = lax.optimization_barrier((tok_half, turned, d_kv))
+    for mask in reversed(masks[:-1]):
+        tok_half = jnp.concatenate([tok_half, swap_tm(tok_half, mask)], axis=0)
+    tok_half, kv_far = lax.optimization_barrier((tok_half.reshape(-1, half_w), kv_far))
+    kvs = (proj_kv, kv_near, kv_far)
+    tok_other = swap_mp(tok_half)
+    blocks += across
     at_rows = order
     if width // n % LANES:
         source = jnp.arange(n, dtype=jnp.int32) ^ me
         found = source[:, None] == jnp.array(members, jnp.int32)[None, :]
         place = jnp.sum(found * jnp.arange(n, dtype=jnp.int32)[None, :], axis=1)
-        blocks = list(jnp.take(jnp.stack(blocks), place, axis=0))
+        stacked = jnp.concatenate([b.reshape((-1,) + blocks[0].shape) for b in blocks])
+        blocks = list(jnp.take(stacked, place, axis=0))
         at_rows = None
-    for mask in reversed(masks[:-1]):
-        tok_half = jnp.concatenate([tok_half, swap_tm(tok_half, mask)], axis=0)
-    tok_half, kv_far = lax.optimization_barrier((tok_half.reshape(-1, half_w), kv_far))
-    kvs = (proj_kv, kv_near, kv_far)
-    tok_other = swap_mp(tok_half)
     table = list(moves(order, piece))
     source_rows = np.concatenate([np.arange(r, r + piece) for r, _ in table])
     owner_rows = np.concatenate([np.arange(r, r + piece) for _, r in table])
@@ -701,14 +697,19 @@
     crossed = [bits[1], bits[0]] + bits[2:]
     d_attn, out_even, out_odd = out_grad(d_ext, weight_out, pooled_attn, at, bits)
     chunks = []
+    out_got = swap_tm(out_odd, bits[0])
     for pair, path in enumerate((bits, bits, bits, crossed)):
+        if pair == 3:
+            at, out_got = lax.optimization_barrier((at, out_got))
         even, odd = encoder_backward(turned, qkv, probs, d_attn, at, path, pair, 1)
         even, odd, at = lax.optimization_barrier((even, odd, at))
         chunks.append((even, odd, path))
-    chunks.append((out_even, out_odd, bits))
-    steps = list(range(len(chunks))) * len(bits)
+    out_low = (out_even.astype(F32) + out_got.astype(F32)).astype(BF)
+    out_half = out_low.shape[0] // 2
+    chunks.append((out_low[:out_half], out_low[out_half:], bits[1:]))
+    steps = [i for t in range(len(bits)) for i, c in enumerate(chunks) if t < len(c[2])]
     if len(bits) == 3:
-        steps = [0, 0, 1, 3, 0, 1, 4, 2, 1, 4, 3, 2, 4, 3, 2]
+        steps = [0, 4, 3, 1, 0, 4, 0, 2, 1, 1, 3, 2, 3, 2]
     chunks = scatter_chunks(chunks, steps, even)
     grad_out = chunks.pop()
     grad_qkv = jnp.transpose(jnp.concatenate(chunks, axis=-1), (1, 0, 2))

time: 251 us -> 252 us (level)
  waiting for transfers between devices: 111 us -> 122 us
  starting transfers between devices: 63.1 us -> 54.5 us
    ppermute x39 -> x37, starting transfers between devices: 47.5 us -> 38.9 us  [swap_tm(): return lax.ppermute(block, 'tm', [(i, i ^ mask) for i in range(n)])]
    ppermute x39 -> x37, waiting for transfers between devices: 101 us -> 106 us  [swap_tm(): return lax.ppermute(block, 'tm', [(i, i ^ mask) for i in range(n)])]
    ppermute x5, waiting for transfers between devices: 4.09 us -> 7.79 us  [to_tm(): return lax.ppermute(block, ('tm', 'mp'), pairs)]
    ppermute x1, waiting for transfers between devices: 0.01 us -> 3.16 us  [on_device(): swap_groups = lambda block: lax.ppermute(block, 'groups', [(0, 1), (1, 0)])]
  transfers between devices with their start and end apart: 54 -> 52, of which waited for: 32 -> 32; matrix products, arithmetic and copies ran while one was open for 9% -> 9% of each run, Pallas kernels for 10% -> 11%
where the time goes in v8:
time: 252 us
  waiting for transfers between devices  122 us (48%)
  starting transfers between devices  54.5 us (22%)
  Pallas kernels  41.4 us (16%)
  local copies, waits for them, and re-layouts  17.1 us (7%)
  other arithmetic  9.64 us (4%)
  between operations  4.03 us (2%)
  matrix products  2.88 us (1%)
    ppermute x37, waiting for transfers between devices, swap_tm(): return lax.ppermute(block, 'tm', [(i, i ^ mask) for i in range(n)])  106 us
    ppermute x37, starting transfers between devices, swap_tm(): return lax.ppermute(block, 'tm', [(i, i ^ mask) for i in range(n)])  38.9 us
    ppermute x5, starting transfers between devices, to_tm(): return lax.ppermute(block, ('tm', 'mp'), pairs)  12.6 us
    pallas_call x4, Pallas kernels, encoder_backward(): pl.pallas_call(functools.partial(backward_kernel, masks), grid_spec=pltpu...  11 us
    pallas_call x1, Pallas kernels, encoder_forward(): pl.pallas_call(forward_kernel, grid_spec=pltpu.PrefetchScalarGridSpec(num...  11 us
    ppermute x5, waiting for transfers between devices, to_tm(): return lax.ppermute(block, ('tm', 'mp'), pairs)  7.79 us
    pallas_call x1, Pallas kernels, lower(): pl.pallas_call(functools.partial(lower_kernel, table, order), in_specs=[p...  7.01 us
    pallas_call x1, Pallas kernels, lift(): pl.pallas_call(functools.partial(lift_kernel, table, order), in_specs=[pl...  6.24 us
  transfers between devices with their start and end apart: 52, of which 32 were waited for; matrix products, arithmetic and copies ran while one was open for 9% of the time, Pallas kernels for 11%

profile of v8, /device:TPU:0, one launch (start us, length us, event | category | flops | bytes accessed | tf_op | source)
XLA Modules:
  0.0 251.6 jit_solution(1052291690175441471)
XLA Ops:
  2.4 6.0 %collective-permute-start = (bf16[128,1024]{1,0:T(8,128)(2,1)}, bf16[128,1024]{1,0:T(8,128)(2,1)}, u32[]{:S(2)}, u32[]{:S(2)}) collective-permute-start(bf16[128,1024]{1,0:T(8,128)(2,1)} %constant_dynamic-slice_fusion.6), channel_id=1, source_target_pairs={{0,14},{1,15},{2,0},{3,1},{4,2},{5,3},{6,4},{7,5},{8,6},{9,7},{10,... | collective-permute-start | bytes 786440 | tf_op jit(solution)/shard_map/ppermute | solution.py:51
  10.6 3.2 %copy.14 = bf16[3,512,1024]{2,1,0:T(8,128)(2,1)S(1)} copy(bf16[3,512,1024]{1,2,0:T(8,128)(2,1)} %bitcast.85) | data formatting | bytes 6291456 | tf_op jit(solution)/shard_map/transpose | solution.py:570
  17.1 3.3 %collective-permute-start.8 = (bf16[128,1024]{1,0:T(8,128)(2,1)}, bf16[128,1024]{1,0:T(8,128)(2,1)}, u32[]{:S(2)}, u32[]{:S(2)}) collective-permute-start(bf16[128,1024]{1,0:T(8,128)(2,1)} %get-tuple-element.173), channel_id=1, source_target_pairs={{0,8},{2,10},{4,12},{6,14},{8,0},{10,2},{12,4},{14,6},{1,9},{3,11}... | collective-permute-start | bytes 786440 | tf_op jit(solution)/shard_map/ppermute | solution.py:37
  28.1 11.0 %encoder_forward.1 = (bf16[512,1024]{1,0:T(8,128)(2,1)}, bf16[3,512,512]{2,1,0:T(8,128)(2,1)}, bf16[4,2,2,256,256]{4,3,2,1,0:T(8,128)(2,1)}, bf16[192,512]{1,0:T...) custom-call(s32[5]{0:T(128)S(1)} %stack.37.at, ...), custom_call_target="tpu_custom_call" | custom-call | tf_op jit(solution)/shard_map/encoder_forward/pallas_call | solution.py:206
  47.8 3.9 %collective-permute-done.5 = bf16[64,512]{1,0:T(8,128)(2,1)S(1)} collective-permute-done((bf16[64,512]{1,0:T(8,128)(2,1)}, bf16[64,512]{1,0:T(8,128)(2,1)S(1)}, u32[]{:S(2)}, u32[]{:S(2)}) %collective-permute-start.5) | collective-permute-done | bytes 65568 | tf_op jit(solution)/shard_map/ppermute | solution.py:51
  55.2 3.3 %collective-permute-done.6 = bf16[64,512]{1,0:T(8,128)(2,1)S(1)} collective-permute-done((bf16[64,512]{1,0:T(8,128)(2,1)S(1)}, bf16[64,512]{1,0:T(8,128)(2,1)S(1)}, u32[]{:S(2)}, u32[]{:S(2)}) %collective-permute-start.6) | collective-permute-done | bytes 65568 | tf_op jit(solution)/shard_map/ppermute | solution.py:37
  58.9 6.8 %collective-permute-done.11 = bf16[1,2,64,512]{3,2,1,0:T(8,128)(2,1)S(1)} collective-permute-done((bf16[1,2,64,512]{3,2,1,0:T(8,128)(2,1)S(1)}, bf16[1,2,64,512]{3,2,1,0:T(8,128)(2,1)S(1)}, u32[]{:S(2)}, u32[]{:S(2)}) %collective-permute-start.11) | collective-permute-done | bytes 131104 | tf_op jit(solution)/shard_map/ppermute | solution.py:37
  68.3 5.6 %collective-permute-done.12 = bf16[2,2,64,512]{3,2,1,0:T(8,128)(2,1)S(1)} collective-permute-done((bf16[2,2,64,512]{3,2,1,0:T(8,128)(2,1)S(1)}, bf16[2,2,64,512]{3,2,1,0:T(8,128)(2,1)S(1)}, u32[]{:S(2)}, u32[]{:S(2)}) %collective-permute-start.12) | collective-permute-done | bytes 262176 | tf_op jit(solution)/shard_map/ppermute | solution.py:37
  73.9 3.2 %collective-permute-done.13.kv_far = bf16[512,1024]{1,0:T(8,128)(2,1)S(1)} collective-permute-done((bf16[512,1024]{1,0:T(8,128)(2,1)}, bf16[512,1024]{1,0:T(8,128)(2,1)S(1)}, u32[]{:S(2)}, u32[]{:S(2)}) %collective-permute-start.13) | collective-permute-done | bytes 1048608 | tf_op jit(solution)/shard_map/ppermute | solution.py:600
  77.8 8.6 %collective-permute-done.15.refs_5_ = bf16[3,128,1024]{2,1,0:T(8,128)(2,1)S(1)} collective-permute-done((bf16[3,128,1024]{2,1,0:T(8,128)(2,1)S(1)}, bf16[3,128,1024]{2,1,0:T(8,128)(2,1)S(1)}, u32[]{:S(2)}, u32[]{:S(2)}) %collective-permute-start.15) | collective-permute-done | bytes 786464 | tf_op jit(solution)/shard_map/ppermute | solution.py:37
  86.4 6.2 %lift.1 = (bf16[512,1024]{1,0:T(8,128)(2,1)S(1)}, f32[4,128]{1,0:T(4,128)S(1)}, bf16[512,1024]{1,0:T(8,128)(2,1)S(1)}, bf16[512,1024]{1,0:T(8,128)(2,1)}) custom-call(s32[5]{0:T(128)S(1)} %stack.37.at, bf16[512,512]{1,0:T(8,128)(2,1)S(1)} %bitcast.71, bf16[512,512]{1,0:T(8,128)(2,1)S(1)} %collective-permute-done.14.tb, f32[1,1024]{1,0:T(1,128)S(1)} %bitcast.80, ...), custom_call_target="tpu_custom_call" | custom-call | tf_op jit(solution)/shard_map/lift/pallas_call | solution.py:418
  95.4 3.3 %keep_columns.1 = bf16[512,1024]{1,0:T(8,128)(2,1)S(1)} custom-call(s32[5]{0:T(128)S(1)} %stack.37.at, bf16[512,1024]{1,0:T(8,128)(2,1)S(1)} %get-tuple-element.109.low, bf16[512,2048]{1,0:T(8,128)(2,1)} %kva.2, bf16[512,1024]{1,0:T(8,128)(2,1)} %collective-permute-done.2.kv_near, bf16[512,1024]{1,0:T(8,128)(2,1)S(1)} %copy-done.4), custom_call_target="tpu_custom_call" | custom-call | tf_op jit(solution)/shard_map/keep_columns/pallas_call | solution.py:441
  102.4 2.8 %collective-permute-start.22 = (f32[1,128]{1,0:T(1,128)S(1)}, f32[1,128]{1,0:T(1,128)S(1)}, u32[]{:S(2)}, u32[]{:S(2)}) collective-permute-start(f32[1,128]{1,0:T(1,128)S(1)} %slice.165), channel_id=1, source_target_pairs={{0,8},{2,10},{4,12},{6,14},{8,0},{10,2},{12,4},{14,6},{1,9},{3,11}... | collective-permute-start | bytes 1544 | tf_op jit(solution)/shard_map/ppermute | solution.py:37
  105.5 4.8 %collective-permute-done.17 = bf16[2,128,512]{2,1,0:T(8,128)(2,1)S(1)} collective-permute-done((bf16[2,128,512]{2,1,0:T(8,128)(2,1)S(1)}, bf16[2,128,512]{2,1,0:T(8,128)(2,1)S(1)}, u32[]{:S(2)}, u32[]{:S(2)}) %collective-permute-start.17) | collective-permute-done | bytes 262176 | tf_op jit(solution)/shard_map/ppermute | solution.py:37
  111.8 5.2 %collective-permute-done.19 = bf16[2,128,512]{2,1,0:T(8,128)(2,1)S(1)} collective-permute-done((bf16[2,128,512]{2,1,0:T(8,128)(2,1)S(1)}, bf16[2,128,512]{2,1,0:T(8,128)(2,1)S(1)}, u32[]{:S(2)}, u32[]{:S(2)}) %collective-permute-start.19) | collective-permute-done | bytes 262176 | tf_op jit(solution)/shard_map/ppermute | solution.py:37
  117.4 3.0 %collective-permute-done.18 = bf16[1,128,512]{2,1,0:T(8,128)(2,1)S(1)} collective-permute-done((bf16[1,128,512]{2,1,0:T(8,128)(2,1)S(1)}, bf16[1,128,512]{2,1,0:T(8,128)(2,1)S(1)}, u32[]{:S(2)}, u32[]{:S(2)}) %collective-permute-start.18) | collective-permute-done | bytes 131104 | tf_op jit(solution)/shard_map/ppermute | solution.py:37
  120.8 5.6 %collective-permute-done.23 = bf16[1,128,512]{2,1,0:T(8,128)(2,1)S(1)} collective-permute-done((bf16[1,128,512]{2,1,0:T(8,128)(2,1)S(1)}, bf16[1,128,512]{2,1,0:T(8,128)(2,1)S(1)}, u32[]{:S(2)}, u32[]{:S(2)}) %collective-permute-start.23) | collective-permute-done | bytes 131104 | tf_op jit(solution)/shard_map/ppermute | solution.py:37
  127.3 2.9 %collective-permute-done.24 = bf16[1,128,512]{2,1,0:T(8,128)(2,1)S(1)} collective-permute-done((bf16[1,128,512]{2,1,0:T(8,128)(2,1)S(1)}, bf16[1,128,512]{2,1,0:T(8,128)(2,1)S(1)}, u32[]{:S(2)}, u32[]{:S(2)}) %collective-permute-start.24) | collective-permute-done | bytes 131104 | tf_op jit(solution)/shard_map/ppermute | solution.py:37
  130.3 3.3 %collective-permute-start.25 = (bf16[2,128,512]{2,1,0:T(8,128)(2,1)S(1)}, bf16[2,128,512]{2,1,0:T(8,128)(2,1)S(1)}, u32[]{:S(2)}, u32[]{:S(2)}) collective-permute-start(bf16[2,128,512]{2,1,0:T(8,128)(2,1)S(1)} %pad_maximum_fusion.6), channel_id=1, source_target_pairs={{0,4},{2,6},{4,0},{6,2},{8,12},{10,14},{12,8},{14,10},{1,5},{3,7},... | collective-permute-start | bytes 786440 | tf_op jit(solution)/shard_map/ppermute | solution.py:37
  133.6 3.5 %collective-permute-done.26 = bf16[1,128,640]{2,1,0:T(8,128)(2,1)S(1)} collective-permute-done((bf16[1,128,640]{2,1,0:T(8,128)(2,1)S(1)}, bf16[1,128,640]{2,1,0:T(8,128)(2,1)S(1)}, u32[]{:S(2)}, u32[]{:S(2)}) %collective-permute-start.26) | collective-permute-done | bytes 163872 | tf_op jit(solution)/shard_map/ppermute | solution.py:37
  137.2 5.0 %collective-permute-done.25 = bf16[2,128,512]{2,1,0:T(8,128)(2,1)S(1)} collective-permute-done((bf16[2,128,512]{2,1,0:T(8,128)(2,1)S(1)}, bf16[2,128,512]{2,1,0:T(8,128)(2,1)S(1)}, u32[]{:S(2)}, u32[]{:S(2)}) %collective-permute-start.25) | collective-permute-done | bytes 262176 | tf_op jit(solution)/shard_map/ppermute | solution.py:37
  142.2 5.5 %collective-permute-done.27 = bf16[2,128,640]{2,1,0:T(8,128)(2,1)S(1)} collective-permute-done((bf16[2,128,640]{2,1,0:T(8,128)(2,1)S(1)}, bf16[2,128,640]{2,1,0:T(8,128)(2,1)S(1)}, u32[]{:S(2)}, u32[]{:S(2)}) %collective-permute-start.27) | collective-permute-done | bytes 327712 | tf_op jit(solution)/shard_map/ppermute | solution.py:37
  150.8 7.0 %lower.1 = (bf16[512,512]{1,0:T(8,128)(2,1)S(1)}, bf16[512,512]{1,0:T(8,128)(2,1)S(1)}) custom-call(s32[5]{0:T(128)S(1)} %stack.37.at, bf16[512,512]{1,0:T(8,128)(2,1)S(1)} %bitcast.69, bf16[512,640]{1,0:T(8,128)(2,1)S(1)} %bitcast.67, bf16[512,512]{1,0:T(8,128)(2,1)S(1)} %collective-permute-done.28.cb0, bf16[512,640]{1,0:T(8,128)(2,1)S(1)} %collective-permute-done.29.cb1, ...), custom_call_target="tpu_custom_call" | custom-call | tf_op jit(solution)/shard_map/lower/pallas_call | solution.py:543
  160.0 8.3 %collective-permute-done.31 = bf16[2,2,64,512]{3,2,1,0:T(8,128)(2,1)S(1)} collective-permute-done((bf16[2,2,64,512]{3,2,1,0:T(8,128)(2,1)S(1)}, bf16[2,2,64,512]{3,2,1,0:T(8,128)(2,1)S(1)}, u32[]{:S(2)}, u32[]{:S(2)}) %collective-permute-start.31) | collective-permute-done | bytes 262176 | tf_op jit(solution)/shard_map/ppermute | solution.py:37
  170.2 6.8 %collective-permute-done.32 = bf16[1,2,64,512]{3,2,1,0:T(8,128)(2,1)S(1)} collective-permute-done((bf16[1,2,64,512]{3,2,1,0:T(8,128)(2,1)S(1)}, bf16[1,2,64,512]{3,2,1,0:T(8,128)(2,1)S(1)}, u32[]{:S(2)}, u32[]{:S(2)}) %collective-permute-start.32) | collective-permute-done | bytes 131104 | tf_op jit(solution)/shard_map/ppermute | solution.py:37
  178.5 2.8 %collective-permute-done.33 = bf16[64,512]{1,0:T(8,128)(2,1)S(1)} collective-permute-done((bf16[64,512]{1,0:T(8,128)(2,1)S(1)}, bf16[64,512]{1,0:T(8,128)(2,1)S(1)}, u32[]{:S(2)}, u32[]{:S(2)}) %collective-permute-start.33) | collective-permute-done | bytes 65568 | tf_op jit(solution)/shard_map/ppermute | solution.py:37
  197.7 2.8 %encoder_backward.6 = (bf16[4,3,128,128]{3,2,1,0:T(8,128)(2,1)S(1)}, bf16[4,3,128,128]{3,2,1,0:T(8,128)(2,1)S(1)}) custom-call(s32[5]{0:T(128)S(1)} %stack.37.at, bf16[1024,512]{1,0:T(8,128)(2,1)S(1)} %bitcast.64, bf16[3,512,512]{2,1,0:T(8,128)(2,1)S(1)} %copy-done.2, bf16[4,2,2,256,256]{4,3,2,1,0:T(8,128)(2,1)S(1)} %copy-done.1, ...), custom_call_target="tpu_custom_call" | custom-call | tf_op jit(solution)/shard_map/encoder_backward/pallas_call | solution.py:317
  200.5 4.5 %collective-permute-done.38 = bf16[4,64,1024]{2,1,0:T(8,128)(2,1)S(1)} collective-permute-done((bf16[4,64,1024]{2,1,0:T(8,128)(2,1)S(1)}, bf16[4,64,1024]{2,1,0:T(8,128)(2,1)S(1)}, u32[]{:S(2)}, u32[]{:S(2)}) %collective-permute-start.38) | collective-permute-done | bytes 524320 | tf_op jit(solution)/shard_map/ppermute | solution.py:37
  217.6 8.5 %collective-permute-done.41 = bf16[4,3,128,128]{3,2,1,0:T(8,128)(2,1)S(1)} collective-permute-done((bf16[4,3,128,128]{3,2,1,0:T(8,128)(2,1)S(1)}, bf16[4,3,128,128]{3,2,1,0:T(8,128)(2,1)S(1)}, u32[]{:S(2)}, u32[]{:S(2)}) %collective-permute-start.41) | collective-permute-done | bytes 393248 | tf_op jit(solution)/shard_map/ppermute | solution.py:37
  234.3 4.4 %collective-permute-done.44 = bf16[2,3,128,128]{3,2,1,0:T(8,128)(2,1)S(1)} collective-permute-done((bf16[2,3,128,128]{3,2,1,0:T(8,128)(2,1)S(1)}, bf16[2,3,128,128]{3,2,1,0:T(8,128)(2,1)S(1)}, u32[]{:S(2)}, u32[]{:S(2)}) %collective-permute-start.44) | collective-permute-done | bytes 196640 | tf_op jit(solution)/shard_map/ppermute | solution.py:37
  238.8 2.8 %collective-permute-start.46 = (bf16[1,3,128,128]{3,2,1,0:T(8,128)(2,1)S(1)}, bf16[1,3,128,128]{3,2,1,0:T(8,128)(2,1)S(1)}, u32[]{:S(2)}, u32[]{:S(2)}) collective-permute-start(bf16[1,3,128,128]{3,2,1,0:T(8,128)(2,1)S(1)} %slice.224), channel_id=1, source_target_pairs={{0,8},{2,10},{4,12},{6,14},{8,0},{10,2},{12,4},{14,6},{1,9},{3,11}... | collective-permute-start | bytes 294920 | tf_op jit(solution)/shard_map/ppermute | solution.py:37
  247.3 3.3 %collective-permute-done.49 = bf16[1,3,128,128]{3,2,1,0:T(8,128)(2,1)S(1)} collective-permute-done((bf16[1,3,128,128]{3,2,1,0:T(8,128)(2,1)S(1)}, bf16[1,3,128,128]{3,2,1,0:T(8,128)(2,1)S(1)}, u32[]{:S(2)}, u32[]{:S(2)}) %collective-permute-start.49) | collective-permute-done | bytes 98336 | tf_op jit(solution)/shard_map/ppermute | solution.py:37
  (199 shorter events, 90.3 us)
Async XLA Ops:
  2.4 18.1 %collective-permute-start = (bf16[128,1024]{1,0:T(8,128)(2,1)}, bf16[128,1024]{1,0:T(8,128)(2,1)}, u32[]{:S(2)}, u32[]{:S(2)}) collective-permute-start(bf16[128,1024]{1,0:T(8,128)(2,1)} %constant_dynamic-slice_fusion.6), channel_id=1, source_target_pairs={{0,14},{1,15},{2,0},{3,1},{4,2},{5,3},{6,4},{7,5},{8,6},{9,7},{10,... | collective-permute-start | bytes 786440 | tf_op jit(solution)/shard_map/ppermute | solution.py:51
  10.6 32.6 %collective-permute-start.2 = (bf16[512,1024]{1,0:T(8,128)(2,1)}, bf16[512,1024]{1,0:T(8,128)(2,1)}, u32[]{:S(2)}, u32[]{:S(2)}) collective-permute-start(bf16[512,1024]{1,0:T(8,128)(2,1)} %constant_dynamic-slice_fusion.4), channel_id=1, source_target_pairs={{0,2},{2,0},{4,6},{6,4},{8,10},{10,8},{12,14},{14,12},{1,3},{3,1},... | collective-permute-start | bytes 3145736 | tf_op jit(solution)/shard_map/ppermute | solution.py:37
  16.1 37.4 %collective-permute-start.10 = (bf16[128,1024]{1,0:T(8,128)(2,1)}, bf16[128,1024]{1,0:T(8,128)(2,1)}, u32[]{:S(2)}, u32[]{:S(2)}) collective-permute-start(bf16[128,1024]{1,0:T(8,128)(2,1)} %get-tuple-element.171), channel_id=1, source_target_pairs={{0,12},{2,14},{4,8},{6,10},{8,4},{10,6},{12,0},{14,2},{1,13},{3,15... | collective-permute-start | bytes 786440 | tf_op jit(solution)/shard_map/ppermute | solution.py:37
  17.1 38.1 %collective-permute-start.9 = (bf16[128,1024]{1,0:T(8,128)(2,1)}, bf16[128,1024]{1,0:T(8,128)(2,1)}, u32[]{:S(2)}, u32[]{:S(2)}) collective-permute-start(bf16[128,1024]{1,0:T(8,128)(2,1)} %get-tuple-element.172), channel_id=1, source_target_pairs={{0,4},{2,6},{4,0},{6,2},{8,12},{10,14},{12,8},{14,10},{1,5},{3,7},... | collective-permute-start | bytes 786440 | tf_op jit(solution)/shard_map/ppermute | solution.py:37
  17.1 38.1 %collective-permute-start.8 = (bf16[128,1024]{1,0:T(8,128)(2,1)}, bf16[128,1024]{1,0:T(8,128)(2,1)}, u32[]{:S(2)}, u32[]{:S(2)}) collective-permute-start(bf16[128,1024]{1,0:T(8,128)(2,1)} %get-tuple-element.173), channel_id=1, source_target_pairs={{0,8},{2,10},{4,12},{6,14},{8,0},{10,2},{12,4},{14,6},{1,9},{3,11}... | collective-permute-start | bytes 786440 | tf_op jit(solution)/shard_map/ppermute | solution.py:37
  47.8 10.7 %collective-permute-start.7 = (bf16[128,1024]{1,0:T(8,128)(2,1)S(1)}, bf16[128,1024]{1,0:T(8,128)(2,1)S(1)}, u32[]{:S(2)}, u32[]{:S(2)}) collective-permute-start(bf16[128,1024]{1,0:T(8,128)(2,1)S(1)} %copy-done.7), channel_id=1, source_target_pairs={{0,2},{2,0},{4,6},{6,4},{8,10},{10,8},{12,14},{14,12},{1,3},{3,1},... | collective-permute-start | bytes 786440 | tf_op jit(solution)/shard_map/ppermute | solution.py:37
  51.7 25.4 %collective-permute-start.13 = (bf16[512,1024]{1,0:T(8,128)(2,1)}, bf16[512,1024]{1,0:T(8,128)(2,1)S(1)}, u32[]{:S(2)}, u32[]{:S(2)}) collective-permute-start(bf16[512,1024]{1,0:T(8,128)(2,1)} %collective-permute-done.2.kv_near), channel_id=1, source_target_pairs={{0,16},{16,0},{1,17},{17,1},{2,18},{18,2},{3,19},{19,3},{4,20},{20... | collective-permute-start | bytes 3145736 | tf_op jit(solution)/shard_map/ppermute | solution.py:600
  65.7 8.2 %collective-permute-start.12 = (bf16[2,2,64,512]{3,2,1,0:T(8,128)(2,1)S(1)}, bf16[2,2,64,512]{3,2,1,0:T(8,128)(2,1)S(1)}, u32[]{:S(2)}, u32[]{:S(2)}) collective-permute-start(bf16[2,2,64,512]{3,2,1,0:T(8,128)(2,1)S(1)} %pad_maximum_fusion.5), channel_id=1, source_target_pairs={{0,4},{2,6},{4,0},{6,2},{8,12},{10,14},{12,8},{14,10},{1,5},{3,7},... | collective-permute-start | bytes 786440 | tf_op jit(solution)/shard_map/ppermute | solution.py:37
  67.0 19.4 %collective-permute-start.15 = (bf16[3,128,1024]{2,1,0:T(8,128)(2,1)S(1)}, bf16[3,128,1024]{2,1,0:T(8,128)(2,1)S(1)}, u32[]{:S(2)}, u32[]{:S(2)}) collective-permute-start(bf16[3,128,1024]{2,1,0:T(8,128)(2,1)S(1)} %pad_maximum_fusion), channel_id=1, source_target_pairs={{0,2},{2,0},{4,6},{6,4},{8,10},{10,8},{12,14},{14,12},{1,3},{3,1},... | collective-permute-start | bytes 2359304 | tf_op jit(solution)/shard_map/ppermute | solution.py:37
  77.1 9.3 %collective-permute-start.14 = (bf16[512,512]{1,0:T(8,128)(2,1)S(1)}, bf16[512,512]{1,0:T(8,128)(2,1)S(1)}, u32[]{:S(2)}, u32[]{:S(2)}) collective-permute-start(bf16[512,512]{1,0:T(8,128)(2,1)S(1)} %bitcast.70), channel_id=1, source_target_pairs={{0,1},{1,0},{2,3},{3,2},{4,5},{5,4},{6,7},{7,6},{8,9},{9,8},{10,11... | collective-permute-start | bytes 1572872 | tf_op jit(solution)/shard_map/ppermute | solution.py:42
  101.0 9.3 %collective-permute-start.17 = (bf16[2,128,512]{2,1,0:T(8,128)(2,1)S(1)}, bf16[2,128,512]{2,1,0:T(8,128)(2,1)S(1)}, u32[]{:S(2)}, u32[]{:S(2)}) collective-permute-start(bf16[2,128,512]{2,1,0:T(8,128)(2,1)S(1)} %get-tuple-element.169), channel_id=1, source_target_pairs={{0,4},{2,6},{4,0},{6,2},{8,12},{10,14},{12,8},{14,10},{1,5},{3,7},... | collective-permute-start | bytes 786440 | tf_op jit(solution)/shard_map/ppermute | solution.py:37
  102.4 15.1 %collective-permute-start.22 = (f32[1,128]{1,0:T(1,128)S(1)}, f32[1,128]{1,0:T(1,128)S(1)}, u32[]{:S(2)}, u32[]{:S(2)}) collective-permute-start(f32[1,128]{1,0:T(1,128)S(1)} %slice.165), channel_id=1, source_target_pairs={{0,8},{2,10},{4,12},{6,14},{8,0},{10,2},{12,4},{14,6},{1,9},{3,11}... | collective-permute-start | bytes 1544 | tf_op jit(solution)/shard_map/ppermute | solution.py:37
  105.2 11.8 %collective-permute-start.19 = (bf16[2,128,512]{2,1,0:T(8,128)(2,1)S(1)}, bf16[2,128,512]{2,1,0:T(8,128)(2,1)S(1)}, u32[]{:S(2)}, u32[]{:S(2)}) collective-permute-start(bf16[2,128,512]{2,1,0:T(8,128)(2,1)S(1)} %get-tuple-element.170), channel_id=1, source_target_pairs={{0,4},{2,6},{4,0},{6,2},{8,12},{10,14},{12,8},{14,10},{1,5},{3,7},... | collective-permute-start | bytes 786440 | tf_op jit(solution)/shard_map/ppermute | solution.py:37
  110.4 10.0 %collective-permute-start.18 = (bf16[1,128,512]{2,1,0:T(8,128)(2,1)S(1)}, bf16[1,128,512]{2,1,0:T(8,128)(2,1)S(1)}, u32[]{:S(2)}, u32[]{:S(2)}) collective-permute-start(bf16[1,128,512]{2,1,0:T(8,128)(2,1)S(1)} %get-tuple-element.180), channel_id=1, source_target_pairs={{0,8},{2,10},{4,12},{6,14},{8,0},{10,2},{12,4},{14,6},{1,9},{3,11}... | collective-permute-start | bytes 393224 | tf_op jit(solution)/shard_map/ppermute | solution.py:37
  117.1 9.3 %collective-permute-start.23 = (bf16[1,128,512]{2,1,0:T(8,128)(2,1)S(1)}, bf16[1,128,512]{2,1,0:T(8,128)(2,1)S(1)}, u32[]{:S(2)}, u32[]{:S(2)}) collective-permute-start(bf16[1,128,512]{2,1,0:T(8,128)(2,1)S(1)} %get-tuple-element.181), channel_id=1, source_target_pairs={{0,8},{2,10},{4,12},{6,14},{8,0},{10,2},{12,4},{14,6},{1,9},{3,11}... | collective-permute-start | bytes 393224 | tf_op jit(solution)/shard_map/ppermute | solution.py:37
  120.7 9.5 %collective-permute-start.24 = (bf16[1,128,512]{2,1,0:T(8,128)(2,1)S(1)}, bf16[1,128,512]{2,1,0:T(8,128)(2,1)S(1)}, u32[]{:S(2)}, u32[]{:S(2)}) collective-permute-start(bf16[1,128,512]{2,1,0:T(8,128)(2,1)S(1)} %bitcast.75), channel_id=1, source_target_pairs={{0,8},{2,10},{4,12},{6,14},{8,0},{10,2},{12,4},{14,6},{1,9},{3,11}... | collective-permute-start | bytes 393224 | tf_op jit(solution)/shard_map/ppermute | solution.py:37
  127.3 9.8 %collective-permute-start.26 = (bf16[1,128,640]{2,1,0:T(8,128)(2,1)S(1)}, bf16[1,128,640]{2,1,0:T(8,128)(2,1)S(1)}, u32[]{:S(2)}, u32[]{:S(2)}) collective-permute-start(bf16[1,128,640]{2,1,0:T(8,128)(2,1)S(1)} %bitcast.72), channel_id=1, source_target_pairs={{0,8},{2,10},{4,12},{6,14},{8,0},{10,2},{12,4},{14,6},{1,9},{3,11}... | collective-permute-start | bytes 491528 | tf_op jit(solution)/shard_map/ppermute | solution.py:37
  130.3 11.9 %collective-permute-start.25 = (bf16[2,128,512]{2,1,0:T(8,128)(2,1)S(1)}, bf16[2,128,512]{2,1,0:T(8,128)(2,1)S(1)}, u32[]{:S(2)}, u32[]{:S(2)}) collective-permute-start(bf16[2,128,512]{2,1,0:T(8,128)(2,1)S(1)} %pad_maximum_fusion.6), channel_id=1, source_target_pairs={{0,4},{2,6},{4,0},{6,2},{8,12},{10,14},{12,8},{14,10},{1,5},{3,7},... | collective-permute-start | bytes 786440 | tf_op jit(solution)/shard_map/ppermute | solution.py:37
  137.2 10.6 %collective-permute-start.27 = (bf16[2,128,640]{2,1,0:T(8,128)(2,1)S(1)}, bf16[2,128,640]{2,1,0:T(8,128)(2,1)S(1)}, u32[]{:S(2)}, u32[]{:S(2)}) collective-permute-start(bf16[2,128,640]{2,1,0:T(8,128)(2,1)S(1)} %pad_maximum_fusion.4), channel_id=1, source_target_pairs={{0,4},{2,6},{4,0},{6,2},{8,12},{10,14},{12,8},{14,10},{1,5},{3,7},... | collective-permute-start | bytes 983048 | tf_op jit(solution)/shard_map/ppermute | solution.py:37
  160.0 8.4 %collective-permute-start.31 = (bf16[2,2,64,512]{3,2,1,0:T(8,128)(2,1)S(1)}, bf16[2,2,64,512]{3,2,1,0:T(8,128)(2,1)S(1)}, u32[]{:S(2)}, u32[]{:S(2)}) collective-permute-start(bf16[2,2,64,512]{3,2,1,0:T(8,128)(2,1)S(1)} %bitcast.87), channel_id=1, source_target_pairs={{0,4},{2,6},{4,0},{6,2},{8,12},{10,14},{12,8},{14,10},{1,5},{3,7},... | collective-permute-start | bytes 786440 | tf_op jit(solution)/shard_map/ppermute | solution.py:37
  168.5 8.5 %collective-permute-start.32 = (bf16[1,2,64,512]{3,2,1,0:T(8,128)(2,1)S(1)}, bf16[1,2,64,512]{3,2,1,0:T(8,128)(2,1)S(1)}, u32[]{:S(2)}, u32[]{:S(2)}) collective-permute-start(bf16[1,2,64,512]{3,2,1,0:T(8,128)(2,1)S(1)} %slice.211), channel_id=1, source_target_pairs={{0,8},{2,10},{4,12},{6,14},{8,0},{10,2},{12,4},{14,6},{1,9},{3,11}... | collective-permute-start | bytes 393224 | tf_op jit(solution)/shard_map/ppermute | solution.py:37
  190.0 14.9 %collective-permute-start.38 = (bf16[4,64,1024]{2,1,0:T(8,128)(2,1)S(1)}, bf16[4,64,1024]{2,1,0:T(8,128)(2,1)S(1)}, u32[]{:S(2)}, u32[]{:S(2)}) collective-permute-start(bf16[4,64,1024]{2,1,0:T(8,128)(2,1)S(1)} %get-tuple-element.143), channel_id=1, source_target_pairs={{0,2},{2,0},{4,6},{6,4},{8,10},{10,8},{12,14},{14,12},{1,3},{3,1},... | collective-permute-start | bytes 1572872 | tf_op jit(solution)/shard_map/ppermute | solution.py:37
  194.4 18.9 %collective-permute-start.37 = (bf16[4,3,128,128]{3,2,1,0:T(8,128)(2,1)S(1)}, bf16[4,3,128,128]{3,2,1,0:T(8,128)(2,1)S(1)}, u32[]{:S(2)}, u32[]{:S(2)}) collective-permute-start(bf16[4,3,128,128]{3,2,1,0:T(8,128)(2,1)S(1)} %get-tuple-element.135), channel_id=1, source_target_pairs={{0,2},{2,0},{4,6},{6,4},{8,10},{10,8},{12,14},{14,12},{1,3},{3,1},... | collective-permute-start | bytes 1179656 | tf_op jit(solution)/shard_map/ppermute | solution.py:37
  205.2 10.4 %collective-permute-start.42 = (bf16[2,64,1024]{2,1,0:T(8,128)(2,1)S(1)}, bf16[2,64,1024]{2,1,0:T(8,128)(2,1)S(1)}, u32[]{:S(2)}, u32[]{:S(2)}) collective-permute-start(bf16[2,64,1024]{2,1,0:T(8,128)(2,1)S(1)} %slice.218), channel_id=1, source_target_pairs={{0,4},{2,6},{4,0},{6,2},{8,12},{10,14},{12,8},{14,10},{1,5},{3,7},... | collective-permute-start | bytes 786440 | tf_op jit(solution)/shard_map/ppermute | solution.py:37
  206.8 19.5 %collective-permute-start.40 = (bf16[4,3,128,128]{3,2,1,0:T(8,128)(2,1)S(1)}, bf16[4,3,128,128]{3,2,1,0:T(8,128)(2,1)S(1)}, u32[]{:S(2)}, u32[]{:S(2)}) collective-permute-start(bf16[4,3,128,128]{3,2,1,0:T(8,128)(2,1)S(1)} %get-tuple-element.150), channel_id=1, source_target_pairs={{0,2},{2,0},{4,6},{6,4},{8,10},{10,8},{12,14},{14,12},{1,3},{3,1},... | collective-permute-start | bytes 1179656 | tf_op jit(solution)/shard_map/ppermute | solution.py:37
  207.7 26.3 %collective-permute-start.45 = (bf16[4,3,128,128]{3,2,1,0:T(8,128)(2,1)S(1)}, bf16[4,3,128,128]{3,2,1,0:T(8,128)(2,1)S(1)}, u32[]{:S(2)}, u32[]{:S(2)}) collective-permute-start(bf16[4,3,128,128]{3,2,1,0:T(8,128)(2,1)S(1)} %get-tuple-element.160), channel_id=1, source_target_pairs={{0,2},{2,0},{4,6},{6,4},{8,10},{10,8},{12,14},{14,12},{1,3},{3,1},... | collective-permute-start | bytes 1179656 | tf_op jit(solution)/shard_map/ppermute | solution.py:37
  213.4 12.7 %collective-permute-start.41 = (bf16[4,3,128,128]{3,2,1,0:T(8,128)(2,1)S(1)}, bf16[4,3,128,128]{3,2,1,0:T(8,128)(2,1)S(1)}, u32[]{:S(2)}, u32[]{:S(2)}) collective-permute-start(bf16[4,3,128,128]{3,2,1,0:T(8,128)(2,1)S(1)} %get-tuple-element.151), channel_id=1, source_target_pairs={{0,4},{2,6},{4,0},{6,2},{8,12},{10,14},{12,8},{14,10},{1,5},{3,7},... | collective-permute-start | bytes 1179656 | tf_op jit(solution)/shard_map/ppermute | solution.py:37
  214.1 14.1 %collective-permute-start.39 = (bf16[2,3,128,128]{3,2,1,0:T(8,128)(2,1)S(1)}, bf16[2,3,128,128]{3,2,1,0:T(8,128)(2,1)S(1)}, u32[]{:S(2)}, u32[]{:S(2)}) collective-permute-start(bf16[2,3,128,128]{3,2,1,0:T(8,128)(2,1)S(1)} %slice.216), channel_id=1, source_target_pairs={{0,4},{2,6},{4,0},{6,2},{8,12},{10,14},{12,8},{14,10},{1,5},{3,7},... | collective-permute-start | bytes 589832 | tf_op jit(solution)/shard_map/ppermute | solution.py:37
  215.7 12.6 %collective-permute-start.51 = (bf16[1,64,1024]{2,1,0:T(8,128)(2,1)S(1)}, bf16[1,64,1024]{2,1,0:T(8,128)(2,1)S(1)}, u32[]{:S(2)}, u32[]{:S(2)}) collective-permute-start(bf16[1,64,1024]{2,1,0:T(8,128)(2,1)S(1)} %slice.234), channel_id=1, source_target_pairs={{0,8},{2,10},{4,12},{6,14},{8,0},{10,2},{12,4},{14,6},{1,9},{3,11}... | collective-permute-start | bytes 393224 | tf_op jit(solution)/shard_map/ppermute | solution.py:37
  229.4 9.4 %collective-permute-start.48 = (bf16[2,3,128,128]{3,2,1,0:T(8,128)(2,1)S(1)}, bf16[2,3,128,128]{3,2,1,0:T(8,128)(2,1)S(1)}, u32[]{:S(2)}, u32[]{:S(2)}) collective-permute-start(bf16[2,3,128,128]{3,2,1,0:T(8,128)(2,1)S(1)} %slice.228), channel_id=1, source_target_pairs={{0,2},{2,0},{4,6},{6,4},{8,10},{10,8},{12,14},{14,12},{1,3},{3,1},... | collective-permute-start | bytes 589832 | tf_op jit(solution)/shard_map/ppermute | solution.py:37
  234.2 8.7 %collective-permute-start.47 = (bf16[2,3,128,128]{3,2,1,0:T(8,128)(2,1)S(1)}, bf16[2,3,128,128]{3,2,1,0:T(8,128)(2,1)S(1)}, u32[]{:S(2)}, u32[]{:S(2)}) collective-permute-start(bf16[2,3,128,128]{3,2,1,0:T(8,128)(2,1)S(1)} %slice.226), channel_id=1, source_target_pairs={{0,4},{2,6},{4,0},{6,2},{8,12},{10,14},{12,8},{14,10},{1,5},{3,7},... | collective-permute-start | bytes 589832 | tf_op jit(solution)/shard_map/ppermute | solution.py:37
  243.0 7.7 %collective-permute-start.49 = (bf16[1,3,128,128]{3,2,1,0:T(8,128)(2,1)S(1)}, bf16[1,3,128,128]{3,2,1,0:T(8,128)(2,1)S(1)}, u32[]{:S(2)}, u32[]{:S(2)}) collective-permute-start(bf16[1,3,128,128]{3,2,1,0:T(8,128)(2,1)S(1)} %slice.230), channel_id=1, source_target_pairs={{0,8},{2,10},{4,12},{6,14},{8,0},{10,2},{12,4},{14,6},{1,9},{3,11}... | collective-permute-start | bytes 294920 | tf_op jit(solution)/shard_map/ppermute | solution.py:37
  (37 other events, 352.9 us)

commit v9 on v6

--- a/solution.py
+++ b/solution.py
@@ -695,14 +695,19 @@
     crossed = [bits[1], bits[0]] + bits[2:]
     d_attn, out_even, out_odd = out_grad(d_ext, weight_out, pooled_attn, at, bits)
     chunks = []
+    out_got = swap_tm(out_odd, bits[0])
     for pair, path in enumerate((bits, bits, bits, crossed)):
+        if pair == 3:
+            at, out_got = lax.optimization_barrier((at, out_got))
         even, odd = encoder_backward(turned, qkv, probs, d_attn, at, path, pair, 1)
         even, odd, at = lax.optimization_barrier((even, odd, at))
         chunks.append((even, odd, path))
-    chunks.append((out_even, out_odd, bits))
-    steps = list(range(len(chunks))) * len(bits)
+    out_low = (out_even.astype(F32) + out_got.astype(F32)).astype(BF)
+    out_half = out_low.shape[0] // 2
+    chunks.append((out_low[:out_half], out_low[out_half:], bits[1:]))
+    steps = [i for t in range(len(bits)) for i, c in enumerate(chunks) if t < len(c[2])]
     if len(bits) == 3:
-        steps = [0, 0, 1, 3, 0, 1, 4, 1, 4, 2, 3, 4, 2, 3, 2]
+        steps = [0, 4, 1, 0, 4, 3, 2, 0, 1, 3, 2, 1, 3, 2]
     chunks = scatter_chunks(chunks, steps, even)
     grad_out = chunks.pop()
     grad_qkv = jnp.transpose(jnp.concatenate(chunks, axis=-1), (1, 0, 2))

time: 247 us -> 246 us (level)
  waiting for transfers between devices: 112 us -> 109 us
    ppermute x36, waiting for transfers between devices: 100 us -> 96.6 us  [swap_tm(): return lax.ppermute(block, 'tm', [(i, i ^ mask) for i in range(n)])]
  transfers between devices with their start and end apart: 51 -> 51, of which waited for: 31 -> 29; matrix products, arithmetic and copies ran while one was open for 11% -> 11% of each run, Pallas kernels for 10% -> 11%
where the time goes in v9:
time: 246 us; the launch traced here: 243 us
  waiting for transfers between devices  109 us (44%)
  starting transfers between devices  57.1 us (23%)
  Pallas kernels  39.4 us (16%)
  local copies, waits for them, and re-layouts  16.2 us (7%)
  other arithmetic  13.7 us (6%)
  between operations  4.11 us (2%)
  matrix products  3.59 us (1%)
    ppermute x36, waiting for transfers between devices, swap_tm(): return lax.ppermute(block, 'tm', [(i, i ^ mask) for i in range(n)])  96.6 us
    ppermute x36, starting transfers between devices, swap_tm(): return lax.ppermute(block, 'tm', [(i, i ^ mask) for i in range(n)])  40.6 us
    ppermute x5, starting transfers between devices, to_tm(): return lax.ppermute(block, ('tm', 'mp'), pairs)  13.4 us
    pallas_call x1, Pallas kernels, encoder_forward(): pl.pallas_call(forward_kernel, grid_spec=pltpu.PrefetchScalarGridSpec(num...  11.1 us
    pallas_call x4, Pallas kernels, encoder_backward(): pl.pallas_call(functools.partial(backward_kernel, masks), grid_spec=pltpu...  11 us
    ppermute x5, waiting for transfers between devices, to_tm(): return lax.ppermute(block, ('tm', 'mp'), pairs)  8.02 us
    pallas_call x1, Pallas kernels, lower(): pl.pallas_call(functools.partial(lower_kernel, table, order), in_specs=[p...  6.42 us
    pallas_call x1, Pallas kernels, lift(): pl.pallas_call(functools.partial(lift_kernel, table, order), in_specs=[pl...  5.22 us
  transfers between devices with their start and end apart: 51, of which 29 were waited for; matrix products, arithmetic and copies ran while one was open for 11% of the time, Pallas kernels for 11%

profile of v9, /device:TPU:0, one launch (start us, length us, event | category | flops | bytes accessed | tf_op | source)
XLA Modules:
  0.0 242.9 jit_solution(8540762100386108849)
XLA Ops:
  2.4 6.0 %collective-permute-start = (bf16[128,1024]{1,0:T(8,128)(2,1)}, bf16[128,1024]{1,0:T(8,128)(2,1)}, u32[]{:S(2)}, u32[]{:S(2)}) collective-permute-start(bf16[128,1024]{1,0:T(8,128)(2,1)} %constant_dynamic-slice_fusion.6), channel_id=1, source_target_pairs={{0,14},{1,15},{2,0},{3,1},{4,2},{5,3},{6,4},{7,5},{8,6},{9,7},{10,... | collective-permute-start | bytes 786440 | tf_op jit(solution)/shard_map/ppermute | solution.py:51
  10.7 3.2 %copy.14 = bf16[3,512,1024]{2,1,0:T(8,128)(2,1)S(1)} copy(bf16[3,512,1024]{1,2,0:T(8,128)(2,1)} %bitcast.88) | data formatting | bytes 6291456 | tf_op jit(solution)/shard_map/transpose | solution.py:563
  17.1 3.3 %collective-permute-start.6 = (bf16[128,1024]{1,0:T(8,128)(2,1)}, bf16[128,1024]{1,0:T(8,128)(2,1)}, u32[]{:S(2)}, u32[]{:S(2)}) collective-permute-start(bf16[128,1024]{1,0:T(8,128)(2,1)} %get-tuple-element.175), channel_id=1, source_target_pairs={{0,8},{2,10},{4,12},{6,14},{8,0},{10,2},{12,4},{14,6},{1,9},{3,11}... | collective-permute-start | bytes 786440 | tf_op jit(solution)/shard_map/ppermute | solution.py:37
  28.1 11.1 %encoder_forward.1 = (bf16[512,1024]{1,0:T(8,128)(2,1)}, bf16[3,512,512]{2,1,0:T(8,128)(2,1)}, bf16[4,2,2,256,256]{4,3,2,1,0:T(8,128)(2,1)}, bf16[192,512]{1,0:T...) custom-call(s32[5]{0:T(128)S(1)} %stack.49.at, ...), custom_call_target="tpu_custom_call" | custom-call | tf_op jit(solution)/shard_map/encoder_forward/pallas_call | solution.py:206
  52.8 3.0 %collective-permute-done.9 = bf16[64,512]{1,0:T(8,128)(2,1)S(1)} collective-permute-done((bf16[64,512]{1,0:T(8,128)(2,1)S(1)}, bf16[64,512]{1,0:T(8,128)(2,1)S(1)}, u32[]{:S(2)}, u32[]{:S(2)}) %collective-permute-start.9) | collective-permute-done | bytes 65568 | tf_op jit(solution)/shard_map/ppermute | solution.py:37
  58.5 3.7 %collective-permute-done.10 = bf16[1,2,64,512]{3,2,1,0:T(8,128)(2,1)} collective-permute-done((bf16[1,2,64,512]{3,2,1,0:T(8,128)(2,1)S(1)}, bf16[1,2,64,512]{3,2,1,0:T(8,128)(2,1)}, u32[]{:S(2)}, u32[]{:S(2)}) %collective-permute-start.10) | collective-permute-done | bytes 131104 | tf_op jit(solution)/shard_map/ppermute | solution.py:37
  63.3 7.3 %collective-permute-done.11 = bf16[2,2,64,512]{3,2,1,0:T(8,128)(2,1)S(1)} collective-permute-done((bf16[2,2,64,512]{3,2,1,0:T(8,128)(2,1)S(1)}, bf16[2,2,64,512]{3,2,1,0:T(8,128)(2,1)S(1)}, u32[]{:S(2)}, u32[]{:S(2)}) %collective-permute-start.11) | collective-permute-done | bytes 262176 | tf_op jit(solution)/shard_map/ppermute | solution.py:37
  71.4 3.1 %pad_maximum_fusion.kvb = bf16[2,512,1024]{2,1,0:T(8,128)(2,1)} fusion(bf16[1,512,1024]{2,1,0:T(8,128)(2,1)} %bitcast.19, bf16[1,512,1024]{2,1,0:T(8,128)(2,1)} %bitcast.18), kind=kLoop, calls=%fused_computation | loop fusion | flops 1048576 | bytes 4194304 | tf_op jit(solution)/shard_map/stack | solution.py:636
  74.5 5.8 %collective-permute-done.13.there = bf16[4,128,1024]{2,1,0:T(8,128)(2,1)S(1)} collective-permute-done((bf16[4,128,1024]{2,1,0:T(8,128)(2,1)S(1)}, bf16[4,128,1024]{2,1,0:T(8,128)(2,1)S(1)}, u32[]{:S(2)}, u32[]{:S(2)}) %collective-permute-start.13) | collective-permute-done | bytes 1048608 | tf_op jit(solution)/shard_map/ppermute | solution.py:37
  81.3 5.2 %lift.1 = (bf16[512,1024]{1,0:T(8,128)(2,1)S(1)}, f32[4,128]{1,0:T(4,128)S(1)}, bf16[512,1024]{1,0:T(8,128)(2,1)S(1)}, bf16[512,1024]{1,0:T(8,128)(2,1)S(1)}) custom-call(s32[5]{0:T(128)S(1)} %stack.49.at, bf16[512,512]{1,0:T(8,128)(2,1)S(1)} %bitcast.74, bf16[512,512]{1,0:T(8,128)(2,1)S(1)} %collective-permute-done.12.tb, ...), custom_call_target="tpu_custom_call" | custom-call | tf_op jit(solution)/shard_map/lift/pallas_call | solution.py:414
  88.1 2.9 %keep_columns.1 = bf16[512,1024]{1,0:T(8,128)(2,1)S(1)} custom-call(s32[5]{0:T(128)S(1)} %stack.49.at, bf16[512,1024]{1,0:T(8,128)(2,1)S(1)} %get-tuple-element.111.low, bf16[512,2048]{1,0:T(8,128)(2,1)S(1)} %copy-done.2, bf16[2,512,1024]{2,1,0:T(8,128)(2,1)} %pad_maximum_fusion.kvb), custom_call_target="tpu_custom_call" | custom-call | tf_op jit(solution)/shard_map/keep_columns/pallas_call | solution.py:437
  97.2 3.6 %collective-permute-done.16 = bf16[2,128,512]{2,1,0:T(8,128)(2,1)S(1)} collective-permute-done((bf16[2,128,512]{2,1,0:T(8,128)(2,1)S(1)}, bf16[2,128,512]{2,1,0:T(8,128)(2,1)S(1)}, u32[]{:S(2)}, u32[]{:S(2)}) %collective-permute-start.16) | collective-permute-done | bytes 262176 | tf_op jit(solution)/shard_map/ppermute | solution.py:37
  103.5 4.7 %collective-permute-done.18 = bf16[2,128,512]{2,1,0:T(8,128)(2,1)S(1)} collective-permute-done((bf16[2,128,512]{2,1,0:T(8,128)(2,1)S(1)}, bf16[2,128,512]{2,1,0:T(8,128)(2,1)S(1)}, u32[]{:S(2)}, u32[]{:S(2)}) %collective-permute-start.18) | collective-permute-done | bytes 262176 | tf_op jit(solution)/shard_map/ppermute | solution.py:37
  111.7 8.3 %collective-permute-done.22 = bf16[1,128,512]{2,1,0:T(8,128)(2,1)S(1)} collective-permute-done((bf16[1,128,512]{2,1,0:T(8,128)(2,1)S(1)}, bf16[1,128,512]{2,1,0:T(8,128)(2,1)S(1)}, u32[]{:S(2)}, u32[]{:S(2)}) %collective-permute-start.22) | collective-permute-done | bytes 131104 | tf_op jit(solution)/shard_map/ppermute | solution.py:37
  123.7 5.1 %collective-permute-done.25 = bf16[1,128,640]{2,1,0:T(8,128)(2,1)S(1)} collective-permute-done((bf16[1,128,640]{2,1,0:T(8,128)(2,1)S(1)}, bf16[1,128,640]{2,1,0:T(8,128)(2,1)S(1)}, u32[]{:S(2)}, u32[]{:S(2)}) %collective-permute-start.25) | collective-permute-done | bytes 163872 | tf_op jit(solution)/shard_map/ppermute | solution.py:37
  128.9 3.8 %collective-permute-done.24 = bf16[2,128,512]{2,1,0:T(8,128)(2,1)S(1)} collective-permute-done((bf16[2,128,512]{2,1,0:T(8,128)(2,1)S(1)}, bf16[2,128,512]{2,1,0:T(8,128)(2,1)S(1)}, u32[]{:S(2)}, u32[]{:S(2)}) %collective-permute-start.24) | collective-permute-done | bytes 262176 | tf_op jit(solution)/shard_map/ppermute | solution.py:37
  132.8 5.9 %collective-permute-done.26 = bf16[2,128,640]{2,1,0:T(8,128)(2,1)S(1)} collective-permute-done((bf16[2,128,640]{2,1,0:T(8,128)(2,1)S(1)}, bf16[2,128,640]{2,1,0:T(8,128)(2,1)S(1)}, u32[]{:S(2)}, u32[]{:S(2)}) %collective-permute-start.26) | collective-permute-done | bytes 327712 | tf_op jit(solution)/shard_map/ppermute | solution.py:37
  141.7 6.4 %lower.1 = (bf16[512,512]{1,0:T(8,128)(2,1)S(1)}, bf16[512,512]{1,0:T(8,128)(2,1)S(1)}) custom-call(s32[5]{0:T(128)S(1)} %stack.49.at, bf16[512,512]{1,0:T(8,128)(2,1)S(1)} %bitcast.72, bf16[512,640]{1,0:T(8,128)(2,1)S(1)} %bitcast.70, bf16[512,512]{1,0:T(8,128)(2,1)S(1)} %collective-permute-done.27.cb0, bf16[512,640]{1,0:T(8,128)(2,1)S(1)} %collective-permute-done.28.cb1, ...), custom_call_target="tpu_custom_call" | custom-call | tf_op jit(solution)/shard_map/lower/pallas_call | solution.py:536
  150.5 8.2 %collective-permute-done.30 = bf16[2,2,64,512]{3,2,1,0:T(8,128)(2,1)S(1)} collective-permute-done((bf16[2,2,64,512]{3,2,1,0:T(8,128)(2,1)S(1)}, bf16[2,2,64,512]{3,2,1,0:T(8,128)(2,1)S(1)}, u32[]{:S(2)}, u32[]{:S(2)}) %collective-permute-start.30) | collective-permute-done | bytes 262176 | tf_op jit(solution)/shard_map/ppermute | solution.py:37
  158.8 3.2 %collective-permute-start.31 = (bf16[1,2,64,512]{3,2,1,0:T(8,128)(2,1)S(1)}, bf16[1,2,64,512]{3,2,1,0:T(8,128)(2,1)S(1)}, u32[]{:S(2)}, u32[]{:S(2)}) collective-permute-start(bf16[1,2,64,512]{3,2,1,0:T(8,128)(2,1)S(1)} %slice.211), channel_id=1, source_target_pairs={{0,8},{2,10},{4,12},{6,14},{8,0},{10,2},{12,4},{14,6},{1,9},{3,11}... | collective-permute-start | bytes 393224 | tf_op jit(solution)/shard_map/ppermute | solution.py:37
  162.0 6.1 %collective-permute-done.31 = bf16[1,2,64,512]{3,2,1,0:T(8,128)(2,1)S(1)} collective-permute-done((bf16[1,2,64,512]{3,2,1,0:T(8,128)(2,1)S(1)}, bf16[1,2,64,512]{3,2,1,0:T(8,128)(2,1)S(1)}, u32[]{:S(2)}, u32[]{:S(2)}) %collective-permute-start.31) | collective-permute-done | bytes 131104 | tf_op jit(solution)/shard_map/ppermute | solution.py:37
  169.4 3.1 %collective-permute-done.32 = bf16[64,512]{1,0:T(8,128)(2,1)S(1)} collective-permute-done((bf16[64,512]{1,0:T(8,128)(2,1)S(1)}, bf16[64,512]{1,0:T(8,128)(2,1)S(1)}, u32[]{:S(2)}, u32[]{:S(2)}) %collective-permute-start.32) | collective-permute-done | bytes 65568 | tf_op jit(solution)/shard_map/ppermute | solution.py:37
  172.8 4.2 %collective-permute-start.35 = (bf16[64,512]{1,0:T(8,128)(2,1)S(1)}, bf16[64,512]{1,0:T(8,128)(2,1)S(1)}, u32[]{:S(2)}, u32[]{:S(2)}) collective-permute-start(bf16[64,512]{1,0:T(8,128)(2,1)S(1)} %slice.214), channel_id=1, source_target_pairs={{0,15},{1,14},{2,1},{3,0},{4,3},{5,2},{6,5},{7,4},{8,7},{9,6},{10,... | collective-permute-start | bytes 196616 | tf_op jit(solution)/shard_map/ppermute | solution.py:51
  183.1 2.8 %encoder_backward.4 = (bf16[4,3,128,128]{3,2,1,0:T(8,128)(2,1)S(1)}, bf16[4,3,128,128]{3,2,1,0:T(8,128)(2,1)S(1)}) custom-call(s32[5]{0:T(128)S(1)} %stack.49.at, bf16[1024,512]{1,0:T(8,128)(2,1)S(1)} %bitcast.65, bf16[3,512,512]{2,1,0:T(8,128)(2,1)S(1)} %copy-done.3, bf16[4,2,2,256,256]{4,3,2,1,0:T(8,128)(2,1)S(1)} %copy-done.1, ...), custom_call_target="tpu_custom_call" | custom-call | tf_op jit(solution)/shard_map/encoder_backward/pallas_call | solution.py:317
  188.0 2.8 %encoder_backward.5 = (bf16[4,3,128,128]{3,2,1,0:T(8,128)(2,1)S(1)}, bf16[4,3,128,128]{3,2,1,0:T(8,128)(2,1)S(1)}) custom-call(s32[5]{0:T(128)S(1)} %stack.49.at, bf16[1024,512]{1,0:T(8,128)(2,1)S(1)} %bitcast.66, bf16[3,512,512]{2,1,0:T(8,128)(2,1)S(1)} %copy-done.3, bf16[4,2,2,256,256]{4,3,2,1,0:T(8,128)(2,1)S(1)} %copy-done.1, ...), custom_call_target="tpu_custom_call" | custom-call | tf_op jit(solution)/shard_map/encoder_backward/pallas_call | solution.py:317
  190.7 2.8 %encoder_backward.6 = (bf16[4,3,128,128]{3,2,1,0:T(8,128)(2,1)S(1)}, bf16[4,3,128,128]{3,2,1,0:T(8,128)(2,1)S(1)}) custom-call(s32[5]{0:T(128)S(1)} %stack.49.at, bf16[1024,512]{1,0:T(8,128)(2,1)S(1)} %bitcast.67, bf16[3,512,512]{2,1,0:T(8,128)(2,1)S(1)} %copy-done.3, bf16[4,2,2,256,256]{4,3,2,1,0:T(8,128)(2,1)S(1)} %copy-done.1, ...), custom_call_target="tpu_custom_call" | custom-call | tf_op jit(solution)/shard_map/encoder_backward/pallas_call | solution.py:317
  193.5 4.4 %collective-permute-done.37 = bf16[4,64,1024]{2,1,0:T(8,128)(2,1)S(1)} collective-permute-done((bf16[4,64,1024]{2,1,0:T(8,128)(2,1)S(1)}, bf16[4,64,1024]{2,1,0:T(8,128)(2,1)S(1)}, u32[]{:S(2)}, u32[]{:S(2)}) %collective-permute-start.37) | collective-permute-done | bytes 524320 | tf_op jit(solution)/shard_map/ppermute | solution.py:37
  208.7 6.1 %collective-permute-done.39 = bf16[4,3,128,128]{3,2,1,0:T(8,128)(2,1)S(1)} collective-permute-done((bf16[4,3,128,128]{3,2,1,0:T(8,128)(2,1)S(1)}, bf16[4,3,128,128]{3,2,1,0:T(8,128)(2,1)S(1)}, u32[]{:S(2)}, u32[]{:S(2)}) %collective-permute-start.39) | collective-permute-done | bytes 393248 | tf_op jit(solution)/shard_map/ppermute | solution.py:37
  218.5 3.8 %collective-permute-done.50 = bf16[1,64,1024]{2,1,0:T(8,128)(2,1)S(1)} collective-permute-done((bf16[1,64,1024]{2,1,0:T(8,128)(2,1)S(1)}, bf16[1,64,1024]{2,1,0:T(8,128)(2,1)S(1)}, u32[]{:S(2)}, u32[]{:S(2)}) %collective-permute-start.50) | collective-permute-done | bytes 131104 | tf_op jit(solution)/shard_map/ppermute | solution.py:37
  222.3 3.3 %collective-permute-done.43 = bf16[4,3,128,128]{3,2,1,0:T(8,128)(2,1)S(1)} collective-permute-done((bf16[4,3,128,128]{3,2,1,0:T(8,128)(2,1)S(1)}, bf16[4,3,128,128]{3,2,1,0:T(8,128)(2,1)S(1)}, u32[]{:S(2)}, u32[]{:S(2)}) %collective-permute-start.43) | collective-permute-done | bytes 393248 | tf_op jit(solution)/shard_map/ppermute | solution.py:37
  226.7 3.4 %collective-permute-start.46 = (bf16[2,3,128,128]{3,2,1,0:T(8,128)(2,1)S(1)}, bf16[2,3,128,128]{3,2,1,0:T(8,128)(2,1)S(1)}, u32[]{:S(2)}, u32[]{:S(2)}) collective-permute-start(bf16[2,3,128,128]{3,2,1,0:T(8,128)(2,1)S(1)} %slice.226), channel_id=1, source_target_pairs={{0,4},{2,6},{4,0},{6,2},{8,12},{10,14},{12,8},{14,10},{1,5},{3,7},... | collective-permute-start | bytes 589832 | tf_op jit(solution)/shard_map/ppermute | solution.py:37
  230.2 3.1 %collective-permute-start.45 = (bf16[1,3,128,128]{3,2,1,0:T(8,128)(2,1)S(1)}, bf16[1,3,128,128]{3,2,1,0:T(8,128)(2,1)S(1)}, u32[]{:S(2)}, u32[]{:S(2)}) collective-permute-start(bf16[1,3,128,128]{3,2,1,0:T(8,128)(2,1)S(1)} %slice.224), channel_id=1, source_target_pairs={{0,8},{2,10},{4,12},{6,14},{8,0},{10,2},{12,4},{14,6},{1,9},{3,11}... | collective-permute-start | bytes 294920 | tf_op jit(solution)/shard_map/ppermute | solution.py:37
  (204 shorter events, 89.2 us)
Async XLA Ops:
  2.4 18.1 %collective-permute-start = (bf16[128,1024]{1,0:T(8,128)(2,1)}, bf16[128,1024]{1,0:T(8,128)(2,1)}, u32[]{:S(2)}, u32[]{:S(2)}) collective-permute-start(bf16[128,1024]{1,0:T(8,128)(2,1)} %constant_dynamic-slice_fusion.6), channel_id=1, source_target_pairs={{0,14},{1,15},{2,0},{3,1},{4,2},{5,3},{6,4},{7,5},{8,6},{9,7},{10,... | collective-permute-start | bytes 786440 | tf_op jit(solution)/shard_map/ppermute | solution.py:51
  10.7 31.9 %collective-permute-start.4 = (bf16[512,1024]{1,0:T(8,128)(2,1)}, bf16[512,1024]{1,0:T(8,128)(2,1)}, u32[]{:S(2)}, u32[]{:S(2)}) collective-permute-start(bf16[512,1024]{1,0:T(8,128)(2,1)} %constant_dynamic-slice_fusion.4), channel_id=1, source_target_pairs={{0,2},{2,0},{4,6},{6,4},{8,10},{10,8},{12,14},{14,12},{1,3},{3,1},... | collective-permute-start | bytes 3145736 | tf_op jit(solution)/shard_map/ppermute | solution.py:37
  16.1 26.9 %collective-permute-start.8 = (bf16[128,1024]{1,0:T(8,128)(2,1)}, bf16[128,1024]{1,0:T(8,128)(2,1)}, u32[]{:S(2)}, u32[]{:S(2)}) collective-permute-start(bf16[128,1024]{1,0:T(8,128)(2,1)} %get-tuple-element.173), channel_id=1, source_target_pairs={{0,12},{2,14},{4,8},{6,10},{8,4},{10,6},{12,0},{14,2},{1,13},{3,15... | collective-permute-start | bytes 786440 | tf_op jit(solution)/shard_map/ppermute | solution.py:37
  17.1 26.5 %collective-permute-start.7 = (bf16[128,1024]{1,0:T(8,128)(2,1)}, bf16[128,1024]{1,0:T(8,128)(2,1)}, u32[]{:S(2)}, u32[]{:S(2)}) collective-permute-start(bf16[128,1024]{1,0:T(8,128)(2,1)} %get-tuple-element.174), channel_id=1, source_target_pairs={{0,4},{2,6},{4,0},{6,2},{8,12},{10,14},{12,8},{14,10},{1,5},{3,7},... | collective-permute-start | bytes 786440 | tf_op jit(solution)/shard_map/ppermute | solution.py:37
  17.1 28.1 %collective-permute-start.6 = (bf16[128,1024]{1,0:T(8,128)(2,1)}, bf16[128,1024]{1,0:T(8,128)(2,1)}, u32[]{:S(2)}, u32[]{:S(2)}) collective-permute-start(bf16[128,1024]{1,0:T(8,128)(2,1)} %get-tuple-element.175), channel_id=1, source_target_pairs={{0,8},{2,10},{4,12},{6,14},{8,0},{10,2},{12,4},{14,6},{1,9},{3,11}... | collective-permute-start | bytes 786440 | tf_op jit(solution)/shard_map/ppermute | solution.py:37
  39.8 7.4 %collective-permute-start.2 = (bf16[64,512]{1,0:T(8,128)(2,1)}, bf16[64,512]{1,0:T(8,128)(2,1)S(1)}, u32[]{:S(2)}, u32[]{:S(2)}) collective-permute-start(bf16[64,512]{1,0:T(8,128)(2,1)} %get-tuple-element.91), channel_id=1, source_target_pairs={{0,2},{1,3},{2,4},{3,5},{4,6},{5,7},{6,8},{7,9},{8,10},{9,11},{10,... | collective-permute-start | bytes 196616 | tf_op jit(solution)/shard_map/ppermute | solution.py:51
  43.6 27.7 %collective-permute-start.14 = (bf16[512,1024]{1,0:T(8,128)(2,1)}, bf16[512,1024]{1,0:T(8,128)(2,1)}, u32[]{:S(2)}, u32[]{:S(2)}) collective-permute-start(bf16[512,1024]{1,0:T(8,128)(2,1)} %collective-permute-done.4), channel_id=1, source_target_pairs={{0,16},{16,0},{1,17},{17,1},{2,18},{18,2},{3,19},{19,3},{4,20},{20... | collective-permute-start | bytes 3145736 | tf_op jit(solution)/shard_map/ppermute | solution.py:592
  55.8 24.5 %collective-permute-start.13 = (bf16[4,128,1024]{2,1,0:T(8,128)(2,1)S(1)}, bf16[4,128,1024]{2,1,0:T(8,128)(2,1)S(1)}, u32[]{:S(2)}, u32[]{:S(2)}) collective-permute-start(bf16[4,128,1024]{2,1,0:T(8,128)(2,1)S(1)} %pad_maximum_fusion.1.here), channel_id=1, source_target_pairs={{0,2},{2,0},{4,6},{6,4},{8,10},{10,8},{12,14},{14,12},{1,3},{3,1},... | collective-permute-start | bytes 3145736 | tf_op jit(solution)/shard_map/ppermute | solution.py:37
  63.2 7.4 %collective-permute-start.11 = (bf16[2,2,64,512]{3,2,1,0:T(8,128)(2,1)S(1)}, bf16[2,2,64,512]{3,2,1,0:T(8,128)(2,1)S(1)}, u32[]{:S(2)}, u32[]{:S(2)}) collective-permute-start(bf16[2,2,64,512]{3,2,1,0:T(8,128)(2,1)S(1)} %pad_maximum_fusion.6), channel_id=1, source_target_pairs={{0,4},{2,6},{4,0},{6,2},{8,12},{10,14},{12,8},{14,10},{1,5},{3,7},... | collective-permute-start | bytes 786440 | tf_op jit(solution)/shard_map/ppermute | solution.py:37
  91.5 9.3 %collective-permute-start.16 = (bf16[2,128,512]{2,1,0:T(8,128)(2,1)S(1)}, bf16[2,128,512]{2,1,0:T(8,128)(2,1)S(1)}, u32[]{:S(2)}, u32[]{:S(2)}) collective-permute-start(bf16[2,128,512]{2,1,0:T(8,128)(2,1)S(1)} %get-tuple-element.171), channel_id=1, source_target_pairs={{0,4},{2,6},{4,0},{6,2},{8,12},{10,14},{12,8},{14,10},{1,5},{3,7},... | collective-permute-start | bytes 786440 | tf_op jit(solution)/shard_map/ppermute | solution.py:37
  94.6 14.7 %collective-permute-start.21 = (f32[1,128]{1,0:T(1,128)S(1)}, f32[1,128]{1,0:T(1,128)S(1)}, u32[]{:S(2)}, u32[]{:S(2)}) collective-permute-start(f32[1,128]{1,0:T(1,128)S(1)} %slice.165), channel_id=1, source_target_pairs={{0,8},{2,10},{4,12},{6,14},{8,0},{10,2},{12,4},{14,6},{1,9},{3,11}... | collective-permute-start | bytes 1544 | tf_op jit(solution)/shard_map/ppermute | solution.py:37
  97.2 11.1 %collective-permute-start.18 = (bf16[2,128,512]{2,1,0:T(8,128)(2,1)S(1)}, bf16[2,128,512]{2,1,0:T(8,128)(2,1)S(1)}, u32[]{:S(2)}, u32[]{:S(2)}) collective-permute-start(bf16[2,128,512]{2,1,0:T(8,128)(2,1)S(1)} %get-tuple-element.172), channel_id=1, source_target_pairs={{0,4},{2,6},{4,0},{6,2},{8,12},{10,14},{12,8},{14,10},{1,5},{3,7},... | collective-permute-start | bytes 786440 | tf_op jit(solution)/shard_map/ppermute | solution.py:37
  100.9 8.5 %collective-permute-start.17 = (bf16[1,128,512]{2,1,0:T(8,128)(2,1)S(1)}, bf16[1,128,512]{2,1,0:T(8,128)(2,1)S(1)}, u32[]{:S(2)}, u32[]{:S(2)}) collective-permute-start(bf16[1,128,512]{2,1,0:T(8,128)(2,1)S(1)} %get-tuple-element.182), channel_id=1, source_target_pairs={{0,8},{2,10},{4,12},{6,14},{8,0},{10,2},{12,4},{14,6},{1,9},{3,11}... | collective-permute-start | bytes 393224 | tf_op jit(solution)/shard_map/ppermute | solution.py:37
  108.3 11.6 %collective-permute-start.22 = (bf16[1,128,512]{2,1,0:T(8,128)(2,1)S(1)}, bf16[1,128,512]{2,1,0:T(8,128)(2,1)S(1)}, u32[]{:S(2)}, u32[]{:S(2)}) collective-permute-start(bf16[1,128,512]{2,1,0:T(8,128)(2,1)S(1)} %get-tuple-element.183), channel_id=1, source_target_pairs={{0,8},{2,10},{4,12},{6,14},{8,0},{10,2},{12,4},{14,6},{1,9},{3,11}... | collective-permute-start | bytes 393224 | tf_op jit(solution)/shard_map/ppermute | solution.py:37
  109.6 12.7 %collective-permute-start.23 = (bf16[1,128,512]{2,1,0:T(8,128)(2,1)S(1)}, bf16[1,128,512]{2,1,0:T(8,128)(2,1)S(1)}, u32[]{:S(2)}, u32[]{:S(2)}) collective-permute-start(bf16[1,128,512]{2,1,0:T(8,128)(2,1)S(1)} %bitcast.78), channel_id=1, source_target_pairs={{0,8},{2,10},{4,12},{6,14},{8,0},{10,2},{12,4},{14,6},{1,9},{3,11}... | collective-permute-start | bytes 393224 | tf_op jit(solution)/shard_map/ppermute | solution.py:37
  120.9 7.9 %collective-permute-start.25 = (bf16[1,128,640]{2,1,0:T(8,128)(2,1)S(1)}, bf16[1,128,640]{2,1,0:T(8,128)(2,1)S(1)}, u32[]{:S(2)}, u32[]{:S(2)}) collective-permute-start(bf16[1,128,640]{2,1,0:T(8,128)(2,1)S(1)} %bitcast.75), channel_id=1, source_target_pairs={{0,8},{2,10},{4,12},{6,14},{8,0},{10,2},{12,4},{14,6},{1,9},{3,11}... | collective-permute-start | bytes 491528 | tf_op jit(solution)/shard_map/ppermute | solution.py:37
  122.4 10.3 %collective-permute-start.24 = (bf16[2,128,512]{2,1,0:T(8,128)(2,1)S(1)}, bf16[2,128,512]{2,1,0:T(8,128)(2,1)S(1)}, u32[]{:S(2)}, u32[]{:S(2)}) collective-permute-start(bf16[2,128,512]{2,1,0:T(8,128)(2,1)S(1)} %pad_maximum_fusion.7), channel_id=1, source_target_pairs={{0,4},{2,6},{4,0},{6,2},{8,12},{10,14},{12,8},{14,10},{1,5},{3,7},... | collective-permute-start | bytes 786440 | tf_op jit(solution)/shard_map/ppermute | solution.py:37
  128.8 9.8 %collective-permute-start.26 = (bf16[2,128,640]{2,1,0:T(8,128)(2,1)S(1)}, bf16[2,128,640]{2,1,0:T(8,128)(2,1)S(1)}, u32[]{:S(2)}, u32[]{:S(2)}) collective-permute-start(bf16[2,128,640]{2,1,0:T(8,128)(2,1)S(1)} %pad_maximum_fusion.5), channel_id=1, source_target_pairs={{0,4},{2,6},{4,0},{6,2},{8,12},{10,14},{12,8},{14,10},{1,5},{3,7},... | collective-permute-start | bytes 983048 | tf_op jit(solution)/shard_map/ppermute | solution.py:37
  150.3 8.4 %collective-permute-start.30 = (bf16[2,2,64,512]{3,2,1,0:T(8,128)(2,1)S(1)}, bf16[2,2,64,512]{3,2,1,0:T(8,128)(2,1)S(1)}, u32[]{:S(2)}, u32[]{:S(2)}) collective-permute-start(bf16[2,2,64,512]{3,2,1,0:T(8,128)(2,1)S(1)} %bitcast.91), channel_id=1, source_target_pairs={{0,4},{2,6},{4,0},{6,2},{8,12},{10,14},{12,8},{14,10},{1,5},{3,7},... | collective-permute-start | bytes 786440 | tf_op jit(solution)/shard_map/ppermute | solution.py:37
  158.8 9.3 %collective-permute-start.31 = (bf16[1,2,64,512]{3,2,1,0:T(8,128)(2,1)S(1)}, bf16[1,2,64,512]{3,2,1,0:T(8,128)(2,1)S(1)}, u32[]{:S(2)}, u32[]{:S(2)}) collective-permute-start(bf16[1,2,64,512]{3,2,1,0:T(8,128)(2,1)S(1)} %slice.211), channel_id=1, source_target_pairs={{0,8},{2,10},{4,12},{6,14},{8,0},{10,2},{12,4},{14,6},{1,9},{3,11}... | collective-permute-start | bytes 393224 | tf_op jit(solution)/shard_map/ppermute | solution.py:37
  183.0 14.9 %collective-permute-start.37 = (bf16[4,64,1024]{2,1,0:T(8,128)(2,1)S(1)}, bf16[4,64,1024]{2,1,0:T(8,128)(2,1)S(1)}, u32[]{:S(2)}, u32[]{:S(2)}) collective-permute-start(bf16[4,64,1024]{2,1,0:T(8,128)(2,1)S(1)} %get-tuple-element.145), channel_id=1, source_target_pairs={{0,2},{2,0},{4,6},{6,4},{8,10},{10,8},{12,14},{14,12},{1,3},{3,1},... | collective-permute-start | bytes 1572872 | tf_op jit(solution)/shard_map/ppermute | solution.py:37
  185.9 20.5 %collective-permute-start.36 = (bf16[4,3,128,128]{3,2,1,0:T(8,128)(2,1)S(1)}, bf16[4,3,128,128]{3,2,1,0:T(8,128)(2,1)S(1)}, u32[]{:S(2)}, u32[]{:S(2)}) collective-permute-start(bf16[4,3,128,128]{3,2,1,0:T(8,128)(2,1)S(1)} %get-tuple-element.137), channel_id=1, source_target_pairs={{0,2},{2,0},{4,6},{6,4},{8,10},{10,8},{12,14},{14,12},{1,3},{3,1},... | collective-permute-start | bytes 1179656 | tf_op jit(solution)/shard_map/ppermute | solution.py:37
  198.2 10.4 %collective-permute-start.40 = (bf16[2,64,1024]{2,1,0:T(8,128)(2,1)S(1)}, bf16[2,64,1024]{2,1,0:T(8,128)(2,1)S(1)}, u32[]{:S(2)}, u32[]{:S(2)}) collective-permute-start(bf16[2,64,1024]{2,1,0:T(8,128)(2,1)S(1)} %slice.218), channel_id=1, source_target_pairs={{0,4},{2,6},{4,0},{6,2},{8,12},{10,14},{12,8},{14,10},{1,5},{3,7},... | collective-permute-start | bytes 786440 | tf_op jit(solution)/shard_map/ppermute | solution.py:37
  199.2 15.6 %collective-permute-start.39 = (bf16[4,3,128,128]{3,2,1,0:T(8,128)(2,1)S(1)}, bf16[4,3,128,128]{3,2,1,0:T(8,128)(2,1)S(1)}, u32[]{:S(2)}, u32[]{:S(2)}) collective-permute-start(bf16[4,3,128,128]{3,2,1,0:T(8,128)(2,1)S(1)} %get-tuple-element.152), channel_id=1, source_target_pairs={{0,2},{2,0},{4,6},{6,4},{8,10},{10,8},{12,14},{14,12},{1,3},{3,1},... | collective-permute-start | bytes 1179656 | tf_op jit(solution)/shard_map/ppermute | solution.py:37
  199.3 27.3 %collective-permute-start.42 = (bf16[4,3,128,128]{3,2,1,0:T(8,128)(2,1)S(1)}, bf16[4,3,128,128]{3,2,1,0:T(8,128)(2,1)S(1)}, u32[]{:S(2)}, u32[]{:S(2)}) collective-permute-start(bf16[4,3,128,128]{3,2,1,0:T(8,128)(2,1)S(1)} %get-tuple-element.159), channel_id=1, source_target_pairs={{0,2},{2,0},{4,6},{6,4},{8,10},{10,8},{12,14},{14,12},{1,3},{3,1},... | collective-permute-start | bytes 1179656 | tf_op jit(solution)/shard_map/ppermute | solution.py:37
  206.5 8.4 %collective-permute-start.38 = (bf16[2,3,128,128]{3,2,1,0:T(8,128)(2,1)S(1)}, bf16[2,3,128,128]{3,2,1,0:T(8,128)(2,1)S(1)}, u32[]{:S(2)}, u32[]{:S(2)}) collective-permute-start(bf16[2,3,128,128]{3,2,1,0:T(8,128)(2,1)S(1)} %slice.216), channel_id=1, source_target_pairs={{0,4},{2,6},{4,0},{6,2},{8,12},{10,14},{12,8},{14,10},{1,5},{3,7},... | collective-permute-start | bytes 589832 | tf_op jit(solution)/shard_map/ppermute | solution.py:37
  206.6 19.0 %collective-permute-start.43 = (bf16[4,3,128,128]{3,2,1,0:T(8,128)(2,1)S(1)}, bf16[4,3,128,128]{3,2,1,0:T(8,128)(2,1)S(1)}, u32[]{:S(2)}, u32[]{:S(2)}) collective-permute-start(bf16[4,3,128,128]{3,2,1,0:T(8,128)(2,1)S(1)} %get-tuple-element.160), channel_id=1, source_target_pairs={{0,4},{2,6},{4,0},{6,2},{8,12},{10,14},{12,8},{14,10},{1,5},{3,7},... | collective-permute-start | bytes 1179656 | tf_op jit(solution)/shard_map/ppermute | solution.py:37
  215.0 7.3 %collective-permute-start.50 = (bf16[1,64,1024]{2,1,0:T(8,128)(2,1)S(1)}, bf16[1,64,1024]{2,1,0:T(8,128)(2,1)S(1)}, u32[]{:S(2)}, u32[]{:S(2)}) collective-permute-start(bf16[1,64,1024]{2,1,0:T(8,128)(2,1)S(1)} %slice.234), channel_id=1, source_target_pairs={{0,8},{2,10},{4,12},{6,14},{8,0},{10,2},{12,4},{14,6},{1,9},{3,11}... | collective-permute-start | bytes 393224 | tf_op jit(solution)/shard_map/ppermute | solution.py:37
  215.7 11.0 %collective-permute-start.41 = (bf16[1,3,128,128]{3,2,1,0:T(8,128)(2,1)S(1)}, bf16[1,3,128,128]{3,2,1,0:T(8,128)(2,1)S(1)}, u32[]{:S(2)}, u32[]{:S(2)}) collective-permute-start(bf16[1,3,128,128]{3,2,1,0:T(8,128)(2,1)S(1)} %slice.220), channel_id=1, source_target_pairs={{0,8},{2,10},{4,12},{6,14},{8,0},{10,2},{12,4},{14,6},{1,9},{3,11}... | collective-permute-start | bytes 294920 | tf_op jit(solution)/shard_map/ppermute | solution.py:37
  218.1 12.0 %collective-permute-start.44 = (bf16[2,3,128,128]{3,2,1,0:T(8,128)(2,1)S(1)}, bf16[2,3,128,128]{3,2,1,0:T(8,128)(2,1)S(1)}, u32[]{:S(2)}, u32[]{:S(2)}) collective-permute-start(bf16[2,3,128,128]{3,2,1,0:T(8,128)(2,1)S(1)} %slice.222), channel_id=1, source_target_pairs={{0,4},{2,6},{4,0},{6,2},{8,12},{10,14},{12,8},{14,10},{1,5},{3,7},... | collective-permute-start | bytes 589832 | tf_op jit(solution)/shard_map/ppermute | solution.py:37
  225.7 7.6 %collective-permute-start.47 = (bf16[2,3,128,128]{3,2,1,0:T(8,128)(2,1)S(1)}, bf16[2,3,128,128]{3,2,1,0:T(8,128)(2,1)S(1)}, u32[]{:S(2)}, u32[]{:S(2)}) collective-permute-start(bf16[2,3,128,128]{3,2,1,0:T(8,128)(2,1)S(1)} %slice.228), channel_id=1, source_target_pairs={{0,2},{2,0},{4,6},{6,4},{8,10},{10,8},{12,14},{14,12},{1,3},{3,1},... | collective-permute-start | bytes 589832 | tf_op jit(solution)/shard_map/ppermute | solution.py:37
  226.7 9.6 %collective-permute-start.46 = (bf16[2,3,128,128]{3,2,1,0:T(8,128)(2,1)S(1)}, bf16[2,3,128,128]{3,2,1,0:T(8,128)(2,1)S(1)}, u32[]{:S(2)}, u32[]{:S(2)}) collective-permute-start(bf16[2,3,128,128]{3,2,1,0:T(8,128)(2,1)S(1)} %slice.226), channel_id=1, source_target_pairs={{0,4},{2,6},{4,0},{6,2},{8,12},{10,14},{12,8},{14,10},{1,5},{3,7},... | collective-permute-start | bytes 589832 | tf_op jit(solution)/shard_map/ppermute | solution.py:37
  (39 other events, 400.3 us)

commit v10 on v9

--- a/solution.py
+++ b/solution.py
@@ -707,7 +707,7 @@
     chunks.append((out_low[:out_half], out_low[out_half:], bits[1:]))
     steps = [i for t in range(len(bits)) for i, c in enumerate(chunks) if t < len(c[2])]
     if len(bits) == 3:
-        steps = [0, 4, 1, 0, 4, 3, 2, 0, 1, 3, 2, 1, 3, 2]
+        steps = [0, 4, 1, 0, 4, 2, 3, 0, 1, 2, 3, 1, 2, 3]
     chunks = scatter_chunks(chunks, steps, even)
     grad_out = chunks.pop()
     grad_qkv = jnp.transpose(jnp.concatenate(chunks, axis=-1), (1, 0, 2))

time: 246 us -> 250 us (1.016); the launches traced: 243 us -> 250 us
  waiting for transfers between devices: 109 us -> 119 us
  starting transfers between devices: 57.1 us -> 53.4 us
    ppermute x36, waiting for transfers between devices: 96.6 us -> 107 us  [swap_tm(): return lax.ppermute(block, 'tm', [(i, i ^ mask) for i in range(n)])]
    ppermute x36, starting transfers between devices: 40.6 us -> 36.9 us  [swap_tm(): return lax.ppermute(block, 'tm', [(i, i ^ mask) for i in range(n)])]
  transfers between devices with their start and end apart: 51 -> 51, of which waited for: 29 -> 30; matrix products, arithmetic and copies ran while one was open for 11% -> 11% of each run, Pallas kernels for 11% -> 10%
where the time goes in v10:
time: 250 us
  waiting for transfers between devices  119 us (48%)
  starting transfers between devices  53.4 us (21%)
  Pallas kernels  39.4 us (16%)
  local copies, waits for them, and re-layouts  16.2 us (6%)
  other arithmetic  13.6 us (5%)
  between operations  4.12 us (2%)
  matrix products  3.59 us (1%)
    ppermute x36, waiting for transfers between devices, swap_tm(): return lax.ppermute(block, 'tm', [(i, i ^ mask) for i in range(n)])  107 us
    ppermute x36, starting transfers between devices, swap_tm(): return lax.ppermute(block, 'tm', [(i, i ^ mask) for i in range(n)])  36.9 us
    ppermute x5, starting transfers between devices, to_tm(): return lax.ppermute(block, ('tm', 'mp'), pairs)  13.4 us
    pallas_call x1, Pallas kernels, encoder_forward(): pl.pallas_call(forward_kernel, grid_spec=pltpu.PrefetchScalarGridSpec(num...  11.1 us
    pallas_call x4, Pallas kernels, encoder_backward(): pl.pallas_call(functools.partial(backward_kernel, masks), grid_spec=pltpu...  11 us
    ppermute x5, waiting for transfers between devices, to_tm(): return lax.ppermute(block, ('tm', 'mp'), pairs)  7.99 us
    pallas_call x1, Pallas kernels, lower(): pl.pallas_call(functools.partial(lower_kernel, table, order), in_specs=[p...  6.42 us
    pallas_call x1, Pallas kernels, lift(): pl.pallas_call(functools.partial(lift_kernel, table, order), in_specs=[pl...  5.22 us
  transfers between devices with their start and end apart: 51, of which 30 were waited for; matrix products, arithmetic and copies ran while one was open for 11% of the time, Pallas kernels for 10%

profile of v10, /device:TPU:0, one launch (start us, length us, event | category | flops | bytes accessed | tf_op | source)
XLA Modules:
  0.0 249.7 jit_solution(9029216486836829861)
XLA Ops:
  2.4 6.0 %collective-permute-start = (bf16[128,1024]{1,0:T(8,128)(2,1)}, bf16[128,1024]{1,0:T(8,128)(2,1)}, u32[]{:S(2)}, u32[]{:S(2)}) collective-permute-start(bf16[128,1024]{1,0:T(8,128)(2,1)} %constant_dynamic-slice_fusion.6), channel_id=1, source_target_pairs={{0,14},{1,15},{2,0},{3,1},{4,2},{5,3},{6,4},{7,5},{8,6},{9,7},{10,... | collective-permute-start | bytes 786440 | tf_op jit(solution)/shard_map/ppermute | solution.py:51
  10.7 3.2 %copy.14 = bf16[3,512,1024]{2,1,0:T(8,128)(2,1)S(1)} copy(bf16[3,512,1024]{1,2,0:T(8,128)(2,1)} %bitcast.88) | data formatting | bytes 6291456 | tf_op jit(solution)/shard_map/transpose | solution.py:563
  17.1 3.3 %collective-permute-start.6 = (bf16[128,1024]{1,0:T(8,128)(2,1)}, bf16[128,1024]{1,0:T(8,128)(2,1)}, u32[]{:S(2)}, u32[]{:S(2)}) collective-permute-start(bf16[128,1024]{1,0:T(8,128)(2,1)} %get-tuple-element.175), channel_id=1, source_target_pairs={{0,8},{2,10},{4,12},{6,14},{8,0},{10,2},{12,4},{14,6},{1,9},{3,11}... | collective-permute-start | bytes 786440 | tf_op jit(solution)/shard_map/ppermute | solution.py:37
  28.0 11.1 %encoder_forward.1 = (bf16[512,1024]{1,0:T(8,128)(2,1)}, bf16[3,512,512]{2,1,0:T(8,128)(2,1)}, bf16[4,2,2,256,256]{4,3,2,1,0:T(8,128)(2,1)}, bf16[192,512]{1,0:T...) custom-call(s32[5]{0:T(128)S(1)} %stack.49.at, ...), custom_call_target="tpu_custom_call" | custom-call | tf_op jit(solution)/shard_map/encoder_forward/pallas_call | solution.py:206
  52.7 3.0 %collective-permute-done.9 = bf16[64,512]{1,0:T(8,128)(2,1)S(1)} collective-permute-done((bf16[64,512]{1,0:T(8,128)(2,1)S(1)}, bf16[64,512]{1,0:T(8,128)(2,1)S(1)}, u32[]{:S(2)}, u32[]{:S(2)}) %collective-permute-start.9) | collective-permute-done | bytes 65568 | tf_op jit(solution)/shard_map/ppermute | solution.py:37
  58.4 3.7 %collective-permute-done.10 = bf16[1,2,64,512]{3,2,1,0:T(8,128)(2,1)} collective-permute-done((bf16[1,2,64,512]{3,2,1,0:T(8,128)(2,1)S(1)}, bf16[1,2,64,512]{3,2,1,0:T(8,128)(2,1)}, u32[]{:S(2)}, u32[]{:S(2)}) %collective-permute-start.10) | collective-permute-done | bytes 131104 | tf_op jit(solution)/shard_map/ppermute | solution.py:37
  63.2 7.3 %collective-permute-done.11 = bf16[2,2,64,512]{3,2,1,0:T(8,128)(2,1)S(1)} collective-permute-done((bf16[2,2,64,512]{3,2,1,0:T(8,128)(2,1)S(1)}, bf16[2,2,64,512]{3,2,1,0:T(8,128)(2,1)S(1)}, u32[]{:S(2)}, u32[]{:S(2)}) %collective-permute-start.11) | collective-permute-done | bytes 262176 | tf_op jit(solution)/shard_map/ppermute | solution.py:37
  71.3 3.1 %pad_maximum_fusion.kvb = bf16[2,512,1024]{2,1,0:T(8,128)(2,1)} fusion(bf16[1,512,1024]{2,1,0:T(8,128)(2,1)} %bitcast.19, bf16[1,512,1024]{2,1,0:T(8,128)(2,1)} %bitcast.18), kind=kLoop, calls=%fused_computation | loop fusion | flops 1048576 | bytes 4194304 | tf_op jit(solution)/shard_map/stack | solution.py:636
  74.4 5.8 %collective-permute-done.13.there = bf16[4,128,1024]{2,1,0:T(8,128)(2,1)S(1)} collective-permute-done((bf16[4,128,1024]{2,1,0:T(8,128)(2,1)S(1)}, bf16[4,128,1024]{2,1,0:T(8,128)(2,1)S(1)}, u32[]{:S(2)}, u32[]{:S(2)}) %collective-permute-start.13) | collective-permute-done | bytes 1048608 | tf_op jit(solution)/shard_map/ppermute | solution.py:37
  81.3 5.2 %lift.1 = (bf16[512,1024]{1,0:T(8,128)(2,1)S(1)}, f32[4,128]{1,0:T(4,128)S(1)}, bf16[512,1024]{1,0:T(8,128)(2,1)S(1)}, bf16[512,1024]{1,0:T(8,128)(2,1)S(1)}) custom-call(s32[5]{0:T(128)S(1)} %stack.49.at, bf16[512,512]{1,0:T(8,128)(2,1)S(1)} %bitcast.74, bf16[512,512]{1,0:T(8,128)(2,1)S(1)} %collective-permute-done.12.tb, ...), custom_call_target="tpu_custom_call" | custom-call | tf_op jit(solution)/shard_map/lift/pallas_call | solution.py:414
  88.0 2.9 %keep_columns.1 = bf16[512,1024]{1,0:T(8,128)(2,1)S(1)} custom-call(s32[5]{0:T(128)S(1)} %stack.49.at, bf16[512,1024]{1,0:T(8,128)(2,1)S(1)} %get-tuple-element.111.low, bf16[512,2048]{1,0:T(8,128)(2,1)S(1)} %copy-done.2, bf16[2,512,1024]{2,1,0:T(8,128)(2,1)} %pad_maximum_fusion.kvb), custom_call_target="tpu_custom_call" | custom-call | tf_op jit(solution)/shard_map/keep_columns/pallas_call | solution.py:437
  97.1 3.6 %collective-permute-done.16 = bf16[2,128,512]{2,1,0:T(8,128)(2,1)S(1)} collective-permute-done((bf16[2,128,512]{2,1,0:T(8,128)(2,1)S(1)}, bf16[2,128,512]{2,1,0:T(8,128)(2,1)S(1)}, u32[]{:S(2)}, u32[]{:S(2)}) %collective-permute-start.16) | collective-permute-done | bytes 262176 | tf_op jit(solution)/shard_map/ppermute | solution.py:37
  103.4 4.7 %collective-permute-done.18 = bf16[2,128,512]{2,1,0:T(8,128)(2,1)S(1)} collective-permute-done((bf16[2,128,512]{2,1,0:T(8,128)(2,1)S(1)}, bf16[2,128,512]{2,1,0:T(8,128)(2,1)S(1)}, u32[]{:S(2)}, u32[]{:S(2)}) %collective-permute-start.18) | collective-permute-done | bytes 262176 | tf_op jit(solution)/shard_map/ppermute | solution.py:37
  111.6 8.2 %collective-permute-done.22 = bf16[1,128,512]{2,1,0:T(8,128)(2,1)S(1)} collective-permute-done((bf16[1,128,512]{2,1,0:T(8,128)(2,1)S(1)}, bf16[1,128,512]{2,1,0:T(8,128)(2,1)S(1)}, u32[]{:S(2)}, u32[]{:S(2)}) %collective-permute-start.22) | collective-permute-done | bytes 131104 | tf_op jit(solution)/shard_map/ppermute | solution.py:37
  123.6 5.1 %collective-permute-done.25 = bf16[1,128,640]{2,1,0:T(8,128)(2,1)S(1)} collective-permute-done((bf16[1,128,640]{2,1,0:T(8,128)(2,1)S(1)}, bf16[1,128,640]{2,1,0:T(8,128)(2,1)S(1)}, u32[]{:S(2)}, u32[]{:S(2)}) %collective-permute-start.25) | collective-permute-done | bytes 163872 | tf_op jit(solution)/shard_map/ppermute | solution.py:37
  128.8 3.7 %collective-permute-done.24 = bf16[2,128,512]{2,1,0:T(8,128)(2,1)S(1)} collective-permute-done((bf16[2,128,512]{2,1,0:T(8,128)(2,1)S(1)}, bf16[2,128,512]{2,1,0:T(8,128)(2,1)S(1)}, u32[]{:S(2)}, u32[]{:S(2)}) %collective-permute-start.24) | collective-permute-done | bytes 262176 | tf_op jit(solution)/shard_map/ppermute | solution.py:37
  132.6 5.9 %collective-permute-done.26 = bf16[2,128,640]{2,1,0:T(8,128)(2,1)S(1)} collective-permute-done((bf16[2,128,640]{2,1,0:T(8,128)(2,1)S(1)}, bf16[2,128,640]{2,1,0:T(8,128)(2,1)S(1)}, u32[]{:S(2)}, u32[]{:S(2)}) %collective-permute-start.26) | collective-permute-done | bytes 327712 | tf_op jit(solution)/shard_map/ppermute | solution.py:37
  141.6 6.4 %lower.1 = (bf16[512,512]{1,0:T(8,128)(2,1)S(1)}, bf16[512,512]{1,0:T(8,128)(2,1)S(1)}) custom-call(s32[5]{0:T(128)S(1)} %stack.49.at, bf16[512,512]{1,0:T(8,128)(2,1)S(1)} %bitcast.72, bf16[512,640]{1,0:T(8,128)(2,1)S(1)} %bitcast.70, bf16[512,512]{1,0:T(8,128)(2,1)S(1)} %collective-permute-done.27.cb0, bf16[512,640]{1,0:T(8,128)(2,1)S(1)} %collective-permute-done.28.cb1, ...), custom_call_target="tpu_custom_call" | custom-call | tf_op jit(solution)/shard_map/lower/pallas_call | solution.py:536
  150.4 8.2 %collective-permute-done.30 = bf16[2,2,64,512]{3,2,1,0:T(8,128)(2,1)S(1)} collective-permute-done((bf16[2,2,64,512]{3,2,1,0:T(8,128)(2,1)S(1)}, bf16[2,2,64,512]{3,2,1,0:T(8,128)(2,1)S(1)}, u32[]{:S(2)}, u32[]{:S(2)}) %collective-permute-start.30) | collective-permute-done | bytes 262176 | tf_op jit(solution)/shard_map/ppermute | solution.py:37
  158.7 3.3 %collective-permute-start.31 = (bf16[1,2,64,512]{3,2,1,0:T(8,128)(2,1)S(1)}, bf16[1,2,64,512]{3,2,1,0:T(8,128)(2,1)S(1)}, u32[]{:S(2)}, u32[]{:S(2)}) collective-permute-start(bf16[1,2,64,512]{3,2,1,0:T(8,128)(2,1)S(1)} %slice.211), channel_id=1, source_target_pairs={{0,8},{2,10},{4,12},{6,14},{8,0},{10,2},{12,4},{14,6},{1,9},{3,11}... | collective-permute-start | bytes 393224 | tf_op jit(solution)/shard_map/ppermute | solution.py:37
  162.0 6.1 %collective-permute-done.31 = bf16[1,2,64,512]{3,2,1,0:T(8,128)(2,1)S(1)} collective-permute-done((bf16[1,2,64,512]{3,2,1,0:T(8,128)(2,1)S(1)}, bf16[1,2,64,512]{3,2,1,0:T(8,128)(2,1)S(1)}, u32[]{:S(2)}, u32[]{:S(2)}) %collective-permute-start.31) | collective-permute-done | bytes 131104 | tf_op jit(solution)/shard_map/ppermute | solution.py:37
  169.3 3.1 %collective-permute-done.32 = bf16[64,512]{1,0:T(8,128)(2,1)S(1)} collective-permute-done((bf16[64,512]{1,0:T(8,128)(2,1)S(1)}, bf16[64,512]{1,0:T(8,128)(2,1)S(1)}, u32[]{:S(2)}, u32[]{:S(2)}) %collective-permute-start.32) | collective-permute-done | bytes 65568 | tf_op jit(solution)/shard_map/ppermute | solution.py:37
  172.8 4.2 %collective-permute-start.35 = (bf16[64,512]{1,0:T(8,128)(2,1)S(1)}, bf16[64,512]{1,0:T(8,128)(2,1)S(1)}, u32[]{:S(2)}, u32[]{:S(2)}) collective-permute-start(bf16[64,512]{1,0:T(8,128)(2,1)S(1)} %slice.214), channel_id=1, source_target_pairs={{0,15},{1,14},{2,1},{3,0},{4,3},{5,2},{6,5},{7,4},{8,7},{9,6},{10,... | collective-permute-start | bytes 196616 | tf_op jit(solution)/shard_map/ppermute | solution.py:51
  183.0 2.8 %encoder_backward.4 = (bf16[4,3,128,128]{3,2,1,0:T(8,128)(2,1)S(1)}, bf16[4,3,128,128]{3,2,1,0:T(8,128)(2,1)S(1)}) custom-call(s32[5]{0:T(128)S(1)} %stack.49.at, bf16[1024,512]{1,0:T(8,128)(2,1)S(1)} %bitcast.65, bf16[3,512,512]{2,1,0:T(8,128)(2,1)S(1)} %copy-done.3, bf16[4,2,2,256,256]{4,3,2,1,0:T(8,128)(2,1)S(1)} %copy-done.1, ...), custom_call_target="tpu_custom_call" | custom-call | tf_op jit(solution)/shard_map/encoder_backward/pallas_call | solution.py:317
  187.9 2.8 %encoder_backward.5 = (bf16[4,3,128,128]{3,2,1,0:T(8,128)(2,1)S(1)}, bf16[4,3,128,128]{3,2,1,0:T(8,128)(2,1)S(1)}) custom-call(s32[5]{0:T(128)S(1)} %stack.49.at, bf16[1024,512]{1,0:T(8,128)(2,1)S(1)} %bitcast.66, bf16[3,512,512]{2,1,0:T(8,128)(2,1)S(1)} %copy-done.3, bf16[4,2,2,256,256]{4,3,2,1,0:T(8,128)(2,1)S(1)} %copy-done.1, ...), custom_call_target="tpu_custom_call" | custom-call | tf_op jit(solution)/shard_map/encoder_backward/pallas_call | solution.py:317
  190.7 2.8 %encoder_backward.6 = (bf16[4,3,128,128]{3,2,1,0:T(8,128)(2,1)S(1)}, bf16[4,3,128,128]{3,2,1,0:T(8,128)(2,1)S(1)}) custom-call(s32[5]{0:T(128)S(1)} %stack.49.at, bf16[1024,512]{1,0:T(8,128)(2,1)S(1)} %bitcast.67, bf16[3,512,512]{2,1,0:T(8,128)(2,1)S(1)} %copy-done.3, bf16[4,2,2,256,256]{4,3,2,1,0:T(8,128)(2,1)S(1)} %copy-done.1, ...), custom_call_target="tpu_custom_call" | custom-call | tf_op jit(solution)/shard_map/encoder_backward/pallas_call | solution.py:317
  193.4 4.4 %collective-permute-done.37 = bf16[4,64,1024]{2,1,0:T(8,128)(2,1)S(1)} collective-permute-done((bf16[4,64,1024]{2,1,0:T(8,128)(2,1)S(1)}, bf16[4,64,1024]{2,1,0:T(8,128)(2,1)S(1)}, u32[]{:S(2)}, u32[]{:S(2)}) %collective-permute-start.37) | collective-permute-done | bytes 524320 | tf_op jit(solution)/shard_map/ppermute | solution.py:37
  208.6 6.1 %collective-permute-done.39 = bf16[4,3,128,128]{3,2,1,0:T(8,128)(2,1)S(1)} collective-permute-done((bf16[4,3,128,128]{3,2,1,0:T(8,128)(2,1)S(1)}, bf16[4,3,128,128]{3,2,1,0:T(8,128)(2,1)S(1)}, u32[]{:S(2)}, u32[]{:S(2)}) %collective-permute-start.39) | collective-permute-done | bytes 393248 | tf_op jit(solution)/shard_map/ppermute | solution.py:37
  226.6 3.3 %collective-permute-done.44 = bf16[2,3,128,128]{3,2,1,0:T(8,128)(2,1)S(1)} collective-permute-done((bf16[2,3,128,128]{3,2,1,0:T(8,128)(2,1)S(1)}, bf16[2,3,128,128]{3,2,1,0:T(8,128)(2,1)S(1)}, u32[]{:S(2)}, u32[]{:S(2)}) %collective-permute-start.44) | collective-permute-done | bytes 196640 | tf_op jit(solution)/shard_map/ppermute | solution.py:37
  230.0 3.3 %collective-permute-start.45 = (bf16[1,3,128,128]{3,2,1,0:T(8,128)(2,1)S(1)}, bf16[1,3,128,128]{3,2,1,0:T(8,128)(2,1)S(1)}, u32[]{:S(2)}, u32[]{:S(2)}) collective-permute-start(bf16[1,3,128,128]{3,2,1,0:T(8,128)(2,1)S(1)} %slice.224), channel_id=1, source_target_pairs={{0,8},{2,10},{4,12},{6,14},{8,0},{10,2},{12,4},{14,6},{1,9},{3,11}... | collective-permute-start | bytes 294920 | tf_op jit(solution)/shard_map/ppermute | solution.py:37
  235.7 6.4 %collective-permute-done.48 = bf16[1,3,128,128]{3,2,1,0:T(8,128)(2,1)S(1)} collective-permute-done((bf16[1,3,128,128]{3,2,1,0:T(8,128)(2,1)S(1)}, bf16[1,3,128,128]{3,2,1,0:T(8,128)(2,1)S(1)}, u32[]{:S(2)}, u32[]{:S(2)}) %collective-permute-start.48) | collective-permute-done | bytes 98336 | tf_op jit(solution)/shard_map/ppermute | solution.py:37
  242.3 6.4 %collective-permute-done.49 = bf16[1,3,128,128]{3,2,1,0:T(8,128)(2,1)S(1)} collective-permute-done((bf16[1,3,128,128]{3,2,1,0:T(8,128)(2,1)S(1)}, bf16[1,3,128,128]{3,2,1,0:T(8,128)(2,1)S(1)}, u32[]{:S(2)}, u32[]{:S(2)}) %collective-permute-start.49) | collective-permute-done | bytes 98336 | tf_op jit(solution)/shard_map/ppermute | solution.py:37
  (204 shorter events, 90.1 us)
Async XLA Ops:
  2.4 18.1 %collective-permute-start = (bf16[128,1024]{1,0:T(8,128)(2,1)}, bf16[128,1024]{1,0:T(8,128)(2,1)}, u32[]{:S(2)}, u32[]{:S(2)}) collective-permute-start(bf16[128,1024]{1,0:T(8,128)(2,1)} %constant_dynamic-slice_fusion.6), channel_id=1, source_target_pairs={{0,14},{1,15},{2,0},{3,1},{4,2},{5,3},{6,4},{7,5},{8,6},{9,7},{10,... | collective-permute-start | bytes 786440 | tf_op jit(solution)/shard_map/ppermute | solution.py:51
  10.7 31.9 %collective-permute-start.4 = (bf16[512,1024]{1,0:T(8,128)(2,1)}, bf16[512,1024]{1,0:T(8,128)(2,1)}, u32[]{:S(2)}, u32[]{:S(2)}) collective-permute-start(bf16[512,1024]{1,0:T(8,128)(2,1)} %constant_dynamic-slice_fusion.4), channel_id=1, source_target_pairs={{0,2},{2,0},{4,6},{6,4},{8,10},{10,8},{12,14},{14,12},{1,3},{3,1},... | collective-permute-start | bytes 3145736 | tf_op jit(solution)/shard_map/ppermute | solution.py:37
  16.1 26.8 %collective-permute-start.8 = (bf16[128,1024]{1,0:T(8,128)(2,1)}, bf16[128,1024]{1,0:T(8,128)(2,1)}, u32[]{:S(2)}, u32[]{:S(2)}) collective-permute-start(bf16[128,1024]{1,0:T(8,128)(2,1)} %get-tuple-element.173), channel_id=1, source_target_pairs={{0,12},{2,14},{4,8},{6,10},{8,4},{10,6},{12,0},{14,2},{1,13},{3,15... | collective-permute-start | bytes 786440 | tf_op jit(solution)/shard_map/ppermute | solution.py:37
  17.1 26.4 %collective-permute-start.7 = (bf16[128,1024]{1,0:T(8,128)(2,1)}, bf16[128,1024]{1,0:T(8,128)(2,1)}, u32[]{:S(2)}, u32[]{:S(2)}) collective-permute-start(bf16[128,1024]{1,0:T(8,128)(2,1)} %get-tuple-element.174), channel_id=1, source_target_pairs={{0,4},{2,6},{4,0},{6,2},{8,12},{10,14},{12,8},{14,10},{1,5},{3,7},... | collective-permute-start | bytes 786440 | tf_op jit(solution)/shard_map/ppermute | solution.py:37
  17.1 28.0 %collective-permute-start.6 = (bf16[128,1024]{1,0:T(8,128)(2,1)}, bf16[128,1024]{1,0:T(8,128)(2,1)}, u32[]{:S(2)}, u32[]{:S(2)}) collective-permute-start(bf16[128,1024]{1,0:T(8,128)(2,1)} %get-tuple-element.175), channel_id=1, source_target_pairs={{0,8},{2,10},{4,12},{6,14},{8,0},{10,2},{12,4},{14,6},{1,9},{3,11}... | collective-permute-start | bytes 786440 | tf_op jit(solution)/shard_map/ppermute | solution.py:37
  43.6 27.7 %collective-permute-start.14 = (bf16[512,1024]{1,0:T(8,128)(2,1)}, bf16[512,1024]{1,0:T(8,128)(2,1)}, u32[]{:S(2)}, u32[]{:S(2)}) collective-permute-start(bf16[512,1024]{1,0:T(8,128)(2,1)} %collective-permute-done.4), channel_id=1, source_target_pairs={{0,16},{16,0},{1,17},{17,1},{2,18},{18,2},{3,19},{19,3},{4,20},{20... | collective-permute-start | bytes 3145736 | tf_op jit(solution)/shard_map/ppermute | solution.py:592
  55.7 24.5 %collective-permute-start.13 = (bf16[4,128,1024]{2,1,0:T(8,128)(2,1)S(1)}, bf16[4,128,1024]{2,1,0:T(8,128)(2,1)S(1)}, u32[]{:S(2)}, u32[]{:S(2)}) collective-permute-start(bf16[4,128,1024]{2,1,0:T(8,128)(2,1)S(1)} %pad_maximum_fusion.1.here), channel_id=1, source_target_pairs={{0,2},{2,0},{4,6},{6,4},{8,10},{10,8},{12,14},{14,12},{1,3},{3,1},... | collective-permute-start | bytes 3145736 | tf_op jit(solution)/shard_map/ppermute | solution.py:37
  91.4 9.3 %collective-permute-start.16 = (bf16[2,128,512]{2,1,0:T(8,128)(2,1)S(1)}, bf16[2,128,512]{2,1,0:T(8,128)(2,1)S(1)}, u32[]{:S(2)}, u32[]{:S(2)}) collective-permute-start(bf16[2,128,512]{2,1,0:T(8,128)(2,1)S(1)} %get-tuple-element.171), channel_id=1, source_target_pairs={{0,4},{2,6},{4,0},{6,2},{8,12},{10,14},{12,8},{14,10},{1,5},{3,7},... | collective-permute-start | bytes 786440 | tf_op jit(solution)/shard_map/ppermute | solution.py:37
  94.5 14.7 %collective-permute-start.21 = (f32[1,128]{1,0:T(1,128)S(1)}, f32[1,128]{1,0:T(1,128)S(1)}, u32[]{:S(2)}, u32[]{:S(2)}) collective-permute-start(f32[1,128]{1,0:T(1,128)S(1)} %slice.165), channel_id=1, source_target_pairs={{0,8},{2,10},{4,12},{6,14},{8,0},{10,2},{12,4},{14,6},{1,9},{3,11}... | collective-permute-start | bytes 1544 | tf_op jit(solution)/shard_map/ppermute | solution.py:37
  97.1 11.1 %collective-permute-start.18 = (bf16[2,128,512]{2,1,0:T(8,128)(2,1)S(1)}, bf16[2,128,512]{2,1,0:T(8,128)(2,1)S(1)}, u32[]{:S(2)}, u32[]{:S(2)}) collective-permute-start(bf16[2,128,512]{2,1,0:T(8,128)(2,1)S(1)} %get-tuple-element.172), channel_id=1, source_target_pairs={{0,4},{2,6},{4,0},{6,2},{8,12},{10,14},{12,8},{14,10},{1,5},{3,7},... | collective-permute-start | bytes 786440 | tf_op jit(solution)/shard_map/ppermute | solution.py:37
  100.8 8.5 %collective-permute-start.17 = (bf16[1,128,512]{2,1,0:T(8,128)(2,1)S(1)}, bf16[1,128,512]{2,1,0:T(8,128)(2,1)S(1)}, u32[]{:S(2)}, u32[]{:S(2)}) collective-permute-start(bf16[1,128,512]{2,1,0:T(8,128)(2,1)S(1)} %get-tuple-element.182), channel_id=1, source_target_pairs={{0,8},{2,10},{4,12},{6,14},{8,0},{10,2},{12,4},{14,6},{1,9},{3,11}... | collective-permute-start | bytes 393224 | tf_op jit(solution)/shard_map/ppermute | solution.py:37
  108.3 11.6 %collective-permute-start.22 = (bf16[1,128,512]{2,1,0:T(8,128)(2,1)S(1)}, bf16[1,128,512]{2,1,0:T(8,128)(2,1)S(1)}, u32[]{:S(2)}, u32[]{:S(2)}) collective-permute-start(bf16[1,128,512]{2,1,0:T(8,128)(2,1)S(1)} %get-tuple-element.183), channel_id=1, source_target_pairs={{0,8},{2,10},{4,12},{6,14},{8,0},{10,2},{12,4},{14,6},{1,9},{3,11}... | collective-permute-start | bytes 393224 | tf_op jit(solution)/shard_map/ppermute | solution.py:37
  109.5 12.7 %collective-permute-start.23 = (bf16[1,128,512]{2,1,0:T(8,128)(2,1)S(1)}, bf16[1,128,512]{2,1,0:T(8,128)(2,1)S(1)}, u32[]{:S(2)}, u32[]{:S(2)}) collective-permute-start(bf16[1,128,512]{2,1,0:T(8,128)(2,1)S(1)} %bitcast.78), channel_id=1, source_target_pairs={{0,8},{2,10},{4,12},{6,14},{8,0},{10,2},{12,4},{14,6},{1,9},{3,11}... | collective-permute-start | bytes 393224 | tf_op jit(solution)/shard_map/ppermute | solution.py:37
  120.8 7.9 %collective-permute-start.25 = (bf16[1,128,640]{2,1,0:T(8,128)(2,1)S(1)}, bf16[1,128,640]{2,1,0:T(8,128)(2,1)S(1)}, u32[]{:S(2)}, u32[]{:S(2)}) collective-permute-start(bf16[1,128,640]{2,1,0:T(8,128)(2,1)S(1)} %bitcast.75), channel_id=1, source_target_pairs={{0,8},{2,10},{4,12},{6,14},{8,0},{10,2},{12,4},{14,6},{1,9},{3,11}... | collective-permute-start | bytes 491528 | tf_op jit(solution)/shard_map/ppermute | solution.py:37
  122.3 10.2 %collective-permute-start.24 = (bf16[2,128,512]{2,1,0:T(8,128)(2,1)S(1)}, bf16[2,128,512]{2,1,0:T(8,128)(2,1)S(1)}, u32[]{:S(2)}, u32[]{:S(2)}) collective-permute-start(bf16[2,128,512]{2,1,0:T(8,128)(2,1)S(1)} %pad_maximum_fusion.7), channel_id=1, source_target_pairs={{0,4},{2,6},{4,0},{6,2},{8,12},{10,14},{12,8},{14,10},{1,5},{3,7},... | collective-permute-start | bytes 786440 | tf_op jit(solution)/shard_map/ppermute | solution.py:37
  128.7 9.8 %collective-permute-start.26 = (bf16[2,128,640]{2,1,0:T(8,128)(2,1)S(1)}, bf16[2,128,640]{2,1,0:T(8,128)(2,1)S(1)}, u32[]{:S(2)}, u32[]{:S(2)}) collective-permute-start(bf16[2,128,640]{2,1,0:T(8,128)(2,1)S(1)} %pad_maximum_fusion.5), channel_id=1, source_target_pairs={{0,4},{2,6},{4,0},{6,2},{8,12},{10,14},{12,8},{14,10},{1,5},{3,7},... | collective-permute-start | bytes 983048 | tf_op jit(solution)/shard_map/ppermute | solution.py:37
  150.2 8.4 %collective-permute-start.30 = (bf16[2,2,64,512]{3,2,1,0:T(8,128)(2,1)S(1)}, bf16[2,2,64,512]{3,2,1,0:T(8,128)(2,1)S(1)}, u32[]{:S(2)}, u32[]{:S(2)}) collective-permute-start(bf16[2,2,64,512]{3,2,1,0:T(8,128)(2,1)S(1)} %bitcast.91), channel_id=1, source_target_pairs={{0,4},{2,6},{4,0},{6,2},{8,12},{10,14},{12,8},{14,10},{1,5},{3,7},... | collective-permute-start | bytes 786440 | tf_op jit(solution)/shard_map/ppermute | solution.py:37
  158.7 9.4 %collective-permute-start.31 = (bf16[1,2,64,512]{3,2,1,0:T(8,128)(2,1)S(1)}, bf16[1,2,64,512]{3,2,1,0:T(8,128)(2,1)S(1)}, u32[]{:S(2)}, u32[]{:S(2)}) collective-permute-start(bf16[1,2,64,512]{3,2,1,0:T(8,128)(2,1)S(1)} %slice.211), channel_id=1, source_target_pairs={{0,8},{2,10},{4,12},{6,14},{8,0},{10,2},{12,4},{14,6},{1,9},{3,11}... | collective-permute-start | bytes 393224 | tf_op jit(solution)/shard_map/ppermute | solution.py:37
  182.9 14.9 %collective-permute-start.37 = (bf16[4,64,1024]{2,1,0:T(8,128)(2,1)S(1)}, bf16[4,64,1024]{2,1,0:T(8,128)(2,1)S(1)}, u32[]{:S(2)}, u32[]{:S(2)}) collective-permute-start(bf16[4,64,1024]{2,1,0:T(8,128)(2,1)S(1)} %get-tuple-element.145), channel_id=1, source_target_pairs={{0,2},{2,0},{4,6},{6,4},{8,10},{10,8},{12,14},{14,12},{1,3},{3,1},... | collective-permute-start | bytes 1572872 | tf_op jit(solution)/shard_map/ppermute | solution.py:37
  185.8 20.5 %collective-permute-start.36 = (bf16[4,3,128,128]{3,2,1,0:T(8,128)(2,1)S(1)}, bf16[4,3,128,128]{3,2,1,0:T(8,128)(2,1)S(1)}, u32[]{:S(2)}, u32[]{:S(2)}) collective-permute-start(bf16[4,3,128,128]{3,2,1,0:T(8,128)(2,1)S(1)} %get-tuple-element.137), channel_id=1, source_target_pairs={{0,2},{2,0},{4,6},{6,4},{8,10},{10,8},{12,14},{14,12},{1,3},{3,1},... | collective-permute-start | bytes 1179656 | tf_op jit(solution)/shard_map/ppermute | solution.py:37
  198.1 10.4 %collective-permute-start.40 = (bf16[2,64,1024]{2,1,0:T(8,128)(2,1)S(1)}, bf16[2,64,1024]{2,1,0:T(8,128)(2,1)S(1)}, u32[]{:S(2)}, u32[]{:S(2)}) collective-permute-start(bf16[2,64,1024]{2,1,0:T(8,128)(2,1)S(1)} %slice.218), channel_id=1, source_target_pairs={{0,4},{2,6},{4,0},{6,2},{8,12},{10,14},{12,8},{14,10},{1,5},{3,7},... | collective-permute-start | bytes 786440 | tf_op jit(solution)/shard_map/ppermute | solution.py:37
  199.1 15.6 %collective-permute-start.39 = (bf16[4,3,128,128]{3,2,1,0:T(8,128)(2,1)S(1)}, bf16[4,3,128,128]{3,2,1,0:T(8,128)(2,1)S(1)}, u32[]{:S(2)}, u32[]{:S(2)}) collective-permute-start(bf16[4,3,128,128]{3,2,1,0:T(8,128)(2,1)S(1)} %get-tuple-element.152), channel_id=1, source_target_pairs={{0,2},{2,0},{4,6},{6,4},{8,10},{10,8},{12,14},{14,12},{1,3},{3,1},... | collective-permute-start | bytes 1179656 | tf_op jit(solution)/shard_map/ppermute | solution.py:37
  199.2 21.8 %collective-permute-start.43 = (bf16[4,3,128,128]{3,2,1,0:T(8,128)(2,1)S(1)}, bf16[4,3,128,128]{3,2,1,0:T(8,128)(2,1)S(1)}, u32[]{:S(2)}, u32[]{:S(2)}) collective-permute-start(bf16[4,3,128,128]{3,2,1,0:T(8,128)(2,1)S(1)} %get-tuple-element.160), channel_id=1, source_target_pairs={{0,2},{2,0},{4,6},{6,4},{8,10},{10,8},{12,14},{14,12},{1,3},{3,1},... | collective-permute-start | bytes 1179656 | tf_op jit(solution)/shard_map/ppermute | solution.py:37
  206.4 8.4 %collective-permute-start.38 = (bf16[2,3,128,128]{3,2,1,0:T(8,128)(2,1)S(1)}, bf16[2,3,128,128]{3,2,1,0:T(8,128)(2,1)S(1)}, u32[]{:S(2)}, u32[]{:S(2)}) collective-permute-start(bf16[2,3,128,128]{3,2,1,0:T(8,128)(2,1)S(1)} %slice.216), channel_id=1, source_target_pairs={{0,4},{2,6},{4,0},{6,2},{8,12},{10,14},{12,8},{14,10},{1,5},{3,7},... | collective-permute-start | bytes 589832 | tf_op jit(solution)/shard_map/ppermute | solution.py:37
  206.5 19.1 %collective-permute-start.42 = (bf16[4,3,128,128]{3,2,1,0:T(8,128)(2,1)S(1)}, bf16[4,3,128,128]{3,2,1,0:T(8,128)(2,1)S(1)}, u32[]{:S(2)}, u32[]{:S(2)}) collective-permute-start(bf16[4,3,128,128]{3,2,1,0:T(8,128)(2,1)S(1)} %get-tuple-element.158), channel_id=1, source_target_pairs={{0,4},{2,6},{4,0},{6,2},{8,12},{10,14},{12,8},{14,10},{1,5},{3,7},... | collective-permute-start | bytes 1179656 | tf_op jit(solution)/shard_map/ppermute | solution.py:37
  215.0 11.5 %collective-permute-start.41 = (bf16[1,3,128,128]{3,2,1,0:T(8,128)(2,1)S(1)}, bf16[1,3,128,128]{3,2,1,0:T(8,128)(2,1)S(1)}, u32[]{:S(2)}, u32[]{:S(2)}) collective-permute-start(bf16[1,3,128,128]{3,2,1,0:T(8,128)(2,1)S(1)} %slice.220), channel_id=1, source_target_pairs={{0,8},{2,10},{4,12},{6,14},{8,0},{10,2},{12,4},{14,6},{1,9},{3,11}... | collective-permute-start | bytes 294920 | tf_op jit(solution)/shard_map/ppermute | solution.py:37
  215.7 7.8 %collective-permute-start.50 = (bf16[1,64,1024]{2,1,0:T(8,128)(2,1)S(1)}, bf16[1,64,1024]{2,1,0:T(8,128)(2,1)S(1)}, u32[]{:S(2)}, u32[]{:S(2)}) collective-permute-start(bf16[1,64,1024]{2,1,0:T(8,128)(2,1)S(1)} %slice.234), channel_id=1, source_target_pairs={{0,8},{2,10},{4,12},{6,14},{8,0},{10,2},{12,4},{14,6},{1,9},{3,11}... | collective-permute-start | bytes 393224 | tf_op jit(solution)/shard_map/ppermute | solution.py:37
  218.0 11.9 %collective-permute-start.44 = (bf16[2,3,128,128]{3,2,1,0:T(8,128)(2,1)S(1)}, bf16[2,3,128,128]{3,2,1,0:T(8,128)(2,1)S(1)}, u32[]{:S(2)}, u32[]{:S(2)}) collective-permute-start(bf16[2,3,128,128]{3,2,1,0:T(8,128)(2,1)S(1)} %slice.222), channel_id=1, source_target_pairs={{0,4},{2,6},{4,0},{6,2},{8,12},{10,14},{12,8},{14,10},{1,5},{3,7},... | collective-permute-start | bytes 589832 | tf_op jit(solution)/shard_map/ppermute | solution.py:37
  221.2 12.1 %collective-permute-start.47 = (bf16[2,3,128,128]{3,2,1,0:T(8,128)(2,1)S(1)}, bf16[2,3,128,128]{3,2,1,0:T(8,128)(2,1)S(1)}, u32[]{:S(2)}, u32[]{:S(2)}) collective-permute-start(bf16[2,3,128,128]{3,2,1,0:T(8,128)(2,1)S(1)} %slice.228), channel_id=1, source_target_pairs={{0,4},{2,6},{4,0},{6,2},{8,12},{10,14},{12,8},{14,10},{1,5},{3,7},... | collective-permute-start | bytes 589832 | tf_op jit(solution)/shard_map/ppermute | solution.py:37
  226.5 9.2 %collective-permute-start.46 = (bf16[2,3,128,128]{3,2,1,0:T(8,128)(2,1)S(1)}, bf16[2,3,128,128]{3,2,1,0:T(8,128)(2,1)S(1)}, u32[]{:S(2)}, u32[]{:S(2)}) collective-permute-start(bf16[2,3,128,128]{3,2,1,0:T(8,128)(2,1)S(1)} %slice.226), channel_id=1, source_target_pairs={{0,2},{2,0},{4,6},{6,4},{8,10},{10,8},{12,14},{14,12},{1,3},{3,1},... | collective-permute-start | bytes 589832 | tf_op jit(solution)/shard_map/ppermute | solution.py:37
  230.0 12.2 %collective-permute-start.45 = (bf16[1,3,128,128]{3,2,1,0:T(8,128)(2,1)S(1)}, bf16[1,3,128,128]{3,2,1,0:T(8,128)(2,1)S(1)}, u32[]{:S(2)}, u32[]{:S(2)}) collective-permute-start(bf16[1,3,128,128]{3,2,1,0:T(8,128)(2,1)S(1)} %slice.224), channel_id=1, source_target_pairs={{0,8},{2,10},{4,12},{6,14},{8,0},{10,2},{12,4},{14,6},{1,9},{3,11}... | collective-permute-start | bytes 294920 | tf_op jit(solution)/shard_map/ppermute | solution.py:37
  233.3 8.8 %collective-permute-start.48 = (bf16[1,3,128,128]{3,2,1,0:T(8,128)(2,1)S(1)}, bf16[1,3,128,128]{3,2,1,0:T(8,128)(2,1)S(1)}, u32[]{:S(2)}, u32[]{:S(2)}) collective-permute-start(bf16[1,3,128,128]{3,2,1,0:T(8,128)(2,1)S(1)} %slice.230), channel_id=1, source_target_pairs={{0,8},{2,10},{4,12},{6,14},{8,0},{10,2},{12,4},{14,6},{1,9},{3,11}... | collective-permute-start | bytes 294920 | tf_op jit(solution)/shard_map/ppermute | solution.py:37
  (39 other events, 402.9 us)

commit v11 on v9

--- a/solution.py
+++ b/solution.py
@@ -697,9 +697,9 @@
     chunks = []
     out_got = swap_tm(out_odd, bits[0])
     for pair, path in enumerate((bits, bits, bits, crossed)):
+        even, odd = encoder_backward(turned, qkv, probs, d_attn, at, path, pair, 1)
         if pair == 3:
-            at, out_got = lax.optimization_barrier((at, out_got))
-        even, odd = encoder_backward(turned, qkv, probs, d_attn, at, path, pair, 1)
+            even, out_got = lax.optimization_barrier((even, out_got))
         even, odd, at = lax.optimization_barrier((even, odd, at))
         chunks.append((even, odd, path))
     out_low = (out_even.astype(F32) + out_got.astype(F32)).astype(BF)

time: 246 us -> 246 us (level)
  no operation moved by 1% of the time
where the time goes in v11:
time: 246 us; the launch traced here: 243 us
  waiting for transfers between devices  109 us (44%)
  starting transfers between devices  57.2 us (23%)
  Pallas kernels  39.4 us (16%)
  local copies, waits for them, and re-layouts  16.2 us (7%)
  other arithmetic  13.7 us (6%)
  between operations  4.11 us (2%)
  matrix products  3.59 us (1%)
    ppermute x36, waiting for transfers between devices, swap_tm(): return lax.ppermute(block, 'tm', [(i, i ^ mask) for i in range(n)])  96.6 us
    ppermute x36, starting transfers between devices, swap_tm(): return lax.ppermute(block, 'tm', [(i, i ^ mask) for i in range(n)])  40.6 us
    ppermute x5, starting transfers between devices, to_tm(): return lax.ppermute(block, ('tm', 'mp'), pairs)  13.4 us
    pallas_call x1, Pallas kernels, encoder_forward(): pl.pallas_call(forward_kernel, grid_spec=pltpu.PrefetchScalarGridSpec(num...  11.1 us
    pallas_call x4, Pallas kernels, encoder_backward(): pl.pallas_call(functools.partial(backward_kernel, masks), grid_spec=pltpu...  11.1 us
    ppermute x5, waiting for transfers between devices, to_tm(): return lax.ppermute(block, ('tm', 'mp'), pairs)  7.99 us
    pallas_call x1, Pallas kernels, lower(): pl.pallas_call(functools.partial(lower_kernel, table, order), in_specs=[p...  6.42 us
    pallas_call x1, Pallas kernels, lift(): pl.pallas_call(functools.partial(lift_kernel, table, order), in_specs=[pl...  5.22 us
  transfers between devices with their start and end apart: 51, of which 29 were waited for; matrix products, arithmetic and copies ran while one was open for 11% of the time, Pallas kernels for 11%

profile of v11, /device:TPU:0, one launch (start us, length us, event | category | flops | bytes accessed | tf_op | source)
XLA Modules:
  0.0 243.0 jit_solution(4737164849808583990)
XLA Ops:
  2.4 6.0 %collective-permute-start = (bf16[128,1024]{1,0:T(8,128)(2,1)}, bf16[128,1024]{1,0:T(8,128)(2,1)}, u32[]{:S(2)}, u32[]{:S(2)}) collective-permute-start(bf16[128,1024]{1,0:T(8,128)(2,1)} %constant_dynamic-slice_fusion.6), channel_id=1, source_target_pairs={{0,14},{1,15},{2,0},{3,1},{4,2},{5,3},{6,4},{7,5},{8,6},{9,7},{10,... | collective-permute-start | bytes 786440 | tf_op jit(solution)/shard_map/ppermute | solution.py:51
  10.7 3.2 %copy.14 = bf16[3,512,1024]{2,1,0:T(8,128)(2,1)S(1)} copy(bf16[3,512,1024]{1,2,0:T(8,128)(2,1)} %bitcast.88) | data formatting | bytes 6291456 | tf_op jit(solution)/shard_map/transpose | solution.py:563
  17.1 3.3 %collective-permute-start.6 = (bf16[128,1024]{1,0:T(8,128)(2,1)}, bf16[128,1024]{1,0:T(8,128)(2,1)}, u32[]{:S(2)}, u32[]{:S(2)}) collective-permute-start(bf16[128,1024]{1,0:T(8,128)(2,1)} %get-tuple-element.175), channel_id=1, source_target_pairs={{0,8},{2,10},{4,12},{6,14},{8,0},{10,2},{12,4},{14,6},{1,9},{3,11}... | collective-permute-start | bytes 786440 | tf_op jit(solution)/shard_map/ppermute | solution.py:37
  28.1 11.1 %encoder_forward.1 = (bf16[512,1024]{1,0:T(8,128)(2,1)}, bf16[3,512,512]{2,1,0:T(8,128)(2,1)}, bf16[4,2,2,256,256]{4,3,2,1,0:T(8,128)(2,1)}, bf16[192,512]{1,0:T...) custom-call(s32[5]{0:T(128)S(1)} %stack.49.at, ...), custom_call_target="tpu_custom_call" | custom-call | tf_op jit(solution)/shard_map/encoder_forward/pallas_call | solution.py:206
  52.8 3.0 %collective-permute-done.9 = bf16[64,512]{1,0:T(8,128)(2,1)S(1)} collective-permute-done((bf16[64,512]{1,0:T(8,128)(2,1)S(1)}, bf16[64,512]{1,0:T(8,128)(2,1)S(1)}, u32[]{:S(2)}, u32[]{:S(2)}) %collective-permute-start.9) | collective-permute-done | bytes 65568 | tf_op jit(solution)/shard_map/ppermute | solution.py:37
  58.5 3.7 %collective-permute-done.10 = bf16[1,2,64,512]{3,2,1,0:T(8,128)(2,1)} collective-permute-done((bf16[1,2,64,512]{3,2,1,0:T(8,128)(2,1)S(1)}, bf16[1,2,64,512]{3,2,1,0:T(8,128)(2,1)}, u32[]{:S(2)}, u32[]{:S(2)}) %collective-permute-start.10) | collective-permute-done | bytes 131104 | tf_op jit(solution)/shard_map/ppermute | solution.py:37
  63.3 7.3 %collective-permute-done.11 = bf16[2,2,64,512]{3,2,1,0:T(8,128)(2,1)S(1)} collective-permute-done((bf16[2,2,64,512]{3,2,1,0:T(8,128)(2,1)S(1)}, bf16[2,2,64,512]{3,2,1,0:T(8,128)(2,1)S(1)}, u32[]{:S(2)}, u32[]{:S(2)}) %collective-permute-start.11) | collective-permute-done | bytes 262176 | tf_op jit(solution)/shard_map/ppermute | solution.py:37
  71.4 3.1 %pad_maximum_fusion.kvb = bf16[2,512,1024]{2,1,0:T(8,128)(2,1)} fusion(bf16[1,512,1024]{2,1,0:T(8,128)(2,1)} %bitcast.19, bf16[1,512,1024]{2,1,0:T(8,128)(2,1)} %bitcast.18), kind=kLoop, calls=%fused_computation | loop fusion | flops 1048576 | bytes 4194304 | tf_op jit(solution)/shard_map/stack | solution.py:636
  74.5 5.8 %collective-permute-done.13.there = bf16[4,128,1024]{2,1,0:T(8,128)(2,1)S(1)} collective-permute-done((bf16[4,128,1024]{2,1,0:T(8,128)(2,1)S(1)}, bf16[4,128,1024]{2,1,0:T(8,128)(2,1)S(1)}, u32[]{:S(2)}, u32[]{:S(2)}) %collective-permute-start.13) | collective-permute-done | bytes 1048608 | tf_op jit(solution)/shard_map/ppermute | solution.py:37
  81.4 5.2 %lift.1 = (bf16[512,1024]{1,0:T(8,128)(2,1)S(1)}, f32[4,128]{1,0:T(4,128)S(1)}, bf16[512,1024]{1,0:T(8,128)(2,1)S(1)}, bf16[512,1024]{1,0:T(8,128)(2,1)S(1)}) custom-call(s32[5]{0:T(128)S(1)} %stack.49.at, bf16[512,512]{1,0:T(8,128)(2,1)S(1)} %bitcast.74, bf16[512,512]{1,0:T(8,128)(2,1)S(1)} %collective-permute-done.12.tb, ...), custom_call_target="tpu_custom_call" | custom-call | tf_op jit(solution)/shard_map/lift/pallas_call | solution.py:414
  88.1 2.9 %keep_columns.1 = bf16[512,1024]{1,0:T(8,128)(2,1)S(1)} custom-call(s32[5]{0:T(128)S(1)} %stack.49.at, bf16[512,1024]{1,0:T(8,128)(2,1)S(1)} %get-tuple-element.111.low, bf16[512,2048]{1,0:T(8,128)(2,1)S(1)} %copy-done.2, bf16[2,512,1024]{2,1,0:T(8,128)(2,1)} %pad_maximum_fusion.kvb), custom_call_target="tpu_custom_call" | custom-call | tf_op jit(solution)/shard_map/keep_columns/pallas_call | solution.py:437
  97.2 3.6 %collective-permute-done.16 = bf16[2,128,512]{2,1,0:T(8,128)(2,1)S(1)} collective-permute-done((bf16[2,128,512]{2,1,0:T(8,128)(2,1)S(1)}, bf16[2,128,512]{2,1,0:T(8,128)(2,1)S(1)}, u32[]{:S(2)}, u32[]{:S(2)}) %collective-permute-start.16) | collective-permute-done | bytes 262176 | tf_op jit(solution)/shard_map/ppermute | solution.py:37
  103.5 4.7 %collective-permute-done.18 = bf16[2,128,512]{2,1,0:T(8,128)(2,1)S(1)} collective-permute-done((bf16[2,128,512]{2,1,0:T(8,128)(2,1)S(1)}, bf16[2,128,512]{2,1,0:T(8,128)(2,1)S(1)}, u32[]{:S(2)}, u32[]{:S(2)}) %collective-permute-start.18) | collective-permute-done | bytes 262176 | tf_op jit(solution)/shard_map/ppermute | solution.py:37
  111.7 8.2 %collective-permute-done.22 = bf16[1,128,512]{2,1,0:T(8,128)(2,1)S(1)} collective-permute-done((bf16[1,128,512]{2,1,0:T(8,128)(2,1)S(1)}, bf16[1,128,512]{2,1,0:T(8,128)(2,1)S(1)}, u32[]{:S(2)}, u32[]{:S(2)}) %collective-permute-start.22) | collective-permute-done | bytes 131104 | tf_op jit(solution)/shard_map/ppermute | solution.py:37
  123.8 5.1 %collective-permute-done.25 = bf16[1,128,640]{2,1,0:T(8,128)(2,1)S(1)} collective-permute-done((bf16[1,128,640]{2,1,0:T(8,128)(2,1)S(1)}, bf16[1,128,640]{2,1,0:T(8,128)(2,1)S(1)}, u32[]{:S(2)}, u32[]{:S(2)}) %collective-permute-start.25) | collective-permute-done | bytes 163872 | tf_op jit(solution)/shard_map/ppermute | solution.py:37
  128.9 3.7 %collective-permute-done.24 = bf16[2,128,512]{2,1,0:T(8,128)(2,1)S(1)} collective-permute-done((bf16[2,128,512]{2,1,0:T(8,128)(2,1)S(1)}, bf16[2,128,512]{2,1,0:T(8,128)(2,1)S(1)}, u32[]{:S(2)}, u32[]{:S(2)}) %collective-permute-start.24) | collective-permute-done | bytes 262176 | tf_op jit(solution)/shard_map/ppermute | solution.py:37
  132.7 5.9 %collective-permute-done.26 = bf16[2,128,640]{2,1,0:T(8,128)(2,1)S(1)} collective-permute-done((bf16[2,128,640]{2,1,0:T(8,128)(2,1)S(1)}, bf16[2,128,640]{2,1,0:T(8,128)(2,1)S(1)}, u32[]{:S(2)}, u32[]{:S(2)}) %collective-permute-start.26) | collective-permute-done | bytes 327712 | tf_op jit(solution)/shard_map/ppermute | solution.py:37
  141.7 6.4 %lower.1 = (bf16[512,512]{1,0:T(8,128)(2,1)S(1)}, bf16[512,512]{1,0:T(8,128)(2,1)S(1)}) custom-call(s32[5]{0:T(128)S(1)} %stack.49.at, bf16[512,512]{1,0:T(8,128)(2,1)S(1)} %bitcast.72, bf16[512,640]{1,0:T(8,128)(2,1)S(1)} %bitcast.70, bf16[512,512]{1,0:T(8,128)(2,1)S(1)} %collective-permute-done.27.cb0, bf16[512,640]{1,0:T(8,128)(2,1)S(1)} %collective-permute-done.28.cb1, ...), custom_call_target="tpu_custom_call" | custom-call | tf_op jit(solution)/shard_map/lower/pallas_call | solution.py:536
  150.5 8.2 %collective-permute-done.30 = bf16[2,2,64,512]{3,2,1,0:T(8,128)(2,1)S(1)} collective-permute-done((bf16[2,2,64,512]{3,2,1,0:T(8,128)(2,1)S(1)}, bf16[2,2,64,512]{3,2,1,0:T(8,128)(2,1)S(1)}, u32[]{:S(2)}, u32[]{:S(2)}) %collective-permute-start.30) | collective-permute-done | bytes 262176 | tf_op jit(solution)/shard_map/ppermute | solution.py:37
  158.8 3.3 %collective-permute-start.31 = (bf16[1,2,64,512]{3,2,1,0:T(8,128)(2,1)S(1)}, bf16[1,2,64,512]{3,2,1,0:T(8,128)(2,1)S(1)}, u32[]{:S(2)}, u32[]{:S(2)}) collective-permute-start(bf16[1,2,64,512]{3,2,1,0:T(8,128)(2,1)S(1)} %slice.211), channel_id=1, source_target_pairs={{0,8},{2,10},{4,12},{6,14},{8,0},{10,2},{12,4},{14,6},{1,9},{3,11}... | collective-permute-start | bytes 393224 | tf_op jit(solution)/shard_map/ppermute | solution.py:37
  162.1 6.1 %collective-permute-done.31 = bf16[1,2,64,512]{3,2,1,0:T(8,128)(2,1)S(1)} collective-permute-done((bf16[1,2,64,512]{3,2,1,0:T(8,128)(2,1)S(1)}, bf16[1,2,64,512]{3,2,1,0:T(8,128)(2,1)S(1)}, u32[]{:S(2)}, u32[]{:S(2)}) %collective-permute-start.31) | collective-permute-done | bytes 131104 | tf_op jit(solution)/shard_map/ppermute | solution.py:37
  169.5 3.1 %collective-permute-done.32 = bf16[64,512]{1,0:T(8,128)(2,1)S(1)} collective-permute-done((bf16[64,512]{1,0:T(8,128)(2,1)S(1)}, bf16[64,512]{1,0:T(8,128)(2,1)S(1)}, u32[]{:S(2)}, u32[]{:S(2)}) %collective-permute-start.32) | collective-permute-done | bytes 65568 | tf_op jit(solution)/shard_map/ppermute | solution.py:37
  172.9 4.2 %collective-permute-start.35 = (bf16[64,512]{1,0:T(8,128)(2,1)S(1)}, bf16[64,512]{1,0:T(8,128)(2,1)S(1)}, u32[]{:S(2)}, u32[]{:S(2)}) collective-permute-start(bf16[64,512]{1,0:T(8,128)(2,1)S(1)} %slice.214), channel_id=1, source_target_pairs={{0,15},{1,14},{2,1},{3,0},{4,3},{5,2},{6,5},{7,4},{8,7},{9,6},{10,... | collective-permute-start | bytes 196616 | tf_op jit(solution)/shard_map/ppermute | solution.py:51
  183.2 2.8 %encoder_backward.4 = (bf16[4,3,128,128]{3,2,1,0:T(8,128)(2,1)S(1)}, bf16[4,3,128,128]{3,2,1,0:T(8,128)(2,1)S(1)}) custom-call(s32[5]{0:T(128)S(1)} %stack.49.at, bf16[1024,512]{1,0:T(8,128)(2,1)S(1)} %bitcast.65, bf16[3,512,512]{2,1,0:T(8,128)(2,1)S(1)} %copy-done.3, bf16[4,2,2,256,256]{4,3,2,1,0:T(8,128)(2,1)S(1)} %copy-done.1, ...), custom_call_target="tpu_custom_call" | custom-call | tf_op jit(solution)/shard_map/encoder_backward/pallas_call | solution.py:317
  188.0 2.8 %encoder_backward.5 = (bf16[4,3,128,128]{3,2,1,0:T(8,128)(2,1)S(1)}, bf16[4,3,128,128]{3,2,1,0:T(8,128)(2,1)S(1)}) custom-call(s32[5]{0:T(128)S(1)} %stack.49.at, bf16[1024,512]{1,0:T(8,128)(2,1)S(1)} %bitcast.66, bf16[3,512,512]{2,1,0:T(8,128)(2,1)S(1)} %copy-done.3, bf16[4,2,2,256,256]{4,3,2,1,0:T(8,128)(2,1)S(1)} %copy-done.1, ...), custom_call_target="tpu_custom_call" | custom-call | tf_op jit(solution)/shard_map/encoder_backward/pallas_call | solution.py:317
  190.8 2.8 %encoder_backward.6 = (bf16[4,3,128,128]{3,2,1,0:T(8,128)(2,1)S(1)}, bf16[4,3,128,128]{3,2,1,0:T(8,128)(2,1)S(1)}) custom-call(s32[5]{0:T(128)S(1)} %stack.49.at, bf16[1024,512]{1,0:T(8,128)(2,1)S(1)} %bitcast.67, bf16[3,512,512]{2,1,0:T(8,128)(2,1)S(1)} %copy-done.3, bf16[4,2,2,256,256]{4,3,2,1,0:T(8,128)(2,1)S(1)} %copy-done.1, ...), custom_call_target="tpu_custom_call" | custom-call | tf_op jit(solution)/shard_map/encoder_backward/pallas_call | solution.py:317
  201.2 5.2 %collective-permute-done.36 = bf16[4,3,128,128]{3,2,1,0:T(8,128)(2,1)S(1)} collective-permute-done((bf16[4,3,128,128]{3,2,1,0:T(8,128)(2,1)S(1)}, bf16[4,3,128,128]{3,2,1,0:T(8,128)(2,1)S(1)}, u32[]{:S(2)}, u32[]{:S(2)}) %collective-permute-start.36) | collective-permute-done | bytes 393248 | tf_op jit(solution)/shard_map/ppermute | solution.py:37
  208.7 6.1 %collective-permute-done.39 = bf16[4,3,128,128]{3,2,1,0:T(8,128)(2,1)S(1)} collective-permute-done((bf16[4,3,128,128]{3,2,1,0:T(8,128)(2,1)S(1)}, bf16[4,3,128,128]{3,2,1,0:T(8,128)(2,1)S(1)}, u32[]{:S(2)}, u32[]{:S(2)}) %collective-permute-start.39) | collective-permute-done | bytes 393248 | tf_op jit(solution)/shard_map/ppermute | solution.py:37
  218.5 3.8 %collective-permute-done.50 = bf16[1,64,1024]{2,1,0:T(8,128)(2,1)S(1)} collective-permute-done((bf16[1,64,1024]{2,1,0:T(8,128)(2,1)S(1)}, bf16[1,64,1024]{2,1,0:T(8,128)(2,1)S(1)}, u32[]{:S(2)}, u32[]{:S(2)}) %collective-permute-start.50) | collective-permute-done | bytes 131104 | tf_op jit(solution)/shard_map/ppermute | solution.py:37
  222.3 3.3 %collective-permute-done.43 = bf16[4,3,128,128]{3,2,1,0:T(8,128)(2,1)S(1)} collective-permute-done((bf16[4,3,128,128]{3,2,1,0:T(8,128)(2,1)S(1)}, bf16[4,3,128,128]{3,2,1,0:T(8,128)(2,1)S(1)}, u32[]{:S(2)}, u32[]{:S(2)}) %collective-permute-start.43) | collective-permute-done | bytes 393248 | tf_op jit(solution)/shard_map/ppermute | solution.py:37
  226.8 3.4 %collective-permute-start.46 = (bf16[2,3,128,128]{3,2,1,0:T(8,128)(2,1)S(1)}, bf16[2,3,128,128]{3,2,1,0:T(8,128)(2,1)S(1)}, u32[]{:S(2)}, u32[]{:S(2)}) collective-permute-start(bf16[2,3,128,128]{3,2,1,0:T(8,128)(2,1)S(1)} %slice.226), channel_id=1, source_target_pairs={{0,4},{2,6},{4,0},{6,2},{8,12},{10,14},{12,8},{14,10},{1,5},{3,7},... | collective-permute-start | bytes 589832 | tf_op jit(solution)/shard_map/ppermute | solution.py:37
  230.2 3.1 %collective-permute-start.45 = (bf16[1,3,128,128]{3,2,1,0:T(8,128)(2,1)S(1)}, bf16[1,3,128,128]{3,2,1,0:T(8,128)(2,1)S(1)}, u32[]{:S(2)}, u32[]{:S(2)}) collective-permute-start(bf16[1,3,128,128]{3,2,1,0:T(8,128)(2,1)S(1)} %slice.224), channel_id=1, source_target_pairs={{0,8},{2,10},{4,12},{6,14},{8,0},{10,2},{12,4},{14,6},{1,9},{3,11}... | collective-permute-start | bytes 294920 | tf_op jit(solution)/shard_map/ppermute | solution.py:37
  (204 shorter events, 88.5 us)
Async XLA Ops:
  2.4 18.1 %collective-permute-start = (bf16[128,1024]{1,0:T(8,128)(2,1)}, bf16[128,1024]{1,0:T(8,128)(2,1)}, u32[]{:S(2)}, u32[]{:S(2)}) collective-permute-start(bf16[128,1024]{1,0:T(8,128)(2,1)} %constant_dynamic-slice_fusion.6), channel_id=1, source_target_pairs={{0,14},{1,15},{2,0},{3,1},{4,2},{5,3},{6,4},{7,5},{8,6},{9,7},{10,... | collective-permute-start | bytes 786440 | tf_op jit(solution)/shard_map/ppermute | solution.py:51
  10.7 32.0 %collective-permute-start.4 = (bf16[512,1024]{1,0:T(8,128)(2,1)}, bf16[512,1024]{1,0:T(8,128)(2,1)}, u32[]{:S(2)}, u32[]{:S(2)}) collective-permute-start(bf16[512,1024]{1,0:T(8,128)(2,1)} %constant_dynamic-slice_fusion.4), channel_id=1, source_target_pairs={{0,2},{2,0},{4,6},{6,4},{8,10},{10,8},{12,14},{14,12},{1,3},{3,1},... | collective-permute-start | bytes 3145736 | tf_op jit(solution)/shard_map/ppermute | solution.py:37
  16.1 26.9 %collective-permute-start.8 = (bf16[128,1024]{1,0:T(8,128)(2,1)}, bf16[128,1024]{1,0:T(8,128)(2,1)}, u32[]{:S(2)}, u32[]{:S(2)}) collective-permute-start(bf16[128,1024]{1,0:T(8,128)(2,1)} %get-tuple-element.173), channel_id=1, source_target_pairs={{0,12},{2,14},{4,8},{6,10},{8,4},{10,6},{12,0},{14,2},{1,13},{3,15... | collective-permute-start | bytes 786440 | tf_op jit(solution)/shard_map/ppermute | solution.py:37
  17.1 26.5 %collective-permute-start.7 = (bf16[128,1024]{1,0:T(8,128)(2,1)}, bf16[128,1024]{1,0:T(8,128)(2,1)}, u32[]{:S(2)}, u32[]{:S(2)}) collective-permute-start(bf16[128,1024]{1,0:T(8,128)(2,1)} %get-tuple-element.174), channel_id=1, source_target_pairs={{0,4},{2,6},{4,0},{6,2},{8,12},{10,14},{12,8},{14,10},{1,5},{3,7},... | collective-permute-start | bytes 786440 | tf_op jit(solution)/shard_map/ppermute | solution.py:37
  17.1 28.1 %collective-permute-start.6 = (bf16[128,1024]{1,0:T(8,128)(2,1)}, bf16[128,1024]{1,0:T(8,128)(2,1)}, u32[]{:S(2)}, u32[]{:S(2)}) collective-permute-start(bf16[128,1024]{1,0:T(8,128)(2,1)} %get-tuple-element.175), channel_id=1, source_target_pairs={{0,8},{2,10},{4,12},{6,14},{8,0},{10,2},{12,4},{14,6},{1,9},{3,11}... | collective-permute-start | bytes 786440 | tf_op jit(solution)/shard_map/ppermute | solution.py:37
  39.9 7.4 %collective-permute-start.2 = (bf16[64,512]{1,0:T(8,128)(2,1)}, bf16[64,512]{1,0:T(8,128)(2,1)S(1)}, u32[]{:S(2)}, u32[]{:S(2)}) collective-permute-start(bf16[64,512]{1,0:T(8,128)(2,1)} %get-tuple-element.91), channel_id=1, source_target_pairs={{0,2},{1,3},{2,4},{3,5},{4,6},{5,7},{6,8},{7,9},{8,10},{9,11},{10,... | collective-permute-start | bytes 196616 | tf_op jit(solution)/shard_map/ppermute | solution.py:51
  43.7 27.7 %collective-permute-start.14 = (bf16[512,1024]{1,0:T(8,128)(2,1)}, bf16[512,1024]{1,0:T(8,128)(2,1)}, u32[]{:S(2)}, u32[]{:S(2)}) collective-permute-start(bf16[512,1024]{1,0:T(8,128)(2,1)} %collective-permute-done.4), channel_id=1, source_target_pairs={{0,16},{16,0},{1,17},{17,1},{2,18},{18,2},{3,19},{19,3},{4,20},{20... | collective-permute-start | bytes 3145736 | tf_op jit(solution)/shard_map/ppermute | solution.py:592
  55.9 24.5 %collective-permute-start.13 = (bf16[4,128,1024]{2,1,0:T(8,128)(2,1)S(1)}, bf16[4,128,1024]{2,1,0:T(8,128)(2,1)S(1)}, u32[]{:S(2)}, u32[]{:S(2)}) collective-permute-start(bf16[4,128,1024]{2,1,0:T(8,128)(2,1)S(1)} %pad_maximum_fusion.1.here), channel_id=1, source_target_pairs={{0,2},{2,0},{4,6},{6,4},{8,10},{10,8},{12,14},{14,12},{1,3},{3,1},... | collective-permute-start | bytes 3145736 | tf_op jit(solution)/shard_map/ppermute | solution.py:37
  63.2 7.4 %collective-permute-start.11 = (bf16[2,2,64,512]{3,2,1,0:T(8,128)(2,1)S(1)}, bf16[2,2,64,512]{3,2,1,0:T(8,128)(2,1)S(1)}, u32[]{:S(2)}, u32[]{:S(2)}) collective-permute-start(bf16[2,2,64,512]{3,2,1,0:T(8,128)(2,1)S(1)} %pad_maximum_fusion.6), channel_id=1, source_target_pairs={{0,4},{2,6},{4,0},{6,2},{8,12},{10,14},{12,8},{14,10},{1,5},{3,7},... | collective-permute-start | bytes 786440 | tf_op jit(solution)/shard_map/ppermute | solution.py:37
  91.5 9.3 %collective-permute-start.16 = (bf16[2,128,512]{2,1,0:T(8,128)(2,1)S(1)}, bf16[2,128,512]{2,1,0:T(8,128)(2,1)S(1)}, u32[]{:S(2)}, u32[]{:S(2)}) collective-permute-start(bf16[2,128,512]{2,1,0:T(8,128)(2,1)S(1)} %get-tuple-element.171), channel_id=1, source_target_pairs={{0,4},{2,6},{4,0},{6,2},{8,12},{10,14},{12,8},{14,10},{1,5},{3,7},... | collective-permute-start | bytes 786440 | tf_op jit(solution)/shard_map/ppermute | solution.py:37
  94.6 14.7 %collective-permute-start.21 = (f32[1,128]{1,0:T(1,128)S(1)}, f32[1,128]{1,0:T(1,128)S(1)}, u32[]{:S(2)}, u32[]{:S(2)}) collective-permute-start(f32[1,128]{1,0:T(1,128)S(1)} %slice.165), channel_id=1, source_target_pairs={{0,8},{2,10},{4,12},{6,14},{8,0},{10,2},{12,4},{14,6},{1,9},{3,11}... | collective-permute-start | bytes 1544 | tf_op jit(solution)/shard_map/ppermute | solution.py:37
  97.2 11.1 %collective-permute-start.18 = (bf16[2,128,512]{2,1,0:T(8,128)(2,1)S(1)}, bf16[2,128,512]{2,1,0:T(8,128)(2,1)S(1)}, u32[]{:S(2)}, u32[]{:S(2)}) collective-permute-start(bf16[2,128,512]{2,1,0:T(8,128)(2,1)S(1)} %get-tuple-element.172), channel_id=1, source_target_pairs={{0,4},{2,6},{4,0},{6,2},{8,12},{10,14},{12,8},{14,10},{1,5},{3,7},... | collective-permute-start | bytes 786440 | tf_op jit(solution)/shard_map/ppermute | solution.py:37
  100.9 8.5 %collective-permute-start.17 = (bf16[1,128,512]{2,1,0:T(8,128)(2,1)S(1)}, bf16[1,128,512]{2,1,0:T(8,128)(2,1)S(1)}, u32[]{:S(2)}, u32[]{:S(2)}) collective-permute-start(bf16[1,128,512]{2,1,0:T(8,128)(2,1)S(1)} %get-tuple-element.182), channel_id=1, source_target_pairs={{0,8},{2,10},{4,12},{6,14},{8,0},{10,2},{12,4},{14,6},{1,9},{3,11}... | collective-permute-start | bytes 393224 | tf_op jit(solution)/shard_map/ppermute | solution.py:37
  108.4 11.6 %collective-permute-start.22 = (bf16[1,128,512]{2,1,0:T(8,128)(2,1)S(1)}, bf16[1,128,512]{2,1,0:T(8,128)(2,1)S(1)}, u32[]{:S(2)}, u32[]{:S(2)}) collective-permute-start(bf16[1,128,512]{2,1,0:T(8,128)(2,1)S(1)} %get-tuple-element.183), channel_id=1, source_target_pairs={{0,8},{2,10},{4,12},{6,14},{8,0},{10,2},{12,4},{14,6},{1,9},{3,11}... | collective-permute-start | bytes 393224 | tf_op jit(solution)/shard_map/ppermute | solution.py:37
  109.7 12.7 %collective-permute-start.23 = (bf16[1,128,512]{2,1,0:T(8,128)(2,1)S(1)}, bf16[1,128,512]{2,1,0:T(8,128)(2,1)S(1)}, u32[]{:S(2)}, u32[]{:S(2)}) collective-permute-start(bf16[1,128,512]{2,1,0:T(8,128)(2,1)S(1)} %bitcast.78), channel_id=1, source_target_pairs={{0,8},{2,10},{4,12},{6,14},{8,0},{10,2},{12,4},{14,6},{1,9},{3,11}... | collective-permute-start | bytes 393224 | tf_op jit(solution)/shard_map/ppermute | solution.py:37
  120.9 7.9 %collective-permute-start.25 = (bf16[1,128,640]{2,1,0:T(8,128)(2,1)S(1)}, bf16[1,128,640]{2,1,0:T(8,128)(2,1)S(1)}, u32[]{:S(2)}, u32[]{:S(2)}) collective-permute-start(bf16[1,128,640]{2,1,0:T(8,128)(2,1)S(1)} %bitcast.75), channel_id=1, source_target_pairs={{0,8},{2,10},{4,12},{6,14},{8,0},{10,2},{12,4},{14,6},{1,9},{3,11}... | collective-permute-start | bytes 491528 | tf_op jit(solution)/shard_map/ppermute | solution.py:37
  122.4 10.2 %collective-permute-start.24 = (bf16[2,128,512]{2,1,0:T(8,128)(2,1)S(1)}, bf16[2,128,512]{2,1,0:T(8,128)(2,1)S(1)}, u32[]{:S(2)}, u32[]{:S(2)}) collective-permute-start(bf16[2,128,512]{2,1,0:T(8,128)(2,1)S(1)} %pad_maximum_fusion.7), channel_id=1, source_target_pairs={{0,4},{2,6},{4,0},{6,2},{8,12},{10,14},{12,8},{14,10},{1,5},{3,7},... | collective-permute-start | bytes 786440 | tf_op jit(solution)/shard_map/ppermute | solution.py:37
  128.8 9.8 %collective-permute-start.26 = (bf16[2,128,640]{2,1,0:T(8,128)(2,1)S(1)}, bf16[2,128,640]{2,1,0:T(8,128)(2,1)S(1)}, u32[]{:S(2)}, u32[]{:S(2)}) collective-permute-start(bf16[2,128,640]{2,1,0:T(8,128)(2,1)S(1)} %pad_maximum_fusion.5), channel_id=1, source_target_pairs={{0,4},{2,6},{4,0},{6,2},{8,12},{10,14},{12,8},{14,10},{1,5},{3,7},... | collective-permute-start | bytes 983048 | tf_op jit(solution)/shard_map/ppermute | solution.py:37
  150.3 8.4 %collective-permute-start.30 = (bf16[2,2,64,512]{3,2,1,0:T(8,128)(2,1)S(1)}, bf16[2,2,64,512]{3,2,1,0:T(8,128)(2,1)S(1)}, u32[]{:S(2)}, u32[]{:S(2)}) collective-permute-start(bf16[2,2,64,512]{3,2,1,0:T(8,128)(2,1)S(1)} %bitcast.91), channel_id=1, source_target_pairs={{0,4},{2,6},{4,0},{6,2},{8,12},{10,14},{12,8},{14,10},{1,5},{3,7},... | collective-permute-start | bytes 786440 | tf_op jit(solution)/shard_map/ppermute | solution.py:37
  158.8 9.4 %collective-permute-start.31 = (bf16[1,2,64,512]{3,2,1,0:T(8,128)(2,1)S(1)}, bf16[1,2,64,512]{3,2,1,0:T(8,128)(2,1)S(1)}, u32[]{:S(2)}, u32[]{:S(2)}) collective-permute-start(bf16[1,2,64,512]{3,2,1,0:T(8,128)(2,1)S(1)} %slice.211), channel_id=1, source_target_pairs={{0,8},{2,10},{4,12},{6,14},{8,0},{10,2},{12,4},{14,6},{1,9},{3,11}... | collective-permute-start | bytes 393224 | tf_op jit(solution)/shard_map/ppermute | solution.py:37
  183.1 14.9 %collective-permute-start.37 = (bf16[4,64,1024]{2,1,0:T(8,128)(2,1)S(1)}, bf16[4,64,1024]{2,1,0:T(8,128)(2,1)S(1)}, u32[]{:S(2)}, u32[]{:S(2)}) collective-permute-start(bf16[4,64,1024]{2,1,0:T(8,128)(2,1)S(1)} %get-tuple-element.146), channel_id=1, source_target_pairs={{0,2},{2,0},{4,6},{6,4},{8,10},{10,8},{12,14},{14,12},{1,3},{3,1},... | collective-permute-start | bytes 1572872 | tf_op jit(solution)/shard_map/ppermute | solution.py:37
  185.9 20.5 %collective-permute-start.36 = (bf16[4,3,128,128]{3,2,1,0:T(8,128)(2,1)S(1)}, bf16[4,3,128,128]{3,2,1,0:T(8,128)(2,1)S(1)}, u32[]{:S(2)}, u32[]{:S(2)}) collective-permute-start(bf16[4,3,128,128]{3,2,1,0:T(8,128)(2,1)S(1)} %get-tuple-element.137), channel_id=1, source_target_pairs={{0,2},{2,0},{4,6},{6,4},{8,10},{10,8},{12,14},{14,12},{1,3},{3,1},... | collective-permute-start | bytes 1179656 | tf_op jit(solution)/shard_map/ppermute | solution.py:37
  198.2 10.4 %collective-permute-start.40 = (bf16[2,64,1024]{2,1,0:T(8,128)(2,1)S(1)}, bf16[2,64,1024]{2,1,0:T(8,128)(2,1)S(1)}, u32[]{:S(2)}, u32[]{:S(2)}) collective-permute-start(bf16[2,64,1024]{2,1,0:T(8,128)(2,1)S(1)} %slice.218), channel_id=1, source_target_pairs={{0,4},{2,6},{4,0},{6,2},{8,12},{10,14},{12,8},{14,10},{1,5},{3,7},... | collective-permute-start | bytes 786440 | tf_op jit(solution)/shard_map/ppermute | solution.py:37
  199.2 15.6 %collective-permute-start.39 = (bf16[4,3,128,128]{3,2,1,0:T(8,128)(2,1)S(1)}, bf16[4,3,128,128]{3,2,1,0:T(8,128)(2,1)S(1)}, u32[]{:S(2)}, u32[]{:S(2)}) collective-permute-start(bf16[4,3,128,128]{3,2,1,0:T(8,128)(2,1)S(1)} %get-tuple-element.152), channel_id=1, source_target_pairs={{0,2},{2,0},{4,6},{6,4},{8,10},{10,8},{12,14},{14,12},{1,3},{3,1},... | collective-permute-start | bytes 1179656 | tf_op jit(solution)/shard_map/ppermute | solution.py:37
  199.3 27.3 %collective-permute-start.42 = (bf16[4,3,128,128]{3,2,1,0:T(8,128)(2,1)S(1)}, bf16[4,3,128,128]{3,2,1,0:T(8,128)(2,1)S(1)}, u32[]{:S(2)}, u32[]{:S(2)}) collective-permute-start(bf16[4,3,128,128]{3,2,1,0:T(8,128)(2,1)S(1)} %get-tuple-element.159), channel_id=1, source_target_pairs={{0,2},{2,0},{4,6},{6,4},{8,10},{10,8},{12,14},{14,12},{1,3},{3,1},... | collective-permute-start | bytes 1179656 | tf_op jit(solution)/shard_map/ppermute | solution.py:37
  206.5 8.4 %collective-permute-start.38 = (bf16[2,3,128,128]{3,2,1,0:T(8,128)(2,1)S(1)}, bf16[2,3,128,128]{3,2,1,0:T(8,128)(2,1)S(1)}, u32[]{:S(2)}, u32[]{:S(2)}) collective-permute-start(bf16[2,3,128,128]{3,2,1,0:T(8,128)(2,1)S(1)} %slice.216), channel_id=1, source_target_pairs={{0,4},{2,6},{4,0},{6,2},{8,12},{10,14},{12,8},{14,10},{1,5},{3,7},... | collective-permute-start | bytes 589832 | tf_op jit(solution)/shard_map/ppermute | solution.py:37
  206.6 19.0 %collective-permute-start.43 = (bf16[4,3,128,128]{3,2,1,0:T(8,128)(2,1)S(1)}, bf16[4,3,128,128]{3,2,1,0:T(8,128)(2,1)S(1)}, u32[]{:S(2)}, u32[]{:S(2)}) collective-permute-start(bf16[4,3,128,128]{3,2,1,0:T(8,128)(2,1)S(1)} %get-tuple-element.160), channel_id=1, source_target_pairs={{0,4},{2,6},{4,0},{6,2},{8,12},{10,14},{12,8},{14,10},{1,5},{3,7},... | collective-permute-start | bytes 1179656 | tf_op jit(solution)/shard_map/ppermute | solution.py:37
  215.0 7.3 %collective-permute-start.50 = (bf16[1,64,1024]{2,1,0:T(8,128)(2,1)S(1)}, bf16[1,64,1024]{2,1,0:T(8,128)(2,1)S(1)}, u32[]{:S(2)}, u32[]{:S(2)}) collective-permute-start(bf16[1,64,1024]{2,1,0:T(8,128)(2,1)S(1)} %slice.234), channel_id=1, source_target_pairs={{0,8},{2,10},{4,12},{6,14},{8,0},{10,2},{12,4},{14,6},{1,9},{3,11}... | collective-permute-start | bytes 393224 | tf_op jit(solution)/shard_map/ppermute | solution.py:37
  215.7 11.0 %collective-permute-start.41 = (bf16[1,3,128,128]{3,2,1,0:T(8,128)(2,1)S(1)}, bf16[1,3,128,128]{3,2,1,0:T(8,128)(2,1)S(1)}, u32[]{:S(2)}, u32[]{:S(2)}) collective-permute-start(bf16[1,3,128,128]{3,2,1,0:T(8,128)(2,1)S(1)} %slice.220), channel_id=1, source_target_pairs={{0,8},{2,10},{4,12},{6,14},{8,0},{10,2},{12,4},{14,6},{1,9},{3,11}... | collective-permute-start | bytes 294920 | tf_op jit(solution)/shard_map/ppermute | solution.py:37
  218.1 12.0 %collective-permute-start.44 = (bf16[2,3,128,128]{3,2,1,0:T(8,128)(2,1)S(1)}, bf16[2,3,128,128]{3,2,1,0:T(8,128)(2,1)S(1)}, u32[]{:S(2)}, u32[]{:S(2)}) collective-permute-start(bf16[2,3,128,128]{3,2,1,0:T(8,128)(2,1)S(1)} %slice.222), channel_id=1, source_target_pairs={{0,4},{2,6},{4,0},{6,2},{8,12},{10,14},{12,8},{14,10},{1,5},{3,7},... | collective-permute-start | bytes 589832 | tf_op jit(solution)/shard_map/ppermute | solution.py:37
  225.8 7.6 %collective-permute-start.47 = (bf16[2,3,128,128]{3,2,1,0:T(8,128)(2,1)S(1)}, bf16[2,3,128,128]{3,2,1,0:T(8,128)(2,1)S(1)}, u32[]{:S(2)}, u32[]{:S(2)}) collective-permute-start(bf16[2,3,128,128]{3,2,1,0:T(8,128)(2,1)S(1)} %slice.228), channel_id=1, source_target_pairs={{0,2},{2,0},{4,6},{6,4},{8,10},{10,8},{12,14},{14,12},{1,3},{3,1},... | collective-permute-start | bytes 589832 | tf_op jit(solution)/shard_map/ppermute | solution.py:37
  226.8 9.6 %collective-permute-start.46 = (bf16[2,3,128,128]{3,2,1,0:T(8,128)(2,1)S(1)}, bf16[2,3,128,128]{3,2,1,0:T(8,128)(2,1)S(1)}, u32[]{:S(2)}, u32[]{:S(2)}) collective-permute-start(bf16[2,3,128,128]{3,2,1,0:T(8,128)(2,1)S(1)} %slice.226), channel_id=1, source_target_pairs={{0,4},{2,6},{4,0},{6,2},{8,12},{10,14},{12,8},{14,10},{1,5},{3,7},... | collective-permute-start | bytes 589832 | tf_op jit(solution)/shard_map/ppermute | solution.py:37
  (39 other events, 397.7 us)
